TPU v7x, 32 devices: a whole 2x2x4 slice. The times are simulated.
32 devices in a mesh: dp: 2 (over y), row: 4 (over z), col: 4 (over x, core).
Axes of the slice: x: 2, y: 2, z: 4, core: 2. Of those that a mesh axis runs over, the one named last changes fastest.
Arguments:
- tokens: bfloat16 [6144, 2048], P(('dp', 'row'), 'col'), may hold values from -6 to 6
- seq_lengths: int32 [2], P('dp'), may hold values from 1024 to 3072, as said below
- w_query: bfloat16 [2048, 2048], P('row', 'col')
- w_key: bfloat16 [2048, 2048], P('row', 'col')
- w_value: bfloat16 [2048, 2048], P('row', 'col'), may hold values from -0.125 to 0.125
- w_out: bfloat16 [2048, 2048], P('col', 'row')
- w_gate: bfloat16 [2048, 8192], P('row', 'col'), may hold values from -0.125 to 0.125
- w_up: bfloat16 [2048, 8192], P('row', 'col'), may hold values from -0.125 to 0.125
- w_down: bfloat16 [8192, 2048], P('col', 'row')
- q_gain: float32 [2048], P('col')
- k_gain: float32 [2048], P('col')
- attn_gain: float32 [2048], P('col'), may hold values from 0.25 to 1.75
- mlp_gain: float32 [2048], P('col'), may hold values from 0.25 to 1.75
- cotangent: bfloat16 [6144, 2048], P(('dp', 'row'), 'col'), may hold values from -6 to 6
Outputs:
- block_output: bfloat16 [6144, 2048], P(('dp', 'row'), 'col')
- input_grad: float32 [6144, 2048], P(('dp', 'row'), 'col')
- w_query_grad: float32 [2048, 2048], P('row', 'col')
- w_key_grad: float32 [2048, 2048], P('row', 'col')
- w_value_grad: float32 [2048, 2048], P('row', 'col')
- w_out_grad: float32 [2048, 2048], P('col', 'row')
- w_gate_grad: float32 [2048, 8192], P('row', 'col')
- w_up_grad: float32 [2048, 8192], P('row', 'col')
- w_down_grad: float32 [8192, 2048], P('col', 'row')
- q_gain_grad: float32 [2048], P('col')
- k_gain_grad: float32 [2048], P('col')
- attn_gain_grad: float32 [2048], P('col')
- mlp_gain_grad: float32 [2048], P('col')
Inputs may be any that keep to these rules, and one draw needn't show every extreme that they name: `seq_lengths`: the valid tokens of a sequence fill its first slots; some sequence is full.
All inputs are finite; a program needn't handle non-finite values.
Results may differ from a plain program's by a relative error of at most 0.022.
Values may be sent and summed in bfloat16 or wider, within the bound.
A program may use at most 256 MiB of HBM per device.

v0:
```python
import math

import jax
import jax.numpy as jnp
from jax import lax
from jax.sharding import PartitionSpec as P

HEAD_DIM = 128


rope_base = 500000.0
norm_eps = 1e-06
masked_score = -1e30


def rope_tables(positions, head_dim):
    half = head_dim // 2
    freq = 1.0 / rope_base ** (jnp.arange(half, dtype=jnp.float32) / half)
    angle = positions.astype(jnp.float32)[:, None] * freq[None, :]
    angle = jnp.concatenate([angle, angle], axis=1)
    return (jnp.cos(angle), jnp.sin(angle))


def rotate(values, cosine, sine, head_dim):
    count = values.shape[0]
    heads = values.reshape(count, -1, head_dim)
    half = head_dim // 2
    turned = jnp.concatenate([-heads[..., half:], heads[..., :half]], axis=-1)
    return (heads * cosine[:, None, :] + turned * sine[:, None, :]).reshape(count, -1)


def unrotate(values, cosine, sine, head_dim):
    count = values.shape[0]
    heads = values.reshape(count, -1, head_dim)
    half = head_dim // 2
    turned = heads * sine[:, None, :]
    back = jnp.concatenate([turned[..., half:], -turned[..., :half]], axis=-1)
    return (heads * cosine[:, None, :] + back).reshape(count, -1)


def matmul(left, right):
    return jnp.dot(left, right, preferred_element_type=jnp.float32)


def contract_first(left, right):
    return lax.dot_general(
        left, right, (((0,), (0,)), ((), ())), preferred_element_type=jnp.float32
    )


def contract_last(left, right):
    return lax.dot_general(
        left, right, (((1,), (1,)), ((), ())), preferred_element_type=jnp.float32
    )


def widen(values):
    return lax.all_gather(values, "col", axis=1, tiled=True)


def widen_back(values):
    return lax.all_gather(values, "col", axis=1, tiled=True)


def narrow(values):
    return lax.psum_scatter(values, "col", scatter_dimension=1, tiled=True)


def narrow_back(values):
    return lax.psum_scatter(values, "col", scatter_dimension=1, tiled=True)


def feature_total(values):
    return lax.psum(values, "col")


def back_total(values):
    return lax.psum(values, "col")


def reorder(values, row_count, data_count):
    leading, columns = values.shape
    shaped = values.reshape(leading, row_count, data_count, columns // (row_count * data_count))
    return shaped.transpose(0, 2, 1, 3).reshape(leading, columns)


def per_device(
    tokens,
    seq_lengths,
    w_query,
    w_key,
    w_value,
    w_out,
    w_gate,
    w_up,
    w_down,
    q_gain,
    k_gain,
    attn_gain,
    mlp_gain,
    cotangent,
):
    tok_rows = tokens.shape[0]
    feat_part = tokens.shape[1]
    row_count = lax.axis_size("row")
    data_count = lax.axis_size("dp")
    width = feat_part * lax.axis_size("col")
    seq_slots = tok_rows * row_count
    head_count = feat_part // HEAD_DIM
    score_scale = HEAD_DIM ** (-0.5)
    length = seq_lengths[0]
    positions = lax.axis_index("row") * tok_rows + jnp.arange(tok_rows)
    valid = (positions < length).astype(jnp.float32)[:, None]
    key_positions = jnp.arange(seq_slots)
    allowed = (key_positions[None, :] <= positions[:, None]) & (key_positions[None, :] < length)
    cosine, sine = rope_tables(positions, HEAD_DIM)
    query_weight, key_weight, value_weight, gate_weight, up_weight, out_weight, down_weight = (
        lax.all_gather(w_query, "row", axis=0, tiled=True),
        lax.all_gather(w_key, "row", axis=0, tiled=True),
        lax.all_gather(w_value, "row", axis=0, tiled=True),
        lax.all_gather(w_gate, "row", axis=0, tiled=True),
        lax.all_gather(w_up, "row", axis=0, tiled=True),
        lax.all_gather(w_out, "row", axis=1, tiled=True),
        lax.all_gather(w_down, "row", axis=1, tiled=True),
    )
    tokens_wide = widen(tokens)
    query_pre = matmul(tokens_wide, query_weight)
    key_pre = matmul(tokens_wide, key_weight)
    value_pre = matmul(tokens_wide, value_weight)
    squares = feature_total(
        jnp.stack([jnp.sum(query_pre * query_pre, axis=1), jnp.sum(key_pre * key_pre, axis=1)])
    )
    inverse = lax.rsqrt(squares / width + norm_eps)
    query_inv = inverse[0][:, None]
    key_inv = inverse[1][:, None]
    query_rot = rotate(query_pre * query_inv * q_gain, cosine, sine, HEAD_DIM).astype(jnp.bfloat16)
    key_rot = rotate(key_pre * key_inv * k_gain, cosine, sine, HEAD_DIM).astype(jnp.bfloat16)
    value_low = value_pre.astype(jnp.bfloat16)
    keys_all, values_all = (
        lax.all_gather(key_rot, "row", axis=0, tiled=True),
        lax.all_gather(value_low, "row", axis=0, tiled=True),
    )

    def head_scores(index):
        start = index * HEAD_DIM
        query_head = lax.dynamic_slice_in_dim(query_rot, start, HEAD_DIM, 1)
        key_head = lax.dynamic_slice_in_dim(keys_all, start, HEAD_DIM, 1)
        scores = contract_last(query_head, key_head) * score_scale
        return jnp.where(allowed, scores, masked_score)

    def head_forward(index):
        scores = head_scores(index)
        top = jnp.max(scores, axis=1, keepdims=True)
        weights = jnp.exp(scores - top)
        total = jnp.sum(weights, axis=1, keepdims=True)
        value_head = lax.dynamic_slice_in_dim(values_all, index * HEAD_DIM, HEAD_DIM, 1)
        attended = matmul((weights / total).astype(jnp.bfloat16), value_head)
        return (attended, (top + jnp.log(total))[:, 0])

    head_outputs, log_totals = lax.map(head_forward, jnp.arange(head_count))
    attn_low = head_outputs.transpose(1, 0, 2).reshape(tok_rows, feat_part).astype(jnp.bfloat16)
    branch = narrow(matmul(attn_low, out_weight))
    branch_inv = lax.rsqrt(
        feature_total(jnp.sum(branch * branch, axis=1)[None, :])[0] / width + norm_eps
    )[:, None]
    resid = tokens.astype(jnp.float32) + branch * branch_inv * attn_gain
    resid_wide = widen(resid.astype(jnp.bfloat16))
    gate = matmul(resid_wide, gate_weight)
    upper = matmul(resid_wide, up_weight)
    sigma = jax.nn.sigmoid(gate)
    hidden = (gate * sigma * upper).astype(jnp.bfloat16)
    mixed = narrow(matmul(hidden, down_weight))
    mixed_inv = lax.rsqrt(
        feature_total(jnp.sum(mixed * mixed, axis=1)[None, :])[0] / width + norm_eps
    )[:, None]
    block_output = ((resid + mixed * mixed_inv * mlp_gain) * valid).astype(jnp.bfloat16)

    def arrange(values):
        return reorder(values, row_count, data_count)

    incoming = cotangent.astype(jnp.float32) * valid
    mlp_gain_raw = jnp.sum(incoming * mixed * mixed_inv, axis=0)
    gained = incoming * mlp_gain
    inner = back_total(jnp.sum(gained * mixed, axis=1)[None, :])[0][:, None] / width
    d_mixed = (mixed_inv * gained - mixed * mixed_inv**3 * inner).astype(jnp.bfloat16)
    d_mixed_wide = widen_back(d_mixed)
    down_raw = contract_first(hidden, arrange(d_mixed_wide))
    d_hidden = contract_last(d_mixed_wide, down_weight)
    d_gate = (d_hidden * upper * sigma * (1.0 + gate * (1.0 - sigma))).astype(jnp.bfloat16)
    d_upper = (d_hidden * gate * sigma).astype(jnp.bfloat16)
    resid_arranged = arrange(resid_wide)
    gate_raw = contract_first(resid_arranged, d_gate)
    up_raw = contract_first(resid_arranged, d_upper)
    d_resid = incoming + narrow_back(
        contract_last(d_gate, gate_weight) + contract_last(d_upper, up_weight)
    )
    attn_gain_raw = jnp.sum(d_resid * branch * branch_inv, axis=0)
    gained = d_resid * attn_gain
    inner = back_total(jnp.sum(gained * branch, axis=1)[None, :])[0][:, None] / width
    d_branch = (branch_inv * gained - branch * branch_inv**3 * inner).astype(jnp.bfloat16)
    d_branch_wide = widen_back(d_branch)
    out_raw = contract_first(attn_low, arrange(d_branch_wide))
    d_attn = contract_last(d_branch_wide, out_weight).astype(jnp.bfloat16)

    def head_backward(operands):
        index, log_total = operands
        start = index * HEAD_DIM
        probs = jnp.exp(head_scores(index) - log_total[:, None])
        query_head = lax.dynamic_slice_in_dim(query_rot, start, HEAD_DIM, 1)
        key_head = lax.dynamic_slice_in_dim(keys_all, start, HEAD_DIM, 1)
        value_head = lax.dynamic_slice_in_dim(values_all, start, HEAD_DIM, 1)
        d_head = lax.dynamic_slice_in_dim(d_attn, start, HEAD_DIM, 1)
        d_probs = contract_last(d_head, value_head)
        delta = jnp.sum(probs * d_probs, axis=1, keepdims=True)
        d_scores = (probs * (d_probs - delta)).astype(jnp.bfloat16)
        d_query_head = matmul(d_scores, key_head) * score_scale
        d_key_head = contract_first(d_scores, query_head) * score_scale
        d_value_head = contract_first(probs.astype(jnp.bfloat16), d_head)
        return (d_query_head, d_key_head, d_value_head)

    d_queries, d_keys, d_values = lax.map(head_backward, (jnp.arange(head_count), log_totals))
    d_query_rot = d_queries.transpose(1, 0, 2).reshape(tok_rows, feat_part)
    d_key_all = d_keys.transpose(1, 0, 2).reshape(seq_slots, feat_part)
    d_value_all = d_values.transpose(1, 0, 2).reshape(seq_slots, feat_part)
    d_key_rot, d_value_sum = (
        lax.psum_scatter(
            d_key_all.astype(jnp.bfloat16), "row", scatter_dimension=0, tiled=True
        ).astype(jnp.float32),
        lax.psum_scatter(
            d_value_all.astype(jnp.bfloat16), "row", scatter_dimension=0, tiled=True
        ).astype(jnp.float32),
    )
    d_query_norm = unrotate(d_query_rot, cosine, sine, HEAD_DIM)
    d_key_norm = unrotate(d_key_rot, cosine, sine, HEAD_DIM)
    q_gain_raw = jnp.sum(d_query_norm * query_pre * query_inv, axis=0)
    k_gain_raw = jnp.sum(d_key_norm * key_pre * key_inv, axis=0)
    query_scaled = d_query_norm * q_gain
    key_scaled = d_key_norm * k_gain
    inner = (
        back_total(
            jnp.stack(
                [jnp.sum(query_scaled * query_pre, axis=1), jnp.sum(key_scaled * key_pre, axis=1)]
            )
        )
        / width
    )
    d_query = (query_inv * query_scaled - query_pre * query_inv**3 * inner[0][:, None]).astype(
        jnp.bfloat16
    )
    d_key = (key_inv * key_scaled - key_pre * key_inv**3 * inner[1][:, None]).astype(jnp.bfloat16)
    d_value = d_value_sum.astype(jnp.bfloat16)
    tokens_arranged = arrange(tokens_wide)
    query_raw = contract_first(tokens_arranged, d_query)
    key_raw = contract_first(tokens_arranged, d_key)
    value_raw = contract_first(tokens_arranged, d_value)
    projected = (
        contract_last(d_query, query_weight)
        + contract_last(d_key, key_weight)
        + contract_last(d_value, value_weight)
    )
    input_grad = d_resid + narrow_back(projected)
    factor = 1.0 / math.sqrt(tok_rows * row_count * data_count)
    gains = lax.psum(
        jnp.stack([q_gain_raw, k_gain_raw, attn_gain_raw, mlp_gain_raw]) * factor, ("dp", "row")
    )
    pieces = (
        lax.psum_scatter(
            (query_raw * factor).astype(jnp.bfloat16),
            ("dp", "row"),
            scatter_dimension=0,
            tiled=True,
        ).astype(jnp.float32),
        lax.psum_scatter(
            (key_raw * factor).astype(jnp.bfloat16), ("dp", "row"), scatter_dimension=0, tiled=True
        ).astype(jnp.float32),
        lax.psum_scatter(
            (value_raw * factor).astype(jnp.bfloat16),
            ("dp", "row"),
            scatter_dimension=0,
            tiled=True,
        ).astype(jnp.float32),
        lax.psum_scatter(
            (out_raw * factor).astype(jnp.bfloat16), ("dp", "row"), scatter_dimension=1, tiled=True
        ).astype(jnp.float32),
        lax.psum_scatter(
            (gate_raw * factor).astype(jnp.bfloat16), ("dp", "row"), scatter_dimension=0, tiled=True
        ).astype(jnp.float32),
        lax.psum_scatter(
            (up_raw * factor).astype(jnp.bfloat16), ("dp", "row"), scatter_dimension=0, tiled=True
        ).astype(jnp.float32),
        lax.psum_scatter(
            (down_raw * factor).astype(jnp.bfloat16), ("dp", "row"), scatter_dimension=1, tiled=True
        ).astype(jnp.float32),
    )
    finals = (
        lax.all_gather(pieces[0].astype(jnp.bfloat16), "dp", axis=0, tiled=True).astype(
            jnp.float32
        ),
        lax.all_gather(pieces[1].astype(jnp.bfloat16), "dp", axis=0, tiled=True).astype(
            jnp.float32
        ),
        lax.all_gather(pieces[2].astype(jnp.bfloat16), "dp", axis=0, tiled=True).astype(
            jnp.float32
        ),
        lax.all_gather(pieces[3].astype(jnp.bfloat16), "dp", axis=1, tiled=True).astype(
            jnp.float32
        ),
        lax.all_gather(pieces[4].astype(jnp.bfloat16), "dp", axis=0, tiled=True).astype(
            jnp.float32
        ),
        lax.all_gather(pieces[5].astype(jnp.bfloat16), "dp", axis=0, tiled=True).astype(
            jnp.float32
        ),
        lax.all_gather(pieces[6].astype(jnp.bfloat16), "dp", axis=1, tiled=True).astype(
            jnp.float32
        ),
    )
    return (
        block_output,
        input_grad,
        finals[0],
        finals[1],
        finals[2],
        finals[3],
        finals[4],
        finals[5],
        finals[6],
        gains[0],
        gains[1],
        gains[2],
        gains[3],
    )


def solution(mesh):
    return jax.shard_map(
        per_device,
        mesh=mesh,
        in_specs=(
            P(("dp", "row"), "col"),
            P("dp"),
            P("row", "col"),
            P("row", "col"),
            P("row", "col"),
            P("col", "row"),
            P("row", "col"),
            P("row", "col"),
            P("col", "row"),
            P("col"),
            P("col"),
            P("col"),
            P("col"),
            P(("dp", "row"), "col"),
        ),
        out_specs=(
            P(("dp", "row"), "col"),
            P(("dp", "row"), "col"),
            P("row", "col"),
            P("row", "col"),
            P("row", "col"),
            P("col", "row"),
            P("row", "col"),
            P("row", "col"),
            P("col", "row"),
            P("col"),
            P("col"),
            P("col"),
            P("col"),
        ),
        check_vma=False,
    )
```

profile of v0, /device:TPU:0, one launch (start us, length us, event | category | flops | bytes accessed | tf_op | source)
XLA Modules:
  0.0 2207.9 jit_solution(10388546232227162972)
XLA Ops:
  14.7 43.3 %all-gather.19.cloned.1.call-done = bf16[2048,512]{1,0:T(8,128)(2,1)} async-done(((bf16[512,512]{1,0:T(8,128)(2,1)}), bf16[2048,512]{1,0:T(8,128)(2,1)}) %all-gather.19.cloned.1.call-update) | async-done | bytes 2097168 | tf_op jit(solution)/shard_map/all_gather | solution.py:118
  58.0 29.5 %all-gather.17.cloned.1.call-done = bf16[768,2048]{0,1:T(8,128)(2,1)} async-done(((bf16[768,512]{0,1:T(8,128)(2,1)}), bf16[768,2048]{0,1:T(8,128)(2,1)}) %all-gather.17.cloned.1.call-update) | async-done | bytes 3145744 | tf_op jit(solution)/shard_map/all_gather | solution.py:58
  91.9 42.8 %all-gather.21.cloned.1.call-done = bf16[2048,512]{1,0:T(8,128)(2,1)} async-done(((bf16[512,512]{1,0:T(8,128)(2,1)}), bf16[2048,512]{1,0:T(8,128)(2,1)}) %all-gather.21.cloned.1.call-update) | async-done | bytes 2097168 | tf_op jit(solution)/shard_map/all_gather | solution.py:119
  151.2 29.4 %all-gather.25.cloned.1.call-done = bf16[2048,512]{1,0:T(8,128)(2,1)} async-done(((bf16[512,512]{1,0:T(8,128)(2,1)}), bf16[2048,512]{1,0:T(8,128)(2,1)}) %all-gather.25.cloned.1.call-update) | async-done | bytes 2097168 | tf_op jit(solution)/shard_map/all_gather | solution.py:120
  187.9 57.0 %all-gather.23.cloned.1.call-done = bf16[3072,512]{0,1:T(8,128)(2,1)} async-done(((bf16[768,512]{0,1:T(8,128)(2,1)}), bf16[3072,512]{0,1:T(8,128)(2,1)}) %all-gather.23.cloned.1.call-update) | async-done | bytes 3145744 | tf_op jit(solution)/shard_map/all_gather | solution.py:140
  249.5 59.5 %all-gather.27.cloned.1.call-done = bf16[3072,512]{1,0:T(8,128)(2,1)} async-done(((bf16[768,512]{1,0:T(8,128)(2,1)}), bf16[3072,512]{1,0:T(8,128)(2,1)}) %all-gather.27.cloned.1.call-update) | async-done | bytes 3145744 | tf_op jit(solution)/shard_map/all_gather | solution.py:141
  309.0 65.3 %while.28 = (s32[]{:T(128)}, bf16[4,768,128]{1,2,0:T(8,128)(2,1)S(1)}, f32[4,768]{1,0:T(4,128)}, s32[4]{0:T(128)S(1)}, bf16[768,512]{1,0:T(8,128)(2,1)S(1)}, /*i...) while((s32[]{:T(128)}, ...), condition=%wide.region_6.7_spmd.clone, body=%wide.region_3.6_spmd.clone.sunk | while | flops 1231551744 | bytes 68270800 | solution.py:160
  381.9 55.9 %reduce-scatter.14.cloned.1.call-done = f32[768,512]{1,0:T(8,128)} async-done(((f32[768,2048]{1,0:T(8,128)}), f32[768,512]{1,0:T(8,128)}) %reduce-scatter.14.cloned.1.call-update) | async-done | bytes 1572880 | tf_op jit(solution)/shard_map/reduce_scatter | solution.py:66
  448.3 140.7 %all-gather.33.cloned.1.call-done = bf16[2048,2048]{1,0:T(8,128)(2,1)} async-done(((bf16[512,2048]{1,0:T(8,128)(2,1)}), bf16[2048,2048]{1,0:T(8,128)(2,1)}) %all-gather.33.cloned.1.call-update) | async-done | bytes 8388624 | tf_op jit(solution)/shard_map/all_gather | solution.py:121
  589.0 28.7 %all-gather.31.cloned.1.call-done = bf16[768,2048]{1,0:T(8,128)(2,1)} async-done(((bf16[768,512]{1,0:T(8,128)(2,1)}), bf16[768,2048]{1,0:T(8,128)(2,1)}) %all-gather.31.cloned.1.call-update) | async-done | bytes 3145744 | tf_op jit(solution)/shard_map/all_gather | solution.py:58
  617.7 11.8 fusion.62
  629.5 139.5 %all-gather.35.cloned.1.call-done = bf16[2048,2048]{1,0:T(8,128)(2,1)} async-done(((bf16[512,2048]{1,0:T(8,128)(2,1)}), bf16[2048,2048]{1,0:T(8,128)(2,1)}) %all-gather.35.cloned.1.call-update) | async-done | bytes 8388624 | tf_op jit(solution)/shard_map/all_gather | solution.py:122
  769.0 14.2 multiply_convert_fusion.6
  783.2 135.0 %all-gather.37.cloned.1.call-done = bf16[2048,2048]{1,0:T(8,128)(2,1)} async-done(((bf16[2048,512]{1,0:T(8,128)(2,1)}), bf16[2048,2048]{1,0:T(8,128)(2,1)}) %all-gather.37.cloned.1.call-update) | async-done | bytes 8388624 | tf_op jit(solution)/shard_map/all_gather | solution.py:124
  918.2 11.7 fusion.63
  930.0 56.2 %reduce-scatter.16.cloned.1.call-done = f32[768,512]{1,0:T(8,128)} async-done(((f32[768,2048]{1,0:T(8,128)}), f32[768,512]{1,0:T(8,128)}) %reduce-scatter.16.cloned.1.call-update) | async-done | bytes 1572880 | tf_op jit(solution)/shard_map/reduce_scatter | solution.py:66
  1004.5 29.3 %all-gather.39.cloned.1.call-done = bf16[768,2048]{1,0:T(8,128)(2,1)} async-done(((bf16[768,512]{1,0:T(8,128)(2,1)}), bf16[768,2048]{1,0:T(8,128)(2,1)}) %all-gather.39.cloned.1.call-update) | async-done | bytes 3145744 | tf_op jit(solution)/shard_map/all_gather | solution.py:62
  1033.7 16.1 multiply_convert_fusion.4
  1049.8 11.2 fusion.64
  1061.0 10.9 convolution_add_fusion
  1072.0 58.0 %reduce-scatter.18.cloned.1.call-done = f32[768,512]{1,0:T(8,128)} async-done(((f32[768,2048]{1,0:T(8,128)}), f32[768,512]{1,0:T(8,128)}) %reduce-scatter.18.cloned.1.call-update) | async-done | bytes 1572880 | tf_op jit(solution)/shard_map/reduce_scatter | solution.py:70
  1153.3 11.4 multiply_convert_fusion.1
  1175.5 11.3 multiply_convert_fusion.3
  1188.7 10.8 multiply_convert_fusion.2
  1204.6 139.6 %while.29 = (s32[]{:T(128)}, f32[4,768,128]{2,1,0:T(8,128)S(1)}, bf16[4,3072,128]{2,1,0:T(8,128)(2,1)}, bf16[4,3072,128]{1,2,0:T(8,128)(2,1)}, s32[4]{0:T(128)S(...) while((s32[]{:T(128)}, f32[4,768,128]{2,1,0:T(8,128)S(1)}, ...), condition=%wide.region_20.21_spmd.clone, body=%wide.region_18.20_spmd.clone.sunk | while | flops 3046341888 | bytes 152988432 | solution.py:221
  1209.2 8.5 multiply_reduce_fusion.15
  1217.7 11.4 multiply_convert_fusion.13
  1244.2 8.5 multiply_reduce_fusion.15
  1252.7 11.2 multiply_convert_fusion.13
  1279.0 8.5 multiply_reduce_fusion.15
  1287.6 11.1 multiply_convert_fusion.13
  1313.8 8.5 multiply_reduce_fusion.15
  1322.4 11.2 multiply_convert_fusion.13
  1350.9 121.8 %reduce-scatter.34.cloned.1.call-done = bf16[256,2048]{1,0:T(8,128)(2,1)} async-done(((bf16[2048,2048]{1,0:T(8,128)(2,1)}), bf16[256,2048]{1,0:T(8,128)(2,1)}) %reduce-scatter.34.cloned.1.call-update) | async-done | bytes 1048592 | tf_op jit(solution)/shard_map/reduce_scatter | solution.py:285
  1472.8 150.1 %reduce-scatter.36.cloned.1.call-done = bf16[256,2048]{1,0:T(8,128)(2,1)} async-done(((bf16[2048,2048]{1,0:T(8,128)(2,1)}), bf16[256,2048]{1,0:T(8,128)(2,1)}) %reduce-scatter.36.cloned.1.call-update) | async-done | bytes 1048592 | tf_op jit(solution)/shard_map/reduce_scatter | solution.py:288
  1645.3 39.9 %reduce-scatter.20.cloned.1.call-done = bf16[768,512]{0,1:T(8,128)(2,1)} async-done(((bf16[3072,512]{0,1:T(8,128)(2,1)}), bf16[768,512]{0,1:T(8,128)(2,1)}) %reduce-scatter.20.cloned.1.call-update) | async-done | bytes 786448 | tf_op jit(solution)/shard_map/reduce_scatter | solution.py:226
  1711.8 36.6 %reduce-scatter.22.cloned.1.call-done = bf16[768,512]{0,1:T(8,128)(2,1)} async-done(((bf16[3072,512]{0,1:T(8,128)(2,1)}), bf16[768,512]{0,1:T(8,128)(2,1)}) %reduce-scatter.22.cloned.1.call-update) | async-done | bytes 786448 | tf_op jit(solution)/shard_map/reduce_scatter | solution.py:229
  1763.3 19.6 all-gather.47.cloned.1.call-done
  1787.1 30.5 %all-gather.43.cloned.1.call-done = bf16[512,2048]{1,0:T(8,128)(2,1)} async-done(((bf16[256,2048]{1,0:T(8,128)(2,1)}), bf16[512,2048]{1,0:T(8,128)(2,1)}) %all-gather.43.cloned.1.call-update) | async-done | bytes 2097168 | tf_op jit(solution)/shard_map/all_gather | solution.py:308
  1821.7 30.4 %all-gather.45.cloned.1.call-done = bf16[512,2048]{1,0:T(8,128)(2,1)} async-done(((bf16[256,2048]{1,0:T(8,128)(2,1)}), bf16[512,2048]{1,0:T(8,128)(2,1)}) %all-gather.45.cloned.1.call-update) | async-done | bytes 2097168 | tf_op jit(solution)/shard_map/all_gather | solution.py:311
  1856.3 68.1 %reduce-scatter.32.cloned.1.call-done = bf16[512,256]{1,0:T(8,128)(2,1)} async-done(((bf16[512,2048]{1,0:T(8,128)(2,1)}), bf16[512,256]{1,0:T(8,128)(2,1)}) %reduce-scatter.32.cloned.1.call-update) | async-done | bytes 262160 | tf_op jit(solution)/shard_map/reduce_scatter | solution.py:282
  1924.4 7.4 all_gather.76
  1932.9 20.0 psum.55
  1953.6 42.9 %reduce-scatter.28.cloned.1.call-done = bf16[256,512]{0,1:T(8,128)(2,1)} async-done(((bf16[2048,512]{0,1:T(8,128)(2,1)}), bf16[256,512]{0,1:T(8,128)(2,1)}) %reduce-scatter.28.cloned.1.call-update) | async-done | bytes 262160 | tf_op jit(solution)/shard_map/reduce_scatter | solution.py:273
  2004.9 62.6 %reduce-scatter.26.cloned.1.call-done = bf16[256,512]{0,1:T(8,128)(2,1)} async-done(((bf16[2048,512]{0,1:T(8,128)(2,1)}), bf16[256,512]{0,1:T(8,128)(2,1)}) %reduce-scatter.26.cloned.1.call-update) | async-done | bytes 262160 | tf_op jit(solution)/shard_map/reduce_scatter | solution.py:267
  2067.5 7.4 all_gather.73
  2076.1 62.7 %reduce-scatter.30.cloned.1.call-done = bf16[256,512]{0,1:T(8,128)(2,1)} async-done(((bf16[2048,512]{0,1:T(8,128)(2,1)}), bf16[256,512]{0,1:T(8,128)(2,1)}) %reduce-scatter.30.cloned.1.call-update) | async-done | bytes 262160 | tf_op jit(solution)/shard_map/reduce_scatter | solution.py:276
  2147.4 50.9 %reduce-scatter.24.cloned.1.call-done = f32[768,512]{1,0:T(8,128)} async-done(((f32[768,2048]{1,0:T(8,128)}), f32[768,512]{1,0:T(8,128)}) %reduce-scatter.24.cloned.1.call-update) | async-done | bytes 1572880 | tf_op jit(solution)/shard_map/reduce_scatter | solution.py:70
  (359 shorter events, 342.2 us)
Async XLA Ops:
  7.2 50.8 %all-gather.19.cloned.1.call-start = ((), (), s32[]{:S(2)}) async-start(), calls=%async_computation.14 | async-start | bytes 2621440 | tf_op jit(solution)/shard_map/all_gather | solution.py:118
  7.9 79.5 %all-gather.17.cloned.1.call-start = ((), (), s32[]{:S(2)}) async-start(), calls=%async_computation.13 | async-start | bytes 3932160 | tf_op jit(solution)/shard_map/all_gather | solution.py:58
  10.3 124.4 %all-gather.21.cloned.1.call-start = ((), (), s32[]{:S(2)}) async-start(), calls=%async_computation.15 | async-start | bytes 2621440 | tf_op jit(solution)/shard_map/all_gather | solution.py:119
  11.0 169.6 %all-gather.25.cloned.1.call-start = ((), (), s32[]{:S(2)}) async-start(), calls=%async_computation.17 | async-start | bytes 2621440 | tf_op jit(solution)/shard_map/all_gather | solution.py:120
  11.6 233.3 %all-gather.23.cloned.1.call-start = ((), (), s32[]{:S(2)}) async-start(), calls=%async_computation.16 | async-start | bytes 3932160 | tf_op jit(solution)/shard_map/all_gather | solution.py:140
  13.5 44.5 %copy-start.24 = (f32[768,128]{1,0:T(8,128)}, f32[768,128]{1,0:T(8,128)S(1)}, u32[]{:S(2)}) copy-start(f32[768,128]{1,0:T(8,128)S(1)} %get-tuple-element.346) | copy-start | bytes 1179652
  13.5 44.4 %copy-start.26 = (f32[768,128]{1,0:T(8,128)}, f32[768,128]{1,0:T(8,128)S(1)}, u32[]{:S(2)}) copy-start(f32[768,128]{1,0:T(8,128)S(1)} %get-tuple-element.347) | copy-start | bytes 1179652
  14.7 134.6 %copy-start.18 = (f32[768,128]{0,1:T(8,128)}, f32[768,128]{0,1:T(8,128)S(1)}, u32[]{:S(2)}) copy-start(f32[768,128]{0,1:T(8,128)S(1)} %copy.55) | copy-start | bytes 1179652
  91.8 57.5 %copy-start.3 = (f32[768,512]{0,1:T(8,128)}, f32[768,512]{0,1:T(8,128)S(1)}, u32[]{:S(2)}) copy-start(f32[768,512]{0,1:T(8,128)S(1)} %get-tuple-element.355) | copy-start | bytes 4718596
  91.9 55.1 %copy-start.49 = (f32[512]{0:T(512)S(1)}, f32[512]{0:T(512)}, u32[]{:S(2)}) copy-start(f32[512]{0:T(512)} %param.27) | copy-start | bytes 6148
  151.1 36.5 %copy-start.30 = (bf16[768,512]{0,1:T(8,128)(2,1)S(1)}, bf16[768,512]{0,1:T(8,128)(2,1)}, u32[]{:S(2)}) copy-start(bf16[768,512]{0,1:T(8,128)(2,1)} %get-tuple-element.343) | copy-start | bytes 2359300
  151.1 157.9 %all-gather.27.cloned.1.call-start = ((), (), s32[]{:S(2)}) async-start(), calls=%async_computation.18 | async-start | bytes 3932160 | tf_op jit(solution)/shard_map/all_gather | solution.py:141
  185.9 188.5 %all-gather.29.cloned.1.call-start = ((), (), s32[]{:S(2)}) async-start(), calls=%async_computation.19 | async-start | bytes 2621440 | tf_op jit(solution)/shard_map/all_gather | solution.py:123
  186.6 251.1 %reduce-scatter.14.cloned.1.call-start = ((), (), s32[]{:S(2)}) async-start(), calls=%async_computation.20 | async-start | bytes 7864320 | tf_op jit(solution)/shard_map/reduce_scatter | solution.py:66
  381.1 64.2 %copy-start.16 = (bf16[768,512]{1,0:T(8,128)(2,1)S(1)}, bf16[768,512]{1,0:T(8,128)(2,1)}, u32[]{:S(2)}) copy-start(bf16[768,512]{1,0:T(8,128)(2,1)} %param.18) | copy-start | bytes 2359300
  381.1 64.2 %copy-start.51 = (f32[512]{0:T(512)S(1)}, f32[512]{0:T(512)}, u32[]{:S(2)}) copy-start(f32[512]{0:T(512)} %param.29) | copy-start | bytes 6148
  381.1 207.9 %all-gather.33.cloned.1.call-start = ((), (), s32[]{:S(2)}) async-start(), calls=%async_computation.22 | async-start | bytes 10485760 | tf_op jit(solution)/shard_map/all_gather | solution.py:121
  381.9 235.9 %all-gather.31.cloned.1.call-start = ((), (), s32[]{:S(2)}) async-start(), calls=%async_computation.21 | async-start | bytes 3932160 | tf_op jit(solution)/shard_map/all_gather | solution.py:58
  446.5 322.4 %all-gather.35.cloned.1.call-start = ((), (), s32[]{:S(2)}) async-start(), calls=%async_computation.23 | async-start | bytes 10485760 | tf_op jit(solution)/shard_map/all_gather | solution.py:122
  447.3 470.9 %all-gather.37.cloned.1.call-start = ((), (), s32[]{:S(2)}) async-start(), calls=%async_computation.24 | async-start | bytes 10485760 | tf_op jit(solution)/shard_map/all_gather | solution.py:124
  447.9 538.3 %reduce-scatter.16.cloned.1.call-start = ((), (), s32[]{:S(2)}) async-start(), calls=%async_computation.25 | async-start | bytes 7864320 | tf_op jit(solution)/shard_map/reduce_scatter | solution.py:66
  929.9 63.8 %copy-start.52 = (f32[512]{0:T(512)S(1)}, f32[512]{0:T(512)}, u32[]{:S(2)}) copy-start(f32[512]{0:T(512)} %param.30) | copy-start | bytes 6148
  930.0 103.8 %all-gather.39.cloned.1.call-start = ((), (), s32[]{:S(2)}) async-start(), calls=%async_computation.26 | async-start | bytes 3932160 | tf_op jit(solution)/shard_map/all_gather | solution.py:62
  930.0 208.6 %copy-start.41 = (f32[768]{0:T(1024)}, f32[768]{0:T(1024)S(1)}, u32[]{:S(2)}) copy-start(f32[768]{0:T(1024)S(1)} %compare_convert_fusion) | copy-start | bytes 9220
  1004.3 125.7 %reduce-scatter.18.cloned.1.call-start = ((), (), s32[]{:S(2)}) async-start(), calls=%async_computation.27 | async-start | bytes 7864320 | tf_op jit(solution)/shard_map/reduce_scatter | solution.py:70
  1071.9 128.1 %all-gather.41.cloned.1.call-start = ((), (), s32[]{:S(2)}) async-start(), calls=%async_computation.28 | async-start | bytes 3932160 | tf_op jit(solution)/shard_map/all_gather | solution.py:62
  1142.0 208.2 %reduce-scatter.38.cloned.1.call-start = ((), (), s32[]{:S(2)}) async-start(), calls=%async_computation.40 | async-start | bytes 9437184 | tf_op jit(solution)/shard_map/reduce_scatter | solution.py:291
  1164.7 308.0 %reduce-scatter.34.cloned.1.call-start = ((), (), s32[]{:S(2)}) async-start(), calls=%async_computation.36 | async-start | bytes 9437184 | tf_op jit(solution)/shard_map/reduce_scatter | solution.py:285
  1186.8 436.1 %reduce-scatter.36.cloned.1.call-start = ((), (), s32[]{:S(2)}) async-start(), calls=%async_computation.38 | async-start | bytes 9437184 | tf_op jit(solution)/shard_map/reduce_scatter | solution.py:288
  1199.5 485.7 %reduce-scatter.20.cloned.1.call-start = ((), (), s32[]{:S(2)}) async-start(), calls=%async_computation.29 | async-start | bytes 3932160 | tf_op jit(solution)/shard_map/reduce_scatter | solution.py:226
  1349.4 399.0 %reduce-scatter.22.cloned.1.call-start = ((), (), s32[]{:S(2)}) async-start(), calls=%async_computation.30 | async-start | bytes 3932160 | tf_op jit(solution)/shard_map/reduce_scatter | solution.py:229
  1350.1 432.8 %all-gather.47.cloned.1.call-start = ((), (), s32[]{:S(2)}) async-start(), calls=%async_computation.41 | async-start | bytes 3145728 | tf_op jit(solution)/shard_map/all_gather | solution.py:314
  1350.9 466.8 %all-gather.43.cloned.1.call-start = ((), (), s32[]{:S(2)}) async-start(), calls=%async_computation.37 | async-start | bytes 3145728 | tf_op jit(solution)/shard_map/all_gather | solution.py:308
  1472.7 379.4 %all-gather.45.cloned.1.call-start = ((), (), s32[]{:S(2)}) async-start(), calls=%async_computation.39 | async-start | bytes 3145728 | tf_op jit(solution)/shard_map/all_gather | solution.py:311
  1622.9 301.5 %reduce-scatter.32.cloned.1.call-start = ((), (), s32[]{:S(2)}) async-start(), calls=%async_computation.35 | async-start | bytes 2359296 | tf_op jit(solution)/shard_map/reduce_scatter | solution.py:282
  1639.4 357.0 %reduce-scatter.28.cloned.1.call-start = ((), (), s32[]{:S(2)}) async-start(), calls=%async_computation.33 | async-start | bytes 2359296 | tf_op jit(solution)/shard_map/reduce_scatter | solution.py:273
  1643.6 41.6 %copy-start.29 = (f32[768,128]{0,1:T(8,128)S(1)}, f32[768,128]{0,1:T(8,128)}, u32[]{:S(2)}) copy-start(f32[768,128]{0,1:T(8,128)} %copy.56) | copy-start | bytes 1179652
  1706.0 361.5 %reduce-scatter.26.cloned.1.call-start = ((), (), s32[]{:S(2)}) async-start(), calls=%async_computation.32 | async-start | bytes 2359296 | tf_op jit(solution)/shard_map/reduce_scatter | solution.py:267
  1708.6 39.8 %copy-start.33 = (bf16[768,2,4,256]{0,3,2,1:T(8,128)(2,1)S(1)}, bf16[768,2,4,256]{0,3,2,1:T(8,128)(2,1)}, u32[]{:S(2)}) copy-start(bf16[768,2,4,256]{0,3,2,1:T(8,128)(2,1)} %copy.65) | copy-start | bytes 9437188
  1711.8 427.0 %reduce-scatter.30.cloned.1.call-start = ((), (), s32[]{:S(2)}) async-start(), calls=%async_computation.34 | async-start | bytes 2359296 | tf_op jit(solution)/shard_map/reduce_scatter | solution.py:276
  1752.7 445.6 %reduce-scatter.24.cloned.1.call-start = ((), (), s32[]{:S(2)}) async-start(), calls=%async_computation.31 | async-start | bytes 7864320 | tf_op jit(solution)/shard_map/reduce_scatter | solution.py:70
  1856.3 76.6 %copy-start.54 = (f32[512]{0:T(512)S(1)}, f32[512]{0:T(512)}, u32[]{:S(2)}) copy-start(f32[512]{0:T(512)} %get-tuple-element.278) | copy-start | bytes 6148
  1856.3 76.6 %copy-start.55 = (f32[512]{0:T(512)S(1)}, f32[512]{0:T(512)}, u32[]{:S(2)}) copy-start(f32[512]{0:T(512)} %get-tuple-element.274) | copy-start | bytes 6148
  1856.3 76.6 %copy-start.56 = (f32[512]{0:T(512)S(1)}, f32[512]{0:T(512)}, u32[]{:S(2)}) copy-start(f32[512]{0:T(512)} %get-tuple-element.276) | copy-start | bytes 6148
  1856.3 76.6 %copy-start.57 = (f32[512]{0:T(512)S(1)}, f32[512]{0:T(512)}, u32[]{:S(2)}) copy-start(f32[512]{0:T(512)} %get-tuple-element.359) | copy-start | bytes 6148
  2004.9 193.4 %copy-start.9 = (bf16[768,512]{1,0:T(8,128)(2,1)S(1)}, bf16[768,512]{1,0:T(8,128)(2,1)}, u32[]{:S(2)}) copy-start(bf16[768,512]{1,0:T(8,128)(2,1)} %param.31) | copy-start | bytes 2359300
  2004.9 193.4 %copy-start.13 = (f32[768,512]{1,0:T(8,128)S(1)}, f32[768,512]{1,0:T(8,128)}, u32[]{:S(2)}) copy-start(f32[768,512]{1,0:T(8,128)} %reduce-scatter.18.cloned.1.call-done) | copy-start | bytes 4718596
  2004.9 193.4 %copy-start.42 = (f32[768]{0:T(1024)S(1)}, f32[768]{0:T(1024)}, u32[]{:S(2)}) copy-start(f32[768]{0:T(1024)} %copy-done.41) | copy-start | bytes 9220
  (53 other events, 232.2 us)
Sparse Core Ops, SparseCore 0:
  9.6 48.3 all-gather.18
  60.1 27.2 all-gather.16
  89.0 45.6 all-gather.20
  136.1 44.4 all-gather.24
  182.6 62.2 all-gather.22
  246.9 62.0 all-gather.26
  310.6 44.2 all-gather.28
  381.2 56.5 reduce-scatter.13
  439.4 149.6 all-gather.32
  591.0 26.6 all-gather.30
  619.3 149.6 all-gather.34
  770.4 147.7 all-gather.36
  930.1 56.0 reduce-scatter.15
  1004.4 29.3 all-gather.38
  1072.1 57.8 reduce-scatter.17
  1142.1 29.1 all-gather.40
  1174.7 147.8 reduce-scatter.37
  1326.1 146.5 reduce-scatter.33
  1476.3 146.5 reduce-scatter.35
  1625.6 59.4 reduce-scatter.19
  1688.0 60.3 reduce-scatter.21
  1749.9 32.9 all-gather.46
  1784.5 33.0 all-gather.42
  1819.0 33.0 all-gather.44
  1855.7 68.6 reduce-scatter.31
  1927.8 68.5 reduce-scatter.27
  1999.8 67.6 reduce-scatter.25
  2071.0 67.7 reduce-scatter.29
  2141.4 56.8 reduce-scatter.23
where the time goes:
time: 2220 us; the launch traced here: 2210 us
  waiting for transfers between devices  1630 us (73%)
  matrix products  287 us (13%)
  other arithmetic  96.4 us (4%)
  blocking collectives  86.4 us (4%)
  local copies, waits for them, and re-layouts  86.2 us (4%)
    reduce_scatter x1, waiting for transfers between devices, per_device(): lax.psum_scatter((up_raw * factor).astype(jnp.bfloat16), ('dp', 'row'), s...  150 us
    all_gather x1, waiting for transfers between devices, per_device(): lax.all_gather(w_gate, 'row', axis=0, tiled=True)  141 us
    all_gather x1, waiting for transfers between devices, per_device(): lax.all_gather(w_up, 'row', axis=0, tiled=True)  139 us
    all_gather x1, waiting for transfers between devices, per_device(): lax.all_gather(w_down, 'row', axis=1, tiled=True)  135 us
    reduce_scatter x1, waiting for transfers between devices, per_device(): lax.psum_scatter((gate_raw * factor).astype(jnp.bfloat16), ('dp', 'row'),...  122 us
    dot_general x19, matrix products, contract_last(): lax.dot_general(left, right, (((1,), (1,)), ((), ())), preferred_element_...  113 us
    reduce_scatter x2, waiting for transfers between devices, narrow(): return lax.psum_scatter(values, 'col', scatter_dimension=1, tiled=True)  112 us
    reduce_scatter x2, waiting for transfers between devices, narrow_back(): return lax.psum_scatter(values, 'col', scatter_dimension=1, tiled=True)  109 us
  transfers between devices with their start and end apart: 29, of which 26 were waited for; matrix products, arithmetic and copies ran while one was open for 17% of the time, Pallas kernels for 0%

commit v1 on v0

v1 whole, which is shorter than its diff:
```python
import functools
import math

import jax
import jax.numpy as jnp
from jax import lax
from jax.experimental import pallas as pl
from jax.experimental.pallas import tpu as pltpu
from jax.sharding import PartitionSpec as P

HEAD_DIM = 128
rope_base = 500000.0
norm_eps = 1e-06
masked_score = -1e30

MESH = pl.DeviceIdType.MESH
bf16 = jnp.bfloat16
f32 = jnp.float32


def rope_tables(positions, head_dim):
    half = head_dim // 2
    freq = 1.0 / rope_base ** (jnp.arange(half, dtype=f32) / half)
    angle = positions.astype(f32)[:, None] * freq[None, :]
    angle = jnp.concatenate([angle, angle], axis=1)
    return (jnp.cos(angle), jnp.sin(angle))


def rotate(values, cosine, sine, head_dim):
    count = values.shape[0]
    heads = values.reshape(count, -1, head_dim)
    half = head_dim // 2
    turned = jnp.concatenate([-heads[..., half:], heads[..., :half]], axis=-1)
    return (heads * cosine[:, None, :] + turned * sine[:, None, :]).reshape(count, -1)


def unrotate(values, cosine, sine, head_dim):
    count = values.shape[0]
    heads = values.reshape(count, -1, head_dim)
    half = head_dim // 2
    turned = heads * sine[:, None, :]
    back = jnp.concatenate([turned[..., half:], -turned[..., :half]], axis=-1)
    return (heads * cosine[:, None, :] + back).reshape(count, -1)


def matmul(left, right):
    return jnp.dot(left, right, preferred_element_type=f32)


def contract_first(left, right):
    return lax.dot_general(left, right, (((0,), (0,)), ((), ())), preferred_element_type=f32)


def contract_last(left, right):
    return lax.dot_general(left, right, (((1,), (1,)), ((), ())), preferred_element_type=f32)


def flip(axis, bit):
    return lax.axis_index(axis) ^ bit


def side(axis):
    return lax.axis_index(axis) & 1


def greet(peers):
    barrier = pltpu.get_barrier_semaphore()
    for peer in peers:
        pl.semaphore_signal(barrier, inc=1, device_id=peer, device_id_type=MESH)
    pl.semaphore_wait(barrier, len(peers))


def gather_kernel(x_ref, out_ref, local_sem, send_sem, recv_sem):
    rows, width = x_ref.shape
    half = rows // 2
    y, b = side("dp"), lax.axis_index("col")
    to_x, to_y, to_c = {"col": flip("col", 2)}, {"dp": flip("dp", 1)}, {"col": flip("col", 1)}
    greet([to_x, to_y, to_c])

    def slot(yy, h, bb, n=half):
        return out_ref.at[
            pl.ds(pl.multiple_of(yy * rows + h * half, half), n),
            pl.ds(pl.multiple_of(bb * width, width), width),
        ]

    started = []

    def send(src, dst, number, peer):
        copy = pltpu.make_async_remote_copy(
            src_ref=src,
            dst_ref=dst,
            send_sem=send_sem.at[number],
            recv_sem=recv_sem.at[number],
            device_id=peer,
            device_id_type=MESH,
        )
        copy.start()
        started.append(copy)
        return copy

    low, high = x_ref.at[pl.ds(0, half)], x_ref.at[pl.ds(half, half)]
    own = pltpu.make_async_copy(x_ref, slot(y, 0, b, rows), local_sem)
    xa = send(low, slot(y, 0, b), 0, to_x)
    ya = send(high, slot(y, 1, b), 1, to_y)
    c0 = send(x_ref, slot(y, 0, b, rows), 6, to_c)
    yb = send(low, slot(y, 0, b), 2, to_y)
    xb = send(high, slot(y, 1, b), 3, to_x)
    own.start()
    xa.wait_recv()
    piece = slot(y, 0, b ^ 2)
    yc = send(piece, piece, 4, to_y)
    c1 = send(piece, piece, 7, to_c)
    ya.wait_recv()
    piece = slot(y ^ 1, 1, b)
    xc = send(piece, piece, 5, to_x)
    c2 = send(piece, piece, 8, to_c)
    yb.wait_recv()
    piece = slot(y ^ 1, 0, b)
    c3 = send(piece, piece, 9, to_c)
    xb.wait_recv()
    piece = slot(y, 1, b ^ 2)
    c4 = send(piece, piece, 10, to_c)
    yc.wait_recv()
    piece = slot(y ^ 1, 0, b ^ 2)
    c5 = send(piece, piece, 11, to_c)
    xc.wait_recv()
    piece = slot(y ^ 1, 1, b ^ 2)
    c6 = send(piece, piece, 12, to_c)
    for copy in (c0, c1, c2, c3, c4, c5, c6):
        copy.wait_recv()
    for copy in started:
        copy.wait_send()
    own.wait()


def gather_wide(values, number, name):
    rows, width = values.shape
    return pl.pallas_call(
        gather_kernel,
        name=name,
        out_shape=jax.ShapeDtypeStruct((2 * rows, 4 * width), values.dtype),
        in_specs=[pl.BlockSpec(memory_space=pltpu.VMEM)],
        out_specs=pl.BlockSpec(memory_space=pl.ANY),
        scratch_shapes=[
            pltpu.SemaphoreType.DMA,
            pltpu.SemaphoreType.DMA((13,)),
            pltpu.SemaphoreType.DMA((13,)),
        ],
        compiler_params=pltpu.CompilerParams(collective_id=number, has_side_effects=True),
        cost_estimate=pl.CostEstimate(flops=0, bytes_accessed=60_000_000, transcendentals=0),
    )(values)


def scatter_kernel(p_ref, out_ref, rc, s1, ry, rx, s2, fy, fx, send_sem, recv_sem):
    rows, width = out_ref.shape
    half = rows // 2
    y, b = side("dp"), lax.axis_index("col")
    x, c = b >> 1, b & 1
    to_x, to_y, to_c = {"col": flip("col", 2)}, {"dp": flip("dp", 1)}, {"col": flip("col", 1)}
    greet([to_x, to_y, to_c])
    started = []

    def send(src, dst, number, peer):
        copy = pltpu.make_async_remote_copy(
            src_ref=src,
            dst_ref=dst,
            send_sem=send_sem.at[number],
            recv_sem=recv_sem.at[number],
            device_id=peer,
            device_id_type=MESH,
        )
        copy.start()
        started.append(copy)
        return copy

    def place(yy, h):
        return pl.ds(pl.multiple_of(yy * rows + h * half, half), half)

    def column(bb):
        return pl.ds(pl.multiple_of(bb * width, width), width)

    order = [(0, y ^ 1, 0), (1, y ^ 1, 0), (x ^ 1, 0, 1), (x ^ 1, 1, 1)]
    order += [(0, y, 0), (1, y, 0), (x, 0, 1), (x, 1, 1)]
    core = []
    for number, (xx, yy, h) in enumerate(order):
        core.append(
            send(
                p_ref.at[place(yy, h), column(2 * xx + (c ^ 1))],
                rc.at[xx, place(yy, h)],
                number,
                to_c,
            )
        )

    def settle(number):
        core[number].wait_recv()
        xx, yy, h = order[number]
        s1[xx, place(yy, h), :] = (
            p_ref[place(yy, h), column(2 * xx + c)].astype(f32)
            + rc[xx, place(yy, h), :].astype(f32)
        ).astype(s1.dtype)

    settle(0)
    settle(1)
    ya = send(s1.at[:, place(y ^ 1, 0), :], ry, 8, to_y)
    settle(2)
    settle(3)
    lower = s1.at[x ^ 1, pl.ds(half, half), :]
    upper = s1.at[x ^ 1, pl.ds(rows + half, half), :]
    xa0 = send(lower, rx.at[0], 9, to_x)
    xa1 = send(upper, rx.at[1], 10, to_x)
    settle(4)
    settle(5)
    settle(6)
    settle(7)
    ya.wait_recv()
    s2[0] = (s1[x ^ 1, place(y, 0), :].astype(f32) + ry[x ^ 1].astype(f32)).astype(s2.dtype)
    xb = send(s2.at[0], fx, 11, to_x)
    xa0.wait_recv()
    xa1.wait_recv()
    s2[1] = (s1[x, place(y ^ 1, 1), :].astype(f32) + rx[y ^ 1].astype(f32)).astype(s2.dtype)
    yb = send(s2.at[1], fy, 12, to_y)
    keep0 = s1[x, place(y, 0), :].astype(f32) + ry[x].astype(f32)
    xb.wait_recv()
    out_ref[pl.ds(0, half), :] = keep0 + fx[...].astype(f32)
    keep1 = s1[x, place(y, 1), :].astype(f32) + rx[y].astype(f32)
    yb.wait_recv()
    out_ref[pl.ds(half, half), :] = keep1 + fy[...].astype(f32)
    for copy in started:
        copy.wait_send()


def scatter_wide(partial, number, name):
    rows, width = partial.shape[0] // 2, partial.shape[1] // 4
    half = rows // 2
    return pl.pallas_call(
        scatter_kernel,
        name=name,
        out_shape=jax.ShapeDtypeStruct((rows, width), f32),
        in_specs=[pl.BlockSpec(memory_space=pltpu.VMEM)],
        out_specs=pl.BlockSpec(memory_space=pltpu.VMEM),
        scratch_shapes=[
            pltpu.VMEM((2, 2 * rows, width), bf16),
            pltpu.VMEM((2, 2 * rows, width), bf16),
            pltpu.VMEM((2, half, width), bf16),
            pltpu.VMEM((2, half, width), bf16),
            pltpu.VMEM((2, half, width), bf16),
            pltpu.VMEM((half, width), bf16),
            pltpu.VMEM((half, width), bf16),
            pltpu.SemaphoreType.DMA((13,)),
            pltpu.SemaphoreType.DMA((13,)),
        ],
        compiler_params=pltpu.CompilerParams(
            collective_id=number, has_side_effects=True, vmem_limit_bytes=40 * 2**20
        ),
        cost_estimate=pl.CostEstimate(flops=0, bytes_accessed=80_000_000, transcendentals=0),
    )(partial)


def total_kernel(wide, v_ref, out_ref, slots, send_sem, recv_sem):
    b = lax.axis_index("col")
    y = side("dp")
    me = y * 4 + b if wide else b
    count = 8 if wide else 4
    peers = []
    for d in range(1, count):
        peer = {"col": flip("col", d & 3)}
        if wide and d >> 2:
            peer["dp"] = flip("dp", 1)
        peers.append(peer)
    greet(peers)
    copies = []
    for d, peer in enumerate(peers):
        copy = pltpu.make_async_remote_copy(
            src_ref=v_ref,
            dst_ref=slots.at[me],
            send_sem=send_sem.at[d],
            recv_sem=recv_sem.at[d],
            device_id=peer,
            device_id_type=MESH,
        )
        copy.start()
        copies.append(copy)
    slots[me] = v_ref[...]
    for copy in copies:
        copy.wait_recv()
    total = slots[0]
    for i in range(1, count):
        total = total + slots[i]
    out_ref[...] = total
    for copy in copies:
        copy.wait_send()


def feature_total(values, wide, number, name):
    k, t = values.shape
    count = 8 if wide else 4
    flat = values.reshape(k * t // 128, 128)
    total = pl.pallas_call(
        functools.partial(total_kernel, wide),
        name=name,
        out_shape=jax.ShapeDtypeStruct(flat.shape, f32),
        in_specs=[pl.BlockSpec(memory_space=pltpu.VMEM)],
        out_specs=pl.BlockSpec(memory_space=pltpu.VMEM),
        scratch_shapes=[
            pltpu.VMEM((count,) + flat.shape, f32),
            pltpu.SemaphoreType.DMA((count - 1,)),
            pltpu.SemaphoreType.DMA((count - 1,)),
        ],
        compiler_params=pltpu.CompilerParams(collective_id=number, has_side_effects=True),
    )(flat)
    return total.reshape(k, t)


def turn_kernel(x_ref, out_ref, local_sem, send_sem, recv_sem):
    z = lax.axis_index("row")
    peers = [{"row": flip("row", d)} for d in (1, 2, 3)]
    greet(peers)
    copies = []
    for d in (3, 2, 1):
        copy = pltpu.make_async_remote_copy(
            src_ref=x_ref.at[z ^ d],
            dst_ref=out_ref.at[z],
            send_sem=send_sem.at[d - 1],
            recv_sem=recv_sem.at[d - 1],
            device_id={"row": flip("row", d)},
            device_id_type=MESH,
        )
        copy.start()
        copies.append(copy)
    own = pltpu.make_async_copy(x_ref.at[z], out_ref.at[z], local_sem)
    own.start()
    for copy in copies:
        copy.wait()
    own.wait()


def turn(values, number, name):
    return pl.pallas_call(
        turn_kernel,
        name=name,
        out_shape=jax.ShapeDtypeStruct(values.shape, values.dtype),
        in_specs=[pl.BlockSpec(memory_space=pltpu.VMEM)],
        out_specs=pl.BlockSpec(memory_space=pl.ANY),
        scratch_shapes=[
            pltpu.SemaphoreType.DMA,
            pltpu.SemaphoreType.DMA((3,)),
            pltpu.SemaphoreType.DMA((3,)),
        ],
        compiler_params=pltpu.CompilerParams(collective_id=number, has_side_effects=True),
        cost_estimate=pl.CostEstimate(flops=0, bytes_accessed=100_000_000, transcendentals=0),
    )(values)


def swap_kernel(x_ref, out_ref, send_sem, recv_sem):
    peer = {"dp": flip("dp", 1)}
    greet([peer])
    copy = pltpu.make_async_remote_copy(
        src_ref=x_ref,
        dst_ref=out_ref,
        send_sem=send_sem,
        recv_sem=recv_sem,
        device_id=peer,
        device_id_type=MESH,
    )
    copy.start()
    copy.wait()


BLOCK = 512


def allow(i0, j0, length, bq, bk):
    rows = i0 + lax.broadcasted_iota(jnp.int32, (bk, bq), 1)
    cols = j0 + lax.broadcasted_iota(jnp.int32, (bk, bq), 0)
    return (cols <= rows) & (cols < length)


def attend_kernel(len_ref, q_ref, k_ref, v_ref, o_ref, o32_ref, lse_ref):
    i = pl.program_id(0)
    bq, bk = q_ref.shape[0], BLOCK
    length = len_ref[0]
    scale = HEAD_DIM ** (-0.5)
    q = q_ref[...]
    rows = i * bq + lax.broadcasted_iota(jnp.int32, (bq, bk), 0)
    cols0 = lax.broadcasted_iota(jnp.int32, (bq, bk), 1)

    def step(j, carry, masked):
        top, total, acc = carry
        j0 = pl.multiple_of(j * bk, bk)
        scores = contract_last(q, k_ref[pl.ds(j0, bk), :]) * scale
        if masked:
            cols = j0 + cols0
            scores = jnp.where((cols <= rows) & (cols < length), scores, masked_score)
        new = jnp.maximum(top, jnp.max(scores, axis=1, keepdims=True))
        weights = jnp.exp(scores - new)
        fix = jnp.exp(top - new)
        total = total * fix + jnp.sum(weights, axis=1, keepdims=True)
        acc = acc * fix + matmul(weights.astype(bf16), v_ref[pl.ds(j0, bk), :])
        return new, total, acc

    carry = (
        jnp.full((bq, 1), -jnp.inf, f32),
        jnp.zeros((bq, 1), f32),
        jnp.zeros((bq, HEAD_DIM), f32),
    )
    whole = jnp.minimum(i, length // bk)
    last = jnp.minimum(i + 1, (length + bk - 1) // bk)
    carry = lax.fori_loop(0, whole, lambda j, s: step(j, s, False), carry)
    top, total, acc = lax.fori_loop(whole, last, lambda j, s: step(j, s, True), carry)
    out = acc / total
    o_ref[...] = out.astype(bf16)
    o32_ref[...] = out
    lse_ref[...] = jnp.broadcast_to((top + jnp.log(total)).T, lse_ref.shape)


def attend(length, q, k, v):
    slots = q.shape[0]
    whole = pl.BlockSpec((slots, HEAD_DIM), lambda i: (0, 0))
    part = pl.BlockSpec((BLOCK, HEAD_DIM), lambda i: (i, 0))
    return pl.pallas_call(
        attend_kernel,
        name="attend",
        grid=(slots // BLOCK,),
        out_shape=(
            jax.ShapeDtypeStruct((slots, HEAD_DIM), bf16),
            jax.ShapeDtypeStruct((slots, HEAD_DIM), f32),
            jax.ShapeDtypeStruct((8, slots), f32),
        ),
        in_specs=[pl.BlockSpec(memory_space=pltpu.SMEM), part, whole, whole],
        out_specs=(part, part, pl.BlockSpec((8, BLOCK), lambda i: (0, i))),
        cost_estimate=pl.CostEstimate(
            flops=2 * slots * slots * HEAD_DIM,
            bytes_accessed=8 * slots * HEAD_DIM,
            transcendentals=slots * slots // 2,
        ),
    )(length, q, k, v)


def attend_back_kernel(
    len_ref, q_ref, k_ref, v_ref, do_ref, lse_ref, delta_ref, dq_ref, dk_ref, dv_ref, dq_acc
):
    j = pl.program_id(0)
    bk, bq = k_ref.shape[0], BLOCK
    slots = q_ref.shape[0]
    length = len_ref[0]
    scale = HEAD_DIM ** (-0.5)

    @pl.when(j == 0)
    def _():
        dq_acc[...] = jnp.zeros_like(dq_acc)

    k, v = k_ref[...], v_ref[...]
    j0 = j * bk
    cols = j0 + lax.broadcasted_iota(jnp.int32, (bk, bq), 0)
    rows0 = lax.broadcasted_iota(jnp.int32, (bk, bq), 1)

    def step(i, carry, masked):
        dk, dv = carry
        i0 = pl.multiple_of(i * bq, bq)
        here = pl.ds(i0, bq)
        q, do = q_ref[here, :], do_ref[here, :]
        scores = contract_last(k, q) * scale
        probs = jnp.exp(scores - lse_ref[0:1, here])
        if masked:
            probs = jnp.where((cols <= i0 + rows0) & (cols < length), probs, 0.0)
        dv = dv + matmul(probs.astype(bf16), do)
        d_probs = contract_last(v, do)
        d_scores = (probs * (d_probs - delta_ref[0:1, here])).astype(bf16)
        dk = dk + matmul(d_scores, q)
        dq_acc[here, :] += contract_first(d_scores, k)
        return dk, dv

    zero = jnp.zeros((bk, HEAD_DIM), f32)
    top = slots // bq
    inside = j0 + bk <= length
    first = jnp.where(inside, j + 1, top)
    first = jnp.where(j0 < length, first, j)
    carry = lax.fori_loop(j, first, lambda i, s: step(i, s, True), (zero, zero))
    stop = jnp.where(j0 < length, top, j)
    dk, dv = lax.fori_loop(first, stop, lambda i, s: step(i, s, False), carry)
    dk_ref[...] = (dk * scale).astype(bf16)
    dv_ref[...] = dv.astype(bf16)

    @pl.when(j == pl.num_programs(0) - 1)
    def _():
        dq_ref[...] = (dq_acc[...] * scale).astype(bf16)


def attend_back(length, q, k, v, do, lse, delta):
    slots = q.shape[0]
    whole = pl.BlockSpec((slots, HEAD_DIM), lambda j: (0, 0))
    part = pl.BlockSpec((BLOCK, HEAD_DIM), lambda j: (j, 0))
    line = pl.BlockSpec((8, slots), lambda j: (0, 0))
    shape = jax.ShapeDtypeStruct((slots, HEAD_DIM), bf16)
    return pl.pallas_call(
        attend_back_kernel,
        name="attend_back",
        grid=(slots // BLOCK,),
        out_shape=(shape, shape, shape),
        in_specs=[pl.BlockSpec(memory_space=pltpu.SMEM), whole, part, part, whole, line, line],
        out_specs=(whole, part, part),
        scratch_shapes=[pltpu.VMEM((slots, HEAD_DIM), f32)],
        cost_estimate=pl.CostEstimate(
            flops=5 * slots * slots * HEAD_DIM,
            bytes_accessed=14 * slots * HEAD_DIM,
            transcendentals=slots * slots // 2,
        ),
    )(length, q, k, v, do, lse, delta)


def per_device(
    tokens,
    seq_lengths,
    w_query,
    w_key,
    w_value,
    w_out,
    w_gate,
    w_up,
    w_down,
    q_gain,
    k_gain,
    attn_gain,
    mlp_gain,
    cotangent,
):
    tok_rows, feat_part = tokens.shape
    row_count, data_count = lax.axis_size("row"), lax.axis_size("dp")
    width = feat_part * lax.axis_size("col")
    slots = tok_rows * row_count
    half_feat = feat_part // 2
    y, z = side("dp"), lax.axis_index("row")
    heads = half_feat // HEAD_DIM
    units = 2 * heads
    pairs = [(i, i ^ 1) for i in range(data_count)]

    def y_half(values, axis):
        size = values.shape[axis] // 2
        return lax.dynamic_slice_in_dim(values, y * size, size, axis)

    qkv_weight = lax.all_gather(
        jnp.concatenate([y_half(w_query, 1), y_half(w_key, 1), y_half(w_value, 1)], axis=1),
        "row",
        axis=0,
        tiled=True,
    )
    out_weight = lax.all_gather(y_half(w_out, 0), "row", axis=1, tiled=True)
    gate_weight = lax.all_gather(y_half(w_gate, 1), "row", axis=0, tiled=True)
    up_weight = lax.all_gather(y_half(w_up, 1), "row", axis=0, tiled=True)
    down_weight = lax.all_gather(y_half(w_down, 0), "row", axis=1, tiled=True)

    positions = z * tok_rows + jnp.arange(tok_rows)
    length = seq_lengths[0]
    valid = (positions < length).astype(f32)[:, None]
    cosine, sine = rope_tables(positions, HEAD_DIM)
    cosine, sine = jnp.concatenate([cosine, cosine]), jnp.concatenate([sine, sine])
    other_length = lax.ppermute(seq_lengths, "dp", pairs)
    pair_lengths = jnp.where(
        y == 0,
        jnp.concatenate([seq_lengths, other_length]),
        jnp.concatenate([other_length, seq_lengths]),
    )
    unit_length = lax.dynamic_slice_in_dim(pair_lengths, z // heads, 1)

    def to_units(*arrays):
        parts = [
            a.reshape(2, tok_rows, heads, HEAD_DIM).transpose(0, 2, 1, 3).reshape(
                units, 1, tok_rows, HEAD_DIM
            )
            for a in arrays
        ]
        return jnp.concatenate(parts, axis=1)

    def from_units(values):
        return [
            values[:, i]
            .reshape(2, heads, tok_rows, HEAD_DIM)
            .transpose(0, 2, 1, 3)
            .reshape(2 * tok_rows, heads * HEAD_DIM)
            for i in range(values.shape[1])
        ]

    def as_slots(values, i):
        return values[:, i].reshape(slots, HEAD_DIM)

    tokens_wide = gather_wide(tokens, 0, "gather_tokens")
    qkv = matmul(tokens_wide, qkv_weight)
    query_pre, key_pre, value_pre = (
        qkv[:, :half_feat],
        qkv[:, half_feat : 2 * half_feat],
        qkv[:, 2 * half_feat :],
    )
    squares = feature_total(
        jnp.stack([jnp.sum(query_pre * query_pre, axis=1), jnp.sum(key_pre * key_pre, axis=1)]),
        True,
        1,
        "total_qk",
    )
    inverse = lax.rsqrt(squares / width + norm_eps)
    query_inv, key_inv = inverse[0][:, None], inverse[1][:, None]
    q_gain_half, k_gain_half = y_half(q_gain, 0), y_half(k_gain, 0)
    query_rot = rotate(query_pre * query_inv * q_gain_half, cosine, sine, HEAD_DIM).astype(bf16)
    key_rot = rotate(key_pre * key_inv * k_gain_half, cosine, sine, HEAD_DIM).astype(bf16)
    turned = turn(to_units(query_rot, key_rot, value_pre.astype(bf16)), 2, "turn_qkv")
    q_unit, k_unit, v_unit = (as_slots(turned, i) for i in range(3))
    attn_unit, attn_exact, log_total = attend(unit_length, q_unit, k_unit, v_unit)
    (attn_low,) = from_units(
        turn(attn_unit.reshape(row_count, 1, tok_rows, HEAD_DIM), 3, "turn_attn")
    )
    branch = scatter_wide(matmul(attn_low, out_weight).astype(bf16), 4, "scatter_branch")
    branch_inv = lax.rsqrt(
        feature_total(jnp.sum(branch * branch, axis=1)[None, :], False, 5, "total_branch")[0]
        / width
        + norm_eps
    )[:, None]
    resid = tokens.astype(f32) + branch * branch_inv * attn_gain
    resid_wide = gather_wide(resid.astype(bf16), 6, "gather_resid")
    gate = matmul(resid_wide, gate_weight)
    upper = matmul(resid_wide, up_weight)
    sigma = jax.nn.sigmoid(gate)
    hidden = (gate * sigma * upper).astype(bf16)
    mixed = scatter_wide(matmul(hidden, down_weight).astype(bf16), 7, "scatter_mixed")
    incoming = cotangent.astype(f32) * valid
    gained = incoming * mlp_gain
    sums = feature_total(
        jnp.stack([jnp.sum(mixed * mixed, axis=1), jnp.sum(gained * mixed, axis=1)]),
        False,
        8,
        "total_mixed",
    )
    mixed_inv = lax.rsqrt(sums[0] / width + norm_eps)[:, None]
    inner = (sums[1] / width)[:, None]
    block_output = ((resid + mixed * mixed_inv * mlp_gain) * valid).astype(bf16)
    mlp_gain_raw = jnp.sum(incoming * mixed * mixed_inv, axis=0)
    d_mixed = (mixed_inv * gained - mixed * mixed_inv**3 * inner).astype(bf16)
    d_mixed_wide = gather_wide(d_mixed, 9, "gather_d_mixed")

    factor = 1.0 / math.sqrt(slots * data_count)

    def reduce_rows(raw, axis):
        return lax.psum_scatter(
            (raw * factor).astype(bf16), "row", scatter_dimension=axis, tiled=True
        )

    down_piece = reduce_rows(contract_first(hidden, d_mixed_wide), 1)
    d_hidden = contract_last(d_mixed_wide, down_weight)
    d_gate = (d_hidden * upper * sigma * (1.0 + gate * (1.0 - sigma))).astype(bf16)
    d_upper = (d_hidden * gate * sigma).astype(bf16)
    gate_piece = reduce_rows(contract_first(resid_wide, d_gate), 0)
    up_piece = reduce_rows(contract_first(resid_wide, d_upper), 0)
    d_resid = incoming + scatter_wide(
        (contract_last(d_gate, gate_weight) + contract_last(d_upper, up_weight)).astype(bf16),
        10,
        "scatter_d_resid",
    )
    attn_gain_raw = jnp.sum(d_resid * branch * branch_inv, axis=0)
    gained = d_resid * attn_gain
    inner = (
        feature_total(jnp.sum(gained * branch, axis=1)[None, :], False, 11, "total_d_resid")[0][
            :, None
        ]
        / width
    )
    d_branch = (branch_inv * gained - branch * branch_inv**3 * inner).astype(bf16)
    d_branch_wide = gather_wide(d_branch, 12, "gather_d_branch")
    d_attn = contract_last(d_branch_wide, out_weight).astype(bf16)
    d_attn_unit = as_slots(turn(to_units(d_attn), 13, "turn_d_attn"), 0)
    out_piece = reduce_rows(contract_first(attn_low, d_branch_wide), 1)
    delta = jnp.sum(d_attn_unit.astype(f32) * attn_exact, axis=1)
    delta = jnp.broadcast_to(delta[None, :], (8, slots))
    d_units = attend_back(unit_length, q_unit, k_unit, v_unit, d_attn_unit, log_total, delta)
    d_units = jnp.stack([d.reshape(row_count, tok_rows, HEAD_DIM) for d in d_units], axis=1)
    d_query_rot, d_key_rot, d_value = from_units(turn(d_units, 14, "turn_d_qkv"))
    d_query_norm = unrotate(d_query_rot.astype(f32), cosine, sine, HEAD_DIM)
    d_key_norm = unrotate(d_key_rot.astype(f32), cosine, sine, HEAD_DIM)
    q_gain_raw = jnp.sum(d_query_norm * query_pre * query_inv, axis=0)
    k_gain_raw = jnp.sum(d_key_norm * key_pre * key_inv, axis=0)
    query_scaled = d_query_norm * q_gain_half
    key_scaled = d_key_norm * k_gain_half
    inner = (
        feature_total(
            jnp.stack(
                [jnp.sum(query_scaled * query_pre, axis=1), jnp.sum(key_scaled * key_pre, axis=1)]
            ),
            True,
            15,
            "total_d_qk",
        )
        / width
    )
    d_query = (query_inv * query_scaled - query_pre * query_inv**3 * inner[0][:, None]).astype(
        bf16
    )
    d_key = (key_inv * key_scaled - key_pre * key_inv**3 * inner[1][:, None]).astype(bf16)
    d_qkv = jnp.concatenate([d_query, d_key, d_value], axis=1)
    qkv_piece = reduce_rows(contract_first(tokens_wide, d_qkv), 0)
    projected = contract_last(d_qkv, qkv_weight).astype(bf16)
    d_resid_total = scatter_wide(projected, 16, "scatter_projected")
    input_grad = d_resid + d_resid_total

    def spread(half):
        return lax.dynamic_update_slice_in_dim(jnp.zeros((feat_part,), f32), half, y * half_feat, 0)

    gains = lax.psum(
        jnp.stack([spread(q_gain_raw), spread(k_gain_raw), attn_gain_raw, mlp_gain_raw]) * factor,
        ("dp", "row"),
    )

    def finish(piece, axis):
        if data_count > 2:
            groups = [list(range(s, data_count, 2)) for s in (0, 1)]
            piece = lax.psum(piece, "dp", axis_index_groups=groups)
        other = lax.ppermute(piece, "dp", pairs)
        low = jnp.where(y == 0, piece, other).astype(f32)
        high = jnp.where(y == 0, other, piece).astype(f32)
        return jnp.concatenate([low, high], axis=axis)

    def columns(i):
        return qkv_piece[:, i * half_feat : (i + 1) * half_feat]

    return (
        block_output,
        input_grad,
        finish(columns(0), 1),
        finish(columns(1), 1),
        finish(columns(2), 1),
        finish(out_piece, 0),
        finish(gate_piece, 1),
        finish(up_piece, 1),
        finish(down_piece, 0),
        gains[0],
        gains[1],
        gains[2],
        gains[3],
    )


def solution(mesh):
    tok, row_col, col_row, gain = P(("dp", "row"), "col"), P("row", "col"), P("col", "row"), P("col")
    weights = (row_col, row_col, row_col, col_row, row_col, row_col, col_row)
    gains = (gain, gain, gain, gain)
    return jax.shard_map(
        per_device,
        mesh=mesh,
        in_specs=(tok, P("dp")) + weights + gains + (tok,),
        out_specs=(tok, tok) + weights + gains,
        check_vma=False,
    )
```

time: 2220 us -> 1140 us (0.51)
  waiting for transfers between devices: 1630 us -> 222 us
  Pallas kernels: 0 us -> 549 us
  matrix products: 287 us -> 149 us
  blocking collectives: 86.4 us -> 22.8 us
    all_gather x16 -> x5, waiting for transfers between devices: 815 us -> 23.6 us  [the longest x1 20 us: per_device(): lax.all_gather(jnp.concatenate([y_half(w_query, 1), y_half(w_key, 1), y_h...]
    reduce_scatter x13 -> x5, waiting for transfers between devices: 806 us -> 181 us  [reduce_rows(): lax.psum_scatter((raw * factor).astype(bf16), 'row', scatter_dimension=ax...]
    pallas_call x0 -> x19, Pallas kernels: none -> 549 us  [the longest x4 220 us: turn(): pl.pallas_call(turn_kernel, name=name, out_shape=jax.ShapeDtypeStruct(val...]
    dot_general x19 -> x5, matrix products: 113 us -> 51.6 us  [contract_last(): lax.dot_general(left, right, (((1,), (1,)), ((), ())), preferred_element_...]
    convert_element_type x15 -> x8, other arithmetic: 69.5 us -> 13 us  [the longest x1 4.1 us: per_device(): rotate(query_pre * query_inv * q_gain_half, cosine, sine, HEAD_DIM)]
    dot_general x15 -> x5, matrix products: 98 us -> 47.6 us  [matmul(): return jnp.dot(left, right, preferred_element_type=f32)]
    psum x7 -> x1, blocking collectives: 56.9 us -> 22.8 us  [per_device(): lax.psum(jnp.stack([spread(q_gain_raw), spread(k_gain_raw), attn_gain_raw...]
    all_gather x4 -> x0, blocking collectives: 29.5 us -> none  [the longest x1 7.41 us: per_device(): lax.all_gather(pieces[3].astype(jnp.bfloat16), 'dp', axis=1, tiled=True)]
  transfers between devices with their start and end apart: 29 -> 18, of which waited for: 26 -> 6; matrix products, arithmetic and copies ran while one was open for 17% -> 17% of each run, Pallas kernels for 0% -> 27%
where the time goes in v1:
time: 1140 us; the launch traced here: 1130 us
  Pallas kernels  549 us (48%)
  waiting for transfers between devices  222 us (19%)
  matrix products  149 us (13%)
  local copies, waits for them, and re-layouts  79.6 us (7%)
  other arithmetic  76.9 us (7%)
  blocking collectives  22.8 us (2%)
  between operations  16 us (1%)
    pallas_call x4, Pallas kernels, turn(): pl.pallas_call(turn_kernel, name=name, out_shape=jax.ShapeDtypeStruct(val...  220 us
    reduce_scatter x5, waiting for transfers between devices, reduce_rows(): lax.psum_scatter((raw * factor).astype(bf16), 'row', scatter_dimension=ax...  181 us
    pallas_call x4, Pallas kernels, scatter_wide(): pl.pallas_call(scatter_kernel, name=name, out_shape=jax.ShapeDtypeStruct(...  137 us
    pallas_call x4, Pallas kernels, gather_wide(): pl.pallas_call(gather_kernel, name=name, out_shape=jax.ShapeDtypeStruct((...  127 us
    dot_general x5, matrix products, contract_last(): lax.dot_general(left, right, (((1,), (1,)), ((), ())), preferred_element_...  51.6 us
    dot_general x5, matrix products, contract_first(): lax.dot_general(left, right, (((0,), (0,)), ((), ())), preferred_element_...  49.8 us
    dot_general x5, matrix products, matmul(): return jnp.dot(left, right, preferred_element_type=f32)  47.6 us
    pallas_call x5, Pallas kernels, feature_total(): pl.pallas_call(functools.partial(total_kernel, wide), name=name, out_shap...  27.5 us
  transfers between devices with their start and end apart: 18, of which 6 were waited for; matrix products, arithmetic and copies ran while one was open for 17% of the time, Pallas kernels for 27%

profile of v1, /device:TPU:0, one launch (start us, length us, event | category | flops | bytes accessed | tf_op | source)
XLA Modules:
  0.0 1125.8 jit_solution(13979636075220478940)
XLA Ops:
  19.9 31.4 %gather_tokens.1 = bf16[1536,2048]{1,0:T(8,128)(2,1)} custom-call(bf16[768,512]{1,0:T(8,128)(2,1)} %x_ref.1), custom_call_target="tpu_custom_call" | custom-call | bytes 60000000 | tf_op jit(solution)/shard_map/gather_tokens/pallas_call | solution.py:138
  56.8 20.0 %all-gather.6.cloned.1.call-done = bf16[2048,768]{1,0:T(8,128)(2,1)} async-done(((bf16[512,768]{1,0:T(8,128)(2,1)}), bf16[2048,768]{1,0:T(8,128)(2,1)}) %all-gather.6.cloned.1.call-update) | async-done | bytes 3145744 | tf_op jit(solution)/shard_map/all_gather | solution.py:542
  76.8 9.6 convolution_bitcast_fusion
  91.6 6.3 total_qk.1
  119.9 5.6 maximum_multiply_fusion
  131.5 4.1 fusion.3
  142.8 94.7 %turn_qkv.1 = bf16[4,3,768,128]{3,2,1,0:T(8,128)(2,1)} custom-call(bf16[4,3,768,128]{3,2,1,0:T(8,128)(2,1)} %pad_maximum_fusion.x_ref), custom_call_target="tpu_custom_call" | custom-call | bytes 100000000 | tf_op jit(solution)/shard_map/turn_qkv/pallas_call | solution.py:339
  237.4 3.3 fusion.28
  240.7 16.7 %attend.1 = (bf16[3072,128]{1,0:T(8,128)(2,1)}, f32[3072,128]{1,0:T(8,128)}, f32[8,3072]{1,0:T(8,128)}) custom-call(s32[1]{0:T(128)} %dynamic_slice.30.len_ref, bf16[3072,128]{1,0:T(8,128)(2,1)} %bitcast.197, bf16[3072,128]{1,0:T(8,128)(2,1)} %bitcast.195, bf16[3072,128]{1,0:T(8,128)(2,1)} %bitcast.193), custom_call_target="tpu_custom_call" | custom-call | flops 2415919104 | bytes 3145728 | tf_op jit(solution)/shard_map/attend/pallas_call | solution.py:421
  257.4 44.4 %turn_attn.1 = bf16[4,1,768,128]{3,2,1,0:T(8,128)(2,1)} custom-call(bf16[4,1,768,128]{3,2,1,0:T(8,128)(2,1)} %bitcast.204), custom_call_target="tpu_custom_call" | custom-call | bytes 100000000 | tf_op jit(solution)/shard_map/turn_attn/pallas_call | solution.py:339
  307.7 34.5 %scatter_branch.1 = f32[768,512]{1,0:T(8,128)S(1)} custom-call(bf16[1536,2048]{1,0:T(8,128)(2,1)S(1)} %convolution_convert_fusion.1.p_ref), custom_call_target="tpu_custom_call" | custom-call | bytes 80000000 | tf_op jit(solution)/shard_map/scatter_branch/pallas_call | solution.py:236
  343.0 4.9 total_branch.1
  349.8 31.9 %gather_resid.1 = bf16[1536,2048]{1,0:T(8,128)(2,1)} custom-call(bf16[768,512]{1,0:T(8,128)(2,1)} %fusion.10.x_ref), custom_call_target="tpu_custom_call" | custom-call | bytes 60000000 | tf_op jit(solution)/shard_map/gather_resid/pallas_call | solution.py:138
  381.7 11.7 %fusion.34 = f32[1536,1024]{1,0:T(8,128)} fusion(bf16[1536,2048]{1,0:T(8,128)(2,1)} %gather_resid.1, bf16[2048,1024]{1,0:T(8,128)(2,1)} %all-gather.10.cloned.1.call-done), kind=kOutput, calls=%fused_computation.143 | convolution fusion | flops 6442450944 | bytes 16777216 | tf_op jit(solution)/shard_map/dot_general | solution.py:47
  393.4 13.8 %multiply_convert_fusion.6 = (bf16[1536,1024]{1,0:T(8,128)(2,1)}, f32[1536,1024]{1,0:T(8,128)}) fusion(f32[1536,1024]{1,0:T(8,128)} %fusion.34, bf16[1536,2048]{1,0:T(8,128)(2,1)} %gather_resid.1, bf16[2048,1024]{1,0:T(8,128)(2,1)} %all-gather.12.cloned.1.call-done), kind=kOutput, calls=%fused_computation.10 | convolution fusion | flops 6451888128 | bytes 26214400 | tf_op jit(solution)/shard_map/dot_general | solution.py:47
  407.2 3.5 all-gather.14.cloned.1.call-done
  410.8 9.5 convolution_convert_fusion.2.p_ref
  420.3 34.4 %scatter_mixed.1 = f32[768,512]{1,0:T(8,128)S(1)} custom-call(bf16[1536,2048]{1,0:T(8,128)(2,1)S(1)} %convolution_convert_fusion.2.p_ref), custom_call_target="tpu_custom_call" | custom-call | bytes 80000000 | tf_op jit(solution)/shard_map/scatter_mixed/pallas_call | solution.py:236
  456.0 5.0 total_mixed.1
  464.9 31.7 %gather_d_mixed.1 = bf16[1536,2048]{1,0:T(8,128)(2,1)} custom-call(bf16[768,512]{1,0:T(8,128)(2,1)} %subtract_convert_fusion.3.x_ref), custom_call_target="tpu_custom_call" | custom-call | bytes 60000000 | tf_op jit(solution)/shard_map/gather_d_mixed/pallas_call | solution.py:138
  496.7 17.2 %multiply_convert_fusion.4 = (bf16[1536,1024]{1,0:T(8,128)(2,1)}, bf16[1536,1024]{1,0:T(8,128)(2,1)}) fusion(f32[1536,1024]{1,0:T(8,128)} %fusion.34, f32[1536,1024]{1,0:T(8,128)} %get-tuple-element.130, bf16[1536,2048]{1,0:T(8,128)(2,1)} %gather_d_mixed.1, bf16[1024,2048]{1,0:T(8,128)(2,1)} %all-gather.14.cloned.1.call-done), kind=kOutput, calls=%fused_computation.8 | convolution fusion | flops 6462898176 | bytes 29360128 | tf_op jit(solution)/shard_map/dot_general | solution.py:55
  513.9 11.7 %fusion.35 = f32[1536,2048]{1,0:T(8,128)} fusion(bf16[1536,1024]{1,0:T(8,128)(2,1)} %get-tuple-element.67, bf16[2048,1024]{1,0:T(8,128)(2,1)S(1)} %copy-done.43), kind=kOutput, calls=%fused_computation.144 | convolution fusion | flops 6442450944 | bytes 19922944 | tf_op jit(solution)/shard_map/dot_general | solution.py:55
  525.6 10.7 add_convert_fusion.p_ref
  536.4 33.7 %scatter_d_resid.1 = f32[768,512]{1,0:T(8,128)S(1)} custom-call(bf16[1536,2048]{1,0:T(8,128)(2,1)S(1)} %add_convert_fusion.p_ref), custom_call_target="tpu_custom_call" | custom-call | bytes 80000000 | tf_op jit(solution)/shard_map/scatter_d_resid/pallas_call | solution.py:236
  570.1 3.1 multiply_reduce_fusion.1
  573.2 4.9 total_d_resid.1
  581.4 31.8 %gather_d_branch.1 = bf16[1536,2048]{1,0:T(8,128)(2,1)} custom-call(bf16[768,512]{1,0:T(8,128)(2,1)} %subtract_convert_fusion.2.x_ref), custom_call_target="tpu_custom_call" | custom-call | bytes 60000000 | tf_op jit(solution)/shard_map/gather_d_branch/pallas_call | solution.py:138
  613.2 5.6 fusion.1
  618.7 4.9 convolution_convert_fusion.3
  624.8 22.2 %turn_d_attn.1 = bf16[4,1,768,128]{3,2,1,0:T(8,128)(2,1)} custom-call(bf16[4,1,768,128]{3,2,1,0:T(8,128)(2,1)} %bitcast.188), custom_call_target="tpu_custom_call" | custom-call | bytes 100000000 | tf_op jit(solution)/shard_map/turn_d_attn/pallas_call | solution.py:339
  649.2 20.8 %attend_back.1 = (bf16[3072,128]{1,0:T(8,128)(2,1)}, bf16[3072,128]{1,0:T(8,128)(2,1)}, bf16[3072,128]{1,0:T(8,128)(2,1)}) custom-call(s32[1]{0:T(128)} %dynamic_slice.30.len_ref, bf16[3072,128]{1,0:T(8,128)(2,1)} %bitcast.198, bf16[3072,128]{1,0:T(8,128)(2,1)} %bitcast.196, bf16[3072,128]{1,0:T(8,128)(2,1)} %bitcast.194, bf16[3072,128]{1,0:T(8,128)(2,1)} %bitcast.190, ...), custom_call_target="tpu_custom_call" | custom-call | flops 6039797760 | bytes 5505024 | tf_op jit(solution)/shard_map/attend_back/pallas_call | solution.py:496
  670.1 3.3 pad_maximum_fusion.1.x_ref
  673.3 59.0 %turn_d_qkv.1 = bf16[4,3,768,128]{3,2,1,0:T(8,128)(2,1)} custom-call(bf16[4,3,768,128]{3,2,1,0:T(8,128)(2,1)} %pad_maximum_fusion.1.x_ref), custom_call_target="tpu_custom_call" | custom-call | bytes 100000000 | tf_op jit(solution)/shard_map/turn_d_qkv/pallas_call | solution.py:339
  750.8 4.1 copy.53
  757.8 5.9 multiply_reduce_fusion.3
  764.3 6.3 total_d_qk.1
  771.3 3.2 copy.55
  779.9 10.5 fusion
  790.5 11.2 multiply_convert_fusion
  801.8 11.2 multiply_convert_fusion.1
  813.1 11.3 %multiply_convert_fusion.2 = bf16[2048,1024]{1,0:T(8,128)(2,1)} fusion(bf16[1536,2048]{1,0:T(8,128)(2,1)} %gather_resid.1, bf16[1536,1024]{1,0:T(8,128)(2,1)} %get-tuple-element.67), kind=kOutput, calls=%fused_computation.3 | convolution fusion | flops 6446645248 | bytes 13631488 | tf_op jit(solution)/shard_map/dot_general | solution.py:51
  825.8 7.1 convolution_convert_fusion.p_ref
  832.9 34.2 %scatter_projected.1 = f32[768,512]{1,0:T(8,128)S(1)} custom-call(bf16[1536,2048]{1,0:T(8,128)(2,1)S(1)} %convolution_convert_fusion.p_ref), custom_call_target="tpu_custom_call" | custom-call | bytes 80000000 | tf_op jit(solution)/shard_map/scatter_projected/pallas_call | solution.py:236
  869.2 22.8 %psum.7 = f32[4,512]{1,0:T(4,128)S(1)} all-reduce(f32[4,512]{1,0:T(4,128)S(1)} %maximum_multiply_fusion.2), channel_id=1, replica_groups=mesh['dp'=2,'row'=4,'col'=4] {'dp','row'}, use_global_device_ids=true, to_apply=%region_18.19 | all-reduce | flops 2048 | bytes 16384 | tf_op jit(solution)/shard_map/psum | solution.py:705
  895.2 35.9 %reduce-scatter.14.cloned.1.call-done = bf16[1024,512]{1,0:T(8,128)(2,1)} async-done(((bf16[1024,2048]{1,0:T(8,128)(2,1)}), bf16[1024,512]{1,0:T(8,128)(2,1)}) %reduce-scatter.14.cloned.1.call-update) | async-done | bytes 1048592 | tf_op jit(solution)/shard_map/reduce_scatter | solution.py:642
  938.0 73.2 %reduce-scatter.12.cloned.1.call-done = bf16[512,1024]{1,0:T(8,128)(2,1)} async-done(((bf16[2048,1024]{1,0:T(8,128)(2,1)}), bf16[512,1024]{1,0:T(8,128)(2,1)}) %reduce-scatter.12.cloned.1.call-update) | async-done | bytes 1048592 | tf_op jit(solution)/shard_map/reduce_scatter | solution.py:642
  1019.1 72.1 %reduce-scatter.10.cloned.1.call-done = bf16[512,1024]{1,0:T(8,128)(2,1)} async-done(((bf16[2048,1024]{1,0:T(8,128)(2,1)}), bf16[512,1024]{1,0:T(8,128)(2,1)}) %reduce-scatter.10.cloned.1.call-update) | async-done | bytes 1048592 | tf_op jit(solution)/shard_map/reduce_scatter | solution.py:642
  1099.5 16.6 %collective-permute-done.5 = bf16[512,1024]{1,0:T(8,128)(2,1)S(1)} collective-permute-done((bf16[512,1024]{1,0:T(8,128)(2,1)}, bf16[512,1024]{1,0:T(8,128)(2,1)S(1)}, u32[]{:S(2)}, u32[]{:S(2)}) %collective-permute-start.5) | collective-permute-done | bytes 1048608 | tf_op jit(solution)/shard_map/ppermute | solution.py:714
  (243 shorter events, 138.3 us)
Async XLA Ops:
  7.2 4.2 copy-start
  7.2 69.6 %all-gather.6.cloned.1.call-start = ((), (), s32[]{:S(2)}) async-start(), calls=%async_computation.5 | async-start | bytes 3932160 | tf_op jit(solution)/shard_map/all_gather | solution.py:542
  10.5 293.4 %all-gather.8.cloned.1.call-start = ((), (), s32[]{:S(2)}) async-start(), calls=%async_computation.6 | async-start | bytes 1310720 | tf_op jit(solution)/shard_map/all_gather | solution.py:548
  11.3 370.4 %all-gather.10.cloned.1.call-start = ((), (), s32[]{:S(2)}) async-start(), calls=%async_computation.7 | async-start | bytes 5242880 | tf_op jit(solution)/shard_map/all_gather | solution.py:549
  12.4 5.6 copy-start.27
  12.5 381.0 %all-gather.12.cloned.1.call-start = ((), (), s32[]{:S(2)}) async-start(), calls=%async_computation.8 | async-start | bytes 5242880 | tf_op jit(solution)/shard_map/all_gather | solution.py:550
  14.9 395.8 %all-gather.14.cloned.1.call-start = ((), (), s32[]{:S(2)}) async-start(), calls=%async_computation.9 | async-start | bytes 5242880 | tf_op jit(solution)/shard_map/all_gather | solution.py:551
  15.0 40.5 %collective-permute-start = (s32[1]{0:T(128)}, s32[1]{0:T(128)}, u32[]{:S(2)}, u32[]{:S(2)}) collective-permute-start(s32[1]{0:T(128)} %param.15), channel_id=1, source_target_pairs={{0,16},{16,0},{1,17},{17,1},{2,18},{18,2},{3,19},{19,3},{4,20},{20... | collective-permute-start | bytes 20 | tf_op jit(solution)/shard_map/ppermute | solution.py:558
  19.1 849.5 %reduce-scatter.8.cloned.1.call-start = ((), (), s32[]{:S(2)}) async-start(), calls=%async_computation.11 | async-start | bytes 1310720 | tf_op jit(solution)/shard_map/reduce_scatter | solution.py:642
  19.8 31.4 %copy-start.41 = (f32[512]{0:T(512)S(1)}, f32[512]{0:T(512)}, u32[]{:S(2)}) copy-start(f32[512]{0:T(512)} %param.23) | copy-start | bytes 6148
  19.9 31.5 %copy-start.42 = (f32[512]{0:T(512)S(1)}, f32[512]{0:T(512)}, u32[]{:S(2)}) copy-start(f32[512]{0:T(512)} %param.24) | copy-start | bytes 6148
  51.3 47.3 %copy-start.37 = (f32[256]{0:T(256)}, f32[256]{0:T(256)S(1)}, u32[]{:S(2)}) copy-start(f32[256]{0:T(256)S(1)} %dynamic_slice.34) | copy-start | bytes 3076
  51.4 47.2 %copy-start.39 = (f32[256]{0:T(256)}, f32[256]{0:T(256)S(1)}, u32[]{:S(2)}) copy-start(f32[256]{0:T(256)S(1)} %dynamic_slice.35) | copy-start | bytes 3076
  135.6 3.2 copy-start.15
  342.2 6.4 copy-start.11
  342.2 6.4 copy-start.35
  349.8 31.9 %copy-start.34 = (f32[6,128]{1,0:T(8,128)S(1)}, f32[6,128]{1,0:T(8,128)}, u32[]{:S(2)}) copy-start(f32[6,128]{1,0:T(8,128)} %total_branch.1) | copy-start | bytes 9220
  420.3 34.5 %copy-start.4 = (bf16[768,512]{1,0:T(8,128)(2,1)S(1)}, bf16[768,512]{1,0:T(8,128)(2,1)}, u32[]{:S(2)}) copy-start(bf16[768,512]{1,0:T(8,128)(2,1)} %param.27) | copy-start | bytes 2359300
  420.3 34.5 %copy-start.36 = (f32[512]{0:T(512)S(1)}, f32[512]{0:T(512)}, u32[]{:S(2)}) copy-start(f32[512]{0:T(512)} %param.26) | copy-start | bytes 6148
  454.8 10.1 copy-start.2
  496.6 17.3 %copy-start.43 = (bf16[2048,1024]{1,0:T(8,128)(2,1)S(1)}, bf16[2048,1024]{1,0:T(8,128)(2,1)}, u32[]{:S(2)}) copy-start(bf16[2048,1024]{1,0:T(8,128)(2,1)} %all-gather.10.cloned.1.call-done) | copy-start | bytes 12582916
  513.9 11.7 %copy-start.44 = (bf16[2048,1024]{1,0:T(8,128)(2,1)S(1)}, bf16[2048,1024]{1,0:T(8,128)(2,1)}, u32[]{:S(2)}) copy-start(bf16[2048,1024]{1,0:T(8,128)(2,1)} %all-gather.12.cloned.1.call-done) | copy-start | bytes 12582916
  536.3 33.7 %copy-start.3 = (f32[768,512]{1,0:T(8,128)S(1)}, f32[768,512]{1,0:T(8,128)}, u32[]{:S(2)}) copy-start(f32[768,512]{1,0:T(8,128)} %copy-done.2) | copy-start | bytes 4718596
  536.3 33.7 %copy-start.5 = (bf16[768,512]{1,0:T(8,128)(2,1)S(1)}, bf16[768,512]{1,0:T(8,128)(2,1)}, u32[]{:S(2)}) copy-start(bf16[768,512]{1,0:T(8,128)(2,1)} %param.27) | copy-start | bytes 2359300
  536.3 33.7 %copy-start.12 = (bf16[768,512]{1,0:T(8,128)(2,1)S(1)}, bf16[768,512]{1,0:T(8,128)(2,1)}, u32[]{:S(2)}) copy-start(bf16[768,512]{1,0:T(8,128)(2,1)} %x_ref.1) | copy-start | bytes 2359300
  581.4 31.8 %copy-start.8 = (bf16[2,2,768,128]{3,1,2,0:T(2,128)(2,1)S(1)}, bf16[2,2,768,128]{3,1,2,0:T(2,128)(2,1)}, u32[]{:S(2)}) copy-start(bf16[2,2,768,128]{3,1,2,0:T(2,128)(2,1)} %copy-done.7) | copy-start | bytes 2359300
  624.8 22.2 %copy-start.18 = (f32[3072,128]{1,0:T(8,128)S(1)}, f32[3072,128]{1,0:T(8,128)}, u32[]{:S(2)}) copy-start(f32[3072,128]{1,0:T(8,128)} %get-tuple-element.21) | copy-start | bytes 4718596
  754.9 2.8 copy-start.31
  754.9 2.8 copy-start.33
  754.9 2.8 copy-start.38
  754.9 2.9 copy-start.40
  757.7 134.4 %reduce-scatter.6.cloned.1.call-start = ((), (), s32[]{:S(2)}) async-start(), calls=%async_computation.10 | async-start | bytes 3932160 | tf_op jit(solution)/shard_map/reduce_scatter | solution.py:642
  771.3 4.5 copy-start.13
  775.9 3.0 copy-start.26
  790.4 140.7 %reduce-scatter.14.cloned.1.call-start = ((), (), s32[]{:S(2)}) async-start(), calls=%async_computation.14 | async-start | bytes 5242880 | tf_op jit(solution)/shard_map/reduce_scatter | solution.py:642
  801.7 209.5 %reduce-scatter.12.cloned.1.call-start = ((), (), s32[]{:S(2)}) async-start(), calls=%async_computation.13 | async-start | bytes 5242880 | tf_op jit(solution)/shard_map/reduce_scatter | solution.py:642
  813.0 278.3 %reduce-scatter.10.cloned.1.call-start = ((), (), s32[]{:S(2)}) async-start(), calls=%async_computation.12 | async-start | bytes 5242880 | tf_op jit(solution)/shard_map/reduce_scatter | solution.py:642
  832.8 34.3 %copy-start.6 = (bf16[768,512]{1,0:T(8,128)(2,1)S(1)}, bf16[768,512]{1,0:T(8,128)(2,1)}, u32[]{:S(2)}) copy-start(bf16[768,512]{1,0:T(8,128)(2,1)} %param.27) | copy-start | bytes 2359300
  868.6 25.6 %collective-permute-start.4 = (bf16[256,512]{1,0:T(8,128)(2,1)}, bf16[256,512]{1,0:T(8,128)(2,1)S(1)}, u32[]{:S(2)}, u32[]{:S(2)}) collective-permute-start(bf16[256,512]{1,0:T(8,128)(2,1)} %reduce-scatter.8.cloned.1.call-done), channel_id=1, source_target_pairs={{0,16},{16,0},{1,17},{17,1},{2,18},{18,2},{3,19},{19,3},{4,20},{20... | collective-permute-start | bytes 786440 | tf_op jit(solution)/shard_map/ppermute | solution.py:714
  892.1 40.5 %copy-start.16 = (bf16[512,768]{0,1:T(8,128)(2,1)S(1)}, bf16[512,768]{0,1:T(8,128)(2,1)}, u32[]{:S(2)}) copy-start(bf16[512,768]{0,1:T(8,128)(2,1)} %reduce-scatter.6.cloned.1.call-done) | copy-start | bytes 2359300
  893.2 39.4 %collective-permute-start.3 = (bf16[512,256]{0,1:T(8,128)(2,1)S(1)}, bf16[512,256]{0,1:T(8,128)(2,1)S(1)}, u32[]{:S(2)}, u32[]{:S(2)}) collective-permute-start(bf16[512,256]{0,1:T(8,128)(2,1)S(1)} %slice.144), channel_id=1, source_target_pairs={{0,16},{16,0},{1,17},{17,1},{2,18},{18,2},{3,19},{19,3},{4,20},{20... | collective-permute-start | bytes 786440 | tf_op jit(solution)/shard_map/ppermute | solution.py:714
  931.1 161.6 %collective-permute-start.7 = (bf16[1024,512]{1,0:T(8,128)(2,1)}, bf16[1024,512]{1,0:T(8,128)(2,1)S(1)}, u32[]{:S(2)}, u32[]{:S(2)}) collective-permute-start(bf16[1024,512]{1,0:T(8,128)(2,1)} %reduce-scatter.14.cloned.1.call-done), channel_id=1, source_target_pairs={{0,16},{16,0},{1,17},{17,1},{2,18},{18,2},{3,19},{19,3},{4,20},{20... | collective-permute-start | bytes 3145736 | tf_op jit(solution)/shard_map/ppermute | solution.py:714
  933.5 79.3 %collective-permute-start.1 = (bf16[512,256]{0,1:T(8,128)(2,1)}, bf16[512,256]{0,1:T(8,128)(2,1)S(1)}, u32[]{:S(2)}, u32[]{:S(2)}) collective-permute-start(bf16[512,256]{0,1:T(8,128)(2,1)} %get-tuple-element.100), channel_id=1, source_target_pairs={{0,16},{16,0},{1,17},{17,1},{2,18},{18,2},{3,19},{19,3},{4,20},{20... | collective-permute-start | bytes 786440 | tf_op jit(solution)/shard_map/ppermute | solution.py:714
  934.0 79.4 %collective-permute-start.2 = (bf16[512,256]{0,1:T(8,128)(2,1)}, bf16[512,256]{0,1:T(8,128)(2,1)}, u32[]{:S(2)}, u32[]{:S(2)}) collective-permute-start(bf16[512,256]{0,1:T(8,128)(2,1)} %get-tuple-element.99), channel_id=1, source_target_pairs={{0,16},{16,0},{1,17},{17,1},{2,18},{18,2},{3,19},{19,3},{4,20},{20... | collective-permute-start | bytes 786440 | tf_op jit(solution)/shard_map/ppermute | solution.py:714
  1011.2 84.3 %collective-permute-start.6 = (bf16[512,1024]{1,0:T(8,128)(2,1)}, bf16[512,1024]{1,0:T(8,128)(2,1)}, u32[]{:S(2)}, u32[]{:S(2)}) collective-permute-start(bf16[512,1024]{1,0:T(8,128)(2,1)} %reduce-scatter.12.cloned.1.call-done), channel_id=1, source_target_pairs={{0,16},{16,0},{1,17},{17,1},{2,18},{18,2},{3,19},{19,3},{4,20},{20... | collective-permute-start | bytes 3145736 | tf_op jit(solution)/shard_map/ppermute | solution.py:714
  1016.7 76.1 %copy-start.19 = (bf16[1024,512]{1,0:T(8,128)(2,1)S(1)}, bf16[1024,512]{1,0:T(8,128)(2,1)}, u32[]{:S(2)}) copy-start(bf16[1024,512]{1,0:T(8,128)(2,1)} %reduce-scatter.14.cloned.1.call-done) | copy-start | bytes 3145732
  1091.3 24.8 %collective-permute-start.5 = (bf16[512,1024]{1,0:T(8,128)(2,1)}, bf16[512,1024]{1,0:T(8,128)(2,1)S(1)}, u32[]{:S(2)}, u32[]{:S(2)}) collective-permute-start(bf16[512,1024]{1,0:T(8,128)(2,1)} %reduce-scatter.10.cloned.1.call-done), channel_id=1, source_target_pairs={{0,16},{16,0},{1,17},{17,1},{2,18},{18,2},{3,19},{19,3},{4,20},{20... | collective-permute-start | bytes 3145736 | tf_op jit(solution)/shard_map/ppermute | solution.py:714
  1096.9 19.2 %copy-start.21 = (bf16[512,1024]{1,0:T(8,128)(2,1)S(1)}, bf16[512,1024]{1,0:T(8,128)(2,1)}, u32[]{:S(2)}) copy-start(bf16[512,1024]{1,0:T(8,128)(2,1)} %reduce-scatter.10.cloned.1.call-done) | copy-start | bytes 3145732
  (15 other events, 24.8 us)
Sparse Core Ops, SparseCore 0:
  10.6 66.1 all-gather.5
  78.3 26.6 all-gather.7
  107.2 124.5 all-gather.9
  233.8 95.7 all-gather.11
  331.5 79.1 all-gather.13
  757.8 26.5 reduce-scatter.7
  790.6 59.6 reduce-scatter.5
  853.2 77.9 reduce-scatter.13
  934.0 77.2 reduce-scatter.11
  1014.0 77.2 reduce-scatter.9

commit v2 on v1

v2 whole, which is shorter than its diff:
```python
import functools
import math

import jax
import jax.numpy as jnp
from jax import lax
from jax.experimental import pallas as pl
from jax.experimental.pallas import tpu as pltpu
from jax.sharding import PartitionSpec as P

HEAD_DIM = 128
rope_base = 500000.0
norm_eps = 1e-06
masked_score = -1e30

MESH = pl.DeviceIdType.MESH
bf16 = jnp.bfloat16
f32 = jnp.float32


def rope_tables(positions, head_dim):
    half = head_dim // 2
    freq = 1.0 / rope_base ** (jnp.arange(half, dtype=f32) / half)
    angle = positions.astype(f32)[:, None] * freq[None, :]
    angle = jnp.concatenate([angle, angle], axis=1)
    return (jnp.cos(angle), jnp.sin(angle))


def matmul(left, right):
    return jnp.dot(left, right, preferred_element_type=f32)


def contract_first(left, right):
    return lax.dot_general(left, right, (((0,), (0,)), ((), ())), preferred_element_type=f32)


def contract_last(left, right):
    return lax.dot_general(left, right, (((1,), (1,)), ((), ())), preferred_element_type=f32)


def flip(axis, bit):
    return lax.axis_index(axis) ^ bit


def side(axis):
    return lax.axis_index(axis) & 1


def greet(peers):
    barrier = pltpu.get_barrier_semaphore()
    for peer in peers:
        pl.semaphore_signal(barrier, inc=1, device_id=peer, device_id_type=MESH)
    pl.semaphore_wait(barrier, len(peers))


def sender(send_sem, recv_sem, started):
    def send(src, dst, number, peer):
        copy = pltpu.make_async_remote_copy(
            src_ref=src,
            dst_ref=dst,
            send_sem=send_sem.at[number],
            recv_sem=recv_sem.at[number],
            device_id=peer,
            device_id_type=MESH,
        )
        copy.start()
        started.append(copy)
        return copy

    return send


def neighbours():
    return {"col": flip("col", 2)}, {"dp": flip("dp", 1)}, {"col": flip("col", 1)}


def gather_kernel(pair, x_ref, out_ref, local_sem, send_sem, recv_sem):
    rows, width = x_ref.shape
    half = rows // 2
    y, b, p = side("dp"), lax.axis_index("col"), side("row") if pair else 0
    to_x, to_y, to_c = neighbours()
    to_z = {"row": flip("row", 1)}
    greet([to_x, to_y, to_c] + ([to_z] if pair else []))
    started = []
    send = sender(send_sem, recv_sem, started)

    def slot(pp, yy, h, bb, n=half):
        return out_ref.at[
            pl.ds(pl.multiple_of((pp * 2 + yy) * rows + h * half, half), n),
            pl.ds(pl.multiple_of(bb * width, width), width),
        ]

    def open_flow(pp, low, high, base):
        xa = send(low, slot(pp, y, 0, b), base + 0, to_x)
        ya = send(high, slot(pp, y, 1, b), base + 1, to_y)
        c0 = send(low, slot(pp, y, 0, b), base + 6, to_c)
        yb = send(low, slot(pp, y, 0, b), base + 2, to_y)
        xb = send(high, slot(pp, y, 1, b), base + 3, to_x)
        c1 = send(high, slot(pp, y, 1, b), base + 7, to_c)
        return xa, ya, xb, yb, [c0, c1]

    def relay(pp, flow, base):
        xa, ya, xb, yb, core = flow
        xa.wait_recv()
        piece = slot(pp, y, 0, b ^ 2)
        yc = send(piece, piece, base + 4, to_y)
        core.append(send(piece, piece, base + 8, to_c))
        ya.wait_recv()
        piece = slot(pp, y ^ 1, 1, b)
        xc = send(piece, piece, base + 5, to_x)
        core.append(send(piece, piece, base + 9, to_c))
        yb.wait_recv()
        piece = slot(pp, y ^ 1, 0, b)
        core.append(send(piece, piece, base + 10, to_c))
        xb.wait_recv()
        piece = slot(pp, y, 1, b ^ 2)
        core.append(send(piece, piece, base + 11, to_c))
        return yc, xc, core

    def close_flow(pp, state, base):
        yc, xc, core = state
        yc.wait_recv()
        piece = slot(pp, y ^ 1, 0, b ^ 2)
        core.append(send(piece, piece, base + 12, to_c))
        xc.wait_recv()
        piece = slot(pp, y ^ 1, 1, b ^ 2)
        core.append(send(piece, piece, base + 13, to_c))
        for copy in core:
            copy.wait_recv()

    low, high = x_ref.at[pl.ds(0, half)], x_ref.at[pl.ds(half, half)]
    own = pltpu.make_async_copy(x_ref, slot(p, y, 0, b, rows), local_sem)
    if pair:
        z0 = send(low, slot(p, y, 0, b), 28, to_z)
        z1 = send(high, slot(p, y, 1, b), 29, to_z)
    first = open_flow(p, low, high, 0)
    own.start()
    state = relay(p, first, 0)
    if pair:
        z0.wait_recv()
        z1.wait_recv()
        second = open_flow(p ^ 1, slot(p ^ 1, y, 0, b), slot(p ^ 1, y, 1, b), 14)
    close_flow(p, state, 0)
    if pair:
        close_flow(p ^ 1, relay(p ^ 1, second, 14), 14)
    for copy in started:
        copy.wait_send()
    own.wait()


def gather_wide(values, pair, number, name):
    rows, width = values.shape
    copies = 30 if pair else 14
    return pl.pallas_call(
        functools.partial(gather_kernel, pair),
        name=name,
        out_shape=jax.ShapeDtypeStruct(((4 if pair else 2) * rows, 4 * width), values.dtype),
        in_specs=[pl.BlockSpec(memory_space=pltpu.VMEM)],
        out_specs=pl.BlockSpec(memory_space=pl.ANY),
        scratch_shapes=[
            pltpu.SemaphoreType.DMA,
            pltpu.SemaphoreType.DMA((copies,)),
            pltpu.SemaphoreType.DMA((copies,)),
        ],
        compiler_params=pltpu.CompilerParams(collective_id=number, has_side_effects=True),
        cost_estimate=pl.CostEstimate(flops=0, bytes_accessed=60_000_000, transcendentals=0),
    )(values)


def scatter_kernel(pair, p_ref, out_ref, rc, s1, ry, rx, s2, fy, fx, sz, fz, send_sem, recv_sem):
    rows, width = out_ref.shape
    half = rows // 2
    y, b, p = side("dp"), lax.axis_index("col"), side("row") if pair else 0
    x, c = b >> 1, b & 1
    to_x, to_y, to_c = neighbours()
    to_z = {"row": flip("row", 1)}
    greet([to_x, to_y, to_c] + ([to_z] if pair else []))
    started = []
    send = sender(send_sem, recv_sem, started)

    def place(yy, h):
        return pl.ds(pl.multiple_of(yy * rows + h * half, half), half)

    def column(bb):
        return pl.ds(pl.multiple_of(bb * width, width), width)

    order = [(0, y ^ 1, 0), (1, y ^ 1, 0), (x ^ 1, 0, 1), (x ^ 1, 1, 1)]
    order += [(0, y, 0), (1, y, 0), (x, 0, 1), (x, 1, 1)]

    class Flow:
        def __init__(self, f, pp):
            self.f, self.base = f, 14 * f
            self.rows = lambda yy, h: pl.ds(
                pl.multiple_of((pp * 2 + yy) * rows + h * half, half), half
            )
            self.core = [
                send(
                    p_ref.at[self.rows(yy, h), column(2 * xx + (c ^ 1))],
                    rc.at[f, xx, place(yy, h)],
                    self.base + number,
                    to_c,
                )
                for number, (xx, yy, h) in enumerate(order)
            ]

        def settle(self, *numbers):
            for number in numbers:
                self.core[number].wait_recv()
                xx, yy, h = order[number]
                s1[self.f, xx, place(yy, h), :] = (
                    p_ref[self.rows(yy, h), column(2 * xx + c)].astype(f32)
                    + rc[self.f, xx, place(yy, h), :].astype(f32)
                ).astype(s1.dtype)

        def first(self, i):
            f = self.f
            ya = send(s1.at[f, i, place(y ^ 1, 0), :], ry.at[f, i], self.base + 8 + i, to_y)
            part = s1.at[f, x ^ 1, pl.ds(i * rows + half, half), :]
            xa = send(part, rx.at[f, i], self.base + 10 + i, to_x)
            return ya, xa

        def second(self, copies):
            f = self.f
            for ya, _ in copies:
                ya.wait_recv()
            s2[f, 0] = (
                s1[f, x ^ 1, place(y, 0), :].astype(f32) + ry[f, x ^ 1].astype(f32)
            ).astype(s2.dtype)
            xb = send(s2.at[f, 0], fx.at[f], self.base + 12, to_x)
            for _, xa in copies:
                xa.wait_recv()
            s2[f, 1] = (
                s1[f, x, place(y ^ 1, 1), :].astype(f32) + rx[f, y ^ 1].astype(f32)
            ).astype(s2.dtype)
            yb = send(s2.at[f, 1], fy.at[f], self.base + 13, to_y)
            return xb, yb

        def last(self, copies):
            f = self.f
            xb, yb = copies
            keep = s1[f, x, place(y, 0), :].astype(f32) + ry[f, x].astype(f32)
            xb.wait_recv()
            low = keep + fx[f].astype(f32)
            keep = s1[f, x, place(y, 1), :].astype(f32) + rx[f, y].astype(f32)
            yb.wait_recv()
            return low, keep + fy[f].astype(f32)

    if pair:
        far = Flow(0, p ^ 1)
        near = Flow(1, p)
        far.settle(0, 1, 2, 3)
        far_first = [far.first(0), far.first(1)]
        far.settle(4, 5, 6, 7)
        near.settle(0, 1, 2, 3)
        near_first = [near.first(0)]
        near.settle(4, 5, 6, 7)
        far_second = far.second(far_first)
        near_first.append(near.first(1))
        low, high = far.last(far_second)
        sz[pl.ds(0, half), :] = low.astype(bf16)
        z0 = send(sz.at[pl.ds(0, half)], fz.at[pl.ds(0, half)], 28, to_z)
        sz[pl.ds(half, half), :] = high.astype(bf16)
        z1 = send(sz.at[pl.ds(half, half)], fz.at[pl.ds(half, half)], 29, to_z)
        low, high = near.last(near.second(near_first))
        z0.wait_recv()
        out_ref[pl.ds(0, half), :] = low + fz[pl.ds(0, half), :].astype(f32)
        z1.wait_recv()
        out_ref[pl.ds(half, half), :] = high + fz[pl.ds(half, half), :].astype(f32)
    else:
        near = Flow(0, 0)
        near.settle(0, 1, 2, 3)
        near_first = [near.first(0), near.first(1)]
        near.settle(4, 5, 6, 7)
        low, high = near.last(near.second(near_first))
        out_ref[pl.ds(0, half), :] = low
        out_ref[pl.ds(half, half), :] = high
    for copy in started:
        copy.wait_send()


def scatter_wide(partial, pair, number, name):
    flows = 2 if pair else 1
    rows, width = partial.shape[0] // (2 * flows), partial.shape[1] // 4
    half = rows // 2
    copies = 30 if pair else 14
    last = (rows, width) if pair else (16, 128)
    return pl.pallas_call(
        functools.partial(scatter_kernel, pair),
        name=name,
        out_shape=jax.ShapeDtypeStruct((rows, width), f32),
        in_specs=[pl.BlockSpec(memory_space=pltpu.VMEM)],
        out_specs=pl.BlockSpec(memory_space=pltpu.VMEM),
        scratch_shapes=[
            pltpu.VMEM((flows, 2, 2 * rows, width), bf16),
            pltpu.VMEM((flows, 2, 2 * rows, width), bf16),
            pltpu.VMEM((flows, 2, half, width), bf16),
            pltpu.VMEM((flows, 2, half, width), bf16),
            pltpu.VMEM((flows, 2, half, width), bf16),
            pltpu.VMEM((flows, half, width), bf16),
            pltpu.VMEM((flows, half, width), bf16),
            pltpu.VMEM(last, bf16),
            pltpu.VMEM(last, bf16),
            pltpu.SemaphoreType.DMA((copies,)),
            pltpu.SemaphoreType.DMA((copies,)),
        ],
        compiler_params=pltpu.CompilerParams(
            collective_id=number, has_side_effects=True, vmem_limit_bytes=48 * 2**20
        ),
        cost_estimate=pl.CostEstimate(flops=0, bytes_accessed=80_000_000, transcendentals=0),
    )(partial)


def feature_peers(wide):
    peers = []
    for d in range(1, 8 if wide else 4):
        peer = {"col": flip("col", d & 3)}
        if d >> 2:
            peer["dp"] = flip("dp", 1)
        peers.append(peer)
    return peers


def total_kernel(v_ref, out_ref, slots, send_sem, recv_sem):
    me = lax.axis_index("col")
    peers = feature_peers(False)
    greet(peers)
    started = []
    send = sender(send_sem, recv_sem, started)
    for d, peer in enumerate(peers):
        send(v_ref, slots.at[me], d, peer)
    slots[me] = v_ref[...]
    for copy in started:
        copy.wait_recv()
    total = slots[0]
    for i in range(1, 4):
        total = total + slots[i]
    out_ref[...] = total
    for copy in started:
        copy.wait_send()


def feature_total(values, number, name):
    k, t = values.shape
    flat = values.reshape(k * t // 128, 128)
    total = pl.pallas_call(
        total_kernel,
        name=name,
        out_shape=jax.ShapeDtypeStruct(flat.shape, f32),
        in_specs=[pl.BlockSpec(memory_space=pltpu.VMEM)],
        out_specs=pl.BlockSpec(memory_space=pltpu.VMEM),
        scratch_shapes=[
            pltpu.VMEM((4,) + flat.shape, f32),
            pltpu.SemaphoreType.DMA((3,)),
            pltpu.SemaphoreType.DMA((3,)),
        ],
        compiler_params=pltpu.CompilerParams(collective_id=number, has_side_effects=True),
    )(flat)
    return total.reshape(k, t)


def row_peers():
    return [(d, {"row": flip("row", d)}) for d in (3, 2, 1)]


def unit_view(ref, unit, tok, heads):
    rows = pl.ds(pl.multiple_of((unit // heads) * tok, tok), tok)
    cols = pl.ds(pl.multiple_of((unit % heads) * HEAD_DIM, HEAD_DIM), HEAD_DIM)
    return ref.at[rows, cols]


def turn_kernel(back, tok, heads, x_ref, out_ref, local_sem, send_sem, recv_sem):
    z = lax.axis_index("row")
    greet([peer for _, peer in row_peers()])
    started = []
    send = sender(send_sem, recv_sem, started)

    def line(ref, i):
        return ref.at[pl.ds(pl.multiple_of(i * tok, tok), tok)]

    def ends(i):
        if back:
            return line(x_ref, i), unit_view(out_ref, z, tok, heads)
        return unit_view(x_ref, i, tok, heads), line(out_ref, z)

    for d, peer in row_peers():
        send(*ends(z ^ d), d - 1, peer)
    own = pltpu.make_async_copy(*ends(z), local_sem)
    own.start()
    for copy in started:
        copy.wait()
    own.wait()


def turn(values, back, tok, heads, number, name):
    shape = (2 * tok, heads * HEAD_DIM) if back else (2 * heads * tok, HEAD_DIM)
    return pl.pallas_call(
        functools.partial(turn_kernel, back, tok, heads),
        name=name,
        out_shape=jax.ShapeDtypeStruct(shape, values.dtype),
        in_specs=[pl.BlockSpec(memory_space=pltpu.VMEM)],
        out_specs=pl.BlockSpec(memory_space=pl.ANY),
        scratch_shapes=[
            pltpu.SemaphoreType.DMA,
            pltpu.SemaphoreType.DMA((3,)),
            pltpu.SemaphoreType.DMA((3,)),
        ],
        compiler_params=pltpu.CompilerParams(collective_id=number, has_side_effects=True),
        cost_estimate=pl.CostEstimate(flops=0, bytes_accessed=60_000_000, transcendentals=0),
    )(values)


def totals(stat, slots, started):
    for copy in started:
        copy.wait_recv()
    total = slots[0]
    for i in range(1, 8):
        total = total + slots[i]
    return total


def front_kernel(
    width,
    qkv_ref,
    cos_ref,
    sin_ref,
    gain_ref,
    out_ref,
    inv_ref,
    turned,
    packed,
    stat,
    slots,
    local_sem,
    stat_send,
    stat_recv,
    send_sem,
    recv_sem,
):
    count, tok = qkv_ref.shape[0], cos_ref.shape[0]
    part = qkv_ref.shape[1] // 3
    heads = part // HEAD_DIM
    z = lax.axis_index("row")
    me = side("dp") * 4 + lax.axis_index("col")
    peers = feature_peers(True)
    greet(peers + [peer for _, peer in row_peers()])
    for i in range(2):
        values = qkv_ref[:, i * part : (i + 1) * part]
        stat[i : i + 1, :] = jnp.sum(values * values, axis=1, keepdims=True).T
    started, moved, local = [], [], []
    send = sender(stat_send, stat_recv, started)
    for d, peer in enumerate(peers):
        send(stat, slots.at[me], d, peer)
    slots[me] = stat[...]
    move = sender(send_sem, recv_sem, moved)

    def ship(i):
        for d, peer in row_peers():
            move(packed.at[z ^ d, i], out_ref.at[z, i], 3 * i + d - 1, peer)
        copy = pltpu.make_async_copy(packed.at[z, i], out_ref.at[z, i], local_sem.at[i])
        copy.start()
        local.append(copy)

    def spots():
        return [(s, h, s * heads + h) for s in range(2) for h in range(heads)]

    for s, h, unit in spots():
        packed[unit, 2] = qkv_ref[
            s * tok : (s + 1) * tok, 2 * part + h * HEAD_DIM : 2 * part + (h + 1) * HEAD_DIM
        ].astype(bf16)
    ship(2)
    for i in (1, 0):
        for s, h, unit in spots():
            values = (
                qkv_ref[s * tok : (s + 1) * tok, i * part + h * HEAD_DIM : i * part + (h + 1) * HEAD_DIM]
                * gain_ref[i : i + 1, h * HEAD_DIM : (h + 1) * HEAD_DIM]
            )
            turned[i, unit] = values * cos_ref[...] + pltpu.roll(values, HEAD_DIM // 2, 1) * sin_ref[...]
    inverse = lax.rsqrt(totals(stat, slots, started) / width + norm_eps)
    inv_ref[...] = inverse
    for i in (1, 0):
        column = inverse[i : i + 1, :].T
        for s, h, unit in spots():
            packed[unit, i] = (turned[i, unit] * column[s * tok : (s + 1) * tok]).astype(bf16)
        ship(i)
    for copy in moved:
        copy.wait()
    for copy in local:
        copy.wait()
    for copy in started:
        copy.wait_send()


def front(qkv, cosine, sine_signed, gains, width, units, number):
    count, tok = qkv.shape[0], cosine.shape[0]
    return pl.pallas_call(
        functools.partial(front_kernel, width),
        name="front",
        out_shape=(
            jax.ShapeDtypeStruct((units, 3, tok, HEAD_DIM), bf16),
            jax.ShapeDtypeStruct((2, count), f32),
        ),
        in_specs=[pl.BlockSpec(memory_space=pltpu.VMEM)] * 4,
        out_specs=(pl.BlockSpec(memory_space=pl.ANY), pl.BlockSpec(memory_space=pltpu.VMEM)),
        scratch_shapes=[
            pltpu.VMEM((2, units, tok, HEAD_DIM), f32),
            pltpu.VMEM((units, 3, tok, HEAD_DIM), bf16),
            pltpu.VMEM((2, count), f32),
            pltpu.VMEM((8, 2, count), f32),
            pltpu.SemaphoreType.DMA((3,)),
            pltpu.SemaphoreType.DMA((7,)),
            pltpu.SemaphoreType.DMA((7,)),
            pltpu.SemaphoreType.DMA((9,)),
            pltpu.SemaphoreType.DMA((9,)),
        ],
        compiler_params=pltpu.CompilerParams(
            collective_id=number, has_side_effects=True, vmem_limit_bytes=40 * 2**20
        ),
        cost_estimate=pl.CostEstimate(flops=0, bytes_accessed=120_000_000, transcendentals=0),
    )(qkv, cosine, sine_signed, gains)


def rear_kernel(
    width,
    d_ref,
    qkv_ref,
    cos_ref,
    sin_ref,
    gain_ref,
    inv_ref,
    out_ref,
    sums_ref,
    landed,
    normed,
    stat,
    slots,
    stat_send,
    stat_recv,
    send_sem,
    recv_sem,
):
    count, tok = qkv_ref.shape[0], cos_ref.shape[0]
    part = qkv_ref.shape[1] // 2
    heads = part // HEAD_DIM
    z = lax.axis_index("row")
    me = side("dp") * 4 + lax.axis_index("col")
    peers = feature_peers(True)
    greet(peers + [peer for _, peer in row_peers()])
    started, moved = [], []
    move = sender(send_sem, recv_sem, moved)
    for i in (0, 1, 2):
        for d, peer in row_peers():
            there = pl.ds(pl.multiple_of((z ^ d) * tok, tok), tok)
            move(d_ref.at[i, there], landed.at[z, i], 3 * i + d - 1, peer)
    here = pl.ds(pl.multiple_of(z * tok, tok), tok)
    for i in (0, 1, 2):
        landed[z, i] = d_ref[i, here, :]
    spots = [(s, h, s * heads + h) for s in range(2) for h in range(heads)]
    for i in (0, 1):
        for copy in moved[3 * i : 3 * i + 3]:
            copy.wait_recv()
        for h in range(heads):
            cols = slice(i * part + h * HEAD_DIM, i * part + (h + 1) * HEAD_DIM)
            gain = gain_ref[i : i + 1, h * HEAD_DIM : (h + 1) * HEAD_DIM]
            raw = jnp.zeros((1, HEAD_DIM), f32)
            for s in range(2):
                rows = slice(s * tok, (s + 1) * tok)
                values = landed[s * heads + h, i].astype(f32)
                back = values * cos_ref[...] - pltpu.roll(values, HEAD_DIM // 2, 1) * sin_ref[...]
                pre = qkv_ref[rows, cols]
                inverse = inv_ref[i : i + 1, rows].T
                crossed = back * pre
                raw = raw + jnp.sum(crossed * inverse, axis=0, keepdims=True)
                partial = jnp.sum(crossed * gain, axis=1, keepdims=True).T
                if h == 0:
                    stat[i : i + 1, rows] = partial
                else:
                    stat[i : i + 1, rows] = stat[i : i + 1, rows] + partial
                normed[rows, cols] = back * gain
            sums_ref[i : i + 1, h * HEAD_DIM : (h + 1) * HEAD_DIM] = raw
    send = sender(stat_send, stat_recv, started)
    for d, peer in enumerate(peers):
        send(stat, slots.at[me], d, peer)
    slots[me] = stat[...]
    for copy in moved[6:]:
        copy.wait_recv()
    for s, h, unit in spots:
        cols = slice(2 * part + h * HEAD_DIM, 2 * part + (h + 1) * HEAD_DIM)
        out_ref[s * tok : (s + 1) * tok, cols] = landed[unit, 2]
    inner = totals(stat, slots, started) / width
    for i in (0, 1):
        inverse = inv_ref[i : i + 1, :]
        first = inverse.T
        second = (inverse * inverse * inverse * inner[i : i + 1, :]).T
        cols = slice(i * part, (i + 1) * part)
        out_ref[:, cols] = (first * normed[:, cols] - qkv_ref[:, cols] * second).astype(bf16)
    for copy in moved + started:
        copy.wait_send()


def rear(d_units, qkv, cosine, sine_signed, gains, inverse, width, number):
    count, tok = qkv.shape[0], cosine.shape[0]
    part = qkv.shape[1] // 2
    units = d_units.shape[1] // tok
    return pl.pallas_call(
        functools.partial(rear_kernel, width),
        name="rear",
        out_shape=(
            jax.ShapeDtypeStruct((count, 3 * part), bf16),
            jax.ShapeDtypeStruct((2, part), f32),
        ),
        in_specs=[pl.BlockSpec(memory_space=pltpu.VMEM)] * 6,
        out_specs=[pl.BlockSpec(memory_space=pltpu.VMEM)] * 2,
        scratch_shapes=[
            pltpu.VMEM((units, 3, tok, HEAD_DIM), bf16),
            pltpu.VMEM((count, 2 * part), f32),
            pltpu.VMEM((2, count), f32),
            pltpu.VMEM((8, 2, count), f32),
            pltpu.SemaphoreType.DMA((7,)),
            pltpu.SemaphoreType.DMA((7,)),
            pltpu.SemaphoreType.DMA((9,)),
            pltpu.SemaphoreType.DMA((9,)),
        ],
        compiler_params=pltpu.CompilerParams(
            collective_id=number, has_side_effects=True, vmem_limit_bytes=40 * 2**20
        ),
        cost_estimate=pl.CostEstimate(flops=0, bytes_accessed=120_000_000, transcendentals=0),
    )(d_units, qkv, cosine, sine_signed, gains, inverse)


BLOCK = 512


def attend_kernel(len_ref, q_ref, k_ref, v_ref, o_ref, o32_ref, lse_ref):
    i = pl.program_id(0)
    bq, bk = q_ref.shape[0], BLOCK
    length = len_ref[0]
    scale = HEAD_DIM ** (-0.5)
    q = q_ref[...]
    rows = i * bq + lax.broadcasted_iota(jnp.int32, (bq, bk), 0)
    cols0 = lax.broadcasted_iota(jnp.int32, (bq, bk), 1)

    def step(j, carry, masked):
        top, total, acc = carry
        j0 = pl.multiple_of(j * bk, bk)
        scores = contract_last(q, k_ref[pl.ds(j0, bk), :]) * scale
        if masked:
            cols = j0 + cols0
            scores = jnp.where((cols <= rows) & (cols < length), scores, masked_score)
        new = jnp.maximum(top, jnp.max(scores, axis=1, keepdims=True))
        weights = jnp.exp(scores - new)
        fix = jnp.exp(top - new)
        total = total * fix + jnp.sum(weights, axis=1, keepdims=True)
        acc = acc * fix + matmul(weights.astype(bf16), v_ref[pl.ds(j0, bk), :])
        return new, total, acc

    carry = (
        jnp.full((bq, 1), -jnp.inf, f32),
        jnp.zeros((bq, 1), f32),
        jnp.zeros((bq, HEAD_DIM), f32),
    )
    whole = jnp.minimum(i, length // bk)
    last = jnp.minimum(i + 1, (length + bk - 1) // bk)
    carry = lax.fori_loop(0, whole, lambda j, s: step(j, s, False), carry)
    top, total, acc = lax.fori_loop(whole, last, lambda j, s: step(j, s, True), carry)
    out = acc / total
    o_ref[...] = out.astype(bf16)
    o32_ref[...] = out
    lse_ref[...] = jnp.broadcast_to((top + jnp.log(total)).T, lse_ref.shape)


def attend(length, q, k, v):
    slots = q.shape[0]
    whole = pl.BlockSpec((slots, HEAD_DIM), lambda i: (0, 0))
    part = pl.BlockSpec((BLOCK, HEAD_DIM), lambda i: (i, 0))
    return pl.pallas_call(
        attend_kernel,
        name="attend",
        grid=(slots // BLOCK,),
        out_shape=(
            jax.ShapeDtypeStruct((slots, HEAD_DIM), bf16),
            jax.ShapeDtypeStruct((slots, HEAD_DIM), f32),
            jax.ShapeDtypeStruct((8, slots), f32),
        ),
        in_specs=[pl.BlockSpec(memory_space=pltpu.SMEM), part, whole, whole],
        out_specs=(part, part, pl.BlockSpec((8, BLOCK), lambda i: (0, i))),
        cost_estimate=pl.CostEstimate(
            flops=2 * slots * slots * HEAD_DIM,
            bytes_accessed=8 * slots * HEAD_DIM,
            transcendentals=slots * slots // 2,
        ),
    )(length, q, k, v)


def attend_back_kernel(
    len_ref, q_ref, k_ref, v_ref, do_ref, o_ref, lse_ref, out_ref, dq_acc, delta_ref
):
    j = pl.program_id(0)
    bk, bq = k_ref.shape[0], BLOCK
    slots = q_ref.shape[0]
    length = len_ref[0]
    scale = HEAD_DIM ** (-0.5)

    @pl.when(j == 0)
    def _():
        dq_acc[...] = jnp.zeros_like(dq_acc)
        for i in range(slots // bq):
            here = slice(i * bq, (i + 1) * bq)
            product = do_ref[here, :].astype(f32) * o_ref[here, :]
            delta_ref[0:1, here] = jnp.sum(product, axis=1, keepdims=True).T

    k, v = k_ref[...], v_ref[...]
    j0 = j * bk
    cols = j0 + lax.broadcasted_iota(jnp.int32, (bk, bq), 0)
    rows0 = lax.broadcasted_iota(jnp.int32, (bk, bq), 1)

    def step(i, carry, masked):
        dk, dv = carry
        i0 = pl.multiple_of(i * bq, bq)
        here = pl.ds(i0, bq)
        q, do = q_ref[here, :], do_ref[here, :]
        scores = contract_last(k, q) * scale
        if masked:
            scores = jnp.where((cols <= i0 + rows0) & (cols < length), scores, masked_score)
        probs = jnp.exp(scores - lse_ref[0:1, here])
        dv = dv + matmul(probs.astype(bf16), do)
        d_probs = contract_last(v, do)
        d_scores = (probs * (d_probs - delta_ref[0:1, here])).astype(bf16)
        dk = dk + matmul(d_scores, q)
        dq_acc[here, :] += contract_first(d_scores, k)
        return dk, dv

    zero = jnp.zeros((bk, HEAD_DIM), f32)
    top = slots // bq
    first = jnp.where(j0 + bk <= length, j + 1, top)
    first = jnp.where(j0 < length, first, j)
    stop = jnp.where(j0 < length, top, j)
    carry = lax.fori_loop(j, first, lambda i, s: step(i, s, True), (zero, zero))
    dk, dv = lax.fori_loop(first, stop, lambda i, s: step(i, s, False), carry)
    there = pl.ds(pl.multiple_of(j0, bk), bk)
    out_ref[1, there, :] = (dk * scale).astype(bf16)
    out_ref[2, there, :] = dv.astype(bf16)

    @pl.when(j == pl.num_programs(0) - 1)
    def _():
        out_ref[0] = (dq_acc[...] * scale).astype(bf16)


def attend_back(length, q, k, v, do, o, lse):
    slots = q.shape[0]
    whole = pl.BlockSpec((slots, HEAD_DIM), lambda j: (0, 0))
    part = pl.BlockSpec((BLOCK, HEAD_DIM), lambda j: (j, 0))
    line = pl.BlockSpec((8, slots), lambda j: (0, 0))
    return pl.pallas_call(
        attend_back_kernel,
        name="attend_back",
        grid=(slots // BLOCK,),
        out_shape=jax.ShapeDtypeStruct((3, slots, HEAD_DIM), bf16),
        in_specs=[pl.BlockSpec(memory_space=pltpu.SMEM), whole, part, part, whole, whole, line],
        out_specs=pl.BlockSpec((3, slots, HEAD_DIM), lambda j: (0, 0, 0)),
        scratch_shapes=[pltpu.VMEM((slots, HEAD_DIM), f32), pltpu.VMEM((8, slots), f32)],
        cost_estimate=pl.CostEstimate(
            flops=5 * slots * slots * HEAD_DIM,
            bytes_accessed=14 * slots * HEAD_DIM,
            transcendentals=slots * slots // 2,
        ),
    )(length, q, k, v, do, o, lse)


def per_device(
    tokens,
    seq_lengths,
    w_query,
    w_key,
    w_value,
    w_out,
    w_gate,
    w_up,
    w_down,
    q_gain,
    k_gain,
    attn_gain,
    mlp_gain,
    cotangent,
):
    tok_rows, feat_part = tokens.shape
    row_count, data_count = lax.axis_size("row"), lax.axis_size("dp")
    width = feat_part * lax.axis_size("col")
    slots = tok_rows * row_count
    half_feat = feat_part // 2
    y, z = side("dp"), lax.axis_index("row")
    p = z & 1
    heads = half_feat // HEAD_DIM
    hid = w_gate.shape[1] // 4
    pairs = [(i, i ^ 1) for i in range(data_count)]
    after = lambda values, *done: lax.optimization_barrier((values,) + done)[0]

    def y_half(values, axis):
        size = values.shape[axis] // 2
        return lax.dynamic_slice_in_dim(values, y * size, size, axis)

    def row_swap(values, d):
        return lax.ppermute(values, "row", [(i, i ^ d) for i in range(row_count)])

    def hidden_part(weight, axis):
        def quarter(d):
            return lax.dynamic_slice_in_dim(weight, (y * 2 + (p ^ (d & 1))) * hid, hid, axis)

        parts = [quarter(0)] + [row_swap(quarter(d), d) for d in (1, 2, 3)]
        stacked = jnp.stack(parts)
        return [lax.dynamic_index_in_dim(stacked, z ^ i, 0, keepdims=False) for i in range(row_count)]

    qkv_weight = lax.all_gather(
        jnp.concatenate([y_half(w_query, 1), y_half(w_key, 1), y_half(w_value, 1)], axis=1),
        "row",
        axis=0,
        tiled=True,
    )
    out_weight = lax.all_gather(y_half(after(w_out, qkv_weight), 0), "row", axis=1, tiled=True)

    positions = z * tok_rows + jnp.arange(tok_rows)
    length = seq_lengths[0]
    valid = (positions < length).astype(f32)[:, None]
    cosine, sine = rope_tables(positions, HEAD_DIM)
    sine_signed = jnp.where(jnp.arange(HEAD_DIM)[None, :] < HEAD_DIM // 2, -sine, sine)
    other_length = lax.ppermute(seq_lengths, "dp", pairs)
    pair_lengths = jnp.where(
        y == 0,
        jnp.concatenate([seq_lengths, other_length]),
        jnp.concatenate([other_length, seq_lengths]),
    )
    unit_length = lax.dynamic_slice_in_dim(pair_lengths, z // heads, 1)
    qk_gain = jnp.stack([y_half(q_gain, 0), y_half(k_gain, 0)])

    tokens_wide = gather_wide(tokens, False, 0, "gather_tokens")
    qkv = matmul(tokens_wide, qkv_weight)
    units, inverse = front(qkv, cosine, sine_signed, qk_gain, width, 2 * heads, 2)
    q_unit, k_unit, v_unit = (units[:, i].reshape(slots, HEAD_DIM) for i in range(3))
    gate_weight = jnp.concatenate(hidden_part(after(w_gate, units), 1), axis=0)
    up_weight = jnp.concatenate(hidden_part(after(w_up, units), 1), axis=0)
    attn_unit, attn_exact, log_total = attend(unit_length, q_unit, k_unit, v_unit)
    attn_low = turn(attn_unit, True, tok_rows, heads, 3, "turn_attn")
    down_weight = jnp.concatenate(hidden_part(after(w_down, attn_low), 0), axis=1)
    branch = scatter_wide(matmul(attn_low, out_weight).astype(bf16), False, 4, "scatter_branch")
    branch_inv = lax.rsqrt(
        feature_total(jnp.sum(branch * branch, axis=1)[None, :], 5, "total_branch")[0] / width
        + norm_eps
    )[:, None]
    resid = tokens.astype(f32) + branch * branch_inv * attn_gain
    resid_wide = gather_wide(resid.astype(bf16), True, 6, "gather_resid")
    gate = matmul(resid_wide, gate_weight)
    upper = matmul(resid_wide, up_weight)
    sigma = jax.nn.sigmoid(gate)
    hidden = (gate * sigma * upper).astype(bf16)
    mixed = scatter_wide(matmul(hidden, down_weight).astype(bf16), True, 7, "scatter_mixed")
    incoming = cotangent.astype(f32) * valid
    gained = incoming * mlp_gain
    sums = feature_total(
        jnp.stack([jnp.sum(mixed * mixed, axis=1), jnp.sum(gained * mixed, axis=1)]),
        8,
        "total_mixed",
    )
    mixed_inv = lax.rsqrt(sums[0] / width + norm_eps)[:, None]
    inner = (sums[1] / width)[:, None]
    block_output = ((resid + mixed * mixed_inv * mlp_gain) * valid).astype(bf16)
    mlp_gain_raw = jnp.sum(incoming * mixed * mixed_inv, axis=0)
    d_mixed = (mixed_inv * gained - mixed * mixed_inv**3 * inner).astype(bf16)
    d_mixed_wide = gather_wide(d_mixed, True, 9, "gather_d_mixed")

    factor = 1.0 / math.sqrt(slots * data_count)

    def cut(values, index, count, axis):
        size = values.shape[axis] // count
        return lax.dynamic_slice_in_dim(values, index * size, size, axis)

    def over_dp(piece):
        if data_count > 2:
            groups = [list(range(s, data_count, 2)) for s in (0, 1)]
            piece = lax.psum(piece, "dp", axis_index_groups=groups)
        return piece

    def two_sides(piece, other, bit, axis):
        low = jnp.where(bit == 0, piece, other)
        high = jnp.where(bit == 0, other, piece)
        return jnp.concatenate([low, high], axis=axis)

    def hidden_grad(raw, axis):
        far = row_swap(cut(raw, 1 - (z >> 1), 2, axis), 2)
        near = cut(raw, z >> 1, 2, axis)
        near = (near.astype(f32) + far.astype(f32)).astype(bf16)
        near = over_dp(near)
        own, away = cut(near, p, 2, axis), row_swap(cut(near, 1 - p, 2, axis), 1)
        block = two_sides(own, away, p, 1 - axis)
        return two_sides(block, lax.ppermute(block, "dp", pairs), y, 1 - axis).astype(f32)

    def reduce_rows(raw, axis):
        return lax.psum_scatter(raw, "row", scatter_dimension=axis, tiled=True)

    d_hidden = contract_last(d_mixed_wide, down_weight)
    down_raw = (contract_first(hidden, d_mixed_wide) * factor).astype(bf16)
    d_gate = (d_hidden * upper * sigma * (1.0 + gate * (1.0 - sigma))).astype(bf16)
    d_upper = (d_hidden * gate * sigma).astype(bf16)
    gate_raw = (contract_first(resid_wide, d_gate) * factor).astype(bf16)
    up_raw = (contract_first(resid_wide, d_upper) * factor).astype(bf16)
    d_resid_wide = (
        contract_last(d_gate, gate_weight) + contract_last(d_upper, up_weight)
    ).astype(bf16)
    d_resid_wide, down_raw, gate_raw, up_raw = lax.optimization_barrier(
        (d_resid_wide, down_raw, gate_raw, up_raw)
    )
    d_resid = incoming + scatter_wide(d_resid_wide, True, 10, "scatter_d_resid")
    attn_gain_raw = jnp.sum(d_resid * branch * branch_inv, axis=0)
    gained = d_resid * attn_gain
    inner = (
        feature_total(jnp.sum(gained * branch, axis=1)[None, :], 11, "total_d_resid")[0][:, None]
        / width
    )
    d_branch = (branch_inv * gained - branch * branch_inv**3 * inner).astype(bf16)
    d_branch_wide = gather_wide(d_branch, False, 12, "gather_d_branch")
    d_attn = contract_last(d_branch_wide, out_weight).astype(bf16)
    d_attn_unit = turn(d_attn, False, tok_rows, heads, 13, "turn_d_attn")
    out_raw = (contract_first(attn_low, after(d_branch_wide, d_attn_unit)) * factor).astype(bf16)
    d_attn_unit, out_raw = lax.optimization_barrier((d_attn_unit, out_raw))
    out_piece = reduce_rows(out_raw, 1)
    d_units = attend_back(unit_length, q_unit, k_unit, v_unit, d_attn_unit, attn_exact, log_total)
    d_qkv, gain_sums = rear(
        d_units, qkv[:, : 2 * half_feat], cosine, sine_signed, qk_gain, inverse, width, 14
    )
    qkv_raw = (contract_first(tokens_wide, d_qkv) * factor).astype(bf16)
    projected = contract_last(d_qkv, qkv_weight).astype(bf16)
    projected, qkv_raw = lax.optimization_barrier((projected, qkv_raw))
    qkv_piece = over_dp(reduce_rows(qkv_raw, 0))
    input_grad = d_resid + scatter_wide(projected, False, 16, "scatter_projected")

    def spread(half):
        return lax.dynamic_update_slice_in_dim(jnp.zeros((feat_part,), f32), half, y * half_feat, 0)

    gains = lax.psum(
        jnp.stack([spread(gain_sums[0]), spread(gain_sums[1]), attn_gain_raw, mlp_gain_raw])
        * factor,
        ("dp", "row"),
    )
    qkv_other = lax.ppermute(qkv_piece, "dp", pairs)
    q_grad, k_grad, v_grad = (
        two_sides(cut(qkv_piece, i, 3, 1), cut(qkv_other, i, 3, 1), y, 1).astype(f32)
        for i in range(3)
    )
    out_piece = over_dp(out_piece)
    out_grad = two_sides(out_piece, lax.ppermute(out_piece, "dp", pairs), y, 0).astype(f32)
    return (
        block_output,
        input_grad,
        q_grad,
        k_grad,
        v_grad,
        out_grad,
        hidden_grad(gate_raw, 0),
        hidden_grad(up_raw, 0),
        hidden_grad(down_raw, 1),
        gains[0],
        gains[1],
        gains[2],
        gains[3],
    )


def solution(mesh):
    tok, row_col, col_row, gain = P(("dp", "row"), "col"), P("row", "col"), P("col", "row"), P("col")
    weights = (row_col, row_col, row_col, col_row, row_col, row_col, col_row)
    gains = (gain, gain, gain, gain)
    return jax.shard_map(
        per_device,
        mesh=mesh,
        in_specs=(tok, P("dp")) + weights + gains + (tok,),
        out_specs=(tok, tok) + weights + gains,
        check_vma=False,
    )
```

time: 1140 us -> 1250 us (1.096)
  blocking collectives: 22.8 us -> 154 us
  Pallas kernels: 549 us -> 597 us
  local copies, waits for them, and re-layouts: 79.6 us -> 33.9 us
  other arithmetic: 76.9 us -> 48.6 us
  waiting for transfers between devices: 222 us -> 208 us
  starting transfers between devices: 11 us -> 23.8 us
    reduce_scatter x5 -> x2, waiting for transfers between devices: 181 us -> 0.01 us  [reduce_rows(): return lax.psum_scatter(raw, 'row', scatter_dimension=axis, tiled=True)]
    ppermute x7 -> x20, waiting for transfers between devices: 16.7 us -> 180 us  [the longest x15 131 us: row_swap(): return lax.ppermute(values, 'row', [(i, i ^ d) for i in range(row_count)])]
    psum x1, blocking collectives: 22.8 us -> 154 us  [per_device(): lax.psum(jnp.stack([spread(gain_sums[0]), spread(gain_sums[1]), attn_gain...]
    pallas_call x17 -> x15, Pallas kernels: 511 us -> 549 us  [the longest x4 201 us: scatter_wide(): pl.pallas_call(functools.partial(scatter_kernel, pair), name=name, out_sh...]
    unnamed x100 -> x131, local copies, waits for them, and re-layouts: 25.8 us -> 12.7 us
    ppermute x7 -> x20, starting transfers between devices: 7.48 us -> 20.4 us  [the longest x15 16.4 us: row_swap(): return lax.ppermute(values, 'row', [(i, i ^ d) for i in range(row_count)])]
  transfers between devices with their start and end apart: 18 -> 25, of which waited for: 6 -> 9; matrix products, arithmetic and copies ran while one was open for 17% -> 5% of each run, Pallas kernels for 27% -> 16%
where the time goes in v2:
time: 1250 us; the launch traced here: 1240 us
  Pallas kernels  597 us (48%)
  waiting for transfers between devices  208 us (17%)
  matrix products  160 us (13%)
  blocking collectives  154 us (12%)
  other arithmetic  48.6 us (4%)
  local copies, waits for them, and re-layouts  33.9 us (3%)
  starting transfers between devices  23.8 us (2%)
  between operations  15.7 us (1%)
    pallas_call x4, Pallas kernels, scatter_wide(): pl.pallas_call(functools.partial(scatter_kernel, pair), name=name, out_sh...  201 us
    pallas_call x4, Pallas kernels, gather_wide(): pl.pallas_call(functools.partial(gather_kernel, pair), name=name, out_sha...  178 us
    psum x1, blocking collectives, per_device(): lax.psum(jnp.stack([spread(gain_sums[0]), spread(gain_sums[1]), attn_gain...  154 us
    ppermute x15, waiting for transfers between devices, row_swap(): return lax.ppermute(values, 'row', [(i, i ^ d) for i in range(row_count)])  131 us
    dot_general x5, matrix products, contract_last(): lax.dot_general(left, right, (((1,), (1,)), ((), ())), preferred_element_...  63.9 us
    pallas_call x1, Pallas kernels, front(): pl.pallas_call(functools.partial(front_kernel, width), name='front', out_...  56.1 us
    pallas_call x1, Pallas kernels, rear(): pl.pallas_call(functools.partial(rear_kernel, width), name='rear', out_sh...  55.8 us
    dot_general x5, matrix products, matmul(): return jnp.dot(left, right, preferred_element_type=f32)  50.8 us
  transfers between devices with their start and end apart: 25, of which 9 were waited for; matrix products, arithmetic and copies ran while one was open for 5% of the time, Pallas kernels for 16%

profile of v2, /device:TPU:0, one launch (start us, length us, event | category | flops | bytes accessed | tf_op | source)
XLA Modules:
  0.0 1241.4 jit_solution(8330269284724133471)
XLA Ops:
  10.3 3.1 collective-permute-start
  14.2 31.3 %gather_tokens.1 = bf16[1536,2048]{1,0:T(8,128)(2,1)} custom-call(bf16[768,512]{1,0:T(8,128)(2,1)} %x_ref.1), custom_call_target="tpu_custom_call" | custom-call | bytes 60000000 | tf_op jit(solution)/shard_map/gather_tokens/pallas_call | solution.py:154
  48.7 28.0 %all-gather.3.cloned.1.call-done = bf16[2048,768]{1,0:T(8,128)(2,1)} async-done(((bf16[512,768]{1,0:T(8,128)(2,1)}), bf16[2048,768]{1,0:T(8,128)(2,1)}) %all-gather.3.cloned.1.call-update) | async-done | bytes 3145744 | tf_op jit(solution)/shard_map/all_gather | solution.py:812
  76.7 8.1 convolution_bitcast_fusion.qkv_ref
  86.9 56.1 %front.1 = (bf16[4,3,768,128]{3,2,1,0:T(8,128)(2,1)S(1)}, f32[2,1536]{1,0:T(2,128)S(1)}) custom-call(f32[1536,768]{1,0:T(8,128)S(1)} %convolution_bitcast_fusion.qkv_ref, f32[768,128]{1,0:T(8,128)S(1)} %get-tuple-element.116.cos_ref, f32[768,128]{1,0:T(8,128)S(1)} %get-tuple-element.115.sin_ref, f32[2,256]{1,0:T(2,128)S(1)} %pad_maximum_fusion.18.gain_ref), custom_call_target="tpu_custom_call" | custom-call | bytes 120000000 | tf_op jit(solution)/shard_map/front/pallas_call | solution.py:495
  144.8 3.6 collective-permute-start.2
  155.5 74.3 %collective-permute-done.2 = bf16[512,512]{1,0:T(8,128)(2,1)} collective-permute-done((bf16[512,512]{1,0:T(8,128)(2,1)S(1)}, bf16[512,512]{1,0:T(8,128)(2,1)}, u32[]{:S(2)}, u32[]{:S(2)}) %collective-permute-start.2) | collective-permute-done | bytes 524320 | tf_op jit(solution)/shard_map/ppermute | solution.py:802
  229.7 20.5 %attend.1 = (bf16[3072,128]{1,0:T(8,128)(2,1)}, f32[3072,128]{1,0:T(8,128)}, f32[8,3072]{1,0:T(8,128)}) custom-call(s32[1]{0:T(128)} %dynamic_slice.136.len_ref, bf16[3072,128]{1,0:T(8,128)(2,1)} %bitcast.101, bf16[3072,128]{1,0:T(8,128)(2,1)} %bitcast.99, bf16[3072,128]{1,0:T(8,128)(2,1)} %bitcast.97), custom_call_target="tpu_custom_call" | custom-call | flops 2415919104 | bytes 3145728 | tf_op jit(solution)/shard_map/attend/pallas_call | solution.py:675
  250.2 4.0 slice.50.qkv_ref
  254.2 20.7 %turn_attn.1 = bf16[1536,256]{1,0:T(8,128)(2,1)} custom-call(bf16[3072,128]{1,0:T(8,128)(2,1)} %get-tuple-element.34.x_ref), custom_call_target="tpu_custom_call" | custom-call | bytes 60000000 | tf_op jit(solution)/shard_map/turn_attn/pallas_call | solution.py:396
  276.8 2.7 collective-permute-start.8
  285.6 34.3 %collective-permute-done.8 = bf16[512,512]{1,0:T(8,128)(2,1)S(1)} collective-permute-done((bf16[512,512]{1,0:T(8,128)(2,1)S(1)}, bf16[512,512]{1,0:T(8,128)(2,1)S(1)}, u32[]{:S(2)}, u32[]{:S(2)}) %collective-permute-start.8) | collective-permute-done | bytes 524320 | tf_op jit(solution)/shard_map/ppermute | solution.py:802
  321.8 5.6 convolution_convert_fusion.2.p_ref
  327.4 35.3 %scatter_branch.1 = f32[768,512]{1,0:T(8,128)S(1)} custom-call(bf16[1536,2048]{1,0:T(8,128)(2,1)} %convolution_convert_fusion.2.p_ref), custom_call_target="tpu_custom_call" | custom-call | bytes 80000000 | tf_op jit(solution)/shard_map/scatter_branch/pallas_call | solution.py:287
  363.5 4.9 total_branch.1
  371.0 57.6 %gather_resid.1 = bf16[3072,2048]{1,0:T(8,128)(2,1)} custom-call(bf16[768,512]{1,0:T(8,128)(2,1)} %fusion.4.x_ref), custom_call_target="tpu_custom_call" | custom-call | bytes 60000000 | tf_op jit(solution)/shard_map/gather_resid/pallas_call | solution.py:154
  428.7 12.8 %fusion.8 = f32[3072,512]{1,0:T(8,128)} fusion(bf16[3072,2048]{1,0:T(8,128)(2,1)} %gather_resid.1, bf16[512,512]{1,0:T(8,128)(2,1)S(1)} %copy-done.32, bf16[512,512]{1,0:T(8,128)(2,1)S(1)} %copy-done.34, bf16[512,512]{1,0:T(8,128)(2,1)} %get-tuple-element.92, bf16[512,512]{1,0:T(8,128)(2,1)S(1)} %copy-done.30), kind=kOutput, calls=%fused_computation.80 | convolution fusion | flops 6450839552 | bytes 20971520 | tf_op jit(solution)/shard_map/dot_general | solution.py:30
  441.6 12.4 multiply_convert_fusion.3
  454.0 11.9 convolution_convert_fusion.p_ref
  465.9 64.1 %scatter_mixed.1 = f32[768,512]{1,0:T(8,128)S(1)} custom-call(bf16[3072,2048]{1,0:T(8,128)(2,1)} %convolution_convert_fusion.p_ref), custom_call_target="tpu_custom_call" | custom-call | bytes 80000000 | tf_op jit(solution)/shard_map/scatter_mixed/pallas_call | solution.py:287
  531.2 5.0 total_mixed.1
  540.2 57.3 %gather_d_mixed.1 = bf16[3072,2048]{1,0:T(8,128)(2,1)} custom-call(bf16[768,512]{1,0:T(8,128)(2,1)} %subtract_convert_fusion.1.x_ref), custom_call_target="tpu_custom_call" | custom-call | bytes 60000000 | tf_op jit(solution)/shard_map/gather_d_mixed/pallas_call | solution.py:154
  597.5 11.7 multiply_convert_fusion.6
  609.3 16.9 %multiply_convert_fusion.1 = (bf16[3072,512]{1,0:T(8,128)(2,1)}, bf16[3072,512]{1,0:T(8,128)(2,1)S(1)}) fusion(f32[3072,512]{1,0:T(8,128)} %fusion.8, f32[3072,512]{1,0:T(8,128)} %get-tuple-element.124, bf16[3072,2048]{1,0:T(8,128)(2,1)} %gather_d_mixed.1, bf16[512,512]{1,0:T(8,128)(2,1)S(1)} %copy-done.47, bf16[512,512]{1,0:T(8,128)(2,1)S(1)} %copy-done.49, ...), kind=kOutput, calls=%fused_computation.5 | convolution fusion | flops 6471286784 | bytes 33554432 | tf_op jit(solution)/shard_map/dot_general | solution.py:38
  627.9 10.9 multiply_convert_fusion.5
  638.8 15.5 %fusion.7 = f32[3072,2048]{1,0:T(8,128)} fusion(bf16[3072,512]{1,0:T(8,128)(2,1)} %copy-done.58, bf16[512,512]{1,0:T(8,128)(2,1)S(1)} %copy-done.33, bf16[512,512]{1,0:T(8,128)(2,1)S(1)} %copy-done.35, bf16[512,512]{1,0:T(8,128)(2,1)S(1)} %copy-done.36, bf16[512,512]{1,0:T(8,128)(2,1)S(1)} %copy-done.31), kind=kOutput, calls=%fused_computation.79 | convolution fusion | flops 6450839552 | bytes 30408704 | tf_op jit(solution)/shard_map/dot_general | solution.py:38
  654.4 10.9 multiply_convert_fusion.4
  665.3 17.0 %add_convert_fusion.p_ref = bf16[3072,2048]{1,0:T(8,128)(2,1)} fusion(f32[3072,2048]{1,0:T(8,128)} %fusion.7, bf16[3072,512]{1,0:T(8,128)(2,1)} %get-tuple-element.71, bf16[512,512]{1,0:T(8,128)(2,1)S(1)} %copy-done.40, bf16[512,512]{1,0:T(8,128)(2,1)S(1)} %copy-done.42, bf16[512,512]{1,0:T(8,128)(2,1)} %get-tuple-element.98, bf16[512,512]{1,0:T(8,128)(2,1)S(1)} %copy-done.38), kind=kOutput, calls=%fused_computation | convolution fusion | flops 6463422464 | bytes 42991616 | tf_op jit(solution)/shard_map/dot_general | solution.py:38
  682.3 64.9 %scatter_d_resid.1 = f32[768,512]{1,0:T(8,128)S(1)} custom-call(bf16[3072,2048]{1,0:T(8,128)(2,1)} %add_convert_fusion.p_ref), custom_call_target="tpu_custom_call" | custom-call | bytes 80000000 | tf_op jit(solution)/shard_map/scatter_d_resid/pallas_call | solution.py:287
  747.2 2.9 multiply_reduce_fusion.1
  750.2 4.9 total_d_resid.1
  758.3 31.8 %gather_d_branch.1 = bf16[1536,2048]{1,0:T(8,128)(2,1)} custom-call(bf16[768,512]{1,0:T(8,128)(2,1)} %subtract_convert_fusion.x_ref), custom_call_target="tpu_custom_call" | custom-call | bytes 60000000 | tf_op jit(solution)/shard_map/gather_d_branch/pallas_call | solution.py:154
  790.1 5.5 convolution_convert_fusion.3.x_ref
  795.6 22.1 %turn_d_attn.1.do_ref = bf16[3072,128]{1,0:T(8,128)(2,1)} custom-call(bf16[1536,256]{1,0:T(8,128)(2,1)} %convolution_convert_fusion.3.x_ref), custom_call_target="tpu_custom_call" | custom-call | bytes 60000000 | tf_op jit(solution)/shard_map/turn_d_attn/pallas_call | solution.py:396
  817.8 5.6 fusion.1
  823.4 27.7 %attend_back.1.d_ref = bf16[3,3072,128]{2,1,0:T(8,128)(2,1)} custom-call(s32[1]{0:T(128)} %dynamic_slice.136.len_ref, bf16[3072,128]{1,0:T(8,128)(2,1)} %bitcast.102, bf16[3072,128]{1,0:T(8,128)(2,1)} %bitcast.100, bf16[3072,128]{1,0:T(8,128)(2,1)} %bitcast.98, bf16[3072,128]{1,0:T(8,128)(2,1)} %turn_d_attn.1.do_ref, f32[3072,128]{1,0:T(8,128)} %get-tuple-element.42.o_ref, ...), custom_call_target="tpu_custom_call" | custom-call | flops 6039797760 | bytes 5505024 | tf_op jit(solution)/shard_map/attend_back/pallas_call | solution.py:753
  854.7 55.8 %rear.1 = (bf16[1536,768]{1,0:T(8,128)(2,1)S(1)}, f32[2,256]{1,0:T(2,128)S(1)}) custom-call(bf16[3,3072,128]{2,1,0:T(8,128)(2,1)S(1)} %copy-done.10, f32[1536,512]{1,0:T(8,128)S(1)} %copy-done.5, f32[768,128]{1,0:T(8,128)S(1)} %copy-done.9, f32[768,128]{1,0:T(8,128)S(1)} %copy-done.7, f32[2,256]{1,0:T(2,128)S(1)} %pad_maximum_fusion.18.gain_ref, ...), custom_call_target="tpu_custom_call" | custom-call | bytes 120000000 | tf_op jit(solution)/shard_map/rear/pallas_call | solution.py:604
  910.5 9.0 convolution_convert_fusion.1.p_ref
  919.5 6.7 fusion
  929.7 2.9 collective-permute-start.15
  933.7 37.0 %scatter_projected.1 = f32[768,512]{1,0:T(8,128)S(1)} custom-call(bf16[1536,2048]{1,0:T(8,128)(2,1)} %convolution_convert_fusion.1.p_ref), custom_call_target="tpu_custom_call" | custom-call | bytes 80000000 | tf_op jit(solution)/shard_map/scatter_projected/pallas_call | solution.py:287
  972.2 153.9 %psum.7 = f32[4,512]{1,0:T(4,128)S(1)} all-reduce(f32[4,512]{1,0:T(4,128)S(1)} %maximum_multiply_fusion), channel_id=1, replica_groups=mesh['dp'=2,'row'=4,'col'=4] {'dp','row'}, use_global_device_ids=true, to_apply=%region_8.9 | all-reduce | flops 2048 | bytes 16384 | tf_op jit(solution)/shard_map/psum | solution.py:937
  1134.5 9.3 collective-permute-done.19
  1145.7 9.2 collective-permute-done.13
  1158.4 4.1 collective-permute-done.16
  1165.7 33.7 %collective-permute-done.11 = bf16[256,512]{1,0:T(8,128)(2,1)S(1)} collective-permute-done((bf16[256,512]{1,0:T(8,128)(2,1)}, bf16[256,512]{1,0:T(8,128)(2,1)S(1)}, u32[]{:S(2)}, u32[]{:S(2)}) %collective-permute-start.11) | collective-permute-done | bytes 262176 | tf_op jit(solution)/shard_map/ppermute | solution.py:948
  1200.5 3.0 broadcast_select_fusion.1
  1208.5 13.4 %collective-permute-done.17 = bf16[512,1024]{1,0:T(8,128)(2,1)} collective-permute-done((bf16[512,1024]{1,0:T(8,128)(2,1)}, bf16[512,1024]{1,0:T(8,128)(2,1)}, u32[]{:S(2)}, u32[]{:S(2)}) %collective-permute-start.17) | collective-permute-done | bytes 1048608 | tf_op jit(solution)/shard_map/ppermute | solution.py:893
  (247 shorter events, 85.7 us)
Async XLA Ops:
  7.2 69.5 %all-gather.3.cloned.1.call-start = ((), (), s32[]{:S(2)}) async-start(), calls=%async_computation.2 | async-start | bytes 3932160 | tf_op jit(solution)/shard_map/all_gather | solution.py:812
  10.3 311.3 %all-gather.5.cloned.1.call-start = ((), (), s32[]{:S(2)}) async-start(), calls=%async_computation.3 | async-start | bytes 1310720 | tf_op jit(solution)/shard_map/all_gather | solution.py:818
  10.3 37.1 %collective-permute-start = (s32[1]{0:T(128)}, s32[1]{0:T(128)}, u32[]{:S(2)}, u32[]{:S(2)}) collective-permute-start(s32[1]{0:T(128)} %param.15), channel_id=1, source_target_pairs={{0,16},{16,0},{1,17},{17,1},{2,18},{18,2},{3,19},{19,3},{4,20},{20... | collective-permute-start | bytes 20 | tf_op jit(solution)/shard_map/ppermute | solution.py:825
  47.5 37.3 %copy-start.6 = (f32[768,128]{1,0:T(8,128)}, f32[768,128]{1,0:T(8,128)S(1)}, u32[]{:S(2)}) copy-start(f32[768,128]{1,0:T(8,128)S(1)} %get-tuple-element.115.sin_ref) | copy-start | bytes 1179652
  47.5 37.3 %copy-start.8 = (f32[768,128]{1,0:T(8,128)}, f32[768,128]{1,0:T(8,128)S(1)}, u32[]{:S(2)}) copy-start(f32[768,128]{1,0:T(8,128)S(1)} %get-tuple-element.116.cos_ref) | copy-start | bytes 1179652
  86.9 56.2 %copy-start.28 = (bf16[512,2048]{1,0:T(8,128)(2,1)S(1)}, bf16[512,2048]{1,0:T(8,128)(2,1)}, u32[]{:S(2)}) copy-start(bf16[512,2048]{1,0:T(8,128)(2,1)} %param.20) | copy-start | bytes 6291460
  144.0 131.0 %collective-permute-start.3 = (bf16[512,512]{1,0:T(8,128)(2,1)}, bf16[512,512]{1,0:T(8,128)(2,1)}, u32[]{:S(2)}, u32[]{:S(2)}) collective-permute-start(bf16[512,512]{1,0:T(8,128)(2,1)} %get-tuple-element.94), channel_id=1, source_target_pairs={{0,12},{4,8},{8,4},{12,0},{1,13},{5,9},{9,5},{13,1},{2,14},{6,10},... | collective-permute-start | bytes 1572872 | tf_op jit(solution)/shard_map/ppermute | solution.py:802
  144.8 132.0 %collective-permute-start.1 = (bf16[512,512]{1,0:T(8,128)(2,1)}, bf16[512,512]{1,0:T(8,128)(2,1)}, u32[]{:S(2)}, u32[]{:S(2)}) collective-permute-start(bf16[512,512]{1,0:T(8,128)(2,1)} %get-tuple-element.94), channel_id=1, source_target_pairs={{0,4},{4,0},{8,12},{12,8},{1,5},{5,1},{9,13},{13,9},{2,6},{6,2},{1... | collective-permute-start | bytes 1572872 | tf_op jit(solution)/shard_map/ppermute | solution.py:802
  144.8 84.9 %collective-permute-start.2 = (bf16[512,512]{1,0:T(8,128)(2,1)S(1)}, bf16[512,512]{1,0:T(8,128)(2,1)}, u32[]{:S(2)}, u32[]{:S(2)}) collective-permute-start(bf16[512,512]{1,0:T(8,128)(2,1)S(1)} %get-tuple-element.93), channel_id=1, source_target_pairs={{0,8},{4,12},{8,0},{12,4},{1,9},{5,13},{9,1},{13,5},{2,10},{6,14},... | collective-permute-start | bytes 1572872 | tf_op jit(solution)/shard_map/ppermute | solution.py:802
  149.2 1007.9 %reduce-scatter.5.cloned.1.call-start = ((), (), s32[]{:S(2)}) async-start(), calls=%async_computation.5 | async-start | bytes 1310720 | tf_op jit(solution)/shard_map/reduce_scatter | solution.py:896
  151.6 125.2 %collective-permute-start.5 = (bf16[512,512]{1,0:T(8,128)(2,1)}, bf16[512,512]{1,0:T(8,128)(2,1)}, u32[]{:S(2)}, u32[]{:S(2)}) collective-permute-start(bf16[512,512]{1,0:T(8,128)(2,1)} %get-tuple-element.99), channel_id=1, source_target_pairs={{0,8},{4,12},{8,0},{12,4},{1,9},{5,13},{9,1},{13,5},{2,10},{6,14},... | collective-permute-start | bytes 1572872 | tf_op jit(solution)/shard_map/ppermute | solution.py:802
  153.1 129.4 %collective-permute-start.6 = (bf16[512,512]{1,0:T(8,128)(2,1)}, bf16[512,512]{1,0:T(8,128)(2,1)}, u32[]{:S(2)}, u32[]{:S(2)}) collective-permute-start(bf16[512,512]{1,0:T(8,128)(2,1)} %get-tuple-element.100), channel_id=1, source_target_pairs={{0,12},{4,8},{8,4},{12,0},{1,13},{5,9},{9,5},{13,1},{2,14},{6,10},... | collective-permute-start | bytes 1572872 | tf_op jit(solution)/shard_map/ppermute | solution.py:802
  229.7 52.8 %collective-permute-start.4 = (bf16[512,512]{1,0:T(8,128)(2,1)}, bf16[512,512]{1,0:T(8,128)(2,1)}, u32[]{:S(2)}, u32[]{:S(2)}) collective-permute-start(bf16[512,512]{1,0:T(8,128)(2,1)} %get-tuple-element.100), channel_id=1, source_target_pairs={{0,4},{4,0},{8,12},{12,8},{1,5},{5,1},{9,13},{13,9},{2,6},{6,2},{1... | collective-permute-start | bytes 1572872 | tf_op jit(solution)/shard_map/ppermute | solution.py:802
  250.2 24.7 %copy-start.29 = (bf16[2048,512]{1,0:T(8,128)(2,1)S(1)}, bf16[2048,512]{1,0:T(8,128)(2,1)}, u32[]{:S(2)}) copy-start(bf16[2048,512]{1,0:T(8,128)(2,1)} %param.22) | copy-start | bytes 6291460
  275.0 44.9 %collective-permute-start.9 = (bf16[512,512]{1,0:T(8,128)(2,1)S(1)}, bf16[512,512]{1,0:T(8,128)(2,1)S(1)}, u32[]{:S(2)}, u32[]{:S(2)}) collective-permute-start(bf16[512,512]{1,0:T(8,128)(2,1)S(1)} %get-tuple-element.88), channel_id=1, source_target_pairs={{0,12},{4,8},{8,4},{12,0},{1,13},{5,9},{9,5},{13,1},{2,14},{6,10},... | collective-permute-start | bytes 1572872 | tf_op jit(solution)/shard_map/ppermute | solution.py:802
  276.8 43.2 %collective-permute-start.7 = (bf16[512,512]{1,0:T(8,128)(2,1)S(1)}, bf16[512,512]{1,0:T(8,128)(2,1)S(1)}, u32[]{:S(2)}, u32[]{:S(2)}) collective-permute-start(bf16[512,512]{1,0:T(8,128)(2,1)S(1)} %get-tuple-element.88), channel_id=1, source_target_pairs={{0,4},{4,0},{8,12},{12,8},{1,5},{5,1},{9,13},{13,9},{2,6},{6,2},{1... | collective-permute-start | bytes 1572872 | tf_op jit(solution)/shard_map/ppermute | solution.py:802
  276.8 43.2 %collective-permute-start.8 = (bf16[512,512]{1,0:T(8,128)(2,1)S(1)}, bf16[512,512]{1,0:T(8,128)(2,1)S(1)}, u32[]{:S(2)}, u32[]{:S(2)}) collective-permute-start(bf16[512,512]{1,0:T(8,128)(2,1)S(1)} %get-tuple-element.87), channel_id=1, source_target_pairs={{0,8},{4,12},{8,0},{12,4},{1,9},{5,13},{9,1},{13,5},{2,10},{6,14},... | collective-permute-start | bytes 1572872 | tf_op jit(solution)/shard_map/ppermute | solution.py:802
  327.4 42.4 %copy-start.54 = (f32[512]{0:T(512)S(1)}, f32[512]{0:T(512)}, u32[]{:S(2)}) copy-start(f32[512]{0:T(512)} %param.25) | copy-start | bytes 6148
  371.0 57.6 %copy-start.30 = (bf16[512,512]{1,0:T(8,128)(2,1)S(1)}, bf16[512,512]{1,0:T(8,128)(2,1)}, u32[]{:S(2)}) copy-start(bf16[512,512]{1,0:T(8,128)(2,1)} %get-tuple-element.89) | copy-start | bytes 1572868
  371.0 57.6 %copy-start.32 = (bf16[512,512]{1,0:T(8,128)(2,1)S(1)}, bf16[512,512]{1,0:T(8,128)(2,1)}, u32[]{:S(2)}) copy-start(bf16[512,512]{1,0:T(8,128)(2,1)} %get-tuple-element.90) | copy-start | bytes 1572868
  371.0 57.6 %copy-start.34 = (bf16[512,512]{1,0:T(8,128)(2,1)S(1)}, bf16[512,512]{1,0:T(8,128)(2,1)}, u32[]{:S(2)}) copy-start(bf16[512,512]{1,0:T(8,128)(2,1)} %get-tuple-element.91) | copy-start | bytes 1572868
  465.9 64.1 %copy-start.11 = (bf16[768,512]{1,0:T(8,128)(2,1)S(1)}, bf16[768,512]{1,0:T(8,128)(2,1)}, u32[]{:S(2)}) copy-start(bf16[768,512]{1,0:T(8,128)(2,1)} %param.27) | copy-start | bytes 2359300
  465.9 64.1 %copy-start.55 = (f32[512]{0:T(512)S(1)}, f32[512]{0:T(512)}, u32[]{:S(2)}) copy-start(f32[512]{0:T(512)} %param.26) | copy-start | bytes 6148
  627.9 26.5 %slice-start = ((s8[12582912]{0:T(1024)(128)(4,1)}), s8[4194304]{0:T(1024)(128)(4,1)S(1)}, s32[]{:S(2)}) async-start(s8[12582912]{0:T(1024)(128)(4,1)} %bitcast.91), calls=%async_computation.6 | async-start | bytes 8388608
  627.9 26.5 %slice-start.1 = ((s8[12582912]{0:T(1024)(128)(4,1)}), s8[4194304]{0:T(1024)(128)(4,1)S(1)}, s32[]{:S(2)}) async-start(s8[12582912]{0:T(1024)(128)(4,1)} %bitcast.91), calls=%async_computation.7 | async-start | bytes 8388608
  638.8 15.6 %slice-start.2 = ((s8[12582912]{0:T(1024)(128)(4,1)}), s8[4194304]{0:T(1024)(128)(4,1)S(1)}, s32[]{:S(2)}) async-start(s8[12582912]{0:T(1024)(128)(4,1)} %bitcast.91), calls=%async_computation.8 | async-start | bytes 8388608
  682.3 64.9 %copy-start.3 = (f32[768,512]{1,0:T(8,128)S(1)}, f32[768,512]{1,0:T(8,128)}, u32[]{:S(2)}) copy-start(f32[768,512]{1,0:T(8,128)} %copy-done.2) | copy-start | bytes 4718596
  682.3 64.9 %copy-start.12 = (bf16[768,512]{1,0:T(8,128)(2,1)S(1)}, bf16[768,512]{1,0:T(8,128)(2,1)}, u32[]{:S(2)}) copy-start(bf16[768,512]{1,0:T(8,128)(2,1)} %param.27) | copy-start | bytes 2359300
  682.3 64.9 %copy-start.18 = (bf16[768,512]{1,0:T(8,128)(2,1)S(1)}, bf16[768,512]{1,0:T(8,128)(2,1)}, u32[]{:S(2)}) copy-start(bf16[768,512]{1,0:T(8,128)(2,1)} %x_ref.1) | copy-start | bytes 2359300
  758.3 31.8 %copy-start.26 = (bf16[256,2048]{1,0:T(8,128)(2,1)S(1)}, bf16[256,2048]{1,0:T(8,128)(2,1)}, u32[]{:S(2)}) copy-start(bf16[256,2048]{1,0:T(8,128)(2,1)} %all-gather.5.cloned.1.call-done) | copy-start | bytes 3145732
  795.6 22.1 %copy-start.15 = (bf16[1536,256]{1,0:T(8,128)(2,1)S(1)}, bf16[1536,256]{1,0:T(8,128)(2,1)}, u32[]{:S(2)}) copy-start(bf16[1536,256]{1,0:T(8,128)(2,1)} %turn_attn.1) | copy-start | bytes 2359300
  823.4 384.4 %reduce-scatter.3.cloned.1.call-start = ((), (), s32[]{:S(2)}) async-start(), calls=%async_computation.4 | async-start | bytes 3932160 | tf_op jit(solution)/shard_map/reduce_scatter | solution.py:896
  823.4 27.7 %copy-start.7 = (f32[768,128]{1,0:T(8,128)S(1)}, f32[768,128]{1,0:T(8,128)}, u32[]{:S(2)}) copy-start(f32[768,128]{1,0:T(8,128)} %copy-done.6) | copy-start | bytes 1179652
  823.4 27.7 %copy-start.9 = (f32[768,128]{1,0:T(8,128)S(1)}, f32[768,128]{1,0:T(8,128)}, u32[]{:S(2)}) copy-start(f32[768,128]{1,0:T(8,128)} %copy-done.8) | copy-start | bytes 1179652
  854.7 64.8 %slice-start.3 = ((s8[6291456]{0:T(1024)(128)(4,1)}), s8[4194304]{0:T(1024)(128)(4,1)S(1)}, s32[]{:S(2)}) async-start(s8[6291456]{0:T(1024)(128)(4,1)} %bitcast.93), calls=%async_computation.9 | async-start | bytes 8388608
  928.6 198.1 %collective-permute-start.18 = (bf16[512,1024]{1,0:T(8,128)(2,1)}, bf16[512,1024]{1,0:T(8,128)(2,1)}, u32[]{:S(2)}, u32[]{:S(2)}) collective-permute-start(bf16[512,1024]{1,0:T(8,128)(2,1)} %constant_dynamic-slice_fusion.1), channel_id=1, source_target_pairs={{0,8},{4,12},{8,0},{12,4},{1,9},{5,13},{9,1},{13,5},{2,10},{6,14},... | collective-permute-start | bytes 3145736 | tf_op jit(solution)/shard_map/ppermute | solution.py:802
  929.7 202.9 %collective-permute-start.15 = (bf16[1024,512]{1,0:T(8,128)(2,1)}, bf16[1024,512]{1,0:T(8,128)(2,1)}, u32[]{:S(2)}, u32[]{:S(2)}) collective-permute-start(bf16[1024,512]{1,0:T(8,128)(2,1)} %constant_dynamic-slice_fusion.3), channel_id=1, source_target_pairs={{0,8},{4,12},{8,0},{12,4},{1,9},{5,13},{9,1},{13,5},{2,10},{6,14},... | collective-permute-start | bytes 3145736 | tf_op jit(solution)/shard_map/ppermute | solution.py:802
  933.6 37.1 %copy-start.13 = (bf16[768,512]{1,0:T(8,128)(2,1)S(1)}, bf16[768,512]{1,0:T(8,128)(2,1)}, u32[]{:S(2)}) copy-start(bf16[768,512]{1,0:T(8,128)(2,1)} %param.27) | copy-start | bytes 2359300
  933.6 195.3 %collective-permute-start.12 = (bf16[1024,512]{1,0:T(8,128)(2,1)}, bf16[1024,512]{1,0:T(8,128)(2,1)}, u32[]{:S(2)}, u32[]{:S(2)}) collective-permute-start(bf16[1024,512]{1,0:T(8,128)(2,1)} %constant_dynamic-slice_fusion.5), channel_id=1, source_target_pairs={{0,8},{4,12},{8,0},{12,4},{1,9},{5,13},{9,1},{13,5},{2,10},{6,14},... | collective-permute-start | bytes 3145736 | tf_op jit(solution)/shard_map/ppermute | solution.py:802
  1128.9 14.9 %collective-permute-start.19 = (bf16[512,512]{1,0:T(8,128)(2,1)S(1)}, bf16[512,512]{1,0:T(8,128)(2,1)S(1)}, u32[]{:S(2)}, u32[]{:S(2)}) collective-permute-start(bf16[512,512]{1,0:T(8,128)(2,1)S(1)} %constant_dynamic-slice_fusion), channel_id=1, source_target_pairs={{0,4},{4,0},{8,12},{12,8},{1,5},{5,1},{9,13},{13,9},{2,6},{6,2},{1... | collective-permute-start | bytes 1572872 | tf_op jit(solution)/shard_map/ppermute | solution.py:802
  1130.7 24.3 %collective-permute-start.13 = (bf16[512,512]{1,0:T(8,128)(2,1)S(1)}, bf16[512,512]{1,0:T(8,128)(2,1)S(1)}, u32[]{:S(2)}, u32[]{:S(2)}) collective-permute-start(bf16[512,512]{1,0:T(8,128)(2,1)S(1)} %constant_dynamic-slice_fusion.4), channel_id=1, source_target_pairs={{0,4},{4,0},{8,12},{12,8},{1,5},{5,1},{9,13},{13,9},{2,6},{6,2},{1... | collective-permute-start | bytes 1572872 | tf_op jit(solution)/shard_map/ppermute | solution.py:802
  1134.2 28.2 %collective-permute-start.16 = (bf16[512,512]{1,0:T(8,128)(2,1)S(1)}, bf16[512,512]{1,0:T(8,128)(2,1)}, u32[]{:S(2)}, u32[]{:S(2)}) collective-permute-start(bf16[512,512]{1,0:T(8,128)(2,1)S(1)} %constant_dynamic-slice_fusion.2), channel_id=1, source_target_pairs={{0,4},{4,0},{8,12},{12,8},{1,5},{5,1},{9,13},{13,9},{2,6},{6,2},{1... | collective-permute-start | bytes 1572872 | tf_op jit(solution)/shard_map/ppermute | solution.py:802
  1145.1 55.5 %collective-permute-start.20 = (bf16[1024,512]{1,0:T(8,128)(2,1)}, bf16[1024,512]{1,0:T(8,128)(2,1)}, u32[]{:S(2)}, u32[]{:S(2)}) collective-permute-start(bf16[1024,512]{1,0:T(8,128)(2,1)} %pad_maximum_fusion.8), channel_id=1, source_target_pairs={{0,16},{16,0},{1,17},{17,1},{2,18},{18,2},{3,19},{19,3},{4,20},{20... | collective-permute-start | bytes 3145736 | tf_op jit(solution)/shard_map/ppermute | solution.py:893
  1156.4 47.2 %collective-permute-start.14 = (bf16[512,1024]{1,0:T(8,128)(2,1)}, bf16[512,1024]{1,0:T(8,128)(2,1)}, u32[]{:S(2)}, u32[]{:S(2)}) collective-permute-start(bf16[512,1024]{1,0:T(8,128)(2,1)} %pad_maximum_fusion.6), channel_id=1, source_target_pairs={{0,16},{16,0},{1,17},{17,1},{2,18},{18,2},{3,19},{19,3},{4,20},{20... | collective-permute-start | bytes 3145736 | tf_op jit(solution)/shard_map/ppermute | solution.py:893
  1157.1 42.3 %copy-start.52 = (bf16[256,512]{1,0:T(8,128)(2,1)S(1)}, bf16[256,512]{1,0:T(8,128)(2,1)}, u32[]{:S(2)}) copy-start(bf16[256,512]{1,0:T(8,128)(2,1)} %reduce-scatter.5.cloned.1.call-done) | copy-start | bytes 786436
  1157.1 42.3 %collective-permute-start.11 = (bf16[256,512]{1,0:T(8,128)(2,1)}, bf16[256,512]{1,0:T(8,128)(2,1)S(1)}, u32[]{:S(2)}, u32[]{:S(2)}) collective-permute-start(bf16[256,512]{1,0:T(8,128)(2,1)} %reduce-scatter.5.cloned.1.call-done), channel_id=1, source_target_pairs={{0,16},{16,0},{1,17},{17,1},{2,18},{18,2},{3,19},{19,3},{4,20},{20... | collective-permute-start | bytes 786440 | tf_op jit(solution)/shard_map/ppermute | solution.py:948
  1165.0 56.8 %collective-permute-start.17 = (bf16[512,1024]{1,0:T(8,128)(2,1)}, bf16[512,1024]{1,0:T(8,128)(2,1)}, u32[]{:S(2)}, u32[]{:S(2)}) collective-permute-start(bf16[512,1024]{1,0:T(8,128)(2,1)} %pad_maximum_fusion.7), channel_id=1, source_target_pairs={{0,16},{16,0},{1,17},{17,1},{2,18},{18,2},{3,19},{19,3},{4,20},{20... | collective-permute-start | bytes 3145736 | tf_op jit(solution)/shard_map/ppermute | solution.py:893
  1207.8 22.4 %collective-permute-start.10 = (bf16[512,768]{0,1:T(8,128)(2,1)}, bf16[512,768]{0,1:T(8,128)(2,1)S(1)}, u32[]{:S(2)}, u32[]{:S(2)}) collective-permute-start(bf16[512,768]{0,1:T(8,128)(2,1)} %reduce-scatter.3.cloned.1.call-done), channel_id=1, source_target_pairs={{0,16},{16,0},{1,17},{17,1},{2,18},{18,2},{3,19},{19,3},{4,20},{20... | collective-permute-start | bytes 2359304 | tf_op jit(solution)/shard_map/ppermute | solution.py:942
  (41 other events, 330.7 us)
Sparse Core Ops, SparseCore 0:
  10.4 66.2 all-gather.2
  149.3 40.0 all-gather.4
  823.5 26.0 reduce-scatter.4
  926.3 137.7 reduce-scatter.2

commit v3 on v2

--- a/solution.py
+++ b/solution.py
@@ -16,6 +16,7 @@
 MESH = pl.DeviceIdType.MESH
 bf16 = jnp.bfloat16
 f32 = jnp.float32
+COST = pl.CostEstimate(flops=0, bytes_accessed=1000, transcendentals=0)
 
 
 def rope_tables(positions, head_dim):
@@ -163,20 +164,30 @@
             pltpu.SemaphoreType.DMA((copies,)),
         ],
         compiler_params=pltpu.CompilerParams(collective_id=number, has_side_effects=True),
-        cost_estimate=pl.CostEstimate(flops=0, bytes_accessed=60_000_000, transcendentals=0),
+        cost_estimate=COST,
     )(values)
 
 
-def scatter_kernel(pair, p_ref, out_ref, rc, s1, ry, rx, s2, fy, fx, sz, fz, send_sem, recv_sem):
+def scatter_kernel(pair, rider, p_ref, *refs):
+    if rider:
+        cargo_ref, out_ref, far_ref = refs[:3]
+    else:
+        out_ref = refs[0]
+    rc, s1, ry, rx, s2, fy, fx, sz, fz, send_sem, recv_sem = refs[3 if rider else 1 :]
     rows, width = out_ref.shape
     half = rows // 2
     y, b, p = side("dp"), lax.axis_index("col"), side("row") if pair else 0
     x, c = b >> 1, b & 1
     to_x, to_y, to_c = neighbours()
     to_z = {"row": flip("row", 1)}
-    greet([to_x, to_y, to_c] + ([to_z] if pair else []))
+    to_far = {"row": flip("row", 2)}
+    greet([to_x, to_y, to_c] + ([to_z] if pair else []) + ([to_far] if rider else []))
     started = []
     send = sender(send_sem, recv_sem, started)
+    if rider:
+        size = far_ref.shape[1]
+        start = pl.multiple_of((1 - (lax.axis_index("row") >> 1)) * size, size)
+        cargo = send(cargo_ref.at[:, pl.ds(start, size)], far_ref, 30, to_far)
 
     def place(yy, h):
         return pl.ds(pl.multiple_of(yy * rows + h * half, half), half)
@@ -274,22 +285,29 @@
         low, high = near.last(near.second(near_first))
         out_ref[pl.ds(0, half), :] = low
         out_ref[pl.ds(half, half), :] = high
+    if rider:
+        cargo.wait_recv()
     for copy in started:
         copy.wait_send()
 
 
-def scatter_wide(partial, pair, number, name):
+def scatter_wide(partial, pair, number, name, cargo=None):
     flows = 2 if pair else 1
     rows, width = partial.shape[0] // (2 * flows), partial.shape[1] // 4
     half = rows // 2
-    copies = 30 if pair else 14
+    rider = cargo is not None
+    copies = 31 if pair else 14
+    out_shape, out_spec = [jax.ShapeDtypeStruct((rows, width), f32)], [pl.BlockSpec(memory_space=pltpu.VMEM)]
+    anywhere = [pl.BlockSpec(memory_space=pl.ANY)] * rider
+    if rider:
+        out_shape.append(jax.ShapeDtypeStruct((cargo.shape[0], cargo.shape[1] // 2), cargo.dtype))
     last = (rows, width) if pair else (16, 128)
-    return pl.pallas_call(
-        functools.partial(scatter_kernel, pair),
+    out = pl.pallas_call(
+        functools.partial(scatter_kernel, pair, rider),
         name=name,
-        out_shape=jax.ShapeDtypeStruct((rows, width), f32),
-        in_specs=[pl.BlockSpec(memory_space=pltpu.VMEM)],
-        out_specs=pl.BlockSpec(memory_space=pltpu.VMEM),
+        out_shape=out_shape,
+        in_specs=[pl.BlockSpec(memory_space=pltpu.VMEM)] + anywhere,
+        out_specs=out_spec + anywhere,
         scratch_shapes=[
             pltpu.VMEM((flows, 2, 2 * rows, width), bf16),
             pltpu.VMEM((flows, 2, 2 * rows, width), bf16),
@@ -306,8 +324,9 @@
         compiler_params=pltpu.CompilerParams(
             collective_id=number, has_side_effects=True, vmem_limit_bytes=48 * 2**20
         ),
-        cost_estimate=pl.CostEstimate(flops=0, bytes_accessed=80_000_000, transcendentals=0),
-    )(partial)
+        cost_estimate=COST,
+    )(partial, *([cargo] * rider))
+    return out if rider else out[0]
 
 
 def feature_peers(wide):
@@ -358,6 +377,50 @@
     return total.reshape(k, t)
 
 
+def gain_peers():
+    peers = []
+    for d in range(1, 8):
+        peers.append({"row": flip("row", d & 3), "dp": flip("dp", d >> 2)})
+    return peers
+
+
+def gain_kernel(v_ref, out_ref, slots, send_sem, recv_sem):
+    me = side("dp") * 4 + lax.axis_index("row")
+    peers = gain_peers()
+    greet(peers)
+    started = []
+    send = sender(send_sem, recv_sem, started)
+    for d, peer in enumerate(peers):
+        send(v_ref, slots.at[me], d, peer)
+    slots[me] = v_ref[...]
+    for copy in started:
+        copy.wait_recv()
+    total = slots[0]
+    for i in range(1, 8):
+        total = total + slots[i]
+    out_ref[...] = total
+    for copy in started:
+        copy.wait_send()
+
+
+def gain_total(values, number):
+    flat = values.reshape(-1, 128)
+    total = pl.pallas_call(
+        gain_kernel,
+        name="total_gains",
+        out_shape=jax.ShapeDtypeStruct(flat.shape, f32),
+        in_specs=[pl.BlockSpec(memory_space=pltpu.VMEM)],
+        out_specs=pl.BlockSpec(memory_space=pltpu.VMEM),
+        scratch_shapes=[
+            pltpu.VMEM((8,) + flat.shape, f32),
+            pltpu.SemaphoreType.DMA((7,)),
+            pltpu.SemaphoreType.DMA((7,)),
+        ],
+        compiler_params=pltpu.CompilerParams(collective_id=number, has_side_effects=True),
+    )(flat)
+    return total.reshape(values.shape)
+
+
 def row_peers():
     return [(d, {"row": flip("row", d)}) for d in (3, 2, 1)]
 
@@ -405,7 +468,7 @@
             pltpu.SemaphoreType.DMA((3,)),
         ],
         compiler_params=pltpu.CompilerParams(collective_id=number, has_side_effects=True),
-        cost_estimate=pl.CostEstimate(flops=0, bytes_accessed=60_000_000, transcendentals=0),
+        cost_estimate=COST,
     )(values)
 
 
@@ -515,7 +578,7 @@
         compiler_params=pltpu.CompilerParams(
             collective_id=number, has_side_effects=True, vmem_limit_bytes=40 * 2**20
         ),
-        cost_estimate=pl.CostEstimate(flops=0, bytes_accessed=120_000_000, transcendentals=0),
+        cost_estimate=COST,
     )(qkv, cosine, sine_signed, gains)
 
 
@@ -623,7 +686,7 @@
         compiler_params=pltpu.CompilerParams(
             collective_id=number, has_side_effects=True, vmem_limit_bytes=40 * 2**20
         ),
-        cost_estimate=pl.CostEstimate(flops=0, bytes_accessed=120_000_000, transcendentals=0),
+        cost_estimate=COST,
     )(d_units, qkv, cosine, sine_signed, gains, inverse)
 
 
@@ -683,11 +746,7 @@
         ),
         in_specs=[pl.BlockSpec(memory_space=pltpu.SMEM), part, whole, whole],
         out_specs=(part, part, pl.BlockSpec((8, BLOCK), lambda i: (0, i))),
-        cost_estimate=pl.CostEstimate(
-            flops=2 * slots * slots * HEAD_DIM,
-            bytes_accessed=8 * slots * HEAD_DIM,
-            transcendentals=slots * slots // 2,
-        ),
+        cost_estimate=COST,
     )(length, q, k, v)
 
 
@@ -758,11 +817,7 @@
         in_specs=[pl.BlockSpec(memory_space=pltpu.SMEM), whole, part, part, whole, whole, line],
         out_specs=pl.BlockSpec((3, slots, HEAD_DIM), lambda j: (0, 0, 0)),
         scratch_shapes=[pltpu.VMEM((slots, HEAD_DIM), f32), pltpu.VMEM((8, slots), f32)],
-        cost_estimate=pl.CostEstimate(
-            flops=5 * slots * slots * HEAD_DIM,
-            bytes_accessed=14 * slots * HEAD_DIM,
-            transcendentals=slots * slots // 2,
-        ),
+        cost_estimate=COST,
     )(length, q, k, v, do, o, lse)
 
 
@@ -801,13 +856,27 @@
     def row_swap(values, d):
         return lax.ppermute(values, "row", [(i, i ^ d) for i in range(row_count)])
 
-    def hidden_part(weight, axis):
-        def quarter(d):
-            return lax.dynamic_slice_in_dim(weight, (y * 2 + (p ^ (d & 1))) * hid, hid, axis)
-
-        parts = [quarter(0)] + [row_swap(quarter(d), d) for d in (1, 2, 3)]
-        stacked = jnp.stack(parts)
-        return [lax.dynamic_index_in_dim(stacked, z ^ i, 0, keepdims=False) for i in range(row_count)]
+    def hidden_parts(*done):
+        def quarters(d):
+            start = (y * 2 + (p ^ (d & 1))) * hid
+            return jnp.stack(
+                [
+                    lax.dynamic_slice_in_dim(w_gate, start, hid, 1),
+                    lax.dynamic_slice_in_dim(w_up, start, hid, 1),
+                    lax.dynamic_slice_in_dim(w_down, start, hid, 0),
+                ]
+            )
+
+        parts = [quarters(0)] + [row_swap(after(quarters(d), *done), d) for d in (1, 2, 3)]
+        depth = w_gate.shape[0]
+        gate_up = jnp.zeros((width, 2 * hid), bf16)
+        down = jnp.zeros((hid, width), bf16)
+        for d, part in enumerate(parts):
+            spot = (z ^ d) * depth
+            gate_up = lax.dynamic_update_slice(gate_up, part[0], (spot, 0))
+            gate_up = lax.dynamic_update_slice(gate_up, part[1], (spot, hid))
+            down = lax.dynamic_update_slice(down, part[2], (0, spot))
+        return gate_up, down
 
     qkv_weight = lax.all_gather(
         jnp.concatenate([y_half(w_query, 1), y_half(w_key, 1), y_half(w_value, 1)], axis=1),
@@ -835,11 +904,9 @@
     qkv = matmul(tokens_wide, qkv_weight)
     units, inverse = front(qkv, cosine, sine_signed, qk_gain, width, 2 * heads, 2)
     q_unit, k_unit, v_unit = (units[:, i].reshape(slots, HEAD_DIM) for i in range(3))
-    gate_weight = jnp.concatenate(hidden_part(after(w_gate, units), 1), axis=0)
-    up_weight = jnp.concatenate(hidden_part(after(w_up, units), 1), axis=0)
+    gate_up_weight, down_weight = hidden_parts(units)
     attn_unit, attn_exact, log_total = attend(unit_length, q_unit, k_unit, v_unit)
     attn_low = turn(attn_unit, True, tok_rows, heads, 3, "turn_attn")
-    down_weight = jnp.concatenate(hidden_part(after(w_down, attn_low), 0), axis=1)
     branch = scatter_wide(matmul(attn_low, out_weight).astype(bf16), False, 4, "scatter_branch")
     branch_inv = lax.rsqrt(
         feature_total(jnp.sum(branch * branch, axis=1)[None, :], 5, "total_branch")[0] / width
@@ -847,8 +914,8 @@
     )[:, None]
     resid = tokens.astype(f32) + branch * branch_inv * attn_gain
     resid_wide = gather_wide(resid.astype(bf16), True, 6, "gather_resid")
-    gate = matmul(resid_wide, gate_weight)
-    upper = matmul(resid_wide, up_weight)
+    gate = matmul(resid_wide, gate_up_weight[:, :hid])
+    upper = matmul(resid_wide, gate_up_weight[:, hid:])
     sigma = jax.nn.sigmoid(gate)
     hidden = (gate * sigma * upper).astype(bf16)
     mixed = scatter_wide(matmul(hidden, down_weight).astype(bf16), True, 7, "scatter_mixed")
@@ -883,14 +950,30 @@
         high = jnp.where(bit == 0, other, piece)
         return jnp.concatenate([low, high], axis=axis)
 
-    def hidden_grad(raw, axis):
-        far = row_swap(cut(raw, 1 - (z >> 1), 2, axis), 2)
+
+    def from_far(raw, axis):
+        return row_swap(cut(raw, 1 - (z >> 1), 2, axis), 2)
+
+    def with_far(raw, far, axis):
         near = cut(raw, z >> 1, 2, axis)
-        near = (near.astype(f32) + far.astype(f32)).astype(bf16)
-        near = over_dp(near)
+        return over_dp((near.astype(f32) + far.astype(f32)).astype(bf16))
+
+    def from_near(near, axis):
         own, away = cut(near, p, 2, axis), row_swap(cut(near, 1 - p, 2, axis), 1)
-        block = two_sides(own, away, p, 1 - axis)
-        return two_sides(block, lax.ppermute(block, "dp", pairs), y, 1 - axis).astype(f32)
+        return own, away
+
+    def from_twin(own, away):
+        return lax.ppermute(jnp.stack([own, away]), "dp", pairs)
+
+    def blocks(own, away, other, axis, count):
+        def block(i):
+            mine = two_sides(cut(own, i, count, 1 - axis), cut(away, i, count, 1 - axis), p, 1 - axis)
+            theirs = two_sides(
+                cut(other[0], i, count, 1 - axis), cut(other[1], i, count, 1 - axis), p, 1 - axis
+            )
+            return two_sides(mine, theirs, y, 1 - axis).astype(f32)
+
+        return [block(i) for i in range(count)]
 
     def reduce_rows(raw, axis):
         return lax.psum_scatter(raw, "row", scatter_dimension=axis, tiled=True)
@@ -899,15 +982,15 @@
     down_raw = (contract_first(hidden, d_mixed_wide) * factor).astype(bf16)
     d_gate = (d_hidden * upper * sigma * (1.0 + gate * (1.0 - sigma))).astype(bf16)
     d_upper = (d_hidden * gate * sigma).astype(bf16)
-    gate_raw = (contract_first(resid_wide, d_gate) * factor).astype(bf16)
-    up_raw = (contract_first(resid_wide, d_upper) * factor).astype(bf16)
-    d_resid_wide = (
-        contract_last(d_gate, gate_weight) + contract_last(d_upper, up_weight)
-    ).astype(bf16)
-    d_resid_wide, down_raw, gate_raw, up_raw = lax.optimization_barrier(
-        (d_resid_wide, down_raw, gate_raw, up_raw)
-    )
-    d_resid = incoming + scatter_wide(d_resid_wide, True, 10, "scatter_d_resid")
+    d_gate_up = jnp.concatenate([d_gate, d_upper], axis=1)
+    gate_up_raw = (contract_first(resid_wide, d_gate_up) * factor).astype(bf16)
+    d_resid_wide = contract_last(d_gate_up, gate_up_weight).astype(bf16)
+    d_resid_wide, down_raw, gate_up_raw = lax.optimization_barrier(
+        (d_resid_wide, down_raw, gate_up_raw)
+    )
+    d_resid, far_down = scatter_wide(d_resid_wide, True, 10, "scatter_d_resid", down_raw)
+    d_resid = incoming + d_resid
+    far_gate_up = from_far(gate_up_raw, 0)
     attn_gain_raw = jnp.sum(d_resid * branch * branch_inv, axis=0)
     gained = d_resid * attn_gain
     inner = (
@@ -915,16 +998,24 @@
         / width
     )
     d_branch = (branch_inv * gained - branch * branch_inv**3 * inner).astype(bf16)
-    d_branch_wide = gather_wide(d_branch, False, 12, "gather_d_branch")
+    d_branch_wide, far_down = lax.optimization_barrier(
+        (gather_wide(d_branch, False, 12, "gather_d_branch"), far_down)
+    )
+    own_down, away_down = from_near(with_far(down_raw, far_down, 1), 1)
     d_attn = contract_last(d_branch_wide, out_weight).astype(bf16)
     d_attn_unit = turn(d_attn, False, tok_rows, heads, 13, "turn_d_attn")
     out_raw = (contract_first(attn_low, after(d_branch_wide, d_attn_unit)) * factor).astype(bf16)
     d_attn_unit, out_raw = lax.optimization_barrier((d_attn_unit, out_raw))
     out_piece = reduce_rows(out_raw, 1)
     d_units = attend_back(unit_length, q_unit, k_unit, v_unit, d_attn_unit, attn_exact, log_total)
+    d_units, far_gate_up, away_down = lax.optimization_barrier((d_units, far_gate_up, away_down))
+    own_gate_up, away_gate_up = from_near(with_far(gate_up_raw, far_gate_up, 0), 0)
+    other_down = from_twin(own_down, away_down)
     d_qkv, gain_sums = rear(
         d_units, qkv[:, : 2 * half_feat], cosine, sine_signed, qk_gain, inverse, width, 14
     )
+    d_qkv, away_gate_up, other_down = lax.optimization_barrier((d_qkv, away_gate_up, other_down))
+    other_gate_up = from_twin(own_gate_up, away_gate_up)
     qkv_raw = (contract_first(tokens_wide, d_qkv) * factor).astype(bf16)
     projected = contract_last(d_qkv, qkv_weight).astype(bf16)
     projected, qkv_raw = lax.optimization_barrier((projected, qkv_raw))
@@ -934,11 +1025,15 @@
     def spread(half):
         return lax.dynamic_update_slice_in_dim(jnp.zeros((feat_part,), f32), half, y * half_feat, 0)
 
-    gains = lax.psum(
-        jnp.stack([spread(gain_sums[0]), spread(gain_sums[1]), attn_gain_raw, mlp_gain_raw])
-        * factor,
-        ("dp", "row"),
-    )
+    gains = over_dp(
+        gain_total(
+            jnp.stack([spread(gain_sums[0]), spread(gain_sums[1]), attn_gain_raw, mlp_gain_raw])
+            * factor,
+            15,
+        )
+    )
+    (down_grad,) = blocks(own_down, away_down, other_down, 1, 1)
+    gate_grad, up_grad = blocks(own_gate_up, away_gate_up, other_gate_up, 0, 2)
     qkv_other = lax.ppermute(qkv_piece, "dp", pairs)
     q_grad, k_grad, v_grad = (
         two_sides(cut(qkv_piece, i, 3, 1), cut(qkv_other, i, 3, 1), y, 1).astype(f32)
@@ -953,9 +1048,9 @@
         k_grad,
         v_grad,
         out_grad,
-        hidden_grad(gate_raw, 0),
-        hidden_grad(up_raw, 0),
-        hidden_grad(down_raw, 1),
+        gate_grad,
+        up_grad,
+        down_grad,
         gains[0],
         gains[1],
         gains[2],

time: 1250 us -> 1150 us (0.920)
  Pallas kernels: 597 us -> 841 us
  waiting for transfers between devices: 208 us -> 33.4 us
  blocking collectives: 154 us -> 0 us
    pallas_call x2, Pallas kernels: 42.8 us -> 198 us  [turn(): pl.pallas_call(functools.partial(turn_kernel, back, tok, heads), name=nam...]
    psum x1 -> x0, blocking collectives: 154 us -> none  [per_device(): lax.psum(jnp.stack([spread(gain_sums[0]), spread(gain_sums[1]), attn_gain...]
    ppermute x15 -> x6, waiting for transfers between devices: 131 us -> 0.02 us  [row_swap(): return lax.ppermute(values, 'row', [(i, i ^ d) for i in range(row_count)])]
    pallas_call x4 -> x5, Pallas kernels: 201 us -> 259 us  [the longest x4 210 us: scatter_wide(): pl.pallas_call(functools.partial(scatter_kernel, pair, rider), name=name,...]
    ppermute x1, waiting for transfers between devices: 33.7 us -> 0.01 us  [per_device(): lax.ppermute(out_piece, 'dp', pairs)]
    pallas_call x1, Pallas kernels: 55.8 us -> 75.6 us  [rear(): pl.pallas_call(functools.partial(rear_kernel, width), name='rear', out_sh...]
    pallas_call x1, Pallas kernels: 56.1 us -> 69.5 us  [front(): pl.pallas_call(functools.partial(front_kernel, width), name='front', out_...]
    ppermute x3 -> x2, waiting for transfers between devices: 13.4 us -> 0.01 us  [from_twin(): return lax.ppermute(jnp.stack([own, away]), 'dp', pairs)]
  transfers between devices with their start and end apart: 25 -> 15, of which waited for: 9 -> 2; matrix products, arithmetic and copies ran while one was open for 5% -> 8% of each run, Pallas kernels for 16% -> 56%
where the time goes in v3:
time: 1150 us; the launch traced here: 1140 us
  Pallas kernels  841 us (73%)
  matrix products  148 us (13%)
  other arithmetic  46.1 us (4%)
  local copies, waits for them, and re-layouts  44.9 us (4%)
  waiting for transfers between devices  33.4 us (3%)
  between operations  15.8 us (1%)
  starting transfers between devices  14 us (1%)
    pallas_call x4, Pallas kernels, scatter_wide(): pl.pallas_call(functools.partial(scatter_kernel, pair, rider), name=name,...  210 us
    pallas_call x2, Pallas kernels, turn(): pl.pallas_call(functools.partial(turn_kernel, back, tok, heads), name=nam...  198 us
    pallas_call x4, Pallas kernels, gather_wide(): pl.pallas_call(functools.partial(gather_kernel, pair), name=name, out_sha...  178 us
    pallas_call x1, Pallas kernels, rear(): pl.pallas_call(functools.partial(rear_kernel, width), name='rear', out_sh...  75.6 us
    pallas_call x1, Pallas kernels, front(): pl.pallas_call(functools.partial(front_kernel, width), name='front', out_...  69.5 us
    dot_general x5, matrix products, matmul(): return jnp.dot(left, right, preferred_element_type=f32)  54.5 us
    dot_general x4, matrix products, contract_last(): lax.dot_general(left, right, (((1,), (1,)), ((), ())), preferred_element_...  52.3 us
    pallas_call x1, Pallas kernels, gain_total(): pl.pallas_call(gain_kernel, name='total_gains', out_shape=jax.ShapeDtypeS...  49.2 us
  transfers between devices with their start and end apart: 15, of which 2 were waited for; matrix products, arithmetic and copies ran while one was open for 8% of the time, Pallas kernels for 56%

profile of v3, /device:TPU:0, one launch (start us, length us, event | category | flops | bytes accessed | tf_op | source)
XLA Modules:
  0.0 1143.6 jit_solution(16594649783746035057)
XLA Ops:
  10.3 3.1 collective-permute-start
  14.2 31.3 %gather_tokens.1 = bf16[1536,2048]{1,0:T(8,128)(2,1)} custom-call(bf16[768,512]{1,0:T(8,128)(2,1)} %x_ref.1), custom_call_target="tpu_custom_call" | custom-call | bytes 1000 | tf_op jit(solution)/shard_map/gather_tokens/pallas_call | solution.py:155
  55.2 21.4 %all-gather.3.cloned.1.call-done = bf16[2048,768]{1,0:T(8,128)(2,1)} async-done(((bf16[512,768]{1,0:T(8,128)(2,1)}), bf16[2048,768]{1,0:T(8,128)(2,1)}) %all-gather.3.cloned.1.call-update) | async-done | bytes 3145744 | tf_op jit(solution)/shard_map/all_gather | solution.py:881
  78.7 8.1 convolution_bitcast_fusion.qkv_ref
  86.9 69.5 %front.1 = (bf16[4,3,768,128]{3,2,1,0:T(8,128)(2,1)S(1)}, f32[2,1536]{1,0:T(2,128)S(1)}) custom-call(f32[1536,768]{1,0:T(8,128)S(1)} %convolution_bitcast_fusion.qkv_ref, f32[768,128]{1,0:T(8,128)S(1)} %get-tuple-element.140.cos_ref, f32[768,128]{1,0:T(8,128)S(1)} %get-tuple-element.139.sin_ref, f32[2,256]{1,0:T(2,128)S(1)} %pad_maximum_fusion.16.gain_ref), custom_call_target="tpu_custom_call" | custom-call | bytes 1000 | tf_op jit(solution)/shard_map/front/pallas_call | solution.py:558
  157.6 3.3 collective-permute-start.2
  162.4 20.0 %attend.1 = (bf16[3072,128]{1,0:T(8,128)(2,1)}, f32[3072,128]{1,0:T(8,128)}, f32[8,3072]{1,0:T(8,128)}) custom-call(s32[1]{0:T(128)} %dynamic_slice.108.len_ref, bf16[3072,128]{1,0:T(8,128)(2,1)} %bitcast.125, bf16[3072,128]{1,0:T(8,128)(2,1)} %bitcast.123, bf16[3072,128]{1,0:T(8,128)(2,1)} %bitcast.121), custom_call_target="tpu_custom_call" | custom-call | bytes 1000 | tf_op jit(solution)/shard_map/attend/pallas_call | solution.py:738
  182.4 126.7 %turn_attn.1 = bf16[1536,256]{1,0:T(8,128)(2,1)} custom-call(bf16[3072,128]{1,0:T(8,128)(2,1)} %get-tuple-element.42.x_ref), custom_call_target="tpu_custom_call" | custom-call | bytes 1000 | tf_op jit(solution)/shard_map/turn_attn/pallas_call | solution.py:459
  309.1 5.9 convolution_convert_fusion.3.p_ref
  315.0 37.5 %scatter_branch.1 = f32[768,512]{1,0:T(8,128)S(1)} custom-call(bf16[1536,2048]{1,0:T(8,128)(2,1)} %convolution_convert_fusion.3.p_ref), custom_call_target="tpu_custom_call" | custom-call | bytes 1000 | tf_op jit(solution)/shard_map/scatter_branch/pallas_call | solution.py:305
  353.5 4.9 total_branch.1
  360.3 57.3 %gather_resid.1 = bf16[3072,2048]{1,0:T(8,128)(2,1)} custom-call(bf16[768,512]{1,0:T(8,128)(2,1)} %fusion.8.x_ref), custom_call_target="tpu_custom_call" | custom-call | bytes 1000 | tf_op jit(solution)/shard_map/gather_resid/pallas_call | solution.py:155
  420.1 2.2 fusion.11
  424.2 2.2 fusion.10
  428.3 2.2 fusion.9
  430.5 12.1 %fusion.4 = f32[3072,512]{0,1:T(8,128)} fusion(bf16[3072,2048]{1,0:T(8,128)(2,1)} %gather_resid.1, bf16[2048,1024]{1,0:T(8,128)(2,1)} %get-tuple-element.129), kind=kOutput, calls=%fused_computation.20 | convolution fusion | flops 6442450944 | bytes 20971520 | tf_op jit(solution)/shard_map/dot_general | solution.py:31
  442.6 16.7 %multiply_convert_fusion.4 = (bf16[3072,512]{0,1:T(8,128)(2,1)}, f32[3072,512]{0,1:T(8,128)}) fusion(f32[3072,512]{0,1:T(8,128)} %fusion.4, bf16[3072,2048]{1,0:T(8,128)(2,1)} %gather_resid.1, bf16[2048,1024]{1,0:T(8,128)(2,1)} %get-tuple-element.129), kind=kOutput, calls=%fused_computation.9 | convolution fusion | flops 6451888128 | bytes 30408704 | tf_op jit(solution)/shard_map/dot_general | solution.py:31
  459.3 11.8 %convolution_convert_fusion.1.p_ref = bf16[3072,2048]{1,0:T(8,128)(2,1)} fusion(bf16[3072,512]{0,1:T(8,128)(2,1)} %get-tuple-element.147, bf16[512,2048]{1,0:T(8,128)(2,1)S(1)} %copy-done.34), kind=kOutput, calls=%fused_computation.1 | convolution fusion | flops 6448742400 | bytes 17825792 | tf_op jit(solution)/shard_map/dot_general | solution.py:31
  471.1 64.1 %scatter_mixed.1 = f32[768,512]{1,0:T(8,128)S(1)} custom-call(bf16[3072,2048]{1,0:T(8,128)(2,1)} %convolution_convert_fusion.1.p_ref), custom_call_target="tpu_custom_call" | custom-call | bytes 1000 | tf_op jit(solution)/shard_map/scatter_mixed/pallas_call | solution.py:305
  536.5 5.0 total_mixed.1
  544.3 57.3 %gather_d_mixed.1 = bf16[3072,2048]{1,0:T(8,128)(2,1)} custom-call(bf16[768,512]{1,0:T(8,128)(2,1)} %subtract_convert_fusion.1.x_ref), custom_call_target="tpu_custom_call" | custom-call | bytes 1000 | tf_op jit(solution)/shard_map/gather_d_mixed/pallas_call | solution.py:155
  601.6 10.7 multiply_convert_fusion.5.refs_0_
  612.4 17.1 %multiply_convert_fusion.3 = (bf16[3072,512]{0,1:T(8,128)(2,1)S(1)}, bf16[3072,512]{0,1:T(8,128)(2,1)}) fusion(f32[3072,512]{0,1:T(8,128)} %fusion.4, f32[3072,512]{0,1:T(8,128)} %get-tuple-element.148, bf16[3072,2048]{1,0:T(8,128)(2,1)} %gather_d_mixed.1, bf16[512,2048]{1,0:T(8,128)(2,1)S(1)} %copy-done.35), kind=kOutput, calls=%fused_computation.8 | convolution fusion | flops 6462898176 | bytes 33554432 | tf_op jit(solution)/shard_map/dot_general | solution.py:39
  631.1 18.7 %multiply_convert_fusion = bf16[2048,1024]{1,0:T(8,128)(2,1)} fusion(bf16[3072,2048]{1,0:T(8,128)(2,1)} %gather_resid.1, bf16[3072,512]{0,1:T(8,128)(2,1)} %get-tuple-element.88, bf16[3072,512]{0,1:T(8,128)(2,1)S(1)} %get-tuple-element.87), kind=kOutput, calls=%fused_computation.2 | convolution fusion | flops 12901679104 | bytes 23068672 | tf_op jit(solution)/shard_map/dot_general | solution.py:35
  649.8 20.1 %convolution_convert_fusion.p_ref = bf16[3072,2048]{1,0:T(8,128)(2,1)} fusion(bf16[2048,1024]{1,0:T(8,128)(2,1)} %get-tuple-element.129, bf16[3072,512]{0,1:T(8,128)(2,1)} %get-tuple-element.88, bf16[3072,512]{0,1:T(8,128)(2,1)} %copy-done.52), kind=kOutput, calls=%fused_computation | convolution fusion | flops 12903776256 | bytes 23068672 | tf_op jit(solution)/shard_map/dot_general | solution.py:39
  670.0 71.4 %scatter_d_resid.1 = (f32[768,512]{1,0:T(8,128)S(1)}, bf16[512,1024]{1,0:T(8,128)(2,1)S(1)}) custom-call(bf16[3072,2048]{1,0:T(8,128)(2,1)} %convolution_convert_fusion.p_ref, bf16[512,2048]{1,0:T(8,128)(2,1)S(1)} %multiply_convert_fusion.5.refs_0_), custom_call_target="tpu_custom_call" | custom-call | bytes 1000 | tf_op jit(solution)/shard_map/scatter_d_resid/pallas_call | solution.py:305
  741.5 3.1 multiply_reduce_fusion.1
  744.6 5.1 total_d_resid.1
  749.7 3.2 constant_dynamic-slice_fusion.2
  754.6 31.8 %gather_d_branch.1 = bf16[1536,2048]{1,0:T(8,128)(2,1)} custom-call(bf16[768,512]{1,0:T(8,128)(2,1)} %subtract_convert_fusion.x_ref), custom_call_target="tpu_custom_call" | custom-call | bytes 1000 | tf_op jit(solution)/shard_map/gather_d_branch/pallas_call | solution.py:155
  786.4 5.9 convolution_convert_fusion.4.x_ref
  792.2 71.1 %turn_d_attn.1.do_ref = bf16[3072,128]{1,0:T(8,128)(2,1)} custom-call(bf16[1536,256]{1,0:T(8,128)(2,1)} %convolution_convert_fusion.4.x_ref), custom_call_target="tpu_custom_call" | custom-call | bytes 1000 | tf_op jit(solution)/shard_map/turn_d_attn/pallas_call | solution.py:459
  866.2 5.6 fusion.1
  871.8 26.4 %attend_back.1.d_ref = bf16[3,3072,128]{2,1,0:T(8,128)(2,1)} custom-call(s32[1]{0:T(128)} %dynamic_slice.108.len_ref, bf16[3072,128]{1,0:T(8,128)(2,1)} %bitcast.126, bf16[3072,128]{1,0:T(8,128)(2,1)} %bitcast.124, bf16[3072,128]{1,0:T(8,128)(2,1)} %bitcast.122, bf16[3072,128]{1,0:T(8,128)(2,1)} %turn_d_attn.1.do_ref, f32[3072,128]{1,0:T(8,128)} %get-tuple-element.53.o_ref, ...), custom_call_target="tpu_custom_call" | custom-call | bytes 1000 | tf_op jit(solution)/shard_map/attend_back/pallas_call | solution.py:812
  898.2 3.3 add_convert_fusion
  906.5 2.0 collective-permute-start.6
  908.5 2.2 slice.127.qkv_ref
  914.3 75.6 %rear.1 = (bf16[1536,768]{1,0:T(8,128)(2,1)S(1)}, f32[2,256]{1,0:T(2,128)S(1)}) custom-call(bf16[3,3072,128]{2,1,0:T(8,128)(2,1)S(1)} %copy-done.8, f32[1536,512]{1,0:T(8,128)S(1)} %copy-done.7, f32[768,128]{1,0:T(8,128)S(1)} %copy-done.13, f32[768,128]{1,0:T(8,128)S(1)} %copy-done.11, f32[2,256]{1,0:T(2,128)S(1)} %copy-done.17, ...), custom_call_target="tpu_custom_call" | custom-call | bytes 1000 | tf_op jit(solution)/shard_map/rear/pallas_call | solution.py:667
  989.9 9.2 convolution_convert_fusion.2.p_ref
  999.1 6.5 fusion
  1006.5 3.1 pad_maximum_fusion.3
  1011.4 49.2 %total_gains.1 = f32[16,128]{1,0:T(8,128)} custom-call(f32[16,128]{1,0:T(8,128)} %mul.323.v_ref), custom_call_target="tpu_custom_call" | custom-call | tf_op jit(solution)/shard_map/total_gains/pallas_call | solution.py:408
  1063.2 36.9 %scatter_projected.1 = f32[768,512]{1,0:T(8,128)S(1)} custom-call(bf16[1536,2048]{1,0:T(8,128)(2,1)} %convolution_convert_fusion.2.p_ref), custom_call_target="tpu_custom_call" | custom-call | bytes 1000 | tf_op jit(solution)/shard_map/scatter_projected/pallas_call | solution.py:305
  1103.0 2.6 broadcast_select_fusion.11
  1105.6 2.6 maximum_convert_fusion.2
  1115.4 2.6 maximum_convert_fusion
  1117.9 2.5 maximum_convert_fusion.1
  1120.5 11.8 %collective-permute-done.8 = bf16[512,768]{0,1:T(8,128)(2,1)S(1)} collective-permute-done((bf16[512,768]{0,1:T(8,128)(2,1)}, bf16[512,768]{0,1:T(8,128)(2,1)S(1)}, u32[]{:S(2)}, u32[]{:S(2)}) %collective-permute-start.8) | collective-permute-done | bytes 786464 | tf_op jit(solution)/shard_map/ppermute | solution.py:1037
  (212 shorter events, 65.1 us)
Async XLA Ops:
  7.2 6.9 copy-start.50
  7.2 7.0 copy-start.51
  7.2 69.4 %all-gather.3.cloned.1.call-start = ((), (), s32[]{:S(2)}) async-start(), calls=%async_computation.2 | async-start | bytes 3932160 | tf_op jit(solution)/shard_map/all_gather | solution.py:881
  10.3 298.8 %all-gather.5.cloned.1.call-start = ((), (), s32[]{:S(2)}) async-start(), calls=%async_computation.3 | async-start | bytes 1310720 | tf_op jit(solution)/shard_map/all_gather | solution.py:887
  10.3 67.1 %collective-permute-start = (s32[1]{0:T(128)}, s32[1]{0:T(128)}, u32[]{:S(2)}, u32[]{:S(2)}) collective-permute-start(s32[1]{0:T(128)} %param.15), channel_id=1, source_target_pairs={{0,16},{16,0},{1,17},{17,1},{2,18},{18,2},{3,19},{19,3},{4,20},{20... | collective-permute-start | bytes 20 | tf_op jit(solution)/shard_map/ppermute | solution.py:894
  45.7 41.2 %copy-start.16 = (f32[2,256]{1,0:T(2,128)}, f32[2,256]{1,0:T(2,128)S(1)}, u32[]{:S(2)}) copy-start(f32[2,256]{1,0:T(2,128)S(1)} %pad_maximum_fusion.16.gain_ref) | copy-start | bytes 6148
  51.3 25.3 %copy-start.41 = (bf16[512,512]{1,0:T(8,128)(2,1)S(1)}, bf16[512,512]{1,0:T(8,128)(2,1)}, u32[]{:S(2)}) copy-start(bf16[512,512]{1,0:T(8,128)(2,1)} %param.19) | copy-start | bytes 1572868
  55.2 31.7 %copy-start.10 = (f32[768,128]{1,0:T(8,128)}, f32[768,128]{1,0:T(8,128)S(1)}, u32[]{:S(2)}) copy-start(f32[768,128]{1,0:T(8,128)S(1)} %get-tuple-element.139.sin_ref) | copy-start | bytes 1179652
  55.2 31.7 %copy-start.12 = (f32[768,128]{1,0:T(8,128)}, f32[768,128]{1,0:T(8,128)S(1)}, u32[]{:S(2)}) copy-start(f32[768,128]{1,0:T(8,128)S(1)} %get-tuple-element.140.cos_ref) | copy-start | bytes 1179652
  77.4 928.3 %reduce-scatter.5.cloned.1.call-start = ((), (), s32[]{:S(2)}) async-start(), calls=%async_computation.5 | async-start | bytes 1310720 | tf_op jit(solution)/shard_map/reduce_scatter | solution.py:979
  86.8 69.6 %copy-start.6 = (f32[1536,768]{1,0:T(8,128)}, f32[1536,768]{1,0:T(8,128)S(1)}, u32[]{:S(2)}) copy-start(f32[1536,768]{1,0:T(8,128)S(1)} %convolution_bitcast_fusion.qkv_ref) | copy-start | bytes 14155780
  156.4 270.0 %collective-permute-start.3 = (bf16[3,512,512]{2,1,0:T(8,128)(2,1)}, bf16[3,512,512]{2,1,0:T(8,128)(2,1)}, u32[]{:S(2)}, u32[]{:S(2)}) collective-permute-start(bf16[3,512,512]{2,1,0:T(8,128)(2,1)} %pad_maximum_fusion.4), channel_id=1, source_target_pairs={{0,12},{4,8},{8,4},{12,0},{1,13},{5,9},{9,5},{13,1},{2,14},{6,10},... | collective-permute-start | bytes 4718600 | tf_op jit(solution)/shard_map/ppermute | solution.py:857
  157.6 260.6 %collective-permute-start.1 = (bf16[3,512,512]{2,1,0:T(8,128)(2,1)}, bf16[3,512,512]{2,1,0:T(8,128)(2,1)}, u32[]{:S(2)}, u32[]{:S(2)}) collective-permute-start(bf16[3,512,512]{2,1,0:T(8,128)(2,1)} %pad_maximum_fusion.4), channel_id=1, source_target_pairs={{0,4},{4,0},{8,12},{12,8},{1,5},{5,1},{9,13},{13,9},{2,6},{6,2},{1... | collective-permute-start | bytes 4718600 | tf_op jit(solution)/shard_map/ppermute | solution.py:857
  157.6 264.7 %collective-permute-start.2 = (bf16[3,512,512]{2,1,0:T(8,128)(2,1)}, bf16[3,512,512]{2,1,0:T(8,128)(2,1)}, u32[]{:S(2)}, u32[]{:S(2)}) collective-permute-start(bf16[3,512,512]{2,1,0:T(8,128)(2,1)} %pad_maximum_fusion.5), channel_id=1, source_target_pairs={{0,8},{4,12},{8,0},{12,4},{1,9},{5,13},{9,1},{13,5},{2,10},{6,14},... | collective-permute-start | bytes 4718600 | tf_op jit(solution)/shard_map/ppermute | solution.py:857
  315.0 44.1 %copy-start.25 = (bf16[768,512]{1,0:T(8,128)(2,1)S(1)}, bf16[768,512]{1,0:T(8,128)(2,1)}, u32[]{:S(2)}) copy-start(bf16[768,512]{1,0:T(8,128)(2,1)} %x_ref.1) | copy-start | bytes 2359300
  315.0 44.1 %copy-start.45 = (f32[512]{0:T(512)S(1)}, f32[512]{0:T(512)}, u32[]{:S(2)}) copy-start(f32[512]{0:T(512)} %param.25) | copy-start | bytes 6148
  352.5 7.8 copy-start.2
  359.1 58.5 %copy-start.42 = (f32[768]{0:T(1024)}, f32[768]{0:T(1024)S(1)}, u32[]{:S(2)}) copy-start(f32[768]{0:T(1024)S(1)} %rsqrt_bitcast_fusion.1) | copy-start | bytes 9220
  360.3 57.3 %copy-start.44 = (f32[6,128]{1,0:T(8,128)S(1)}, f32[6,128]{1,0:T(8,128)}, u32[]{:S(2)}) copy-start(f32[6,128]{1,0:T(8,128)} %total_branch.1) | copy-start | bytes 9220
  442.6 16.7 %copy-start.34 = (bf16[512,2048]{1,0:T(8,128)(2,1)S(1)}, bf16[512,2048]{1,0:T(8,128)(2,1)}, u32[]{:S(2)}) copy-start(bf16[512,2048]{1,0:T(8,128)(2,1)} %get-tuple-element.128) | copy-start | bytes 6291460
  471.1 64.2 %copy-start.18 = (bf16[768,512]{1,0:T(8,128)(2,1)S(1)}, bf16[768,512]{1,0:T(8,128)(2,1)}, u32[]{:S(2)}) copy-start(bf16[768,512]{1,0:T(8,128)(2,1)} %param.27) | copy-start | bytes 2359300
  471.1 64.2 %copy-start.47 = (f32[512]{0:T(512)S(1)}, f32[512]{0:T(512)}, u32[]{:S(2)}) copy-start(f32[512]{0:T(512)} %param.26) | copy-start | bytes 6148
  601.6 10.8 copy-start.35
  612.4 57.6 %copy-start.9 = (bf16[512,2048]{1,0:T(8,128)(2,1)}, bf16[512,2048]{1,0:T(8,128)(2,1)S(1)}, u32[]{:S(2)}) copy-start(bf16[512,2048]{1,0:T(8,128)(2,1)S(1)} %multiply_convert_fusion.5.refs_0_) | copy-start | bytes 6291460
  670.0 71.5 %copy-start.3 = (f32[768,512]{1,0:T(8,128)S(1)}, f32[768,512]{1,0:T(8,128)}, u32[]{:S(2)}) copy-start(f32[768,512]{1,0:T(8,128)} %copy-done.2) | copy-start | bytes 4718596
  670.0 71.5 %copy-start.19 = (bf16[768,512]{1,0:T(8,128)(2,1)S(1)}, bf16[768,512]{1,0:T(8,128)(2,1)}, u32[]{:S(2)}) copy-start(bf16[768,512]{1,0:T(8,128)(2,1)} %param.27) | copy-start | bytes 2359300
  670.0 71.5 %copy-start.26 = (bf16[768,512]{1,0:T(8,128)(2,1)S(1)}, bf16[768,512]{1,0:T(8,128)(2,1)}, u32[]{:S(2)}) copy-start(bf16[768,512]{1,0:T(8,128)(2,1)} %x_ref.1) | copy-start | bytes 2359300
  670.0 71.5 %copy-start.43 = (f32[768]{0:T(1024)S(1)}, f32[768]{0:T(1024)}, u32[]{:S(2)}) copy-start(f32[768]{0:T(1024)} %copy-done.42) | copy-start | bytes 9220
  670.0 71.5 %copy-start.46 = (f32[512]{0:T(512)S(1)}, f32[512]{0:T(512)}, u32[]{:S(2)}) copy-start(f32[512]{0:T(512)} %param.25) | copy-start | bytes 6148
  744.6 8.6 copy-start.49
  744.6 8.6 copy-start.5
  752.9 145.3 %collective-permute-start.4 = (bf16[1024,1024]{1,0:T(8,128)(2,1)}, bf16[1024,1024]{1,0:T(8,128)(2,1)}, u32[]{:S(2)}, u32[]{:S(2)}) collective-permute-start(bf16[1024,1024]{1,0:T(8,128)(2,1)} %constant_dynamic-slice_fusion.2), channel_id=1, source_target_pairs={{0,8},{4,12},{8,0},{12,4},{1,9},{5,13},{9,1},{13,5},{2,10},{6,14},... | collective-permute-start | bytes 6291464 | tf_op jit(solution)/shard_map/ppermute | solution.py:857
  786.4 77.0 %copy-start.15 = (bf16[512,1024]{1,0:T(8,128)(2,1)S(1)}, bf16[512,1024]{1,0:T(8,128)(2,1)}, u32[]{:S(2)}) copy-start(bf16[512,1024]{1,0:T(8,128)(2,1)} %copy-done.14) | copy-start | bytes 3145732
  866.1 32.1 %collective-permute-start.5 = (bf16[512,512]{1,0:T(8,128)(2,1)S(1)}, bf16[512,512]{1,0:T(8,128)(2,1)S(1)}, u32[]{:S(2)}, u32[]{:S(2)}) collective-permute-start(bf16[512,512]{1,0:T(8,128)(2,1)S(1)} %constant_dynamic-slice_fusion.1), channel_id=1, source_target_pairs={{0,4},{4,0},{8,12},{12,8},{1,5},{5,1},{9,13},{13,9},{2,6},{6,2},{1... | collective-permute-start | bytes 1572872 | tf_op jit(solution)/shard_map/ppermute | solution.py:857
  898.2 10.3 slice-start
  901.5 6.9 slice-start.1
  903.7 86.2 %collective-permute-start.7 = (bf16[2,512,512]{2,1,0:T(8,128)(2,1)}, bf16[2,512,512]{2,1,0:T(8,128)(2,1)}, u32[]{:S(2)}, u32[]{:S(2)}) collective-permute-start(bf16[2,512,512]{2,1,0:T(8,128)(2,1)} %pad_maximum_fusion.6), channel_id=1, source_target_pairs={{0,16},{16,0},{1,17},{17,1},{2,18},{18,2},{3,19},{19,3},{4,20},{20... | collective-permute-start | bytes 3145736 | tf_op jit(solution)/shard_map/ppermute | solution.py:966
  906.5 4.3 copy-start.13
  906.5 4.3 copy-start.17
  906.5 83.4 %collective-permute-start.6 = (bf16[512,1024]{1,0:T(8,128)(2,1)}, bf16[512,1024]{1,0:T(8,128)(2,1)}, u32[]{:S(2)}, u32[]{:S(2)}) collective-permute-start(bf16[512,1024]{1,0:T(8,128)(2,1)} %get-tuple-element.110), channel_id=1, source_target_pairs={{0,4},{4,0},{8,12},{12,8},{1,5},{5,1},{9,13},{13,9},{2,6},{6,2},{1... | collective-permute-start | bytes 3145736 | tf_op jit(solution)/shard_map/ppermute | solution.py:857
  910.7 202.3 %reduce-scatter.3.cloned.1.call-start = ((), (), s32[]{:S(2)}) async-start(), calls=%async_computation.4 | async-start | bytes 3932160 | tf_op jit(solution)/shard_map/reduce_scatter | solution.py:979
  914.3 84.8 %slice-start.2 = ((s8[6291456]{0:T(1024)(128)(4,1)}), s8[4194304]{0:T(1024)(128)(4,1)S(1)}, s32[]{:S(2)}) async-start(s8[6291456]{0:T(1024)(128)(4,1)} %bitcast.127), calls=%async_computation.8 | async-start | bytes 8388608
  989.9 9.2 slice-start.3
  1005.6 56.4 %copy-start.40 = (bf16[256,512]{1,0:T(8,128)(2,1)S(1)}, bf16[256,512]{1,0:T(8,128)(2,1)}, u32[]{:S(2)}) copy-start(bf16[256,512]{1,0:T(8,128)(2,1)} %reduce-scatter.5.cloned.1.call-done) | copy-start | bytes 786436
  1005.6 56.4 %collective-permute-start.9 = (bf16[256,512]{1,0:T(8,128)(2,1)}, bf16[256,512]{1,0:T(8,128)(2,1)S(1)}, u32[]{:S(2)}, u32[]{:S(2)}) collective-permute-start(bf16[256,512]{1,0:T(8,128)(2,1)} %reduce-scatter.5.cloned.1.call-done), channel_id=1, source_target_pairs={{0,16},{16,0},{1,17},{17,1},{2,18},{18,2},{3,19},{19,3},{4,20},{20... | collective-permute-start | bytes 786440 | tf_op jit(solution)/shard_map/ppermute | solution.py:1043
  1009.5 100.1 %collective-permute-start.10 = (bf16[2,512,1024]{2,1,0:T(8,128)(2,1)}, bf16[2,512,1024]{2,1,0:T(8,128)(2,1)}, u32[]{:S(2)}, u32[]{:S(2)}) collective-permute-start(bf16[2,512,1024]{2,1,0:T(8,128)(2,1)} %pad_maximum_fusion.3), channel_id=1, source_target_pairs={{0,16},{16,0},{1,17},{17,1},{2,18},{18,2},{3,19},{19,3},{4,20},{20... | collective-permute-start | bytes 6291464 | tf_op jit(solution)/shard_map/ppermute | solution.py:966
  1113.0 19.3 %collective-permute-start.8 = (bf16[512,768]{0,1:T(8,128)(2,1)}, bf16[512,768]{0,1:T(8,128)(2,1)S(1)}, u32[]{:S(2)}, u32[]{:S(2)}) collective-permute-start(bf16[512,768]{0,1:T(8,128)(2,1)} %reduce-scatter.3.cloned.1.call-done), channel_id=1, source_target_pairs={{0,16},{16,0},{1,17},{17,1},{2,18},{18,2},{3,19},{19,3},{4,20},{20... | collective-permute-start | bytes 2359304 | tf_op jit(solution)/shard_map/ppermute | solution.py:1037
  1117.9 14.4 %copy-start.36 = (bf16[512,768]{0,1:T(8,128)(2,1)S(1)}, bf16[512,768]{0,1:T(8,128)(2,1)}, u32[]{:S(2)}) copy-start(bf16[512,768]{0,1:T(8,128)(2,1)} %reduce-scatter.3.cloned.1.call-done) | copy-start | bytes 2359300
  (24 other events, 57.0 us)
Sparse Core Ops, SparseCore 0:
  10.4 66.1 all-gather.2
  78.7 50.4 all-gather.4
  910.8 43.8 reduce-scatter.4
  1005.7 60.5 reduce-scatter.2

commit v4 on v3

--- a/solution.py
+++ b/solution.py
@@ -843,40 +843,13 @@
     slots = tok_rows * row_count
     half_feat = feat_part // 2
     y, z = side("dp"), lax.axis_index("row")
-    p = z & 1
     heads = half_feat // HEAD_DIM
-    hid = w_gate.shape[1] // 4
     pairs = [(i, i ^ 1) for i in range(data_count)]
     after = lambda values, *done: lax.optimization_barrier((values,) + done)[0]
 
     def y_half(values, axis):
         size = values.shape[axis] // 2
         return lax.dynamic_slice_in_dim(values, y * size, size, axis)
-
-    def row_swap(values, d):
-        return lax.ppermute(values, "row", [(i, i ^ d) for i in range(row_count)])
-
-    def hidden_parts(*done):
-        def quarters(d):
-            start = (y * 2 + (p ^ (d & 1))) * hid
-            return jnp.stack(
-                [
-                    lax.dynamic_slice_in_dim(w_gate, start, hid, 1),
-                    lax.dynamic_slice_in_dim(w_up, start, hid, 1),
-                    lax.dynamic_slice_in_dim(w_down, start, hid, 0),
-                ]
-            )
-
-        parts = [quarters(0)] + [row_swap(after(quarters(d), *done), d) for d in (1, 2, 3)]
-        depth = w_gate.shape[0]
-        gate_up = jnp.zeros((width, 2 * hid), bf16)
-        down = jnp.zeros((hid, width), bf16)
-        for d, part in enumerate(parts):
-            spot = (z ^ d) * depth
-            gate_up = lax.dynamic_update_slice(gate_up, part[0], (spot, 0))
-            gate_up = lax.dynamic_update_slice(gate_up, part[1], (spot, hid))
-            down = lax.dynamic_update_slice(down, part[2], (0, spot))
-        return gate_up, down
 
     qkv_weight = lax.all_gather(
         jnp.concatenate([y_half(w_query, 1), y_half(w_key, 1), y_half(w_value, 1)], axis=1),
@@ -884,7 +857,10 @@
         axis=0,
         tiled=True,
     )
-    out_weight = lax.all_gather(y_half(after(w_out, qkv_weight), 0), "row", axis=1, tiled=True)
+    out_weight = lax.all_gather(y_half(w_out, 0), "row", axis=1, tiled=True)
+    gate_weight = lax.all_gather(y_half(w_gate, 1), "row", axis=0, tiled=True)
+    up_weight = lax.all_gather(y_half(w_up, 1), "row", axis=0, tiled=True)
+    down_weight = lax.all_gather(y_half(w_down, 0), "row", axis=1, tiled=True)
 
     positions = z * tok_rows + jnp.arange(tok_rows)
     length = seq_lengths[0]
@@ -904,7 +880,6 @@
     qkv = matmul(tokens_wide, qkv_weight)
     units, inverse = front(qkv, cosine, sine_signed, qk_gain, width, 2 * heads, 2)
     q_unit, k_unit, v_unit = (units[:, i].reshape(slots, HEAD_DIM) for i in range(3))
-    gate_up_weight, down_weight = hidden_parts(units)
     attn_unit, attn_exact, log_total = attend(unit_length, q_unit, k_unit, v_unit)
     attn_low = turn(attn_unit, True, tok_rows, heads, 3, "turn_attn")
     branch = scatter_wide(matmul(attn_low, out_weight).astype(bf16), False, 4, "scatter_branch")
@@ -913,12 +888,12 @@
         + norm_eps
     )[:, None]
     resid = tokens.astype(f32) + branch * branch_inv * attn_gain
-    resid_wide = gather_wide(resid.astype(bf16), True, 6, "gather_resid")
-    gate = matmul(resid_wide, gate_up_weight[:, :hid])
-    upper = matmul(resid_wide, gate_up_weight[:, hid:])
+    resid_wide = gather_wide(resid.astype(bf16), False, 6, "gather_resid")
+    gate = matmul(resid_wide, gate_weight)
+    upper = matmul(resid_wide, up_weight)
     sigma = jax.nn.sigmoid(gate)
     hidden = (gate * sigma * upper).astype(bf16)
-    mixed = scatter_wide(matmul(hidden, down_weight).astype(bf16), True, 7, "scatter_mixed")
+    mixed = scatter_wide(matmul(hidden, down_weight).astype(bf16), False, 7, "scatter_mixed")
     incoming = cotangent.astype(f32) * valid
     gained = incoming * mlp_gain
     sums = feature_total(
@@ -931,7 +906,7 @@
     block_output = ((resid + mixed * mixed_inv * mlp_gain) * valid).astype(bf16)
     mlp_gain_raw = jnp.sum(incoming * mixed * mixed_inv, axis=0)
     d_mixed = (mixed_inv * gained - mixed * mixed_inv**3 * inner).astype(bf16)
-    d_mixed_wide = gather_wide(d_mixed, True, 9, "gather_d_mixed")
+    d_mixed_wide = gather_wide(d_mixed, False, 9, "gather_d_mixed")
 
     factor = 1.0 / math.sqrt(slots * data_count)
 
@@ -950,31 +925,6 @@
         high = jnp.where(bit == 0, other, piece)
         return jnp.concatenate([low, high], axis=axis)
 
-
-    def from_far(raw, axis):
-        return row_swap(cut(raw, 1 - (z >> 1), 2, axis), 2)
-
-    def with_far(raw, far, axis):
-        near = cut(raw, z >> 1, 2, axis)
-        return over_dp((near.astype(f32) + far.astype(f32)).astype(bf16))
-
-    def from_near(near, axis):
-        own, away = cut(near, p, 2, axis), row_swap(cut(near, 1 - p, 2, axis), 1)
-        return own, away
-
-    def from_twin(own, away):
-        return lax.ppermute(jnp.stack([own, away]), "dp", pairs)
-
-    def blocks(own, away, other, axis, count):
-        def block(i):
-            mine = two_sides(cut(own, i, count, 1 - axis), cut(away, i, count, 1 - axis), p, 1 - axis)
-            theirs = two_sides(
-                cut(other[0], i, count, 1 - axis), cut(other[1], i, count, 1 - axis), p, 1 - axis
-            )
-            return two_sides(mine, theirs, y, 1 - axis).astype(f32)
-
-        return [block(i) for i in range(count)]
-
     def reduce_rows(raw, axis):
         return lax.psum_scatter(raw, "row", scatter_dimension=axis, tiled=True)
 
@@ -982,15 +932,16 @@
     down_raw = (contract_first(hidden, d_mixed_wide) * factor).astype(bf16)
     d_gate = (d_hidden * upper * sigma * (1.0 + gate * (1.0 - sigma))).astype(bf16)
     d_upper = (d_hidden * gate * sigma).astype(bf16)
-    d_gate_up = jnp.concatenate([d_gate, d_upper], axis=1)
-    gate_up_raw = (contract_first(resid_wide, d_gate_up) * factor).astype(bf16)
-    d_resid_wide = contract_last(d_gate_up, gate_up_weight).astype(bf16)
-    d_resid_wide, down_raw, gate_up_raw = lax.optimization_barrier(
-        (d_resid_wide, down_raw, gate_up_raw)
-    )
-    d_resid, far_down = scatter_wide(d_resid_wide, True, 10, "scatter_d_resid", down_raw)
+    gate_raw = (contract_first(resid_wide, d_gate) * factor).astype(bf16)
+    up_raw = (contract_first(resid_wide, d_upper) * factor).astype(bf16)
+    d_resid_wide = (
+        contract_last(d_gate, gate_weight) + contract_last(d_upper, up_weight)
+    ).astype(bf16)
+    d_resid_wide = after(d_resid_wide, down_raw, gate_raw, up_raw)
+    down_piece = reduce_rows(down_raw, 1)
+    gate_piece, up_piece = reduce_rows(gate_raw, 0), reduce_rows(up_raw, 0)
+    d_resid = scatter_wide(d_resid_wide, False, 10, "scatter_d_resid")
     d_resid = incoming + d_resid
-    far_gate_up = from_far(gate_up_raw, 0)
     attn_gain_raw = jnp.sum(d_resid * branch * branch_inv, axis=0)
     gained = d_resid * attn_gain
     inner = (
@@ -998,29 +949,27 @@
         / width
     )
     d_branch = (branch_inv * gained - branch * branch_inv**3 * inner).astype(bf16)
-    d_branch_wide, far_down = lax.optimization_barrier(
-        (gather_wide(d_branch, False, 12, "gather_d_branch"), far_down)
-    )
-    own_down, away_down = from_near(with_far(down_raw, far_down, 1), 1)
+    d_branch_wide, down_piece = lax.optimization_barrier(
+        (gather_wide(d_branch, False, 12, "gather_d_branch"), down_piece)
+    )
     d_attn = contract_last(d_branch_wide, out_weight).astype(bf16)
     d_attn_unit = turn(d_attn, False, tok_rows, heads, 13, "turn_d_attn")
     out_raw = (contract_first(attn_low, after(d_branch_wide, d_attn_unit)) * factor).astype(bf16)
-    d_attn_unit, out_raw = lax.optimization_barrier((d_attn_unit, out_raw))
+    d_attn_unit = after(d_attn_unit, out_raw)
     out_piece = reduce_rows(out_raw, 1)
     d_units = attend_back(unit_length, q_unit, k_unit, v_unit, d_attn_unit, attn_exact, log_total)
-    d_units, far_gate_up, away_down = lax.optimization_barrier((d_units, far_gate_up, away_down))
-    own_gate_up, away_gate_up = from_near(with_far(gate_up_raw, far_gate_up, 0), 0)
-    other_down = from_twin(own_down, away_down)
+    d_units, gate_piece = lax.optimization_barrier((d_units, gate_piece))
     d_qkv, gain_sums = rear(
         d_units, qkv[:, : 2 * half_feat], cosine, sine_signed, qk_gain, inverse, width, 14
     )
-    d_qkv, away_gate_up, other_down = lax.optimization_barrier((d_qkv, away_gate_up, other_down))
-    other_gate_up = from_twin(own_gate_up, away_gate_up)
     qkv_raw = (contract_first(tokens_wide, d_qkv) * factor).astype(bf16)
     projected = contract_last(d_qkv, qkv_weight).astype(bf16)
     projected, qkv_raw = lax.optimization_barrier((projected, qkv_raw))
     qkv_piece = over_dp(reduce_rows(qkv_raw, 0))
-    input_grad = d_resid + scatter_wide(projected, False, 16, "scatter_projected")
+    scattered, up_piece, out_piece = lax.optimization_barrier(
+        (scatter_wide(projected, False, 16, "scatter_projected"), up_piece, out_piece)
+    )
+    input_grad = d_resid + scattered
 
     def spread(half):
         return lax.dynamic_update_slice_in_dim(jnp.zeros((feat_part,), f32), half, y * half_feat, 0)
@@ -1032,25 +981,25 @@
             15,
         )
     )
-    (down_grad,) = blocks(own_down, away_down, other_down, 1, 1)
-    gate_grad, up_grad = blocks(own_gate_up, away_gate_up, other_gate_up, 0, 2)
+    def whole(piece, axis):
+        piece = over_dp(piece)
+        return two_sides(piece, lax.ppermute(piece, "dp", pairs), y, axis).astype(f32)
+
     qkv_other = lax.ppermute(qkv_piece, "dp", pairs)
     q_grad, k_grad, v_grad = (
         two_sides(cut(qkv_piece, i, 3, 1), cut(qkv_other, i, 3, 1), y, 1).astype(f32)
         for i in range(3)
     )
-    out_piece = over_dp(out_piece)
-    out_grad = two_sides(out_piece, lax.ppermute(out_piece, "dp", pairs), y, 0).astype(f32)
     return (
         block_output,
         input_grad,
         q_grad,
         k_grad,
         v_grad,
-        out_grad,
-        gate_grad,
-        up_grad,
-        down_grad,
+        whole(out_piece, 0),
+        whole(gate_piece, 1),
+        whole(up_piece, 1),
+        whole(down_piece, 0),
         gains[0],
         gains[1],
         gains[2],

time: 1150 us -> 1000 us (0.87)
  Pallas kernels: 841 us -> 640 us
  waiting for transfers between devices: 33.4 us -> 108 us
  local copies, waits for them, and re-layouts: 44.9 us -> 27 us
    pallas_call x2, Pallas kernels: 198 us -> 68.3 us  [turn(): pl.pallas_call(functools.partial(turn_kernel, back, tok, heads), name=nam...]
    pallas_call x4, Pallas kernels: 210 us -> 149 us  [scatter_wide(): pl.pallas_call(functools.partial(scatter_kernel, pair, rider), name=name,...]
    pallas_call x4, Pallas kernels: 178 us -> 127 us  [gather_wide(): pl.pallas_call(functools.partial(gather_kernel, pair), name=name, out_sha...]
    all_gather x1 -> x4, waiting for transfers between devices: 0.02 us -> 50.6 us  [the longest x1 50.5 us: per_device(): down_weight = lax.all_gather(y_half(w_down, 0), 'row', axis=1, tiled=True)]
    pallas_call x1, Pallas kernels: 69.5 us -> 105 us  [front(): pl.pallas_call(functools.partial(front_kernel, width), name='front', out_...]
    ppermute x9 -> x4, waiting for transfers between devices: 0.02 us -> 22.9 us  [whole(): lax.ppermute(piece, 'dp', pairs)]
    dynamic_update_slice x7 -> x0, local copies, waits for them, and re-layouts: 12.6 us -> none  [the longest x4 7.01 us: hidden_parts(): down = lax.dynamic_update_slice(down, part[2], (0, spot))]
    dot_general x4 -> x5, matrix products: 41.5 us -> 46.2 us  [contract_first(): lax.dot_general(left, right, (((0,), (0,)), ((), ())), preferred_element_...]
  transfers between devices with their start and end apart: 15 -> 16, of which waited for: 2 -> 4; matrix products, arithmetic and copies ran while one was open for 8% -> 17% of each run, Pallas kernels for 56% -> 57%
where the time goes in v4:
time: 1000 us; the launch traced here: 990 us
  Pallas kernels  640 us (64%)
  matrix products  153 us (15%)
  waiting for transfers between devices  108 us (11%)
  other arithmetic  38 us (4%)
  local copies, waits for them, and re-layouts  27 us (3%)
  between operations  15.9 us (2%)
    pallas_call x4, Pallas kernels, scatter_wide(): pl.pallas_call(functools.partial(scatter_kernel, pair, rider), name=name,...  149 us
    pallas_call x4, Pallas kernels, gather_wide(): pl.pallas_call(functools.partial(gather_kernel, pair), name=name, out_sha...  127 us
    pallas_call x1, Pallas kernels, front(): pl.pallas_call(functools.partial(front_kernel, width), name='front', out_...  105 us
    pallas_call x1, Pallas kernels, rear(): pl.pallas_call(functools.partial(rear_kernel, width), name='rear', out_sh...  80.8 us
    pallas_call x2, Pallas kernels, turn(): pl.pallas_call(functools.partial(turn_kernel, back, tok, heads), name=nam...  68.3 us
    dot_general x5, matrix products, contract_last(): lax.dot_general(left, right, (((1,), (1,)), ((), ())), preferred_element_...  55.5 us
    dot_general x5, matrix products, matmul(): return jnp.dot(left, right, preferred_element_type=f32)  51.1 us
    all_gather x1, waiting for transfers between devices, per_device(): down_weight = lax.all_gather(y_half(w_down, 0), 'row', axis=1, tiled=True)  50.5 us
  transfers between devices with their start and end apart: 16, of which 4 were waited for; matrix products, arithmetic and copies ran while one was open for 17% of the time, Pallas kernels for 57%

profile of v4, /device:TPU:0, one launch (start us, length us, event | category | flops | bytes accessed | tf_op | source)
XLA Modules:
  0.0 990.2 jit_solution(3545925348380277844)
XLA Ops:
  12.5 2.4 constant_dynamic-slice_fusion.1
  15.0 3.1 collective-permute-start
  20.0 31.4 %gather_tokens.1 = bf16[1536,2048]{1,0:T(8,128)(2,1)} custom-call(bf16[768,512]{1,0:T(8,128)(2,1)} %x_ref.1), custom_call_target="tpu_custom_call" | custom-call | bytes 1000 | tf_op jit(solution)/shard_map/gather_tokens/pallas_call | solution.py:155
  54.6 22.2 %all-gather.6.cloned.1.call-done = bf16[2048,768]{1,0:T(8,128)(2,1)} async-done(((bf16[512,768]{1,0:T(8,128)(2,1)}), bf16[2048,768]{1,0:T(8,128)(2,1)}) %all-gather.6.cloned.1.call-update) | async-done | bytes 3145744 | tf_op jit(solution)/shard_map/all_gather | solution.py:854
  76.8 8.1 convolution_bitcast_fusion.qkv_ref
  84.9 2.1 copy-done.4
  87.0 105.0 %front.1 = (bf16[4,3,768,128]{3,2,1,0:T(8,128)(2,1)S(1)}, f32[2,1536]{1,0:T(2,128)S(1)}) custom-call(f32[1536,768]{1,0:T(8,128)S(1)} %convolution_bitcast_fusion.qkv_ref, f32[768,128]{1,0:T(8,128)S(1)} %get-tuple-element.90.cos_ref, f32[768,128]{1,0:T(8,128)S(1)} %get-tuple-element.89.sin_ref, f32[2,256]{1,0:T(2,128)S(1)} %pad_maximum_fusion.3.gain_ref), custom_call_target="tpu_custom_call" | custom-call | bytes 1000 | tf_op jit(solution)/shard_map/front/pallas_call | solution.py:558
  193.4 20.5 %attend.1 = (bf16[3072,128]{1,0:T(8,128)(2,1)}, f32[3072,128]{1,0:T(8,128)}, f32[8,3072]{1,0:T(8,128)}) custom-call(s32[1]{0:T(128)} %dynamic_slice.48.len_ref, bf16[3072,128]{1,0:T(8,128)(2,1)} %bitcast.69, bf16[3072,128]{1,0:T(8,128)(2,1)} %bitcast.67, bf16[3072,128]{1,0:T(8,128)(2,1)} %bitcast.65), custom_call_target="tpu_custom_call" | custom-call | bytes 1000 | tf_op jit(solution)/shard_map/attend/pallas_call | solution.py:738
  213.9 27.0 %turn_attn.1 = bf16[1536,256]{1,0:T(8,128)(2,1)} custom-call(bf16[3072,128]{1,0:T(8,128)(2,1)} %get-tuple-element.33.x_ref), custom_call_target="tpu_custom_call" | custom-call | bytes 1000 | tf_op jit(solution)/shard_map/turn_attn/pallas_call | solution.py:459
  241.0 6.0 convolution_convert_fusion.1.p_ref
  247.0 38.0 %scatter_branch.1 = f32[768,512]{1,0:T(8,128)S(1)} custom-call(bf16[1536,2048]{1,0:T(8,128)(2,1)} %convolution_convert_fusion.1.p_ref), custom_call_target="tpu_custom_call" | custom-call | bytes 1000 | tf_op jit(solution)/shard_map/scatter_branch/pallas_call | solution.py:305
  285.8 4.9 total_branch.1
  292.7 31.9 %gather_resid.1 = bf16[1536,2048]{1,0:T(8,128)(2,1)} custom-call(bf16[768,512]{1,0:T(8,128)(2,1)} %fusion.4.x_ref), custom_call_target="tpu_custom_call" | custom-call | bytes 1000 | tf_op jit(solution)/shard_map/gather_resid/pallas_call | solution.py:155
  324.6 12.4 %fusion.11 = f32[1536,1024]{1,0:T(8,128)} fusion(bf16[1536,2048]{1,0:T(8,128)(2,1)} %gather_resid.1, bf16[2048,1024]{1,0:T(8,128)(2,1)} %all-gather.10.cloned.1.call-done), kind=kOutput, calls=%fused_computation.88 | convolution fusion | flops 6442450944 | bytes 16777216 | tf_op jit(solution)/shard_map/dot_general | solution.py:31
  337.0 13.4 %multiply_convert_fusion.6 = (bf16[1536,1024]{1,0:T(8,128)(2,1)}, f32[1536,1024]{1,0:T(8,128)}) fusion(f32[1536,1024]{1,0:T(8,128)} %fusion.11, bf16[1536,2048]{1,0:T(8,128)(2,1)} %gather_resid.1, bf16[2048,1024]{1,0:T(8,128)(2,1)} %all-gather.12.cloned.1.call-done), kind=kOutput, calls=%fused_computation.10 | convolution fusion | flops 6451888128 | bytes 26214400 | tf_op jit(solution)/shard_map/dot_general | solution.py:31
  350.4 50.5 %all-gather.14.cloned.1.call-done = bf16[1024,2048]{1,0:T(8,128)(2,1)} async-done(((bf16[1024,512]{1,0:T(8,128)(2,1)}), bf16[1024,2048]{1,0:T(8,128)(2,1)}) %all-gather.14.cloned.1.call-update) | async-done | bytes 4194320 | tf_op jit(solution)/shard_map/all_gather | solution.py:863
  400.9 11.2 %convolution_convert_fusion.2.p_ref = bf16[1536,2048]{1,0:T(8,128)(2,1)} fusion(bf16[1536,1024]{1,0:T(8,128)(2,1)} %get-tuple-element.97, bf16[1024,2048]{1,0:T(8,128)(2,1)} %all-gather.14.cloned.1.call-done), kind=kOutput, calls=%fused_computation.6 | convolution fusion | flops 6445596672 | bytes 13631488 | tf_op jit(solution)/shard_map/dot_general | solution.py:31
  412.1 37.6 %scatter_mixed.1 = f32[768,512]{1,0:T(8,128)S(1)} custom-call(bf16[1536,2048]{1,0:T(8,128)(2,1)} %convolution_convert_fusion.2.p_ref), custom_call_target="tpu_custom_call" | custom-call | bytes 1000 | tf_op jit(solution)/shard_map/scatter_mixed/pallas_call | solution.py:305
  450.9 5.0 total_mixed.1
  457.4 2.5 subtract_convert_fusion.1.x_ref
  459.9 31.7 %gather_d_mixed.1 = bf16[1536,2048]{1,0:T(8,128)(2,1)} custom-call(bf16[768,512]{1,0:T(8,128)(2,1)} %subtract_convert_fusion.1.x_ref), custom_call_target="tpu_custom_call" | custom-call | bytes 1000 | tf_op jit(solution)/shard_map/gather_d_mixed/pallas_call | solution.py:155
  491.6 11.6 %multiply_convert_fusion.2 = bf16[1024,2048]{1,0:T(8,128)(2,1)} fusion(bf16[1536,1024]{1,0:T(8,128)(2,1)} %get-tuple-element.97, bf16[1536,2048]{1,0:T(8,128)(2,1)} %gather_d_mixed.1), kind=kOutput, calls=%fused_computation.3 | convolution fusion | flops 6446645248 | bytes 13631488 | tf_op jit(solution)/shard_map/dot_general | solution.py:35
  503.3 17.2 %multiply_convert_fusion.4 = (bf16[1536,1024]{1,0:T(8,128)(2,1)}, bf16[1536,1024]{1,0:T(8,128)(2,1)S(1)}) fusion(f32[1536,1024]{1,0:T(8,128)} %fusion.11, f32[1536,1024]{1,0:T(8,128)} %get-tuple-element.98, bf16[1536,2048]{1,0:T(8,128)(2,1)} %gather_d_mixed.1, bf16[1024,2048]{1,0:T(8,128)(2,1)} %all-gather.14.cloned.1.call-done), kind=kOutput, calls=%fused_computation.8 | convolution fusion | flops 6462898176 | bytes 29360128 | tf_op jit(solution)/shard_map/dot_general | solution.py:39
  522.2 11.1 %multiply_convert_fusion.1 = bf16[2048,1024]{1,0:T(8,128)(2,1)} fusion(bf16[1536,2048]{1,0:T(8,128)(2,1)} %gather_resid.1, bf16[1536,1024]{1,0:T(8,128)(2,1)S(1)} %get-tuple-element.70), kind=kOutput, calls=%fused_computation.2 | convolution fusion | flops 6446645248 | bytes 13631488 | tf_op jit(solution)/shard_map/dot_general | solution.py:35
  533.4 11.4 %multiply_convert_fusion = bf16[2048,1024]{1,0:T(8,128)(2,1)} fusion(bf16[1536,2048]{1,0:T(8,128)(2,1)} %gather_resid.1, bf16[1536,1024]{1,0:T(8,128)(2,1)} %get-tuple-element.69), kind=kOutput, calls=%fused_computation.1 | convolution fusion | flops 6446645248 | bytes 13631488 | tf_op jit(solution)/shard_map/dot_general | solution.py:35
  544.8 4.0 slice.54.qkv_ref
  548.9 11.7 %fusion.12 = f32[1536,2048]{1,0:T(8,128)} fusion(bf16[1536,1024]{1,0:T(8,128)(2,1)} %copy-done.33, bf16[2048,1024]{1,0:T(8,128)(2,1)S(1)} %copy-done.31), kind=kOutput, calls=%fused_computation.89 | convolution fusion | flops 6442450944 | bytes 19922944 | tf_op jit(solution)/shard_map/dot_general | solution.py:39
  560.6 11.6 %add_convert_fusion.p_ref = bf16[1536,2048]{1,0:T(8,128)(2,1)} fusion(f32[1536,2048]{1,0:T(8,128)} %fusion.12, bf16[1536,1024]{1,0:T(8,128)(2,1)S(1)} %copy-done.34, bf16[2048,1024]{1,0:T(8,128)(2,1)S(1)} %copy-done.32), kind=kOutput, calls=%fused_computation | convolution fusion | flops 6448742400 | bytes 26214400 | tf_op jit(solution)/shard_map/dot_general | solution.py:39
  572.2 37.3 %scatter_d_resid.1 = f32[768,512]{1,0:T(8,128)S(1)} custom-call(bf16[1536,2048]{1,0:T(8,128)(2,1)} %add_convert_fusion.p_ref), custom_call_target="tpu_custom_call" | custom-call | bytes 1000 | tf_op jit(solution)/shard_map/scatter_d_resid/pallas_call | solution.py:305
  609.5 3.1 multiply_reduce_fusion.1
  612.7 4.9 total_d_resid.1
  618.3 2.5 subtract_convert_fusion.x_ref
  620.8 31.9 %gather_d_branch.1 = bf16[1536,2048]{1,0:T(8,128)(2,1)} custom-call(bf16[768,512]{1,0:T(8,128)(2,1)} %subtract_convert_fusion.x_ref), custom_call_target="tpu_custom_call" | custom-call | bytes 1000 | tf_op jit(solution)/shard_map/gather_d_branch/pallas_call | solution.py:155
  652.8 5.8 convolution_convert_fusion.3.x_ref
  658.6 41.3 %turn_d_attn.1.do_ref = bf16[3072,128]{1,0:T(8,128)(2,1)} custom-call(bf16[1536,256]{1,0:T(8,128)(2,1)} %convolution_convert_fusion.3.x_ref), custom_call_target="tpu_custom_call" | custom-call | bytes 1000 | tf_op jit(solution)/shard_map/turn_d_attn/pallas_call | solution.py:459
  699.9 5.6 fusion.1
  705.5 27.5 %attend_back.1.d_ref = bf16[3,3072,128]{2,1,0:T(8,128)(2,1)} custom-call(s32[1]{0:T(128)} %dynamic_slice.48.len_ref, bf16[3072,128]{1,0:T(8,128)(2,1)} %bitcast.70, bf16[3072,128]{1,0:T(8,128)(2,1)} %bitcast.68, bf16[3072,128]{1,0:T(8,128)(2,1)} %bitcast.66, bf16[3072,128]{1,0:T(8,128)(2,1)} %turn_d_attn.1.do_ref, f32[3072,128]{1,0:T(8,128)} %get-tuple-element.38.o_ref, ...), custom_call_target="tpu_custom_call" | custom-call | bytes 1000 | tf_op jit(solution)/shard_map/attend_back/pallas_call | solution.py:812
  736.7 80.8 %rear.1 = (bf16[1536,768]{1,0:T(8,128)(2,1)S(1)}, f32[2,256]{1,0:T(2,128)S(1)}) custom-call(bf16[3,3072,128]{2,1,0:T(8,128)(2,1)S(1)} %copy-done.6, f32[1536,512]{1,0:T(8,128)S(1)} %copy-done.5, f32[768,128]{1,0:T(8,128)S(1)} %copy-done.10, f32[768,128]{1,0:T(8,128)S(1)} %copy-done.8, f32[2,256]{1,0:T(2,128)S(1)} %copy-done.12, ...), custom_call_target="tpu_custom_call" | custom-call | bytes 1000 | tf_op jit(solution)/shard_map/rear/pallas_call | solution.py:667
  817.5 9.2 convolution_convert_fusion.p_ref
  826.8 6.6 fusion
  836.1 46.4 %total_gains.1 = f32[16,128]{1,0:T(8,128)} custom-call(f32[16,128]{1,0:T(8,128)} %mul.277.v_ref), custom_call_target="tpu_custom_call" | custom-call | tf_op jit(solution)/shard_map/total_gains/pallas_call | solution.py:408
  882.5 36.5 %scatter_projected.1 = f32[768,512]{1,0:T(8,128)S(1)} custom-call(bf16[1536,2048]{1,0:T(8,128)(2,1)} %convolution_convert_fusion.p_ref), custom_call_target="tpu_custom_call" | custom-call | bytes 1000 | tf_op jit(solution)/shard_map/scatter_projected/pallas_call | solution.py:305
  921.1 2.6 maximum_convert_fusion.2
  923.7 2.7 broadcast_select_fusion.5
  927.7 4.2 maximum_convert_fusion
  934.0 22.9 %collective-permute-done.2 = bf16[256,512]{1,0:T(8,128)(2,1)S(1)} collective-permute-done((bf16[256,512]{1,0:T(8,128)(2,1)S(1)}, bf16[256,512]{1,0:T(8,128)(2,1)S(1)}, u32[]{:S(2)}, u32[]{:S(2)}) %collective-permute-start.2) | collective-permute-done | bytes 262176 | tf_op jit(solution)/shard_map/ppermute | solution.py:986
  961.1 2.6 maximum_convert_fusion.1
  963.6 11.9 %collective-permute-done.1 = bf16[512,768]{0,1:T(8,128)(2,1)S(1)} collective-permute-done((bf16[512,768]{0,1:T(8,128)(2,1)}, bf16[512,768]{0,1:T(8,128)(2,1)S(1)}, u32[]{:S(2)}, u32[]{:S(2)}) %collective-permute-start.1) | collective-permute-done | bytes 786464 | tf_op jit(solution)/shard_map/ppermute | solution.py:988
  (160 shorter events, 42.3 us)
Async XLA Ops:
  7.2 4.1 copy-start
  7.2 3.3 copy-start.24
  7.2 69.6 %all-gather.6.cloned.1.call-start = ((), (), s32[]{:S(2)}) async-start(), calls=%async_computation.5 | async-start | bytes 3932160 | tf_op jit(solution)/shard_map/all_gather | solution.py:854
  10.5 230.5 %all-gather.8.cloned.1.call-start = ((), (), s32[]{:S(2)}) async-start(), calls=%async_computation.6 | async-start | bytes 1310720 | tf_op jit(solution)/shard_map/all_gather | solution.py:860
  11.3 313.3 %all-gather.10.cloned.1.call-start = ((), (), s32[]{:S(2)}) async-start(), calls=%async_computation.7 | async-start | bytes 5242880 | tf_op jit(solution)/shard_map/all_gather | solution.py:861
  12.4 5.6 copy-start.22
  12.4 7.4 copy-start.29
  12.4 7.5 copy-start.30
  12.5 324.5 %all-gather.12.cloned.1.call-start = ((), (), s32[]{:S(2)}) async-start(), calls=%async_computation.8 | async-start | bytes 5242880 | tf_op jit(solution)/shard_map/all_gather | solution.py:862
  14.9 386.0 %all-gather.14.cloned.1.call-start = ((), (), s32[]{:S(2)}) async-start(), calls=%async_computation.9 | async-start | bytes 5242880 | tf_op jit(solution)/shard_map/all_gather | solution.py:863
  15.0 38.3 %collective-permute-start = (s32[1]{0:T(128)}, s32[1]{0:T(128)}, u32[]{:S(2)}, u32[]{:S(2)}) collective-permute-start(s32[1]{0:T(128)} %param.15), channel_id=1, source_target_pairs={{0,16},{16,0},{1,17},{17,1},{2,18},{18,2},{3,19},{19,3},{4,20},{20... | collective-permute-start | bytes 20 | tf_op jit(solution)/shard_map/ppermute | solution.py:870
  19.1 633.7 %reduce-scatter.6.cloned.1.call-start = ((), (), s32[]{:S(2)}) async-start(), calls=%async_computation.10 | async-start | bytes 5242880 | tf_op jit(solution)/shard_map/reduce_scatter | solution.py:929
  51.4 33.4 %copy-start.11 = (f32[2,256]{1,0:T(2,128)}, f32[2,256]{1,0:T(2,128)S(1)}, u32[]{:S(2)}) copy-start(f32[2,256]{1,0:T(2,128)S(1)} %pad_maximum_fusion.3.gain_ref) | copy-start | bytes 6148
  53.2 31.6 %copy-start.7 = (f32[768,128]{1,0:T(8,128)}, f32[768,128]{1,0:T(8,128)S(1)}, u32[]{:S(2)}) copy-start(f32[768,128]{1,0:T(8,128)S(1)} %get-tuple-element.89.sin_ref) | copy-start | bytes 1179652
  53.2 31.6 %copy-start.9 = (f32[768,128]{1,0:T(8,128)}, f32[768,128]{1,0:T(8,128)S(1)}, u32[]{:S(2)}) copy-start(f32[768,128]{1,0:T(8,128)S(1)} %get-tuple-element.90.cos_ref) | copy-start | bytes 1179652
  247.0 44.5 %copy-start.17 = (bf16[768,512]{1,0:T(8,128)(2,1)S(1)}, bf16[768,512]{1,0:T(8,128)(2,1)}, u32[]{:S(2)}) copy-start(bf16[768,512]{1,0:T(8,128)(2,1)} %x_ref.1) | copy-start | bytes 2359300
  247.0 44.5 %copy-start.27 = (f32[512]{0:T(512)S(1)}, f32[512]{0:T(512)}, u32[]{:S(2)}) copy-start(f32[512]{0:T(512)} %param.25) | copy-start | bytes 6148
  412.1 37.6 %copy-start.13 = (bf16[768,512]{1,0:T(8,128)(2,1)S(1)}, bf16[768,512]{1,0:T(8,128)(2,1)}, u32[]{:S(2)}) copy-start(bf16[768,512]{1,0:T(8,128)(2,1)} %param.27) | copy-start | bytes 2359300
  412.1 37.6 %copy-start.28 = (f32[512]{0:T(512)S(1)}, f32[512]{0:T(512)}, u32[]{:S(2)}) copy-start(f32[512]{0:T(512)} %param.26) | copy-start | bytes 6148
  449.7 41.9 %copy-start.2 = (f32[768,512]{1,0:T(8,128)}, f32[768,512]{1,0:T(8,128)S(1)}, u32[]{:S(2)}) copy-start(f32[768,512]{1,0:T(8,128)S(1)} %scatter_mixed.1) | copy-start | bytes 4718596
  503.2 229.8 %reduce-scatter.8.cloned.1.call-start = ((), (), s32[]{:S(2)}) async-start(), calls=%async_computation.11 | async-start | bytes 5242880 | tf_op jit(solution)/shard_map/reduce_scatter | solution.py:929
  533.3 393.0 %reduce-scatter.10.cloned.1.call-start = ((), (), s32[]{:S(2)}) async-start(), calls=%async_computation.12 | async-start | bytes 5242880 | tf_op jit(solution)/shard_map/reduce_scatter | solution.py:929
  544.8 4.1 copy-start.25
  544.8 381.6 %reduce-scatter.12.cloned.1.call-start = ((), (), s32[]{:S(2)}) async-start(), calls=%async_computation.13 | async-start | bytes 1310720 | tf_op jit(solution)/shard_map/reduce_scatter | solution.py:929
  544.8 4.1 copy-start.31
  548.9 11.7 %copy-start.32 = (bf16[2048,1024]{1,0:T(8,128)(2,1)S(1)}, bf16[2048,1024]{1,0:T(8,128)(2,1)}, u32[]{:S(2)}) copy-start(bf16[2048,1024]{1,0:T(8,128)(2,1)} %all-gather.12.cloned.1.call-done) | copy-start | bytes 12582916
  548.9 11.7 %copy-start.34 = (bf16[1536,1024]{1,0:T(8,128)(2,1)S(1)}, bf16[1536,1024]{1,0:T(8,128)(2,1)}, u32[]{:S(2)}) copy-start(bf16[1536,1024]{1,0:T(8,128)(2,1)} %get-tuple-element.69) | copy-start | bytes 9437188
  572.2 37.3 %copy-start.3 = (f32[768,512]{1,0:T(8,128)S(1)}, f32[768,512]{1,0:T(8,128)}, u32[]{:S(2)}) copy-start(f32[768,512]{1,0:T(8,128)} %copy-done.2) | copy-start | bytes 4718596
  572.2 37.3 %copy-start.14 = (bf16[768,512]{1,0:T(8,128)(2,1)S(1)}, bf16[768,512]{1,0:T(8,128)(2,1)}, u32[]{:S(2)}) copy-start(bf16[768,512]{1,0:T(8,128)(2,1)} %param.27) | copy-start | bytes 2359300
  572.2 37.4 %copy-start.18 = (bf16[768,512]{1,0:T(8,128)(2,1)S(1)}, bf16[768,512]{1,0:T(8,128)(2,1)}, u32[]{:S(2)}) copy-start(bf16[768,512]{1,0:T(8,128)(2,1)} %x_ref.1) | copy-start | bytes 2359300
  652.7 47.2 %copy-start.16 = (bf16[1536,256]{1,0:T(8,128)(2,1)S(1)}, bf16[1536,256]{1,0:T(8,128)(2,1)}, u32[]{:S(2)}) copy-start(bf16[1536,256]{1,0:T(8,128)(2,1)} %turn_attn.1) | copy-start | bytes 2359300
  705.5 27.6 %copy-start.8 = (f32[768,128]{1,0:T(8,128)S(1)}, f32[768,128]{1,0:T(8,128)}, u32[]{:S(2)}) copy-start(f32[768,128]{1,0:T(8,128)} %copy-done.7) | copy-start | bytes 1179652
  705.5 27.6 %copy-start.10 = (f32[768,128]{1,0:T(8,128)S(1)}, f32[768,128]{1,0:T(8,128)}, u32[]{:S(2)}) copy-start(f32[768,128]{1,0:T(8,128)} %copy-done.9) | copy-start | bytes 1179652
  705.5 27.6 %copy-start.12 = (f32[2,256]{1,0:T(2,128)S(1)}, f32[2,256]{1,0:T(2,128)}, u32[]{:S(2)}) copy-start(f32[2,256]{1,0:T(2,128)} %copy-done.11) | copy-start | bytes 6148
  733.0 224.0 %reduce-scatter.14.cloned.1.call-start = ((), (), s32[]{:S(2)}) async-start(), calls=%async_computation.14 | async-start | bytes 3932160 | tf_op jit(solution)/shard_map/reduce_scatter | solution.py:929
  736.7 90.1 %slice-start = ((s8[6291456]{0:T(1024)(128)(4,1)}), s8[4194304]{0:T(1024)(128)(4,1)S(1)}, s32[]{:S(2)}) async-start(s8[6291456]{0:T(1024)(128)(4,1)} %bitcast.71), calls=%async_computation.15 | async-start | bytes 8388608
  817.5 9.3 slice-start.1
  833.4 86.3 %collective-permute-start.5 = (bf16[1024,512]{1,0:T(8,128)(2,1)}, bf16[1024,512]{1,0:T(8,128)(2,1)}, u32[]{:S(2)}, u32[]{:S(2)}) collective-permute-start(bf16[1024,512]{1,0:T(8,128)(2,1)} %reduce-scatter.6.cloned.1.call-done), channel_id=1, source_target_pairs={{0,16},{16,0},{1,17},{17,1},{2,18},{18,2},{3,19},{19,3},{4,20},{20... | collective-permute-start | bytes 3145736 | tf_op jit(solution)/shard_map/ppermute | solution.py:986
  834.6 89.1 %collective-permute-start.3 = (bf16[512,1024]{1,0:T(8,128)(2,1)}, bf16[512,1024]{1,0:T(8,128)(2,1)}, u32[]{:S(2)}, u32[]{:S(2)}) collective-permute-start(bf16[512,1024]{1,0:T(8,128)(2,1)} %reduce-scatter.8.cloned.1.call-done), channel_id=1, source_target_pairs={{0,16},{16,0},{1,17},{17,1},{2,18},{18,2},{3,19},{19,3},{4,20},{20... | collective-permute-start | bytes 3145736 | tf_op jit(solution)/shard_map/ppermute | solution.py:986
  882.5 36.6 %copy-start.26 = (f32[16,128]{1,0:T(8,128)S(1)}, f32[16,128]{1,0:T(8,128)}, u32[]{:S(2)}) copy-start(f32[16,128]{1,0:T(8,128)} %total_gains.1) | copy-start | bytes 24580
  882.5 37.2 %copy-start.19 = (bf16[1024,512]{1,0:T(8,128)(2,1)S(1)}, bf16[1024,512]{1,0:T(8,128)(2,1)}, u32[]{:S(2)}) copy-start(bf16[1024,512]{1,0:T(8,128)(2,1)} %reduce-scatter.6.cloned.1.call-done) | copy-start | bytes 3145732
  926.4 33.0 %collective-permute-start.4 = (bf16[512,1024]{1,0:T(8,128)(2,1)}, bf16[512,1024]{1,0:T(8,128)(2,1)}, u32[]{:S(2)}, u32[]{:S(2)}) collective-permute-start(bf16[512,1024]{1,0:T(8,128)(2,1)} %reduce-scatter.10.cloned.1.call-done), channel_id=1, source_target_pairs={{0,16},{16,0},{1,17},{17,1},{2,18},{18,2},{3,19},{19,3},{4,20},{20... | collective-permute-start | bytes 3145736 | tf_op jit(solution)/shard_map/ppermute | solution.py:986
  927.7 4.2 copy-start.23
  927.7 4.9 copy-start.15
  931.8 25.1 %collective-permute-start.2 = (bf16[256,512]{1,0:T(8,128)(2,1)S(1)}, bf16[256,512]{1,0:T(8,128)(2,1)S(1)}, u32[]{:S(2)}, u32[]{:S(2)}) collective-permute-start(bf16[256,512]{1,0:T(8,128)(2,1)S(1)} %copy-done.23), channel_id=1, source_target_pairs={{0,16},{16,0},{1,17},{17,1},{2,18},{18,2},{3,19},{19,3},{4,20},{20... | collective-permute-start | bytes 786440 | tf_op jit(solution)/shard_map/ppermute | solution.py:986
  957.0 18.5 %collective-permute-start.1 = (bf16[512,768]{0,1:T(8,128)(2,1)}, bf16[512,768]{0,1:T(8,128)(2,1)S(1)}, u32[]{:S(2)}, u32[]{:S(2)}) collective-permute-start(bf16[512,768]{0,1:T(8,128)(2,1)} %reduce-scatter.14.cloned.1.call-done), channel_id=1, source_target_pairs={{0,16},{16,0},{1,17},{17,1},{2,18},{18,2},{3,19},{19,3},{4,20},{20... | collective-permute-start | bytes 2359304 | tf_op jit(solution)/shard_map/ppermute | solution.py:988
  961.0 14.5 %copy-start.21 = (bf16[512,768]{0,1:T(8,128)(2,1)S(1)}, bf16[512,768]{0,1:T(8,128)(2,1)}, u32[]{:S(2)}) copy-start(bf16[512,768]{0,1:T(8,128)(2,1)} %reduce-scatter.14.cloned.1.call-done) | copy-start | bytes 2359300
  977.9 5.0 copy-start.1
  (5 other events, 10.0 us)
Sparse Core Ops, SparseCore 0:
  10.6 66.1 all-gather.5
  78.9 50.5 all-gather.7
  131.7 105.8 all-gather.9
  239.6 80.0 all-gather.11
  321.7 79.2 all-gather.13
  503.4 74.4 reduce-scatter.5
  580.7 77.2 reduce-scatter.7
  660.9 88.3 reduce-scatter.9
  752.2 61.0 reduce-scatter.11
  833.5 58.9 reduce-scatter.13

commit v5 on v4

--- a/solution.py
+++ b/solution.py
@@ -602,7 +602,7 @@
     recv_sem,
 ):
     count, tok = qkv_ref.shape[0], cos_ref.shape[0]
-    part = qkv_ref.shape[1] // 2
+    part = qkv_ref.shape[1] // 3
     heads = part // HEAD_DIM
     z = lax.axis_index("row")
     me = side("dp") * 4 + lax.axis_index("col")
@@ -662,7 +662,7 @@
 
 def rear(d_units, qkv, cosine, sine_signed, gains, inverse, width, number):
     count, tok = qkv.shape[0], cosine.shape[0]
-    part = qkv.shape[1] // 2
+    part = qkv.shape[1] // 3
     units = d_units.shape[1] // tok
     return pl.pallas_call(
         functools.partial(rear_kernel, width),
@@ -925,6 +925,9 @@
         high = jnp.where(bit == 0, other, piece)
         return jnp.concatenate([low, high], axis=axis)
 
+    def from_twin(piece):
+        return lax.ppermute(piece, "dp", pairs)
+
     def reduce_rows(raw, axis):
         return lax.psum_scatter(raw, "row", scatter_dimension=axis, tiled=True)
 
@@ -949,28 +952,27 @@
         / width
     )
     d_branch = (branch_inv * gained - branch * branch_inv**3 * inner).astype(bf16)
+    down_piece = over_dp(down_piece)
     d_branch_wide, down_piece = lax.optimization_barrier(
         (gather_wide(d_branch, False, 12, "gather_d_branch"), down_piece)
     )
     d_attn = contract_last(d_branch_wide, out_weight).astype(bf16)
-    d_attn_unit = turn(d_attn, False, tok_rows, heads, 13, "turn_d_attn")
+    other_down = from_twin(down_piece)
+    d_attn_unit, other_down = lax.optimization_barrier(
+        (turn(d_attn, False, tok_rows, heads, 13, "turn_d_attn"), other_down)
+    )
     out_raw = (contract_first(attn_low, after(d_branch_wide, d_attn_unit)) * factor).astype(bf16)
     d_attn_unit = after(d_attn_unit, out_raw)
     out_piece = reduce_rows(out_raw, 1)
     d_units = attend_back(unit_length, q_unit, k_unit, v_unit, d_attn_unit, attn_exact, log_total)
-    d_units, gate_piece = lax.optimization_barrier((d_units, gate_piece))
-    d_qkv, gain_sums = rear(
-        d_units, qkv[:, : 2 * half_feat], cosine, sine_signed, qk_gain, inverse, width, 14
-    )
+    d_units, gate_piece = lax.optimization_barrier((d_units, over_dp(gate_piece)))
+    other_gate = from_twin(gate_piece)
+    d_qkv, gain_sums = rear(d_units, qkv, cosine, sine_signed, qk_gain, inverse, width, 14)
+    d_qkv, gain_sums, other_gate = lax.optimization_barrier((d_qkv, gain_sums, other_gate))
     qkv_raw = (contract_first(tokens_wide, d_qkv) * factor).astype(bf16)
     projected = contract_last(d_qkv, qkv_weight).astype(bf16)
     projected, qkv_raw = lax.optimization_barrier((projected, qkv_raw))
     qkv_piece = over_dp(reduce_rows(qkv_raw, 0))
-    scattered, up_piece, out_piece = lax.optimization_barrier(
-        (scatter_wide(projected, False, 16, "scatter_projected"), up_piece, out_piece)
-    )
-    input_grad = d_resid + scattered
-
     def spread(half):
         return lax.dynamic_update_slice_in_dim(jnp.zeros((feat_part,), f32), half, y * half_feat, 0)
 
@@ -981,11 +983,17 @@
             15,
         )
     )
-    def whole(piece, axis):
-        piece = over_dp(piece)
-        return two_sides(piece, lax.ppermute(piece, "dp", pairs), y, axis).astype(f32)
-
-    qkv_other = lax.ppermute(qkv_piece, "dp", pairs)
+    projected = after(projected, gains)
+    up_piece, out_piece = over_dp(up_piece), over_dp(out_piece)
+    scattered, up_piece, out_piece = lax.optimization_barrier(
+        (scatter_wide(projected, False, 16, "scatter_projected"), up_piece, out_piece)
+    )
+    input_grad = d_resid + scattered
+
+    def whole(piece, other, axis):
+        return two_sides(piece, other, y, axis).astype(f32)
+
+    qkv_other = from_twin(qkv_piece)
     q_grad, k_grad, v_grad = (
         two_sides(cut(qkv_piece, i, 3, 1), cut(qkv_other, i, 3, 1), y, 1).astype(f32)
         for i in range(3)
@@ -996,10 +1004,10 @@
         q_grad,
         k_grad,
         v_grad,
-        whole(out_piece, 0),
-        whole(gate_piece, 1),
-        whole(up_piece, 1),
-        whole(down_piece, 0),
+        whole(out_piece, from_twin(out_piece), 0),
+        whole(gate_piece, other_gate, 1),
+        whole(up_piece, from_twin(up_piece), 1),
+        whole(down_piece, other_down, 0),
         gains[0],
         gains[1],
         gains[2],

time: 1000 us -> 960 us (0.960)
  Pallas kernels: 640 us -> 604 us
    pallas_call x1, Pallas kernels: 46.4 us -> 9.57 us  [gain_total(): pl.pallas_call(gain_kernel, name='total_gains', out_shape=jax.ShapeDtypeS...]
  transfers between devices with their start and end apart: 16 -> 16, of which waited for: 4 -> 4; matrix products, arithmetic and copies ran while one was open for 17% -> 18% of each run, Pallas kernels for 57% -> 56%
where the time goes in v5:
time: 960 us; the launch traced here: 949 us
  Pallas kernels  604 us (63%)
  matrix products  151 us (16%)
  waiting for transfers between devices  110 us (11%)
  other arithmetic  38.2 us (4%)
  local copies, waits for them, and re-layouts  21.9 us (2%)
  between operations  15.9 us (2%)
    pallas_call x4, Pallas kernels, scatter_wide(): pl.pallas_call(functools.partial(scatter_kernel, pair, rider), name=name,...  150 us
    pallas_call x4, Pallas kernels, gather_wide(): pl.pallas_call(functools.partial(gather_kernel, pair), name=name, out_sha...  127 us
    pallas_call x1, Pallas kernels, front(): pl.pallas_call(functools.partial(front_kernel, width), name='front', out_...  106 us
    pallas_call x1, Pallas kernels, rear(): pl.pallas_call(functools.partial(rear_kernel, width), name='rear', out_sh...  79.5 us
    pallas_call x2, Pallas kernels, turn(): pl.pallas_call(functools.partial(turn_kernel, back, tok, heads), name=nam...  69.5 us
    dot_general x5, matrix products, contract_last(): lax.dot_general(left, right, (((1,), (1,)), ((), ())), preferred_element_...  54.4 us
    all_gather x1, waiting for transfers between devices, per_device(): down_weight = lax.all_gather(y_half(w_down, 0), 'row', axis=1, tiled=True)  51.3 us
    dot_general x5, matrix products, matmul(): return jnp.dot(left, right, preferred_element_type=f32)  50.8 us
  transfers between devices with their start and end apart: 16, of which 4 were waited for; matrix products, arithmetic and copies ran while one was open for 18% of the time, Pallas kernels for 56%

profile of v5, /device:TPU:0, one launch (start us, length us, event | category | flops | bytes accessed | tf_op | source)
XLA Modules:
  0.0 949.3 jit_solution(11402341340759613228)
XLA Ops:
  12.5 2.4 constant_dynamic-slice_fusion.1
  15.0 3.1 collective-permute-start
  19.9 31.4 %gather_tokens.1 = bf16[1536,2048]{1,0:T(8,128)(2,1)} custom-call(bf16[768,512]{1,0:T(8,128)(2,1)} %x_ref.1), custom_call_target="tpu_custom_call" | custom-call | bytes 1000 | tf_op jit(solution)/shard_map/gather_tokens/pallas_call | solution.py:155
  54.5 22.3 %all-gather.6.cloned.1.call-done = bf16[2048,768]{1,0:T(8,128)(2,1)} async-done(((bf16[512,768]{1,0:T(8,128)(2,1)}), bf16[2048,768]{1,0:T(8,128)(2,1)}) %all-gather.6.cloned.1.call-update) | async-done | bytes 3145744 | tf_op jit(solution)/shard_map/all_gather | solution.py:854
  76.8 8.1 convolution_bitcast_fusion.qkv_ref
  84.9 105.9 %front.1 = (bf16[4,3,768,128]{3,2,1,0:T(8,128)(2,1)S(1)}, f32[2,1536]{1,0:T(2,128)S(1)}) custom-call(f32[1536,768]{1,0:T(8,128)S(1)} %convolution_bitcast_fusion.qkv_ref, f32[768,128]{1,0:T(8,128)S(1)} %get-tuple-element.100.cos_ref, f32[768,128]{1,0:T(8,128)S(1)} %get-tuple-element.99.sin_ref, f32[2,256]{1,0:T(2,128)S(1)} %pad_maximum_fusion.3.gain_ref), custom_call_target="tpu_custom_call" | custom-call | bytes 1000 | tf_op jit(solution)/shard_map/front/pallas_call | solution.py:558
  192.3 20.5 %attend.1 = (bf16[3072,128]{1,0:T(8,128)(2,1)}, f32[3072,128]{1,0:T(8,128)}, f32[8,3072]{1,0:T(8,128)}) custom-call(s32[1]{0:T(128)} %dynamic_slice.48.len_ref, bf16[3072,128]{1,0:T(8,128)(2,1)} %bitcast.69, bf16[3072,128]{1,0:T(8,128)(2,1)} %bitcast.67, bf16[3072,128]{1,0:T(8,128)(2,1)} %bitcast.65), custom_call_target="tpu_custom_call" | custom-call | bytes 1000 | tf_op jit(solution)/shard_map/attend/pallas_call | solution.py:738
  212.7 28.3 %turn_attn.1 = bf16[1536,256]{1,0:T(8,128)(2,1)} custom-call(bf16[3072,128]{1,0:T(8,128)(2,1)} %get-tuple-element.38.x_ref), custom_call_target="tpu_custom_call" | custom-call | bytes 1000 | tf_op jit(solution)/shard_map/turn_attn/pallas_call | solution.py:459
  241.1 6.0 convolution_convert_fusion.1.p_ref
  247.0 38.2 %scatter_branch.1 = f32[768,512]{1,0:T(8,128)S(1)} custom-call(bf16[1536,2048]{1,0:T(8,128)(2,1)} %convolution_convert_fusion.1.p_ref), custom_call_target="tpu_custom_call" | custom-call | bytes 1000 | tf_op jit(solution)/shard_map/scatter_branch/pallas_call | solution.py:305
  286.0 4.9 total_branch.1
  292.8 31.9 %gather_resid.1 = bf16[1536,2048]{1,0:T(8,128)(2,1)} custom-call(bf16[768,512]{1,0:T(8,128)(2,1)} %fusion.4.x_ref), custom_call_target="tpu_custom_call" | custom-call | bytes 1000 | tf_op jit(solution)/shard_map/gather_resid/pallas_call | solution.py:155
  324.7 12.2 %fusion.11 = f32[1536,1024]{1,0:T(8,128)} fusion(bf16[1536,2048]{1,0:T(8,128)(2,1)} %gather_resid.1, bf16[2048,1024]{1,0:T(8,128)(2,1)} %all-gather.10.cloned.1.call-done), kind=kOutput, calls=%fused_computation.88 | convolution fusion | flops 6442450944 | bytes 16777216 | tf_op jit(solution)/shard_map/dot_general | solution.py:31
  336.9 13.4 %multiply_convert_fusion.6 = (bf16[1536,1024]{1,0:T(8,128)(2,1)}, f32[1536,1024]{1,0:T(8,128)}) fusion(f32[1536,1024]{1,0:T(8,128)} %fusion.11, bf16[1536,2048]{1,0:T(8,128)(2,1)} %gather_resid.1, bf16[2048,1024]{1,0:T(8,128)(2,1)} %all-gather.12.cloned.1.call-done), kind=kOutput, calls=%fused_computation.10 | convolution fusion | flops 6451888128 | bytes 26214400 | tf_op jit(solution)/shard_map/dot_general | solution.py:31
  350.3 51.3 %all-gather.14.cloned.1.call-done = bf16[1024,2048]{1,0:T(8,128)(2,1)} async-done(((bf16[1024,512]{1,0:T(8,128)(2,1)}), bf16[1024,2048]{1,0:T(8,128)(2,1)}) %all-gather.14.cloned.1.call-update) | async-done | bytes 4194320 | tf_op jit(solution)/shard_map/all_gather | solution.py:863
  401.6 11.2 %convolution_convert_fusion.2.p_ref = bf16[1536,2048]{1,0:T(8,128)(2,1)} fusion(bf16[1536,1024]{1,0:T(8,128)(2,1)} %get-tuple-element.107, bf16[1024,2048]{1,0:T(8,128)(2,1)} %all-gather.14.cloned.1.call-done), kind=kOutput, calls=%fused_computation.6 | convolution fusion | flops 6445596672 | bytes 13631488 | tf_op jit(solution)/shard_map/dot_general | solution.py:31
  412.8 37.6 %scatter_mixed.1 = f32[768,512]{1,0:T(8,128)S(1)} custom-call(bf16[1536,2048]{1,0:T(8,128)(2,1)} %convolution_convert_fusion.2.p_ref), custom_call_target="tpu_custom_call" | custom-call | bytes 1000 | tf_op jit(solution)/shard_map/scatter_mixed/pallas_call | solution.py:305
  451.6 5.0 total_mixed.1
  458.0 2.5 subtract_convert_fusion.1.x_ref
  460.5 31.7 %gather_d_mixed.1 = bf16[1536,2048]{1,0:T(8,128)(2,1)} custom-call(bf16[768,512]{1,0:T(8,128)(2,1)} %subtract_convert_fusion.1.x_ref), custom_call_target="tpu_custom_call" | custom-call | bytes 1000 | tf_op jit(solution)/shard_map/gather_d_mixed/pallas_call | solution.py:155
  492.3 11.6 %multiply_convert_fusion.2 = bf16[1024,2048]{1,0:T(8,128)(2,1)} fusion(bf16[1536,1024]{1,0:T(8,128)(2,1)} %get-tuple-element.107, bf16[1536,2048]{1,0:T(8,128)(2,1)} %gather_d_mixed.1), kind=kOutput, calls=%fused_computation.3 | convolution fusion | flops 6446645248 | bytes 13631488 | tf_op jit(solution)/shard_map/dot_general | solution.py:35
  504.0 17.2 %multiply_convert_fusion.4 = (bf16[1536,1024]{1,0:T(8,128)(2,1)}, bf16[1536,1024]{1,0:T(8,128)(2,1)S(1)}) fusion(f32[1536,1024]{1,0:T(8,128)} %fusion.11, f32[1536,1024]{1,0:T(8,128)} %get-tuple-element.108, bf16[1536,2048]{1,0:T(8,128)(2,1)} %gather_d_mixed.1, bf16[1024,2048]{1,0:T(8,128)(2,1)} %all-gather.14.cloned.1.call-done), kind=kOutput, calls=%fused_computation.8 | convolution fusion | flops 6462898176 | bytes 29360128 | tf_op jit(solution)/shard_map/dot_general | solution.py:39
  522.9 11.1 %multiply_convert_fusion.1 = bf16[2048,1024]{1,0:T(8,128)(2,1)} fusion(bf16[1536,2048]{1,0:T(8,128)(2,1)} %gather_resid.1, bf16[1536,1024]{1,0:T(8,128)(2,1)S(1)} %get-tuple-element.80), kind=kOutput, calls=%fused_computation.2 | convolution fusion | flops 6446645248 | bytes 13631488 | tf_op jit(solution)/shard_map/dot_general | solution.py:35
  534.0 11.4 %multiply_convert_fusion = bf16[2048,1024]{1,0:T(8,128)(2,1)} fusion(bf16[1536,2048]{1,0:T(8,128)(2,1)} %gather_resid.1, bf16[1536,1024]{1,0:T(8,128)(2,1)} %get-tuple-element.79), kind=kOutput, calls=%fused_computation.1 | convolution fusion | flops 6446645248 | bytes 13631488 | tf_op jit(solution)/shard_map/dot_general | solution.py:35
  546.1 12.5 %fusion.12 = f32[1536,2048]{1,0:T(8,128)} fusion(bf16[1536,1024]{1,0:T(8,128)(2,1)} %copy-done.32, bf16[2048,1024]{1,0:T(8,128)(2,1)} %all-gather.10.cloned.1.call-done), kind=kOutput, calls=%fused_computation.89 | convolution fusion | flops 6442450944 | bytes 19922944 | tf_op jit(solution)/shard_map/dot_general | solution.py:39
  558.6 11.5 %add_convert_fusion.p_ref = bf16[1536,2048]{1,0:T(8,128)(2,1)} fusion(f32[1536,2048]{1,0:T(8,128)} %fusion.12, bf16[1536,1024]{1,0:T(8,128)(2,1)S(1)} %copy-done.33, bf16[2048,1024]{1,0:T(8,128)(2,1)S(1)} %copy-done.30), kind=kOutput, calls=%fused_computation | convolution fusion | flops 6448742400 | bytes 26214400 | tf_op jit(solution)/shard_map/dot_general | solution.py:39
  570.1 36.9 %scatter_d_resid.1 = f32[768,512]{1,0:T(8,128)S(1)} custom-call(bf16[1536,2048]{1,0:T(8,128)(2,1)} %add_convert_fusion.p_ref), custom_call_target="tpu_custom_call" | custom-call | bytes 1000 | tf_op jit(solution)/shard_map/scatter_d_resid/pallas_call | solution.py:305
  607.0 3.1 multiply_reduce_fusion.1
  610.2 4.9 total_d_resid.1
  615.8 2.5 subtract_convert_fusion.x_ref
  618.3 31.9 %gather_d_branch.1 = bf16[1536,2048]{1,0:T(8,128)(2,1)} custom-call(bf16[768,512]{1,0:T(8,128)(2,1)} %subtract_convert_fusion.x_ref), custom_call_target="tpu_custom_call" | custom-call | bytes 1000 | tf_op jit(solution)/shard_map/gather_d_branch/pallas_call | solution.py:155
  651.3 5.9 convolution_convert_fusion.3.x_ref
  657.2 41.2 %turn_d_attn.1.do_ref = bf16[3072,128]{1,0:T(8,128)(2,1)} custom-call(bf16[1536,256]{1,0:T(8,128)(2,1)} %convolution_convert_fusion.3.x_ref), custom_call_target="tpu_custom_call" | custom-call | bytes 1000 | tf_op jit(solution)/shard_map/turn_d_attn/pallas_call | solution.py:459
  698.4 5.6 fusion.1
  704.0 27.5 %attend_back.1.d_ref = bf16[3,3072,128]{2,1,0:T(8,128)(2,1)} custom-call(s32[1]{0:T(128)} %dynamic_slice.48.len_ref, bf16[3072,128]{1,0:T(8,128)(2,1)} %bitcast.70, bf16[3072,128]{1,0:T(8,128)(2,1)} %bitcast.68, bf16[3072,128]{1,0:T(8,128)(2,1)} %bitcast.66, bf16[3072,128]{1,0:T(8,128)(2,1)} %turn_d_attn.1.do_ref, f32[3072,128]{1,0:T(8,128)} %get-tuple-element.45.o_ref, ...), custom_call_target="tpu_custom_call" | custom-call | bytes 1000 | tf_op jit(solution)/shard_map/attend_back/pallas_call | solution.py:812
  732.3 2.3 copy-done.5
  736.3 79.5 %rear.1 = (bf16[1536,768]{1,0:T(8,128)(2,1)S(1)}, f32[2,256]{1,0:T(2,128)S(1)}) custom-call(bf16[3,3072,128]{2,1,0:T(8,128)(2,1)S(1)} %copy-done.6, f32[1536,768]{1,0:T(8,128)S(1)} %copy-done.5, f32[768,128]{1,0:T(8,128)S(1)} %copy-done.10, f32[768,128]{1,0:T(8,128)S(1)} %copy-done.8, f32[2,256]{1,0:T(2,128)S(1)} %copy-done.12, ...), custom_call_target="tpu_custom_call" | custom-call | bytes 1000 | tf_op jit(solution)/shard_map/rear/pallas_call | solution.py:667
  815.9 7.3 convolution_convert_fusion.p_ref
  823.2 6.5 fusion
  829.8 1.7 broadcast_select_fusion.1
  831.4 2.6 maximum_convert_fusion.2
  834.7 9.6 %total_gains.1 = f32[16,128]{1,0:T(8,128)} custom-call(f32[16,128]{1,0:T(8,128)} %mul.277.v_ref), custom_call_target="tpu_custom_call" | custom-call | tf_op jit(solution)/shard_map/total_gains/pallas_call | solution.py:408
  844.3 37.0 %scatter_projected.1 = f32[768,512]{1,0:T(8,128)S(1)} custom-call(bf16[1536,2048]{1,0:T(8,128)(2,1)} %convolution_convert_fusion.p_ref), custom_call_target="tpu_custom_call" | custom-call | bytes 1000 | tf_op jit(solution)/shard_map/scatter_projected/pallas_call | solution.py:305
  881.9 2.7 broadcast_select_fusion.5
  885.6 4.2 maximum_convert_fusion
  892.2 23.4 %collective-permute-done.4 = bf16[256,512]{1,0:T(8,128)(2,1)S(1)} collective-permute-done((bf16[256,512]{1,0:T(8,128)(2,1)S(1)}, bf16[256,512]{1,0:T(8,128)(2,1)S(1)}, u32[]{:S(2)}, u32[]{:S(2)}) %collective-permute-start.4) | collective-permute-done | bytes 262176 | tf_op jit(solution)/shard_map/ppermute | solution.py:929
  919.6 2.6 maximum_convert_fusion.1
  922.1 12.5 %collective-permute-done.3 = bf16[512,768]{0,1:T(8,128)(2,1)S(1)} collective-permute-done((bf16[512,768]{0,1:T(8,128)(2,1)}, bf16[512,768]{0,1:T(8,128)(2,1)S(1)}, u32[]{:S(2)}, u32[]{:S(2)}) %collective-permute-start.3) | collective-permute-done | bytes 786464 | tf_op jit(solution)/shard_map/ppermute | solution.py:929
  (157 shorter events, 39.1 us)
Async XLA Ops:
  7.2 4.1 copy-start
  7.2 3.3 copy-start.23
  7.2 69.6 %all-gather.6.cloned.1.call-start = ((), (), s32[]{:S(2)}) async-start(), calls=%async_computation.5 | async-start | bytes 3932160 | tf_op jit(solution)/shard_map/all_gather | solution.py:854
  10.5 230.6 %all-gather.8.cloned.1.call-start = ((), (), s32[]{:S(2)}) async-start(), calls=%async_computation.6 | async-start | bytes 1310720 | tf_op jit(solution)/shard_map/all_gather | solution.py:860
  11.3 313.4 %all-gather.10.cloned.1.call-start = ((), (), s32[]{:S(2)}) async-start(), calls=%async_computation.7 | async-start | bytes 5242880 | tf_op jit(solution)/shard_map/all_gather | solution.py:861
  12.4 5.6 copy-start.21
  12.4 324.5 %all-gather.12.cloned.1.call-start = ((), (), s32[]{:S(2)}) async-start(), calls=%async_computation.8 | async-start | bytes 5242880 | tf_op jit(solution)/shard_map/all_gather | solution.py:862
  14.9 386.7 %all-gather.14.cloned.1.call-start = ((), (), s32[]{:S(2)}) async-start(), calls=%async_computation.9 | async-start | bytes 5242880 | tf_op jit(solution)/shard_map/all_gather | solution.py:863
  15.0 38.3 %collective-permute-start = (s32[1]{0:T(128)}, s32[1]{0:T(128)}, u32[]{:S(2)}, u32[]{:S(2)}) collective-permute-start(s32[1]{0:T(128)} %param.15), channel_id=1, source_target_pairs={{0,16},{16,0},{1,17},{17,1},{2,18},{18,2},{3,19},{19,3},{4,20},{20... | collective-permute-start | bytes 20 | tf_op jit(solution)/shard_map/ppermute | solution.py:870
  19.1 631.2 %reduce-scatter.6.cloned.1.call-start = ((), (), s32[]{:S(2)}) async-start(), calls=%async_computation.10 | async-start | bytes 5242880 | tf_op jit(solution)/shard_map/reduce_scatter | solution.py:932
  19.8 31.4 %copy-start.28 = (f32[512]{0:T(512)S(1)}, f32[512]{0:T(512)}, u32[]{:S(2)}) copy-start(f32[512]{0:T(512)} %param.23) | copy-start | bytes 6148
  19.9 31.5 %copy-start.29 = (f32[512]{0:T(512)S(1)}, f32[512]{0:T(512)}, u32[]{:S(2)}) copy-start(f32[512]{0:T(512)} %param.24) | copy-start | bytes 6148
  51.5 33.4 %copy-start.11 = (f32[2,256]{1,0:T(2,128)}, f32[2,256]{1,0:T(2,128)S(1)}, u32[]{:S(2)}) copy-start(f32[2,256]{1,0:T(2,128)S(1)} %pad_maximum_fusion.3.gain_ref) | copy-start | bytes 6148
  53.2 31.6 %copy-start.7 = (f32[768,128]{1,0:T(8,128)}, f32[768,128]{1,0:T(8,128)S(1)}, u32[]{:S(2)}) copy-start(f32[768,128]{1,0:T(8,128)S(1)} %get-tuple-element.99.sin_ref) | copy-start | bytes 1179652
  53.3 31.6 %copy-start.9 = (f32[768,128]{1,0:T(8,128)}, f32[768,128]{1,0:T(8,128)S(1)}, u32[]{:S(2)}) copy-start(f32[768,128]{1,0:T(8,128)S(1)} %get-tuple-element.100.cos_ref) | copy-start | bytes 1179652
  84.8 107.4 %copy-start.4 = (f32[1536,768]{1,0:T(8,128)}, f32[1536,768]{1,0:T(8,128)S(1)}, u32[]{:S(2)}) copy-start(f32[1536,768]{1,0:T(8,128)S(1)} %convolution_bitcast_fusion.qkv_ref) | copy-start | bytes 14155780
  247.0 44.6 %copy-start.17 = (bf16[768,512]{1,0:T(8,128)(2,1)S(1)}, bf16[768,512]{1,0:T(8,128)(2,1)}, u32[]{:S(2)}) copy-start(bf16[768,512]{1,0:T(8,128)(2,1)} %x_ref.1) | copy-start | bytes 2359300
  247.0 44.6 %copy-start.26 = (f32[512]{0:T(512)S(1)}, f32[512]{0:T(512)}, u32[]{:S(2)}) copy-start(f32[512]{0:T(512)} %param.25) | copy-start | bytes 6148
  412.8 37.6 %copy-start.13 = (bf16[768,512]{1,0:T(8,128)(2,1)S(1)}, bf16[768,512]{1,0:T(8,128)(2,1)}, u32[]{:S(2)}) copy-start(bf16[768,512]{1,0:T(8,128)(2,1)} %param.27) | copy-start | bytes 2359300
  412.8 37.6 %copy-start.27 = (f32[512]{0:T(512)S(1)}, f32[512]{0:T(512)}, u32[]{:S(2)}) copy-start(f32[512]{0:T(512)} %param.26) | copy-start | bytes 6148
  450.4 41.9 %copy-start.2 = (f32[768,512]{1,0:T(8,128)}, f32[768,512]{1,0:T(8,128)S(1)}, u32[]{:S(2)}) copy-start(f32[768,512]{1,0:T(8,128)S(1)} %scatter_mixed.1) | copy-start | bytes 4718596
  503.9 227.6 %reduce-scatter.8.cloned.1.call-start = ((), (), s32[]{:S(2)}) async-start(), calls=%async_computation.11 | async-start | bytes 5242880 | tf_op jit(solution)/shard_map/reduce_scatter | solution.py:932
  534.0 350.6 %reduce-scatter.10.cloned.1.call-start = ((), (), s32[]{:S(2)}) async-start(), calls=%async_computation.12 | async-start | bytes 5242880 | tf_op jit(solution)/shard_map/reduce_scatter | solution.py:932
  545.4 339.2 %reduce-scatter.12.cloned.1.call-start = ((), (), s32[]{:S(2)}) async-start(), calls=%async_computation.13 | async-start | bytes 1310720 | tf_op jit(solution)/shard_map/reduce_scatter | solution.py:932
  546.1 12.5 %copy-start.30 = (bf16[2048,1024]{1,0:T(8,128)(2,1)S(1)}, bf16[2048,1024]{1,0:T(8,128)(2,1)}, u32[]{:S(2)}) copy-start(bf16[2048,1024]{1,0:T(8,128)(2,1)} %all-gather.12.cloned.1.call-done) | copy-start | bytes 12582916
  546.1 12.5 %copy-start.33 = (bf16[1536,1024]{1,0:T(8,128)(2,1)S(1)}, bf16[1536,1024]{1,0:T(8,128)(2,1)}, u32[]{:S(2)}) copy-start(bf16[1536,1024]{1,0:T(8,128)(2,1)} %get-tuple-element.79) | copy-start | bytes 9437188
  570.1 36.9 %copy-start.3 = (f32[768,512]{1,0:T(8,128)S(1)}, f32[768,512]{1,0:T(8,128)}, u32[]{:S(2)}) copy-start(f32[768,512]{1,0:T(8,128)} %copy-done.2) | copy-start | bytes 4718596
  570.1 36.9 %copy-start.14 = (bf16[768,512]{1,0:T(8,128)(2,1)S(1)}, bf16[768,512]{1,0:T(8,128)(2,1)}, u32[]{:S(2)}) copy-start(bf16[768,512]{1,0:T(8,128)(2,1)} %param.27) | copy-start | bytes 2359300
  570.1 36.9 %copy-start.18 = (bf16[768,512]{1,0:T(8,128)(2,1)S(1)}, bf16[768,512]{1,0:T(8,128)(2,1)}, u32[]{:S(2)}) copy-start(bf16[768,512]{1,0:T(8,128)(2,1)} %x_ref.1) | copy-start | bytes 2359300
  650.2 48.2 %copy-start.16 = (bf16[1536,256]{1,0:T(8,128)(2,1)S(1)}, bf16[1536,256]{1,0:T(8,128)(2,1)}, u32[]{:S(2)}) copy-start(bf16[1536,256]{1,0:T(8,128)(2,1)} %turn_attn.1) | copy-start | bytes 2359300
  650.3 48.1 %collective-permute-start.1 = (bf16[1024,512]{1,0:T(8,128)(2,1)}, bf16[1024,512]{1,0:T(8,128)(2,1)}, u32[]{:S(2)}, u32[]{:S(2)}) collective-permute-start(bf16[1024,512]{1,0:T(8,128)(2,1)} %reduce-scatter.6.cloned.1.call-done), channel_id=1, source_target_pairs={{0,16},{16,0},{1,17},{17,1},{2,18},{18,2},{3,19},{19,3},{4,20},{20... | collective-permute-start | bytes 3145736 | tf_op jit(solution)/shard_map/ppermute | solution.py:929
  704.0 28.3 %copy-start.8 = (f32[768,128]{1,0:T(8,128)S(1)}, f32[768,128]{1,0:T(8,128)}, u32[]{:S(2)}) copy-start(f32[768,128]{1,0:T(8,128)} %copy-done.7) | copy-start | bytes 1179652
  704.0 28.3 %copy-start.10 = (f32[768,128]{1,0:T(8,128)S(1)}, f32[768,128]{1,0:T(8,128)}, u32[]{:S(2)}) copy-start(f32[768,128]{1,0:T(8,128)} %copy-done.9) | copy-start | bytes 1179652
  704.0 28.3 %copy-start.12 = (f32[2,256]{1,0:T(2,128)S(1)}, f32[2,256]{1,0:T(2,128)}, u32[]{:S(2)}) copy-start(f32[2,256]{1,0:T(2,128)} %copy-done.11) | copy-start | bytes 6148
  731.5 84.4 %collective-permute-start.2 = (bf16[512,1024]{1,0:T(8,128)(2,1)}, bf16[512,1024]{1,0:T(8,128)(2,1)}, u32[]{:S(2)}, u32[]{:S(2)}) collective-permute-start(bf16[512,1024]{1,0:T(8,128)(2,1)} %reduce-scatter.8.cloned.1.call-done), channel_id=1, source_target_pairs={{0,16},{16,0},{1,17},{17,1},{2,18},{18,2},{3,19},{19,3},{4,20},{20... | collective-permute-start | bytes 3145736 | tf_op jit(solution)/shard_map/ppermute | solution.py:929
  732.2 183.5 %reduce-scatter.14.cloned.1.call-start = ((), (), s32[]{:S(2)}) async-start(), calls=%async_computation.14 | async-start | bytes 3932160 | tf_op jit(solution)/shard_map/reduce_scatter | solution.py:932
  736.3 79.6 %copy-start.31 = (bf16[2048,768]{1,0:T(8,128)(2,1)S(1)}, bf16[2048,768]{1,0:T(8,128)(2,1)}, u32[]{:S(2)}) copy-start(bf16[2048,768]{1,0:T(8,128)(2,1)} %all-gather.6.cloned.1.call-done) | copy-start | bytes 9437188
  736.3 86.9 %slice-start = ((s8[6291456]{0:T(1024)(128)(4,1)}), s8[4194304]{0:T(1024)(128)(4,1)S(1)}, s32[]{:S(2)}) async-start(s8[6291456]{0:T(1024)(128)(4,1)} %bitcast.71), calls=%async_computation.15 | async-start | bytes 8388608
  815.9 7.3 slice-start.1
  844.3 37.0 %copy-start.25 = (f32[16,128]{1,0:T(8,128)S(1)}, f32[16,128]{1,0:T(8,128)}, u32[]{:S(2)}) copy-start(f32[16,128]{1,0:T(8,128)} %total_gains.1) | copy-start | bytes 24580
  844.3 37.6 %copy-start.19 = (bf16[512,1024]{1,0:T(8,128)(2,1)S(1)}, bf16[512,1024]{1,0:T(8,128)(2,1)}, u32[]{:S(2)}) copy-start(bf16[512,1024]{1,0:T(8,128)(2,1)} %reduce-scatter.8.cloned.1.call-done) | copy-start | bytes 3145732
  884.6 33.3 %collective-permute-start.5 = (bf16[512,1024]{1,0:T(8,128)(2,1)}, bf16[512,1024]{1,0:T(8,128)(2,1)}, u32[]{:S(2)}, u32[]{:S(2)}) collective-permute-start(bf16[512,1024]{1,0:T(8,128)(2,1)} %reduce-scatter.10.cloned.1.call-done), channel_id=1, source_target_pairs={{0,16},{16,0},{1,17},{17,1},{2,18},{18,2},{3,19},{19,3},{4,20},{20... | collective-permute-start | bytes 3145736 | tf_op jit(solution)/shard_map/ppermute | solution.py:929
  885.6 4.2 copy-start.22
  885.6 5.2 copy-start.15
  889.8 25.8 %collective-permute-start.4 = (bf16[256,512]{1,0:T(8,128)(2,1)S(1)}, bf16[256,512]{1,0:T(8,128)(2,1)S(1)}, u32[]{:S(2)}, u32[]{:S(2)}) collective-permute-start(bf16[256,512]{1,0:T(8,128)(2,1)S(1)} %copy-done.22), channel_id=1, source_target_pairs={{0,16},{16,0},{1,17},{17,1},{2,18},{18,2},{3,19},{19,3},{4,20},{20... | collective-permute-start | bytes 786440 | tf_op jit(solution)/shard_map/ppermute | solution.py:929
  915.7 19.0 %collective-permute-start.3 = (bf16[512,768]{0,1:T(8,128)(2,1)}, bf16[512,768]{0,1:T(8,128)(2,1)S(1)}, u32[]{:S(2)}, u32[]{:S(2)}) collective-permute-start(bf16[512,768]{0,1:T(8,128)(2,1)} %reduce-scatter.14.cloned.1.call-done), channel_id=1, source_target_pairs={{0,16},{16,0},{1,17},{17,1},{2,18},{18,2},{3,19},{19,3},{4,20},{20... | collective-permute-start | bytes 2359304 | tf_op jit(solution)/shard_map/ppermute | solution.py:929
  919.6 15.1 %copy-start.20 = (bf16[512,768]{0,1:T(8,128)(2,1)S(1)}, bf16[512,768]{0,1:T(8,128)(2,1)}, u32[]{:S(2)}) copy-start(bf16[512,768]{0,1:T(8,128)(2,1)} %reduce-scatter.14.cloned.1.call-done) | copy-start | bytes 2359300
  937.0 5.0 copy-start.1
  (4 other events, 6.4 us)
Sparse Core Ops, SparseCore 0:
  10.6 66.1 all-gather.5
  78.9 51.7 all-gather.7
  132.8 106.1 all-gather.9
  241.0 79.2 all-gather.11
  322.3 79.2 all-gather.13
  504.0 74.3 reduce-scatter.5
  581.3 77.2 reduce-scatter.7
  661.5 88.2 reduce-scatter.9
  752.7 57.9 reduce-scatter.11
  829.9 59.4 reduce-scatter.13

commit v6 on v5

--- a/solution.py
+++ b/solution.py
@@ -860,7 +860,10 @@
     out_weight = lax.all_gather(y_half(w_out, 0), "row", axis=1, tiled=True)
     gate_weight = lax.all_gather(y_half(w_gate, 1), "row", axis=0, tiled=True)
     up_weight = lax.all_gather(y_half(w_up, 1), "row", axis=0, tiled=True)
-    down_weight = lax.all_gather(y_half(w_down, 0), "row", axis=1, tiled=True)
+    down_half = y_half(w_down, 0)
+    split = down_half.shape[1] // 2
+    low_weight = lax.all_gather(down_half[:, :split], "row", axis=1, tiled=True)
+    high_weight = lax.all_gather(down_half[:, split:], "row", axis=1, tiled=True)
 
     positions = z * tok_rows + jnp.arange(tok_rows)
     length = seq_lengths[0]
@@ -893,7 +896,10 @@
     upper = matmul(resid_wide, up_weight)
     sigma = jax.nn.sigmoid(gate)
     hidden = (gate * sigma * upper).astype(bf16)
-    mixed = scatter_wide(matmul(hidden, down_weight).astype(bf16), False, 7, "scatter_mixed")
+    mixed_low = scatter_wide(matmul(hidden, low_weight).astype(bf16), False, 7, "scatter_mixed_low")
+    high_weight = after(high_weight, mixed_low)
+    mixed_high = scatter_wide(matmul(hidden, high_weight).astype(bf16), False, 17, "scatter_mixed_high")
+    mixed = jnp.concatenate([mixed_low, mixed_high], axis=1)
     incoming = cotangent.astype(f32) * valid
     gained = incoming * mlp_gain
     sums = feature_total(
@@ -906,9 +912,12 @@
     block_output = ((resid + mixed * mixed_inv * mlp_gain) * valid).astype(bf16)
     mlp_gain_raw = jnp.sum(incoming * mixed * mixed_inv, axis=0)
     d_mixed = (mixed_inv * gained - mixed * mixed_inv**3 * inner).astype(bf16)
-    d_mixed_wide = gather_wide(d_mixed, False, 9, "gather_d_mixed")
-
     factor = 1.0 / math.sqrt(slots * data_count)
+    d_low_wide = gather_wide(d_mixed[:, :split], False, 9, "gather_d_mixed_low")
+    low_raw = (contract_first(hidden, d_low_wide) * factor).astype(bf16)
+    d_high = after(d_mixed[:, split:], low_raw)
+    d_high_wide = gather_wide(d_high, False, 18, "gather_d_mixed_high")
+    high_raw = (contract_first(hidden, d_high_wide) * factor).astype(bf16)
 
     def cut(values, index, count, axis):
         size = values.shape[axis] // count
@@ -931,8 +940,7 @@
     def reduce_rows(raw, axis):
         return lax.psum_scatter(raw, "row", scatter_dimension=axis, tiled=True)
 
-    d_hidden = contract_last(d_mixed_wide, down_weight)
-    down_raw = (contract_first(hidden, d_mixed_wide) * factor).astype(bf16)
+    d_hidden = contract_last(d_low_wide, low_weight) + contract_last(d_high_wide, high_weight)
     d_gate = (d_hidden * upper * sigma * (1.0 + gate * (1.0 - sigma))).astype(bf16)
     d_upper = (d_hidden * gate * sigma).astype(bf16)
     gate_raw = (contract_first(resid_wide, d_gate) * factor).astype(bf16)
@@ -940,8 +948,10 @@
     d_resid_wide = (
         contract_last(d_gate, gate_weight) + contract_last(d_upper, up_weight)
     ).astype(bf16)
-    d_resid_wide = after(d_resid_wide, down_raw, gate_raw, up_raw)
-    down_piece = reduce_rows(down_raw, 1)
+    d_resid_wide, low_piece = lax.optimization_barrier(
+        (after(d_resid_wide, high_raw, gate_raw, up_raw), reduce_rows(low_raw, 1))
+    )
+    down_piece = jnp.concatenate([low_piece, reduce_rows(high_raw, 1)], axis=1)
     gate_piece, up_piece = reduce_rows(gate_raw, 0), reduce_rows(up_raw, 0)
     d_resid = scatter_wide(d_resid_wide, False, 10, "scatter_d_resid")
     d_resid = incoming + d_resid
@@ -968,11 +978,16 @@
     d_units, gate_piece = lax.optimization_barrier((d_units, over_dp(gate_piece)))
     other_gate = from_twin(gate_piece)
     d_qkv, gain_sums = rear(d_units, qkv, cosine, sine_signed, qk_gain, inverse, width, 14)
-    d_qkv, gain_sums, other_gate = lax.optimization_barrier((d_qkv, gain_sums, other_gate))
+    d_qkv, gain_sums, other_gate, up_piece = lax.optimization_barrier(
+        (d_qkv, gain_sums, other_gate, over_dp(up_piece))
+    )
+    other_up = from_twin(up_piece)
     qkv_raw = (contract_first(tokens_wide, d_qkv) * factor).astype(bf16)
-    projected = contract_last(d_qkv, qkv_weight).astype(bf16)
-    projected, qkv_raw = lax.optimization_barrier((projected, qkv_raw))
+    projected = contract_last(after(d_qkv, qkv_raw), qkv_weight).astype(bf16)
+    projected, out_piece = lax.optimization_barrier((projected, over_dp(out_piece)))
+    other_out = from_twin(out_piece)
     qkv_piece = over_dp(reduce_rows(qkv_raw, 0))
+
     def spread(half):
         return lax.dynamic_update_slice_in_dim(jnp.zeros((feat_part,), f32), half, y * half_feat, 0)
 
@@ -983,10 +998,9 @@
             15,
         )
     )
-    projected = after(projected, gains)
-    up_piece, out_piece = over_dp(up_piece), over_dp(out_piece)
-    scattered, up_piece, out_piece = lax.optimization_barrier(
-        (scatter_wide(projected, False, 16, "scatter_projected"), up_piece, out_piece)
+    projected = after(projected, gains, other_up, other_out)
+    scattered, qkv_piece = lax.optimization_barrier(
+        (scatter_wide(projected, False, 16, "scatter_projected"), qkv_piece)
     )
     input_grad = d_resid + scattered
 
@@ -1004,9 +1018,9 @@
         q_grad,
         k_grad,
         v_grad,
-        whole(out_piece, from_twin(out_piece), 0),
+        whole(out_piece, other_out, 0),
         whole(gate_piece, other_gate, 1),
-        whole(up_piece, from_twin(up_piece), 1),
+        whole(up_piece, other_up, 1),
         whole(down_piece, other_down, 0),
         gains[0],
         gains[1],

time: 960 us -> 955 us (level)
  waiting for transfers between devices: 110 us -> 72.5 us
  Pallas kernels: 604 us -> 625 us
    ppermute x5, waiting for transfers between devices: 35.9 us -> 12.8 us  [from_twin(): return lax.ppermute(piece, 'dp', pairs)]
    pallas_call x1, Pallas kernels: 9.57 us -> 25.4 us  [gain_total(): pl.pallas_call(gain_kernel, name='total_gains', out_shape=jax.ShapeDtypeS...]
    all_gather x1 -> x2, waiting for transfers between devices: 51.3 us -> 37.3 us  [the longest x1 19.7 us: per_device(): lax.all_gather(down_half[:, split:], 'row', axis=1, tiled=True)]
    pallas_call x4 -> x5, Pallas kernels: 127 us -> 132 us  [gather_wide(): pl.pallas_call(functools.partial(gather_kernel, pair), name=name, out_sha...]
    pallas_call x4 -> x5, Pallas kernels: 150 us -> 155 us  [scatter_wide(): pl.pallas_call(functools.partial(scatter_kernel, pair, rider), name=name,...]
    dot_general x5 -> x6, matrix products: 46.2 us -> 50.2 us  [contract_first(): lax.dot_general(left, right, (((0,), (0,)), ((), ())), preferred_element_...]
    dot_general x5 -> x6, matrix products: 54.4 us -> 57.5 us  [contract_last(): lax.dot_general(left, right, (((1,), (1,)), ((), ())), preferred_element_...]
    dot_general x5 -> x6, matrix products: 50.8 us -> 51.5 us  [matmul(): return jnp.dot(left, right, preferred_element_type=f32)]
  transfers between devices with their start and end apart: 16 -> 18, of which waited for: 4 -> 4; matrix products, arithmetic and copies ran while one was open for 18% -> 19% of each run, Pallas kernels for 56% -> 62%
where the time goes in v6:
time: 955 us; the launch traced here: 944 us
  Pallas kernels  625 us (65%)
  matrix products  159 us (17%)
  waiting for transfers between devices  72.5 us (8%)
  other arithmetic  37.2 us (4%)
  local copies, waits for them, and re-layouts  26.4 us (3%)
  between operations  15.9 us (2%)
    pallas_call x5, Pallas kernels, scatter_wide(): pl.pallas_call(functools.partial(scatter_kernel, pair, rider), name=name,...  155 us
    pallas_call x5, Pallas kernels, gather_wide(): pl.pallas_call(functools.partial(gather_kernel, pair), name=name, out_sha...  132 us
    pallas_call x1, Pallas kernels, front(): pl.pallas_call(functools.partial(front_kernel, width), name='front', out_...  106 us
    pallas_call x2, Pallas kernels, turn(): pl.pallas_call(functools.partial(turn_kernel, back, tok, heads), name=nam...  77.2 us
    pallas_call x1, Pallas kernels, rear(): pl.pallas_call(functools.partial(rear_kernel, width), name='rear', out_sh...  75.9 us
    dot_general x6, matrix products, contract_last(): lax.dot_general(left, right, (((1,), (1,)), ((), ())), preferred_element_...  57.5 us
    dot_general x6, matrix products, matmul(): return jnp.dot(left, right, preferred_element_type=f32)  51.5 us
    dot_general x6, matrix products, contract_first(): lax.dot_general(left, right, (((0,), (0,)), ((), ())), preferred_element_...  50.2 us
  transfers between devices with their start and end apart: 18, of which 4 were waited for; matrix products, arithmetic and copies ran while one was open for 19% of the time, Pallas kernels for 62%

profile of v6, /device:TPU:0, one launch (start us, length us, event | category | flops | bytes accessed | tf_op | source)
XLA Modules:
  0.0 944.4 jit_solution(11428174779161740032)
XLA Ops:
  16.1 3.1 collective-permute-start
  20.1 31.4 %gather_tokens.1 = bf16[1536,2048]{1,0:T(8,128)(2,1)} custom-call(bf16[768,512]{1,0:T(8,128)(2,1)} %x_ref.1), custom_call_target="tpu_custom_call" | custom-call | bytes 1000 | tf_op jit(solution)/shard_map/gather_tokens/pallas_call | solution.py:155
  54.7 22.1 %all-gather.7.cloned.1.call-done = bf16[2048,768]{1,0:T(8,128)(2,1)} async-done(((bf16[512,768]{1,0:T(8,128)(2,1)}), bf16[2048,768]{1,0:T(8,128)(2,1)}) %all-gather.7.cloned.1.call-update) | async-done | bytes 3145744 | tf_op jit(solution)/shard_map/all_gather | solution.py:854
  76.8 8.1 convolution_bitcast_fusion.qkv_ref
  84.9 105.9 %front.1 = (bf16[4,3,768,128]{3,2,1,0:T(8,128)(2,1)S(1)}, f32[2,1536]{1,0:T(2,128)S(1)}) custom-call(f32[1536,768]{1,0:T(8,128)S(1)} %convolution_bitcast_fusion.qkv_ref, f32[768,128]{1,0:T(8,128)S(1)} %get-tuple-element.116.cos_ref, f32[768,128]{1,0:T(8,128)S(1)} %get-tuple-element.115.sin_ref, f32[2,256]{1,0:T(2,128)S(1)} %pad_maximum_fusion.5.gain_ref), custom_call_target="tpu_custom_call" | custom-call | bytes 1000 | tf_op jit(solution)/shard_map/front/pallas_call | solution.py:558
  192.3 16.3 %attend.1 = (bf16[3072,128]{1,0:T(8,128)(2,1)}, f32[3072,128]{1,0:T(8,128)}, f32[8,3072]{1,0:T(8,128)}) custom-call(s32[1]{0:T(128)} %dynamic_slice.48.len_ref, bf16[3072,128]{1,0:T(8,128)(2,1)} %bitcast.75, bf16[3072,128]{1,0:T(8,128)(2,1)} %bitcast.73, bf16[3072,128]{1,0:T(8,128)(2,1)} %bitcast.71), custom_call_target="tpu_custom_call" | custom-call | bytes 1000 | tf_op jit(solution)/shard_map/attend/pallas_call | solution.py:738
  208.6 32.4 %turn_attn.1 = bf16[1536,256]{1,0:T(8,128)(2,1)} custom-call(bf16[3072,128]{1,0:T(8,128)(2,1)} %get-tuple-element.44.x_ref), custom_call_target="tpu_custom_call" | custom-call | bytes 1000 | tf_op jit(solution)/shard_map/turn_attn/pallas_call | solution.py:459
  241.1 5.9 convolution_convert_fusion.1.p_ref
  247.0 38.2 %scatter_branch.1 = f32[768,512]{1,0:T(8,128)S(1)} custom-call(bf16[1536,2048]{1,0:T(8,128)(2,1)} %convolution_convert_fusion.1.p_ref), custom_call_target="tpu_custom_call" | custom-call | bytes 1000 | tf_op jit(solution)/shard_map/scatter_branch/pallas_call | solution.py:305
  286.0 4.9 total_branch.1
  292.8 31.9 %gather_resid.1 = bf16[1536,2048]{1,0:T(8,128)(2,1)} custom-call(bf16[768,512]{1,0:T(8,128)(2,1)} %fusion.4.x_ref), custom_call_target="tpu_custom_call" | custom-call | bytes 1000 | tf_op jit(solution)/shard_map/gather_resid/pallas_call | solution.py:155
  324.7 12.1 %fusion.12 = f32[1536,1024]{1,0:T(8,128)} fusion(bf16[1536,2048]{1,0:T(8,128)(2,1)} %gather_resid.1, bf16[2048,1024]{1,0:T(8,128)(2,1)} %all-gather.11.cloned.1.call-done), kind=kOutput, calls=%fused_computation.94 | convolution fusion | flops 6442450944 | bytes 16777216 | tf_op jit(solution)/shard_map/dot_general | solution.py:31
  336.8 13.4 %multiply_convert_fusion.5 = (bf16[1536,1024]{1,0:T(8,128)(2,1)}, f32[1536,1024]{1,0:T(8,128)}) fusion(f32[1536,1024]{1,0:T(8,128)} %fusion.12, bf16[1536,2048]{1,0:T(8,128)(2,1)} %gather_resid.1, bf16[2048,1024]{1,0:T(8,128)(2,1)} %all-gather.13.cloned.1.call-done), kind=kOutput, calls=%fused_computation.8 | convolution fusion | flops 6451888128 | bytes 26214400 | tf_op jit(solution)/shard_map/dot_general | solution.py:31
  350.3 17.6 %all-gather.15.cloned.1.call-done = bf16[1024,1024]{1,0:T(8,128)(2,1)} async-done(((bf16[1024,256]{1,0:T(8,128)(2,1)}), bf16[1024,1024]{1,0:T(8,128)(2,1)}) %all-gather.15.cloned.1.call-update) | async-done | bytes 2097168 | tf_op jit(solution)/shard_map/all_gather | solution.py:865
  367.9 6.0 convolution_convert_fusion.3.p_ref
  373.9 20.8 %scatter_mixed_low.1 = f32[768,256]{1,0:T(8,128)S(1)} custom-call(bf16[1536,1024]{1,0:T(8,128)(2,1)S(1)} %convolution_convert_fusion.3.p_ref), custom_call_target="tpu_custom_call" | custom-call | bytes 1000 | tf_op jit(solution)/shard_map/scatter_mixed_low/pallas_call | solution.py:305
  394.7 19.7 %all-gather.17.cloned.1.call-done = bf16[1024,1024]{1,0:T(8,128)(2,1)} async-done(((bf16[1024,256]{1,0:T(8,128)(2,1)}), bf16[1024,1024]{1,0:T(8,128)(2,1)}) %all-gather.17.cloned.1.call-update) | async-done | bytes 2097168 | tf_op jit(solution)/shard_map/all_gather | solution.py:866
  414.4 6.0 convolution_convert_fusion.2.p_ref
  420.4 20.7 %scatter_mixed_high.1 = f32[768,256]{1,0:T(8,128)S(1)} custom-call(bf16[1536,1024]{1,0:T(8,128)(2,1)S(1)} %convolution_convert_fusion.2.p_ref), custom_call_target="tpu_custom_call" | custom-call | bytes 1000 | tf_op jit(solution)/shard_map/scatter_mixed_high/pallas_call | solution.py:305
  442.3 5.0 total_mixed.1
  451.3 18.4 %gather_d_mixed_low.1 = bf16[1536,1024]{1,0:T(8,128)(2,1)} custom-call(bf16[768,256]{1,0:T(8,128)(2,1)} %get-tuple-element.112.x_ref), custom_call_target="tpu_custom_call" | custom-call | bytes 1000 | tf_op jit(solution)/shard_map/gather_d_mixed_low/pallas_call | solution.py:155
  469.7 7.9 multiply_convert_fusion.7
  477.6 18.7 %gather_d_mixed_high.1 = bf16[1536,1024]{1,0:T(8,128)(2,1)} custom-call(bf16[768,256]{1,0:T(8,128)(2,1)} %get-tuple-element.46.x_ref), custom_call_target="tpu_custom_call" | custom-call | bytes 1000 | tf_op jit(solution)/shard_map/gather_d_mixed_high/pallas_call | solution.py:155
  496.3 7.7 multiply_convert_fusion.6
  504.1 8.9 fusion.13
  513.0 11.3 %multiply_convert_fusion.3 = (bf16[1536,1024]{1,0:T(8,128)(2,1)}, bf16[1536,1024]{1,0:T(8,128)(2,1)S(1)}) fusion(f32[1536,1024]{1,0:T(8,128)} %fusion.12, f32[1536,1024]{1,0:T(8,128)} %get-tuple-element.124, f32[1536,1024]{1,0:T(8,128)} %fusion.13, bf16[1536,1024]{1,0:T(8,128)(2,1)S(1)} %copy-done.23, bf16[1024,1024]{1,0:T(8,128)(2,1)S(1)} %copy-done.36), kind=kOutput, calls=%fused_computation.6 | convolution fusion | flops 3243245568 | bytes 30408704 | tf_op jit(solution)/shard_map/dot_general | solution.py:39
  526.0 8.5 multiply_convert_fusion.1
  534.6 11.2 %multiply_convert_fusion = bf16[2048,1024]{1,0:T(8,128)(2,1)} fusion(bf16[1536,2048]{1,0:T(8,128)(2,1)} %gather_resid.1, bf16[1536,1024]{1,0:T(8,128)(2,1)} %get-tuple-element.91), kind=kOutput, calls=%fused_computation.1 | convolution fusion | flops 6446645248 | bytes 13631488 | tf_op jit(solution)/shard_map/dot_general | solution.py:35
  546.5 12.9 %fusion.14 = f32[1536,2048]{1,0:T(8,128)} fusion(bf16[1536,1024]{1,0:T(8,128)(2,1)} %copy-done.37, bf16[2048,1024]{1,0:T(8,128)(2,1)} %all-gather.11.cloned.1.call-done), kind=kOutput, calls=%fused_computation.96 | convolution fusion | flops 6442450944 | bytes 19922944 | tf_op jit(solution)/shard_map/dot_general | solution.py:39
  559.5 11.5 %add_convert_fusion.p_ref = bf16[1536,2048]{1,0:T(8,128)(2,1)} fusion(f32[1536,2048]{1,0:T(8,128)} %fusion.14, bf16[1536,1024]{1,0:T(8,128)(2,1)S(1)} %copy-done.38, bf16[2048,1024]{1,0:T(8,128)(2,1)S(1)} %copy-done.34), kind=kOutput, calls=%fused_computation | convolution fusion | flops 6448742400 | bytes 26214400 | tf_op jit(solution)/shard_map/dot_general | solution.py:39
  571.0 38.3 %scatter_d_resid.1 = f32[768,512]{1,0:T(8,128)S(1)} custom-call(bf16[1536,2048]{1,0:T(8,128)(2,1)} %add_convert_fusion.p_ref), custom_call_target="tpu_custom_call" | custom-call | bytes 1000 | tf_op jit(solution)/shard_map/scatter_d_resid/pallas_call | solution.py:305
  609.3 3.1 multiply_reduce_fusion.1
  612.4 4.9 total_d_resid.1
  618.0 2.5 subtract_convert_fusion.x_ref
  620.6 32.0 %gather_d_branch.1 = bf16[1536,2048]{1,0:T(8,128)(2,1)} custom-call(bf16[768,512]{1,0:T(8,128)(2,1)} %subtract_convert_fusion.x_ref), custom_call_target="tpu_custom_call" | custom-call | bytes 1000 | tf_op jit(solution)/shard_map/gather_d_branch/pallas_call | solution.py:155
  655.6 5.8 convolution_convert_fusion.4.x_ref
  661.4 44.8 %turn_d_attn.1.do_ref = bf16[3072,128]{1,0:T(8,128)(2,1)} custom-call(bf16[1536,256]{1,0:T(8,128)(2,1)} %convolution_convert_fusion.4.x_ref), custom_call_target="tpu_custom_call" | custom-call | bytes 1000 | tf_op jit(solution)/shard_map/turn_d_attn/pallas_call | solution.py:459
  706.2 5.6 fusion.1
  711.7 22.4 %attend_back.1.d_ref = bf16[3,3072,128]{2,1,0:T(8,128)(2,1)} custom-call(s32[1]{0:T(128)} %dynamic_slice.48.len_ref, bf16[3072,128]{1,0:T(8,128)(2,1)} %bitcast.76, bf16[3072,128]{1,0:T(8,128)(2,1)} %bitcast.74, bf16[3072,128]{1,0:T(8,128)(2,1)} %bitcast.72, bf16[3072,128]{1,0:T(8,128)(2,1)} %turn_d_attn.1.do_ref, f32[3072,128]{1,0:T(8,128)} %get-tuple-element.55.o_ref, ...), custom_call_target="tpu_custom_call" | custom-call | bytes 1000 | tf_op jit(solution)/shard_map/attend_back/pallas_call | solution.py:812
  739.4 75.9 %rear.1 = (bf16[1536,768]{1,0:T(8,128)(2,1)S(1)}, f32[2,256]{1,0:T(2,128)S(1)}) custom-call(bf16[3,3072,128]{2,1,0:T(8,128)(2,1)S(1)} %copy-done.8, f32[1536,768]{1,0:T(8,128)S(1)} %copy-done.3, f32[768,128]{1,0:T(8,128)S(1)} %copy-done.12, f32[768,128]{1,0:T(8,128)S(1)} %copy-done.10, f32[2,256]{1,0:T(2,128)S(1)} %copy-done.14, ...), custom_call_target="tpu_custom_call" | custom-call | bytes 1000 | tf_op jit(solution)/shard_map/rear/pallas_call | solution.py:667
  816.7 9.3 fusion
  827.7 2.8 maximum_convert_fusion.2
  831.9 7.1 convolution_convert_fusion.p_ref
  842.8 2.6 maximum_convert_fusion
  845.9 25.4 %total_gains.1 = f32[16,128]{1,0:T(8,128)} custom-call(f32[16,128]{1,0:T(8,128)} %mul.277.v_ref), custom_call_target="tpu_custom_call" | custom-call | tf_op jit(solution)/shard_map/total_gains/pallas_call | solution.py:408
  873.9 36.7 %scatter_projected.1 = f32[768,512]{1,0:T(8,128)S(1)} custom-call(bf16[1536,2048]{1,0:T(8,128)(2,1)} %convolution_convert_fusion.p_ref), custom_call_target="tpu_custom_call" | custom-call | bytes 1000 | tf_op jit(solution)/shard_map/scatter_projected/pallas_call | solution.py:305
  913.1 2.6 maximum_convert_fusion.1
  917.1 12.8 %collective-permute-done.5 = bf16[512,768]{0,1:T(8,128)(2,1)S(1)} collective-permute-done((bf16[512,768]{0,1:T(8,128)(2,1)}, bf16[512,768]{0,1:T(8,128)(2,1)S(1)}, u32[]{:S(2)}, u32[]{:S(2)}) %collective-permute-start.5) | collective-permute-done | bytes 786464 | tf_op jit(solution)/shard_map/ppermute | solution.py:938
  (180 shorter events, 55.6 us)
Async XLA Ops:
  7.2 69.6 %all-gather.7.cloned.1.call-start = ((), (), s32[]{:S(2)}) async-start(), calls=%async_computation.6 | async-start | bytes 3932160 | tf_op jit(solution)/shard_map/all_gather | solution.py:854
  10.5 230.6 %all-gather.9.cloned.1.call-start = ((), (), s32[]{:S(2)}) async-start(), calls=%async_computation.7 | async-start | bytes 1310720 | tf_op jit(solution)/shard_map/all_gather | solution.py:860
  11.3 313.4 %all-gather.11.cloned.1.call-start = ((), (), s32[]{:S(2)}) async-start(), calls=%async_computation.8 | async-start | bytes 5242880 | tf_op jit(solution)/shard_map/all_gather | solution.py:861
  12.4 7.5 copy-start.32
  12.4 7.6 copy-start.33
  12.5 324.4 %all-gather.13.cloned.1.call-start = ((), (), s32[]{:S(2)}) async-start(), calls=%async_computation.9 | async-start | bytes 5242880 | tf_op jit(solution)/shard_map/all_gather | solution.py:862
  14.9 353.0 %all-gather.15.cloned.1.call-start = ((), (), s32[]{:S(2)}) async-start(), calls=%async_computation.10 | async-start | bytes 2621440 | tf_op jit(solution)/shard_map/all_gather | solution.py:865
  16.1 398.3 %all-gather.17.cloned.1.call-start = ((), (), s32[]{:S(2)}) async-start(), calls=%async_computation.11 | async-start | bytes 2621440 | tf_op jit(solution)/shard_map/all_gather | solution.py:866
  16.1 37.2 %collective-permute-start = (s32[1]{0:T(128)}, s32[1]{0:T(128)}, u32[]{:S(2)}, u32[]{:S(2)}) collective-permute-start(s32[1]{0:T(128)} %param.15), channel_id=1, source_target_pairs={{0,16},{16,0},{1,17},{17,1},{2,18},{18,2},{3,19},{19,3},{4,20},{20... | collective-permute-start | bytes 20 | tf_op jit(solution)/shard_map/ppermute | solution.py:873
  19.2 551.8 %reduce-scatter.7.cloned.1.call-start = ((), (), s32[]{:S(2)}) async-start(), calls=%async_computation.12 | async-start | bytes 2621440 | tf_op jit(solution)/shard_map/reduce_scatter | solution.py:941
  51.5 33.3 %copy-start.13 = (f32[2,256]{1,0:T(2,128)}, f32[2,256]{1,0:T(2,128)S(1)}, u32[]{:S(2)}) copy-start(f32[2,256]{1,0:T(2,128)S(1)} %pad_maximum_fusion.5.gain_ref) | copy-start | bytes 6148
  53.3 31.5 %copy-start.9 = (f32[768,128]{1,0:T(8,128)}, f32[768,128]{1,0:T(8,128)S(1)}, u32[]{:S(2)}) copy-start(f32[768,128]{1,0:T(8,128)S(1)} %get-tuple-element.115.sin_ref) | copy-start | bytes 1179652
  53.3 31.5 %copy-start.11 = (f32[768,128]{1,0:T(8,128)}, f32[768,128]{1,0:T(8,128)S(1)}, u32[]{:S(2)}) copy-start(f32[768,128]{1,0:T(8,128)S(1)} %get-tuple-element.116.cos_ref) | copy-start | bytes 1179652
  84.8 107.4 %copy-start.2 = (f32[1536,768]{1,0:T(8,128)}, f32[1536,768]{1,0:T(8,128)S(1)}, u32[]{:S(2)}) copy-start(f32[1536,768]{1,0:T(8,128)S(1)} %convolution_bitcast_fusion.qkv_ref) | copy-start | bytes 14155780
  247.0 44.6 %copy-start.21 = (bf16[768,512]{1,0:T(8,128)(2,1)S(1)}, bf16[768,512]{1,0:T(8,128)(2,1)}, u32[]{:S(2)}) copy-start(bf16[768,512]{1,0:T(8,128)(2,1)} %x_ref.1) | copy-start | bytes 2359300
  247.0 44.6 %copy-start.30 = (f32[512]{0:T(512)S(1)}, f32[512]{0:T(512)}, u32[]{:S(2)}) copy-start(f32[512]{0:T(512)} %param.25) | copy-start | bytes 6148
  394.7 54.1 %copy-start.4 = (f32[768,256]{1,0:T(8,128)}, f32[768,256]{1,0:T(8,128)S(1)}, u32[]{:S(2)}) copy-start(f32[768,256]{1,0:T(8,128)S(1)} %scatter_mixed_low.1) | copy-start | bytes 2359300
  420.4 20.7 %copy-start.17 = (bf16[768,512]{1,0:T(8,128)(2,1)S(1)}, bf16[768,512]{1,0:T(8,128)(2,1)}, u32[]{:S(2)}) copy-start(bf16[768,512]{1,0:T(8,128)(2,1)} %param.27) | copy-start | bytes 2359300
  420.4 20.7 %copy-start.31 = (f32[512]{0:T(512)S(1)}, f32[512]{0:T(512)}, u32[]{:S(2)}) copy-start(f32[512]{0:T(512)} %param.26) | copy-start | bytes 6148
  441.1 10.2 %copy-start.6 = (f32[768,256]{1,0:T(8,128)}, f32[768,256]{1,0:T(8,128)S(1)}, u32[]{:S(2)}) copy-start(f32[768,256]{1,0:T(8,128)S(1)} %scatter_mixed_high.1) | copy-start | bytes 2359300
  477.6 175.0 %reduce-scatter.9.cloned.1.call-start = ((), (), s32[]{:S(2)}) async-start(), calls=%async_computation.13 | async-start | bytes 2621440 | tf_op jit(solution)/shard_map/reduce_scatter | solution.py:941
  504.1 230.1 %reduce-scatter.11.cloned.1.call-start = ((), (), s32[]{:S(2)}) async-start(), calls=%async_computation.14 | async-start | bytes 5242880 | tf_op jit(solution)/shard_map/reduce_scatter | solution.py:941
  504.1 8.9 copy-start.23
  504.1 8.9 copy-start.36
  504.1 21.9 %slice-start = ((s8[6291456]{0:T(1024)(128)(4,1)}), s8[4194304]{0:T(1024)(128)(4,1)S(1)}, s32[]{:S(2)}) async-start(s8[6291456]{0:T(1024)(128)(4,1)} %bitcast.77), calls=%async_computation.18 | async-start | bytes 8388608
  513.0 13.0 %slice-start.1 = ((s8[6291456]{0:T(1024)(128)(4,1)}), s8[2097152]{0:T(1024)(128)(4,1)S(1)}, s32[]{:S(2)}) async-start(s8[6291456]{0:T(1024)(128)(4,1)} %bitcast.77), calls=%async_computation.19 | async-start | bytes 4194304
  534.6 282.1 %reduce-scatter.13.cloned.1.call-start = ((), (), s32[]{:S(2)}) async-start(), calls=%async_computation.15 | async-start | bytes 5242880 | tf_op jit(solution)/shard_map/reduce_scatter | solution.py:941
  545.9 293.1 %reduce-scatter.15.cloned.1.call-start = ((), (), s32[]{:S(2)}) async-start(), calls=%async_computation.16 | async-start | bytes 1310720 | tf_op jit(solution)/shard_map/reduce_scatter | solution.py:941
  546.5 12.9 %copy-start.34 = (bf16[2048,1024]{1,0:T(8,128)(2,1)S(1)}, bf16[2048,1024]{1,0:T(8,128)(2,1)}, u32[]{:S(2)}) copy-start(bf16[2048,1024]{1,0:T(8,128)(2,1)} %all-gather.13.cloned.1.call-done) | copy-start | bytes 12582916
  546.5 12.9 %copy-start.38 = (bf16[1536,1024]{1,0:T(8,128)(2,1)S(1)}, bf16[1536,1024]{1,0:T(8,128)(2,1)}, u32[]{:S(2)}) copy-start(bf16[1536,1024]{1,0:T(8,128)(2,1)} %get-tuple-element.91) | copy-start | bytes 9437188
  571.0 38.3 %copy-start.5 = (f32[768,256]{1,0:T(8,128)S(1)}, f32[768,256]{1,0:T(8,128)}, u32[]{:S(2)}) copy-start(f32[768,256]{1,0:T(8,128)} %copy-done.4) | copy-start | bytes 2359300
  571.0 38.3 %copy-start.7 = (f32[768,256]{1,0:T(8,128)S(1)}, f32[768,256]{1,0:T(8,128)}, u32[]{:S(2)}) copy-start(f32[768,256]{1,0:T(8,128)} %copy-done.6) | copy-start | bytes 2359300
  571.0 38.3 %copy-start.18 = (bf16[768,512]{1,0:T(8,128)(2,1)S(1)}, bf16[768,512]{1,0:T(8,128)(2,1)}, u32[]{:S(2)}) copy-start(bf16[768,512]{1,0:T(8,128)(2,1)} %param.27) | copy-start | bytes 2359300
  571.0 38.3 %copy-start.22 = (bf16[768,512]{1,0:T(8,128)(2,1)S(1)}, bf16[768,512]{1,0:T(8,128)(2,1)}, u32[]{:S(2)}) copy-start(bf16[768,512]{1,0:T(8,128)(2,1)} %x_ref.1) | copy-start | bytes 2359300
  620.6 32.0 %copy-start.26 = (bf16[1024,256]{1,0:T(8,128)(2,1)S(1)}, bf16[1024,256]{1,0:T(8,128)(2,1)}, u32[]{:S(2)}) copy-start(bf16[1024,256]{1,0:T(8,128)(2,1)} %reduce-scatter.7.cloned.1.call-done) | copy-start | bytes 1572868
  654.7 51.5 %copy-start.20 = (bf16[1536,256]{1,0:T(8,128)(2,1)S(1)}, bf16[1536,256]{1,0:T(8,128)(2,1)}, u32[]{:S(2)}) copy-start(bf16[1536,256]{1,0:T(8,128)(2,1)} %turn_attn.1) | copy-start | bytes 2359300
  654.7 51.5 %collective-permute-start.1 = (bf16[1024,512]{1,0:T(8,128)(2,1)}, bf16[1024,512]{1,0:T(8,128)(2,1)}, u32[]{:S(2)}, u32[]{:S(2)}) collective-permute-start(bf16[1024,512]{1,0:T(8,128)(2,1)} %pad_maximum_fusion.1), channel_id=1, source_target_pairs={{0,16},{16,0},{1,17},{17,1},{2,18},{18,2},{3,19},{19,3},{4,20},{20... | collective-permute-start | bytes 3145736 | tf_op jit(solution)/shard_map/ppermute | solution.py:938
  711.7 23.6 %copy-start.10 = (f32[768,128]{1,0:T(8,128)S(1)}, f32[768,128]{1,0:T(8,128)}, u32[]{:S(2)}) copy-start(f32[768,128]{1,0:T(8,128)} %copy-done.9) | copy-start | bytes 1179652
  711.7 23.6 %copy-start.12 = (f32[768,128]{1,0:T(8,128)S(1)}, f32[768,128]{1,0:T(8,128)}, u32[]{:S(2)}) copy-start(f32[768,128]{1,0:T(8,128)} %copy-done.11) | copy-start | bytes 1179652
  711.7 23.6 %copy-start.14 = (f32[2,256]{1,0:T(2,128)S(1)}, f32[2,256]{1,0:T(2,128)}, u32[]{:S(2)}) copy-start(f32[2,256]{1,0:T(2,128)} %copy-done.13) | copy-start | bytes 6148
  734.1 82.6 %collective-permute-start.2 = (bf16[512,1024]{1,0:T(8,128)(2,1)}, bf16[512,1024]{1,0:T(8,128)(2,1)}, u32[]{:S(2)}, u32[]{:S(2)}) collective-permute-start(bf16[512,1024]{1,0:T(8,128)(2,1)} %reduce-scatter.11.cloned.1.call-done), channel_id=1, source_target_pairs={{0,16},{16,0},{1,17},{17,1},{2,18},{18,2},{3,19},{19,3},{4,20},{20... | collective-permute-start | bytes 3145736 | tf_op jit(solution)/shard_map/ppermute | solution.py:938
  735.3 175.3 %reduce-scatter.17.cloned.1.call-start = ((), (), s32[]{:S(2)}) async-start(), calls=%async_computation.17 | async-start | bytes 3932160 | tf_op jit(solution)/shard_map/reduce_scatter | solution.py:941
  839.0 33.8 %collective-permute-start.4 = (bf16[256,512]{1,0:T(8,128)(2,1)}, bf16[256,512]{1,0:T(8,128)(2,1)S(1)}, u32[]{:S(2)}, u32[]{:S(2)}) collective-permute-start(bf16[256,512]{1,0:T(8,128)(2,1)} %reduce-scatter.15.cloned.1.call-done), channel_id=1, source_target_pairs={{0,16},{16,0},{1,17},{17,1},{2,18},{18,2},{3,19},{19,3},{4,20},{20... | collective-permute-start | bytes 786440 | tf_op jit(solution)/shard_map/ppermute | solution.py:938
  840.2 33.7 %collective-permute-start.3 = (bf16[512,1024]{1,0:T(8,128)(2,1)}, bf16[512,1024]{1,0:T(8,128)(2,1)}, u32[]{:S(2)}, u32[]{:S(2)}) collective-permute-start(bf16[512,1024]{1,0:T(8,128)(2,1)} %reduce-scatter.13.cloned.1.call-done), channel_id=1, source_target_pairs={{0,16},{16,0},{1,17},{17,1},{2,18},{18,2},{3,19},{19,3},{4,20},{20... | collective-permute-start | bytes 3145736 | tf_op jit(solution)/shard_map/ppermute | solution.py:938
  842.8 30.0 %copy-start.27 = (bf16[256,512]{1,0:T(8,128)(2,1)S(1)}, bf16[256,512]{1,0:T(8,128)(2,1)}, u32[]{:S(2)}) copy-start(bf16[256,512]{1,0:T(8,128)(2,1)} %reduce-scatter.15.cloned.1.call-done) | copy-start | bytes 786436
  910.7 19.3 %collective-permute-start.5 = (bf16[512,768]{0,1:T(8,128)(2,1)}, bf16[512,768]{0,1:T(8,128)(2,1)S(1)}, u32[]{:S(2)}, u32[]{:S(2)}) collective-permute-start(bf16[512,768]{0,1:T(8,128)(2,1)} %reduce-scatter.17.cloned.1.call-done), channel_id=1, source_target_pairs={{0,16},{16,0},{1,17},{17,1},{2,18},{18,2},{3,19},{19,3},{4,20},{20... | collective-permute-start | bytes 2359304 | tf_op jit(solution)/shard_map/ppermute | solution.py:938
  915.7 14.3 %copy-start.24 = (bf16[512,768]{0,1:T(8,128)(2,1)S(1)}, bf16[512,768]{0,1:T(8,128)(2,1)}, u32[]{:S(2)}) copy-start(bf16[512,768]{0,1:T(8,128)(2,1)} %reduce-scatter.17.cloned.1.call-done) | copy-start | bytes 2359300
  932.3 5.0 copy-start.1
  (11 other events, 27.4 us)
Sparse Core Ops, SparseCore 0:
  10.6 66.1 all-gather.6
  78.9 51.7 all-gather.8
  132.8 107.4 all-gather.10
  242.3 78.7 all-gather.12
  323.1 44.7 all-gather.14
  369.9 44.4 all-gather.16
  477.7 40.9 reduce-scatter.6
  521.0 42.8 reduce-scatter.8
  566.7 75.9 reduce-scatter.10
  645.4 89.9 reduce-scatter.12
  738.3 47.4 reduce-scatter.14
  826.1 58.9 reduce-scatter.16

commit v7 on v6

--- a/solution.py
+++ b/solution.py
@@ -858,8 +858,11 @@
         tiled=True,
     )
     out_weight = lax.all_gather(y_half(w_out, 0), "row", axis=1, tiled=True)
-    gate_weight = lax.all_gather(y_half(w_gate, 1), "row", axis=0, tiled=True)
-    up_weight = lax.all_gather(y_half(w_up, 1), "row", axis=0, tiled=True)
+    gate_up_weight = lax.all_gather(
+        jnp.concatenate([y_half(w_gate, 1), y_half(w_up, 1)], axis=1), "row", axis=0, tiled=True
+    )
+    hidden_part = gate_up_weight.shape[1] // 2
+    gate_weight, up_weight = gate_up_weight[:, :hidden_part], gate_up_weight[:, hidden_part:]
     down_half = y_half(w_down, 0)
     split = down_half.shape[1] // 2
     low_weight = lax.all_gather(down_half[:, :split], "row", axis=1, tiled=True)
@@ -984,9 +987,19 @@
     other_up = from_twin(up_piece)
     qkv_raw = (contract_first(tokens_wide, d_qkv) * factor).astype(bf16)
     projected = contract_last(after(d_qkv, qkv_raw), qkv_weight).astype(bf16)
-    projected, out_piece = lax.optimization_barrier((projected, over_dp(out_piece)))
+    qkv_piece = over_dp(reduce_rows(qkv_raw, 0))
+    scattered, other_down, other_gate, other_up, out_piece, gain_sums = lax.optimization_barrier(
+        (
+            scatter_wide(projected, False, 16, "scatter_projected"),
+            other_down,
+            other_gate,
+            other_up,
+            over_dp(out_piece),
+            gain_sums,
+        )
+    )
     other_out = from_twin(out_piece)
-    qkv_piece = over_dp(reduce_rows(qkv_raw, 0))
+    input_grad = d_resid + scattered
 
     def spread(half):
         return lax.dynamic_update_slice_in_dim(jnp.zeros((feat_part,), f32), half, y * half_feat, 0)
@@ -998,11 +1011,8 @@
             15,
         )
     )
-    projected = after(projected, gains, other_up, other_out)
-    scattered, qkv_piece = lax.optimization_barrier(
-        (scatter_wide(projected, False, 16, "scatter_projected"), qkv_piece)
-    )
-    input_grad = d_resid + scattered
+
+    gains, qkv_piece = lax.optimization_barrier((gains, qkv_piece))
 
     def whole(piece, other, axis):
         return two_sides(piece, other, y, axis).astype(f32)

time: 955 us -> 930 us (0.974)
  waiting for transfers between devices: 72.5 us -> 43.9 us
    all_gather x1, waiting for transfers between devices: 17.6 us -> 0.01 us  [per_device(): low_weight = lax.all_gather(down_half[:, :split], 'row', axis=1, tiled=True)]
    pallas_call x1, Pallas kernels: 25.4 us -> 9.41 us  [gain_total(): pl.pallas_call(gain_kernel, name='total_gains', out_shape=jax.ShapeDtypeS...]
    pallas_call x2, Pallas kernels: 77.2 us -> 89.9 us  [turn(): pl.pallas_call(functools.partial(turn_kernel, back, tok, heads), name=nam...]
  transfers between devices with their start and end apart: 18 -> 17, of which waited for: 4 -> 3; matrix products, arithmetic and copies ran while one was open for 19% -> 20% of each run, Pallas kernels for 62% -> 64%
where the time goes in v7:
time: 930 us; the launch traced here: 919 us
  Pallas kernels  629 us (68%)
  matrix products  157 us (17%)
  waiting for transfers between devices  43.9 us (5%)
  other arithmetic  38.3 us (4%)
  local copies, waits for them, and re-layouts  26.2 us (3%)
  between operations  15.5 us (2%)
    pallas_call x5, Pallas kernels, scatter_wide(): pl.pallas_call(functools.partial(scatter_kernel, pair, rider), name=name,...  157 us
    pallas_call x5, Pallas kernels, gather_wide(): pl.pallas_call(functools.partial(gather_kernel, pair), name=name, out_sha...  132 us
    pallas_call x1, Pallas kernels, front(): pl.pallas_call(functools.partial(front_kernel, width), name='front', out_...  104 us
    pallas_call x2, Pallas kernels, turn(): pl.pallas_call(functools.partial(turn_kernel, back, tok, heads), name=nam...  89.9 us
    pallas_call x1, Pallas kernels, rear(): pl.pallas_call(functools.partial(rear_kernel, width), name='rear', out_sh...  72.4 us
    dot_general x6, matrix products, contract_last(): lax.dot_general(left, right, (((1,), (1,)), ((), ())), preferred_element_...  60.6 us
    dot_general x6, matrix products, contract_first(): lax.dot_general(left, right, (((0,), (0,)), ((), ())), preferred_element_...  50.2 us
    dot_general x6, matrix products, matmul(): return jnp.dot(left, right, preferred_element_type=f32)  46.5 us
  transfers between devices with their start and end apart: 17, of which 3 were waited for; matrix products, arithmetic and copies ran while one was open for 20% of the time, Pallas kernels for 64%

profile of v7, /device:TPU:0, one launch (start us, length us, event | category | flops | bytes accessed | tf_op | source)
XLA Modules:
  0.0 918.9 jit_solution(733963242171741171)
XLA Ops:
  16.1 3.1 collective-permute-start
  20.1 31.4 %gather_tokens.1 = bf16[1536,2048]{1,0:T(8,128)(2,1)} custom-call(bf16[768,512]{1,0:T(8,128)(2,1)} %x_ref.1), custom_call_target="tpu_custom_call" | custom-call | bytes 1000 | tf_op jit(solution)/shard_map/gather_tokens/pallas_call | solution.py:155
  54.6 22.0 %all-gather.6.cloned.1.call-done = bf16[2048,768]{1,0:T(8,128)(2,1)} async-done(((bf16[512,768]{1,0:T(8,128)(2,1)}), bf16[2048,768]{1,0:T(8,128)(2,1)}) %all-gather.6.cloned.1.call-update) | async-done | bytes 3145744 | tf_op jit(solution)/shard_map/all_gather | solution.py:854
  76.6 8.1 convolution_bitcast_fusion.qkv_ref
  84.7 104.3 %front.1 = (bf16[4,3,768,128]{3,2,1,0:T(8,128)(2,1)S(1)}, f32[2,1536]{1,0:T(2,128)S(1)}) custom-call(f32[1536,768]{1,0:T(8,128)S(1)} %convolution_bitcast_fusion.qkv_ref, f32[768,128]{1,0:T(8,128)S(1)} %get-tuple-element.122.cos_ref, f32[768,128]{1,0:T(8,128)S(1)} %get-tuple-element.121.sin_ref, f32[2,256]{1,0:T(2,128)S(1)} %pad_maximum_fusion.6.gain_ref), custom_call_target="tpu_custom_call" | custom-call | bytes 1000 | tf_op jit(solution)/shard_map/front/pallas_call | solution.py:558
  190.5 20.5 %attend.1 = (bf16[3072,128]{1,0:T(8,128)(2,1)}, f32[3072,128]{1,0:T(8,128)}, f32[8,3072]{1,0:T(8,128)}) custom-call(s32[1]{0:T(128)} %dynamic_slice.48.len_ref, bf16[3072,128]{1,0:T(8,128)(2,1)} %bitcast.67, bf16[3072,128]{1,0:T(8,128)(2,1)} %bitcast.65, bf16[3072,128]{1,0:T(8,128)(2,1)} %bitcast.63), custom_call_target="tpu_custom_call" | custom-call | bytes 1000 | tf_op jit(solution)/shard_map/attend/pallas_call | solution.py:738
  211.0 45.5 %turn_attn.1 = bf16[1536,256]{1,0:T(8,128)(2,1)} custom-call(bf16[3072,128]{1,0:T(8,128)(2,1)} %get-tuple-element.47.x_ref), custom_call_target="tpu_custom_call" | custom-call | bytes 1000 | tf_op jit(solution)/shard_map/turn_attn/pallas_call | solution.py:459
  256.5 5.9 convolution_convert_fusion.1.p_ref
  262.4 37.7 %scatter_branch.1 = f32[768,512]{1,0:T(8,128)S(1)} custom-call(bf16[1536,2048]{1,0:T(8,128)(2,1)} %convolution_convert_fusion.1.p_ref), custom_call_target="tpu_custom_call" | custom-call | bytes 1000 | tf_op jit(solution)/shard_map/scatter_branch/pallas_call | solution.py:305
  300.9 4.9 total_branch.1
  307.7 31.9 %gather_resid.1 = bf16[1536,2048]{1,0:T(8,128)(2,1)} custom-call(bf16[768,512]{1,0:T(8,128)(2,1)} %fusion.11.x_ref), custom_call_target="tpu_custom_call" | custom-call | bytes 1000 | tf_op jit(solution)/shard_map/gather_resid/pallas_call | solution.py:155
  339.7 10.6 %fusion.5 = f32[1536,1024]{1,0:T(8,128)S(1)} fusion(bf16[1536,2048]{1,0:T(8,128)(2,1)} %gather_resid.1, bf16[2048,2048]{1,0:T(8,128)(2,1)} %all-gather.10.cloned.1.call-done), kind=kOutput, calls=%fused_computation.21 | convolution fusion | flops 6442450944 | bytes 16777216 | tf_op jit(solution)/shard_map/dot_general | solution.py:31
  350.3 2.7 copy-done.37
  353.0 9.9 %multiply_convert_fusion.5 = (bf16[1536,1024]{1,0:T(8,128)(2,1)}, f32[1536,1024]{1,0:T(8,128)}) fusion(f32[1536,1024]{1,0:T(8,128)S(1)} %fusion.5, bf16[1536,2048]{1,0:T(8,128)(2,1)S(1)} %copy-done.22, bf16[2048,2048]{1,0:T(8,128)(2,1)S(1)} %copy-done.35), kind=kOutput, calls=%fused_computation.8 | convolution fusion | flops 6451888128 | bytes 26214400 | tf_op jit(solution)/shard_map/dot_general | solution.py:31
  362.9 6.1 convolution_convert_fusion.3.p_ref
  369.0 20.7 %scatter_mixed_low.1 = f32[768,256]{1,0:T(8,128)S(1)} custom-call(bf16[1536,1024]{1,0:T(8,128)(2,1)S(1)} %convolution_convert_fusion.3.p_ref), custom_call_target="tpu_custom_call" | custom-call | bytes 1000 | tf_op jit(solution)/shard_map/scatter_mixed_low/pallas_call | solution.py:305
  389.7 12.2 %all-gather.14.cloned.1.call-done = bf16[1024,1024]{1,0:T(8,128)(2,1)} async-done(((bf16[1024,256]{1,0:T(8,128)(2,1)}), bf16[1024,1024]{1,0:T(8,128)(2,1)}) %all-gather.14.cloned.1.call-update) | async-done | bytes 2097168 | tf_op jit(solution)/shard_map/all_gather | solution.py:869
  401.9 6.0 convolution_convert_fusion.2.p_ref
  408.0 20.7 %scatter_mixed_high.1 = f32[768,256]{1,0:T(8,128)S(1)} custom-call(bf16[1536,1024]{1,0:T(8,128)(2,1)S(1)} %convolution_convert_fusion.2.p_ref), custom_call_target="tpu_custom_call" | custom-call | bytes 1000 | tf_op jit(solution)/shard_map/scatter_mixed_high/pallas_call | solution.py:305
  429.9 5.0 total_mixed.1
  438.8 18.4 %gather_d_mixed_low.1 = bf16[1536,1024]{1,0:T(8,128)(2,1)} custom-call(bf16[768,256]{1,0:T(8,128)(2,1)} %get-tuple-element.118.x_ref), custom_call_target="tpu_custom_call" | custom-call | bytes 1000 | tf_op jit(solution)/shard_map/gather_d_mixed_low/pallas_call | solution.py:155
  457.3 7.9 multiply_convert_fusion.7
  465.2 18.7 %gather_d_mixed_high.1 = bf16[1536,1024]{1,0:T(8,128)(2,1)} custom-call(bf16[768,256]{1,0:T(8,128)(2,1)} %get-tuple-element.49.x_ref), custom_call_target="tpu_custom_call" | custom-call | bytes 1000 | tf_op jit(solution)/shard_map/gather_d_mixed_high/pallas_call | solution.py:155
  483.9 7.7 multiply_convert_fusion.6
  491.7 8.8 fusion.20
  500.5 11.3 %multiply_convert_fusion.3 = (bf16[1536,1024]{1,0:T(8,128)(2,1)}, bf16[1536,1024]{1,0:T(8,128)(2,1)S(1)}) fusion(f32[1536,1024]{1,0:T(8,128)} %copy-done.37, f32[1536,1024]{1,0:T(8,128)} %get-tuple-element.130, f32[1536,1024]{1,0:T(8,128)} %fusion.20, bf16[1536,1024]{1,0:T(8,128)(2,1)S(1)} %copy-done.23, bf16[1024,1024]{1,0:T(8,128)(2,1)S(1)} %copy-done.36), kind=kOutput, calls=%fused_computation.6 | convolution fusion | flops 3243245568 | bytes 30408704 | tf_op jit(solution)/shard_map/dot_general | solution.py:39
  513.5 8.5 multiply_convert_fusion.1
  522.2 11.2 %multiply_convert_fusion = bf16[2048,1024]{1,0:T(8,128)(2,1)} fusion(bf16[1536,2048]{1,0:T(8,128)(2,1)} %gather_resid.1, bf16[1536,1024]{1,0:T(8,128)(2,1)} %get-tuple-element.97), kind=kOutput, calls=%fused_computation.1 | convolution fusion | flops 6446645248 | bytes 13631488 | tf_op jit(solution)/shard_map/dot_general | solution.py:35
  534.1 12.9 %fusion.3 = f32[1536,2048]{1,0:T(8,128)} fusion(bf16[1536,1024]{1,0:T(8,128)(2,1)} %copy-done.38, bf16[2048,2048]{1,0:T(8,128)(2,1)} %all-gather.10.cloned.1.call-done), kind=kOutput, calls=%fused_computation.19 | convolution fusion | flops 6442450944 | bytes 19922944 | tf_op jit(solution)/shard_map/dot_general | solution.py:39
  547.0 12.6 %add_convert_fusion.p_ref = bf16[1536,2048]{1,0:T(8,128)(2,1)} fusion(f32[1536,2048]{1,0:T(8,128)} %fusion.3, bf16[1536,1024]{1,0:T(8,128)(2,1)S(1)} %copy-done.39, bf16[2048,2048]{1,0:T(8,128)(2,1)} %all-gather.10.cloned.1.call-done), kind=kOutput, calls=%fused_computation | convolution fusion | flops 6448742400 | bytes 26214400 | tf_op jit(solution)/shard_map/dot_general | solution.py:39
  559.6 37.9 %scatter_d_resid.1 = f32[768,512]{1,0:T(8,128)S(1)} custom-call(bf16[1536,2048]{1,0:T(8,128)(2,1)} %add_convert_fusion.p_ref), custom_call_target="tpu_custom_call" | custom-call | bytes 1000 | tf_op jit(solution)/shard_map/scatter_d_resid/pallas_call | solution.py:305
  597.6 3.1 multiply_reduce_fusion.1
  600.8 4.9 total_d_resid.1
  608.9 31.9 %gather_d_branch.1 = bf16[1536,2048]{1,0:T(8,128)(2,1)} custom-call(bf16[768,512]{1,0:T(8,128)(2,1)} %subtract_convert_fusion.x_ref), custom_call_target="tpu_custom_call" | custom-call | bytes 1000 | tf_op jit(solution)/shard_map/gather_d_branch/pallas_call | solution.py:155
  644.2 5.8 convolution_convert_fusion.4.x_ref
  650.0 44.4 %turn_d_attn.1.do_ref = bf16[3072,128]{1,0:T(8,128)(2,1)} custom-call(bf16[1536,256]{1,0:T(8,128)(2,1)} %convolution_convert_fusion.4.x_ref), custom_call_target="tpu_custom_call" | custom-call | bytes 1000 | tf_op jit(solution)/shard_map/turn_d_attn/pallas_call | solution.py:459
  694.4 5.6 fusion.8
  699.9 27.5 %attend_back.1.d_ref = bf16[3,3072,128]{2,1,0:T(8,128)(2,1)} custom-call(s32[1]{0:T(128)} %dynamic_slice.48.len_ref, bf16[3072,128]{1,0:T(8,128)(2,1)} %bitcast.68, bf16[3072,128]{1,0:T(8,128)(2,1)} %bitcast.66, bf16[3072,128]{1,0:T(8,128)(2,1)} %bitcast.64, bf16[3072,128]{1,0:T(8,128)(2,1)} %turn_d_attn.1.do_ref, f32[3072,128]{1,0:T(8,128)} %get-tuple-element.58.o_ref, ...), custom_call_target="tpu_custom_call" | custom-call | bytes 1000 | tf_op jit(solution)/shard_map/attend_back/pallas_call | solution.py:812
  732.7 72.4 %rear.1 = (bf16[1536,768]{1,0:T(8,128)(2,1)S(1)}, f32[2,256]{1,0:T(2,128)S(1)}) custom-call(bf16[3,3072,128]{2,1,0:T(8,128)(2,1)S(1)} %copy-done.8, f32[1536,768]{1,0:T(8,128)S(1)} %copy-done.3, f32[768,128]{1,0:T(8,128)S(1)} %copy-done.12, f32[768,128]{1,0:T(8,128)S(1)} %copy-done.10, f32[2,256]{1,0:T(2,128)S(1)} %copy-done.14, ...), custom_call_target="tpu_custom_call" | custom-call | bytes 1000 | tf_op jit(solution)/shard_map/rear/pallas_call | solution.py:667
  806.5 9.3 %fusion.7 = bf16[2048,768]{0,1:T(8,128)(2,1)} fusion(bf16[1536,768]{1,0:T(8,128)(2,1)} %copy-done.15, bf16[1536,2048]{1,0:T(8,128)(2,1)} %gather_tokens.1), kind=kOutput, calls=%fused_computation.23 | convolution fusion | flops 4834983936 | bytes 11796480 | tf_op jit(solution)/shard_map/dot_general | solution.py:35
  817.1 9.2 convolution_convert_fusion.p_ref
  826.3 40.3 %scatter_projected.1 = f32[768,512]{1,0:T(8,128)S(1)} custom-call(bf16[1536,2048]{1,0:T(8,128)(2,1)} %convolution_convert_fusion.p_ref), custom_call_target="tpu_custom_call" | custom-call | bytes 1000 | tf_op jit(solution)/shard_map/scatter_projected/pallas_call | solution.py:305
  867.3 9.4 %total_gains.1 = f32[16,128]{1,0:T(8,128)} custom-call(f32[16,128]{1,0:T(8,128)} %mul.277.v_ref), custom_call_target="tpu_custom_call" | custom-call | tf_op jit(solution)/shard_map/total_gains/pallas_call | solution.py:408
  878.6 3.0 broadcast_select_fusion.5
  885.0 2.6 maximum_convert_fusion.1
  887.5 2.6 maximum_convert_fusion.2
  892.4 4.2 maximum_convert_fusion
  898.4 9.3 %collective-permute-done.4 = bf16[512,768]{0,1:T(8,128)(2,1)S(1)} collective-permute-done((bf16[512,768]{0,1:T(8,128)(2,1)}, bf16[512,768]{0,1:T(8,128)(2,1)S(1)}, u32[]{:S(2)}, u32[]{:S(2)}) %collective-permute-start.4) | collective-permute-done | bytes 786464 | tf_op jit(solution)/shard_map/ppermute | solution.py:941
  (180 shorter events, 52.8 us)
Async XLA Ops:
  7.2 3.9 copy-start.25
  7.2 69.4 %all-gather.6.cloned.1.call-start = ((), (), s32[]{:S(2)}) async-start(), calls=%async_computation.6 | async-start | bytes 3932160 | tf_op jit(solution)/shard_map/all_gather | solution.py:854
  10.3 246.2 %all-gather.8.cloned.1.call-start = ((), (), s32[]{:S(2)}) async-start(), calls=%async_computation.7 | async-start | bytes 1310720 | tf_op jit(solution)/shard_map/all_gather | solution.py:860
  11.1 328.6 %all-gather.10.cloned.1.call-start = ((), (), s32[]{:S(2)}) async-start(), calls=%async_computation.8 | async-start | bytes 10485760 | tf_op jit(solution)/shard_map/all_gather | solution.py:861
  14.1 5.8 copy-start.33
  14.1 5.9 copy-start.34
  14.1 348.7 %all-gather.12.cloned.1.call-start = ((), (), s32[]{:S(2)}) async-start(), calls=%async_computation.9 | async-start | bytes 2621440 | tf_op jit(solution)/shard_map/all_gather | solution.py:868
  16.0 385.9 %all-gather.14.cloned.1.call-start = ((), (), s32[]{:S(2)}) async-start(), calls=%async_computation.10 | async-start | bytes 2621440 | tf_op jit(solution)/shard_map/all_gather | solution.py:869
  16.1 37.3 %collective-permute-start = (s32[1]{0:T(128)}, s32[1]{0:T(128)}, u32[]{:S(2)}, u32[]{:S(2)}) collective-permute-start(s32[1]{0:T(128)} %param.15), channel_id=1, source_target_pairs={{0,16},{16,0},{1,17},{17,1},{2,18},{18,2},{3,19},{19,3},{4,20},{20... | collective-permute-start | bytes 20 | tf_op jit(solution)/shard_map/ppermute | solution.py:876
  19.1 540.5 %reduce-scatter.7.cloned.1.call-start = ((), (), s32[]{:S(2)}) async-start(), calls=%async_computation.11 | async-start | bytes 2621440 | tf_op jit(solution)/shard_map/reduce_scatter | solution.py:944
  51.5 33.2 %copy-start.13 = (f32[2,256]{1,0:T(2,128)}, f32[2,256]{1,0:T(2,128)S(1)}, u32[]{:S(2)}) copy-start(f32[2,256]{1,0:T(2,128)S(1)} %pad_maximum_fusion.6.gain_ref) | copy-start | bytes 6148
  53.3 31.4 %copy-start.9 = (f32[768,128]{1,0:T(8,128)}, f32[768,128]{1,0:T(8,128)S(1)}, u32[]{:S(2)}) copy-start(f32[768,128]{1,0:T(8,128)S(1)} %get-tuple-element.121.sin_ref) | copy-start | bytes 1179652
  53.3 31.4 %copy-start.11 = (f32[768,128]{1,0:T(8,128)}, f32[768,128]{1,0:T(8,128)S(1)}, u32[]{:S(2)}) copy-start(f32[768,128]{1,0:T(8,128)S(1)} %get-tuple-element.122.cos_ref) | copy-start | bytes 1179652
  84.7 105.8 %copy-start.2 = (f32[1536,768]{1,0:T(8,128)}, f32[1536,768]{1,0:T(8,128)S(1)}, u32[]{:S(2)}) copy-start(f32[1536,768]{1,0:T(8,128)S(1)} %convolution_bitcast_fusion.qkv_ref) | copy-start | bytes 14155780
  262.4 44.1 %copy-start.20 = (bf16[768,512]{1,0:T(8,128)(2,1)S(1)}, bf16[768,512]{1,0:T(8,128)(2,1)}, u32[]{:S(2)}) copy-start(bf16[768,512]{1,0:T(8,128)(2,1)} %x_ref.1) | copy-start | bytes 2359300
  262.4 44.1 %copy-start.31 = (f32[512]{0:T(512)S(1)}, f32[512]{0:T(512)}, u32[]{:S(2)}) copy-start(f32[512]{0:T(512)} %param.25) | copy-start | bytes 6148
  339.7 13.3 %copy-start.22 = (bf16[1536,2048]{1,0:T(8,128)(2,1)S(1)}, bf16[1536,2048]{1,0:T(8,128)(2,1)}, u32[]{:S(2)}) copy-start(bf16[1536,2048]{1,0:T(8,128)(2,1)} %gather_resid.1) | copy-start | bytes 18874372
  339.7 13.3 %copy-start.35 = (bf16[2048,2048]{1,0:T(8,128)(2,1)S(1)}, bf16[2048,2048]{1,0:T(8,128)(2,1)}, u32[]{:S(2)}) copy-start(bf16[2048,2048]{1,0:T(8,128)(2,1)} %all-gather.10.cloned.1.call-done) | copy-start | bytes 25165828
  389.7 46.6 %copy-start.4 = (f32[768,256]{1,0:T(8,128)}, f32[768,256]{1,0:T(8,128)S(1)}, u32[]{:S(2)}) copy-start(f32[768,256]{1,0:T(8,128)S(1)} %scatter_mixed_low.1) | copy-start | bytes 2359300
  407.9 20.7 %copy-start.16 = (bf16[768,512]{1,0:T(8,128)(2,1)S(1)}, bf16[768,512]{1,0:T(8,128)(2,1)}, u32[]{:S(2)}) copy-start(bf16[768,512]{1,0:T(8,128)(2,1)} %param.27) | copy-start | bytes 2359300
  407.9 20.7 %copy-start.32 = (f32[512]{0:T(512)S(1)}, f32[512]{0:T(512)}, u32[]{:S(2)}) copy-start(f32[512]{0:T(512)} %param.26) | copy-start | bytes 6148
  428.7 10.2 %copy-start.6 = (f32[768,256]{1,0:T(8,128)}, f32[768,256]{1,0:T(8,128)S(1)}, u32[]{:S(2)}) copy-start(f32[768,256]{1,0:T(8,128)S(1)} %scatter_mixed_high.1) | copy-start | bytes 2359300
  465.1 175.7 %reduce-scatter.9.cloned.1.call-start = ((), (), s32[]{:S(2)}) async-start(), calls=%async_computation.12 | async-start | bytes 2621440 | tf_op jit(solution)/shard_map/reduce_scatter | solution.py:944
  491.6 235.9 %reduce-scatter.11.cloned.1.call-start = ((), (), s32[]{:S(2)}) async-start(), calls=%async_computation.13 | async-start | bytes 5242880 | tf_op jit(solution)/shard_map/reduce_scatter | solution.py:944
  491.7 8.8 copy-start.23
  491.7 8.8 copy-start.36
  491.7 21.9 %slice-start = ((s8[6291456]{0:T(1024)(128)(4,1)}), s8[4194304]{0:T(1024)(128)(4,1)S(1)}, s32[]{:S(2)}) async-start(s8[6291456]{0:T(1024)(128)(4,1)} %bitcast.69), calls=%async_computation.17 | async-start | bytes 8388608
  500.5 13.0 %slice-start.1 = ((s8[6291456]{0:T(1024)(128)(4,1)}), s8[2097152]{0:T(1024)(128)(4,1)S(1)}, s32[]{:S(2)}) async-start(s8[6291456]{0:T(1024)(128)(4,1)} %bitcast.69), calls=%async_computation.18 | async-start | bytes 4194304
  522.1 284.4 %reduce-scatter.13.cloned.1.call-start = ((), (), s32[]{:S(2)}) async-start(), calls=%async_computation.14 | async-start | bytes 5242880 | tf_op jit(solution)/shard_map/reduce_scatter | solution.py:944
  533.4 333.2 %reduce-scatter.15.cloned.1.call-start = ((), (), s32[]{:S(2)}) async-start(), calls=%async_computation.15 | async-start | bytes 1310720 | tf_op jit(solution)/shard_map/reduce_scatter | solution.py:944
  534.1 12.9 %copy-start.39 = (bf16[1536,1024]{1,0:T(8,128)(2,1)S(1)}, bf16[1536,1024]{1,0:T(8,128)(2,1)}, u32[]{:S(2)}) copy-start(bf16[1536,1024]{1,0:T(8,128)(2,1)} %get-tuple-element.97) | copy-start | bytes 9437188
  559.6 38.0 %copy-start.5 = (f32[768,256]{1,0:T(8,128)S(1)}, f32[768,256]{1,0:T(8,128)}, u32[]{:S(2)}) copy-start(f32[768,256]{1,0:T(8,128)} %copy-done.4) | copy-start | bytes 2359300
  559.6 38.0 %copy-start.7 = (f32[768,256]{1,0:T(8,128)S(1)}, f32[768,256]{1,0:T(8,128)}, u32[]{:S(2)}) copy-start(f32[768,256]{1,0:T(8,128)} %copy-done.6) | copy-start | bytes 2359300
  559.6 38.0 %copy-start.17 = (bf16[768,512]{1,0:T(8,128)(2,1)S(1)}, bf16[768,512]{1,0:T(8,128)(2,1)}, u32[]{:S(2)}) copy-start(bf16[768,512]{1,0:T(8,128)(2,1)} %param.27) | copy-start | bytes 2359300
  559.6 38.0 %copy-start.21 = (bf16[768,512]{1,0:T(8,128)(2,1)S(1)}, bf16[768,512]{1,0:T(8,128)(2,1)}, u32[]{:S(2)}) copy-start(bf16[768,512]{1,0:T(8,128)(2,1)} %x_ref.1) | copy-start | bytes 2359300
  608.9 32.0 %copy-start.27 = (bf16[1024,256]{1,0:T(8,128)(2,1)S(1)}, bf16[1024,256]{1,0:T(8,128)(2,1)}, u32[]{:S(2)}) copy-start(bf16[1024,256]{1,0:T(8,128)(2,1)} %reduce-scatter.7.cloned.1.call-done) | copy-start | bytes 1572868
  643.0 51.4 %copy-start.19 = (bf16[1536,256]{1,0:T(8,128)(2,1)S(1)}, bf16[1536,256]{1,0:T(8,128)(2,1)}, u32[]{:S(2)}) copy-start(bf16[1536,256]{1,0:T(8,128)(2,1)} %turn_attn.1) | copy-start | bytes 2359300
  643.0 51.4 %collective-permute-start.1 = (bf16[1024,512]{1,0:T(8,128)(2,1)}, bf16[1024,512]{1,0:T(8,128)(2,1)}, u32[]{:S(2)}, u32[]{:S(2)}) collective-permute-start(bf16[1024,512]{1,0:T(8,128)(2,1)} %pad_maximum_fusion.2), channel_id=1, source_target_pairs={{0,16},{16,0},{1,17},{17,1},{2,18},{18,2},{3,19},{19,3},{4,20},{20... | collective-permute-start | bytes 3145736 | tf_op jit(solution)/shard_map/ppermute | solution.py:941
  699.9 28.7 %copy-start.10 = (f32[768,128]{1,0:T(8,128)S(1)}, f32[768,128]{1,0:T(8,128)}, u32[]{:S(2)}) copy-start(f32[768,128]{1,0:T(8,128)} %copy-done.9) | copy-start | bytes 1179652
  699.9 28.8 %copy-start.12 = (f32[768,128]{1,0:T(8,128)S(1)}, f32[768,128]{1,0:T(8,128)}, u32[]{:S(2)}) copy-start(f32[768,128]{1,0:T(8,128)} %copy-done.11) | copy-start | bytes 1179652
  699.9 28.8 %copy-start.14 = (f32[2,256]{1,0:T(2,128)S(1)}, f32[2,256]{1,0:T(2,128)}, u32[]{:S(2)}) copy-start(f32[2,256]{1,0:T(2,128)} %copy-done.13) | copy-start | bytes 6148
  727.5 79.1 %collective-permute-start.2 = (bf16[512,1024]{1,0:T(8,128)(2,1)}, bf16[512,1024]{1,0:T(8,128)(2,1)}, u32[]{:S(2)}, u32[]{:S(2)}) collective-permute-start(bf16[512,1024]{1,0:T(8,128)(2,1)} %reduce-scatter.11.cloned.1.call-done), channel_id=1, source_target_pairs={{0,16},{16,0},{1,17},{17,1},{2,18},{18,2},{3,19},{19,3},{4,20},{20... | collective-permute-start | bytes 3145736 | tf_op jit(solution)/shard_map/ppermute | solution.py:941
  728.6 162.9 %reduce-scatter.17.cloned.1.call-start = ((), (), s32[]{:S(2)}) async-start(), calls=%async_computation.16 | async-start | bytes 3932160 | tf_op jit(solution)/shard_map/reduce_scatter | solution.py:944
  815.9 50.8 %collective-permute-start.3 = (bf16[512,1024]{1,0:T(8,128)(2,1)}, bf16[512,1024]{1,0:T(8,128)(2,1)}, u32[]{:S(2)}, u32[]{:S(2)}) collective-permute-start(bf16[512,1024]{1,0:T(8,128)(2,1)} %reduce-scatter.13.cloned.1.call-done), channel_id=1, source_target_pairs={{0,16},{16,0},{1,17},{17,1},{2,18},{18,2},{3,19},{19,3},{4,20},{20... | collective-permute-start | bytes 3145736 | tf_op jit(solution)/shard_map/ppermute | solution.py:941
  877.5 19.1 %collective-permute-start.5 = (bf16[256,512]{1,0:T(8,128)(2,1)}, bf16[256,512]{1,0:T(8,128)(2,1)S(1)}, u32[]{:S(2)}, u32[]{:S(2)}) collective-permute-start(bf16[256,512]{1,0:T(8,128)(2,1)} %reduce-scatter.15.cloned.1.call-done), channel_id=1, source_target_pairs={{0,16},{16,0},{1,17},{17,1},{2,18},{18,2},{3,19},{19,3},{4,20},{20... | collective-permute-start | bytes 786440 | tf_op jit(solution)/shard_map/ppermute | solution.py:941
  891.6 16.1 %collective-permute-start.4 = (bf16[512,768]{0,1:T(8,128)(2,1)}, bf16[512,768]{0,1:T(8,128)(2,1)S(1)}, u32[]{:S(2)}, u32[]{:S(2)}) collective-permute-start(bf16[512,768]{0,1:T(8,128)(2,1)} %reduce-scatter.17.cloned.1.call-done), channel_id=1, source_target_pairs={{0,16},{16,0},{1,17},{17,1},{2,18},{18,2},{3,19},{19,3},{4,20},{20... | collective-permute-start | bytes 2359304 | tf_op jit(solution)/shard_map/ppermute | solution.py:941
  892.4 4.2 copy-start.28
  892.4 15.2 %copy-start.24 = (bf16[512,768]{0,1:T(8,128)(2,1)S(1)}, bf16[512,768]{0,1:T(8,128)(2,1)}, u32[]{:S(2)}) copy-start(bf16[512,768]{0,1:T(8,128)(2,1)} %reduce-scatter.17.cloned.1.call-done) | copy-start | bytes 2359300
  (11 other events, 22.5 us)
Sparse Core Ops, SparseCore 0:
  10.4 66.1 all-gather.5
  78.7 51.6 all-gather.7
  132.6 175.7 all-gather.9
  310.5 44.9 all-gather.11
  357.5 44.4 all-gather.13
  465.3 40.9 reduce-scatter.6
  508.5 42.8 reduce-scatter.8
  554.3 75.9 reduce-scatter.10
  633.1 89.9 reduce-scatter.12
  728.8 46.4 reduce-scatter.14
  816.0 59.1 reduce-scatter.16

commit v8 on v7

--- a/solution.py
+++ b/solution.py
@@ -75,258 +75,351 @@
     return {"col": flip("col", 2)}, {"dp": flip("dp", 1)}, {"col": flip("col", 1)}
 
 
-def gather_kernel(pair, x_ref, out_ref, local_sem, send_sem, recv_sem):
+def gather_flow(x_ref, out_ref, local_sem, send, base, meanwhile=None):
     rows, width = x_ref.shape
     half = rows // 2
-    y, b, p = side("dp"), lax.axis_index("col"), side("row") if pair else 0
+    y, b = side("dp"), lax.axis_index("col")
     to_x, to_y, to_c = neighbours()
-    to_z = {"row": flip("row", 1)}
-    greet([to_x, to_y, to_c] + ([to_z] if pair else []))
-    started = []
-    send = sender(send_sem, recv_sem, started)
-
-    def slot(pp, yy, h, bb, n=half):
+
+    def slot(yy, h, bb, n=half):
         return out_ref.at[
-            pl.ds(pl.multiple_of((pp * 2 + yy) * rows + h * half, half), n),
+            pl.ds(pl.multiple_of(yy * rows + h * half, half), n),
             pl.ds(pl.multiple_of(bb * width, width), width),
         ]
 
-    def open_flow(pp, low, high, base):
-        xa = send(low, slot(pp, y, 0, b), base + 0, to_x)
-        ya = send(high, slot(pp, y, 1, b), base + 1, to_y)
-        c0 = send(low, slot(pp, y, 0, b), base + 6, to_c)
-        yb = send(low, slot(pp, y, 0, b), base + 2, to_y)
-        xb = send(high, slot(pp, y, 1, b), base + 3, to_x)
-        c1 = send(high, slot(pp, y, 1, b), base + 7, to_c)
-        return xa, ya, xb, yb, [c0, c1]
-
-    def relay(pp, flow, base):
-        xa, ya, xb, yb, core = flow
-        xa.wait_recv()
-        piece = slot(pp, y, 0, b ^ 2)
-        yc = send(piece, piece, base + 4, to_y)
-        core.append(send(piece, piece, base + 8, to_c))
-        ya.wait_recv()
-        piece = slot(pp, y ^ 1, 1, b)
-        xc = send(piece, piece, base + 5, to_x)
-        core.append(send(piece, piece, base + 9, to_c))
-        yb.wait_recv()
-        piece = slot(pp, y ^ 1, 0, b)
-        core.append(send(piece, piece, base + 10, to_c))
-        xb.wait_recv()
-        piece = slot(pp, y, 1, b ^ 2)
-        core.append(send(piece, piece, base + 11, to_c))
-        return yc, xc, core
-
-    def close_flow(pp, state, base):
-        yc, xc, core = state
-        yc.wait_recv()
-        piece = slot(pp, y ^ 1, 0, b ^ 2)
-        core.append(send(piece, piece, base + 12, to_c))
-        xc.wait_recv()
-        piece = slot(pp, y ^ 1, 1, b ^ 2)
-        core.append(send(piece, piece, base + 13, to_c))
-        for copy in core:
-            copy.wait_recv()
-
     low, high = x_ref.at[pl.ds(0, half)], x_ref.at[pl.ds(half, half)]
-    own = pltpu.make_async_copy(x_ref, slot(p, y, 0, b, rows), local_sem)
-    if pair:
-        z0 = send(low, slot(p, y, 0, b), 28, to_z)
-        z1 = send(high, slot(p, y, 1, b), 29, to_z)
-    first = open_flow(p, low, high, 0)
+    own = pltpu.make_async_copy(x_ref, slot(y, 0, b, rows), local_sem)
+    xa = send(low, slot(y, 0, b), base + 0, to_x)
+    ya = send(high, slot(y, 1, b), base + 1, to_y)
+    core = [send(low, slot(y, 0, b), base + 6, to_c)]
+    yb = send(low, slot(y, 0, b), base + 2, to_y)
+    xb = send(high, slot(y, 1, b), base + 3, to_x)
+    core.append(send(high, slot(y, 1, b), base + 7, to_c))
     own.start()
-    state = relay(p, first, 0)
-    if pair:
-        z0.wait_recv()
-        z1.wait_recv()
-        second = open_flow(p ^ 1, slot(p ^ 1, y, 0, b), slot(p ^ 1, y, 1, b), 14)
-    close_flow(p, state, 0)
-    if pair:
-        close_flow(p ^ 1, relay(p ^ 1, second, 14), 14)
+    if meanwhile is not None:
+        meanwhile()
+    xa.wait_recv()
+    piece = slot(y, 0, b ^ 2)
+    yc = send(piece, piece, base + 4, to_y)
+    core.append(send(piece, piece, base + 8, to_c))
+    ya.wait_recv()
+    piece = slot(y ^ 1, 1, b)
+    xc = send(piece, piece, base + 5, to_x)
+    core.append(send(piece, piece, base + 9, to_c))
+    yb.wait_recv()
+    piece = slot(y ^ 1, 0, b)
+    core.append(send(piece, piece, base + 10, to_c))
+    xb.wait_recv()
+    piece = slot(y, 1, b ^ 2)
+    core.append(send(piece, piece, base + 11, to_c))
+    yc.wait_recv()
+    piece = slot(y ^ 1, 0, b ^ 2)
+    core.append(send(piece, piece, base + 12, to_c))
+    xc.wait_recv()
+    piece = slot(y ^ 1, 1, b ^ 2)
+    core.append(send(piece, piece, base + 13, to_c))
+    for copy in core:
+        copy.wait_recv()
+    own.wait()
+
+
+def gather_kernel(x_ref, out_ref, local_sem, send_sem, recv_sem):
+    greet(neighbours())
+    started = []
+    gather_flow(x_ref, out_ref, local_sem, sender(send_sem, recv_sem, started), 0)
     for copy in started:
         copy.wait_send()
-    own.wait()
-
-
-def gather_wide(values, pair, number, name):
+
+
+def gather_wide(values, number, name):
     rows, width = values.shape
-    copies = 30 if pair else 14
     return pl.pallas_call(
-        functools.partial(gather_kernel, pair),
+        gather_kernel,
         name=name,
-        out_shape=jax.ShapeDtypeStruct(((4 if pair else 2) * rows, 4 * width), values.dtype),
+        out_shape=jax.ShapeDtypeStruct((2 * rows, 4 * width), values.dtype),
         in_specs=[pl.BlockSpec(memory_space=pltpu.VMEM)],
         out_specs=pl.BlockSpec(memory_space=pl.ANY),
         scratch_shapes=[
             pltpu.SemaphoreType.DMA,
-            pltpu.SemaphoreType.DMA((copies,)),
-            pltpu.SemaphoreType.DMA((copies,)),
+            pltpu.SemaphoreType.DMA((14,)),
+            pltpu.SemaphoreType.DMA((14,)),
         ],
         compiler_params=pltpu.CompilerParams(collective_id=number, has_side_effects=True),
         cost_estimate=COST,
     )(values)
 
 
-def scatter_kernel(pair, rider, p_ref, *refs):
-    if rider:
-        cargo_ref, out_ref, far_ref = refs[:3]
-    else:
-        out_ref = refs[0]
-    rc, s1, ry, rx, s2, fy, fx, sz, fz, send_sem, recv_sem = refs[3 if rider else 1 :]
-    rows, width = out_ref.shape
+def scatter_flow(p_ref, buffers, send):
+    rc, s1, ry, rx, s2, fy, fx = buffers
+    rows, width = p_ref.shape[0] // 2, p_ref.shape[1] // 4
     half = rows // 2
-    y, b, p = side("dp"), lax.axis_index("col"), side("row") if pair else 0
+    y, b = side("dp"), lax.axis_index("col")
     x, c = b >> 1, b & 1
     to_x, to_y, to_c = neighbours()
-    to_z = {"row": flip("row", 1)}
-    to_far = {"row": flip("row", 2)}
-    greet([to_x, to_y, to_c] + ([to_z] if pair else []) + ([to_far] if rider else []))
+
+    def place(yy, h):
+        return pl.ds(pl.multiple_of(yy * rows + h * half, half), half)
+
+    def column(bb):
+        return pl.ds(pl.multiple_of(bb * width, width), width)
+
+    order = [(0, y ^ 1, 0), (1, y ^ 1, 0), (x ^ 1, 0, 1), (x ^ 1, 1, 1)]
+    order += [(0, y, 0), (1, y, 0), (x, 0, 1), (x, 1, 1)]
+    core = [
+        send(
+            p_ref.at[place(yy, h), column(2 * xx + (c ^ 1))],
+            rc.at[xx, place(yy, h)],
+            number,
+            to_c,
+        )
+        for number, (xx, yy, h) in enumerate(order)
+    ]
+
+    def settle(*numbers):
+        for number in numbers:
+            core[number].wait_recv()
+            xx, yy, h = order[number]
+            s1[xx, place(yy, h), :] = (
+                p_ref[place(yy, h), column(2 * xx + c)].astype(f32)
+                + rc[xx, place(yy, h), :].astype(f32)
+            ).astype(s1.dtype)
+
+    settle(0, 1, 2, 3)
+    ya, xa = [], []
+    for i in range(2):
+        ya.append(send(s1.at[i, place(y ^ 1, 0), :], ry.at[i], 8 + i, to_y))
+        xa.append(send(s1.at[x ^ 1, pl.ds(i * rows + half, half), :], rx.at[i], 10 + i, to_x))
+    settle(4, 5, 6, 7)
+    for copy in ya:
+        copy.wait_recv()
+    s2[0] = (s1[x ^ 1, place(y, 0), :].astype(f32) + ry[x ^ 1].astype(f32)).astype(s2.dtype)
+    xb = send(s2.at[0], fx, 12, to_x)
+    for copy in xa:
+        copy.wait_recv()
+    s2[1] = (s1[x, place(y ^ 1, 1), :].astype(f32) + rx[y ^ 1].astype(f32)).astype(s2.dtype)
+    yb = send(s2.at[1], fy, 13, to_y)
+    keep = s1[x, place(y, 0), :].astype(f32) + ry[x].astype(f32)
+    xb.wait_recv()
+    low = keep + fx[...].astype(f32)
+    keep = s1[x, place(y, 1), :].astype(f32) + rx[y].astype(f32)
+    yb.wait_recv()
+    return low, keep + fy[...].astype(f32)
+
+
+def scatter_buffers(rows, width):
+    half = rows // 2
+    return [
+        pltpu.VMEM((2, 2 * rows, width), bf16),
+        pltpu.VMEM((2, 2 * rows, width), bf16),
+        pltpu.VMEM((2, half, width), bf16),
+        pltpu.VMEM((2, half, width), bf16),
+        pltpu.VMEM((2, half, width), bf16),
+        pltpu.VMEM((half, width), bf16),
+        pltpu.VMEM((half, width), bf16),
+    ]
+
+
+def scatter_kernel(p_ref, out_ref, *refs):
+    buffers, (send_sem, recv_sem) = refs[:7], refs[7:]
+    half = out_ref.shape[0] // 2
+    greet(neighbours())
+    started = []
+    low, high = scatter_flow(p_ref, buffers, sender(send_sem, recv_sem, started))
+    out_ref[:half, :] = low
+    out_ref[half:, :] = high
+    for copy in started:
+        copy.wait_send()
+
+
+def scatter_wide(partial, number, name):
+    rows, width = partial.shape[0] // 2, partial.shape[1] // 4
+    return pl.pallas_call(
+        scatter_kernel,
+        name=name,
+        out_shape=jax.ShapeDtypeStruct((rows, width), f32),
+        in_specs=[pl.BlockSpec(memory_space=pltpu.VMEM)],
+        out_specs=pl.BlockSpec(memory_space=pltpu.VMEM),
+        scratch_shapes=scatter_buffers(rows, width)
+        + [pltpu.SemaphoreType.DMA((14,)), pltpu.SemaphoreType.DMA((14,))],
+        compiler_params=pltpu.CompilerParams(
+            collective_id=number, has_side_effects=True, vmem_limit_bytes=48 * 2**20
+        ),
+        cost_estimate=COST,
+    )(partial)
+
+
+def exchange(stat, slots, send, base):
+    me = lax.axis_index("col")
+    copies = [send(stat, slots.at[me], base + d, peer) for d, peer in enumerate(feature_peers(False))]
+    slots[me] = stat[...]
+    return copies
+
+
+def column_total(slots, copies):
+    for copy in copies:
+        copy.wait_recv()
+    return (slots[0] + slots[1]) + (slots[2] + slots[3])
+
+
+def junction_peers():
+    to_x, to_y, to_c = neighbours()
+    return [to_x, to_y, to_c, {"col": flip("col", 3)}]
+
+
+def mixed_kernel(
+    width,
+    p_ref,
+    low_ref,
+    incoming_ref,
+    resid_ref,
+    valid_ref,
+    gain_ref,
+    block_ref,
+    raw_ref,
+    rest_ref,
+    wide_ref,
+    mixed,
+    x_ref,
+    stat,
+    slots,
+    *refs,
+):
+    buffers, (local_sem, send_sem, recv_sem) = refs[:7], refs[7:]
+    rows, split = low_ref.shape
+    half = rows // 2
+    greet(junction_peers())
     started = []
     send = sender(send_sem, recv_sem, started)
-    if rider:
-        size = far_ref.shape[1]
-        start = pl.multiple_of((1 - (lax.axis_index("row") >> 1)) * size, size)
-        cargo = send(cargo_ref.at[:, pl.ds(start, size)], far_ref, 30, to_far)
-
-    def place(yy, h):
-        return pl.ds(pl.multiple_of(yy * rows + h * half, half), half)
-
-    def column(bb):
-        return pl.ds(pl.multiple_of(bb * width, width), width)
-
-    order = [(0, y ^ 1, 0), (1, y ^ 1, 0), (x ^ 1, 0, 1), (x ^ 1, 1, 1)]
-    order += [(0, y, 0), (1, y, 0), (x, 0, 1), (x, 1, 1)]
-
-    class Flow:
-        def __init__(self, f, pp):
-            self.f, self.base = f, 14 * f
-            self.rows = lambda yy, h: pl.ds(
-                pl.multiple_of((pp * 2 + yy) * rows + h * half, half), half
-            )
-            self.core = [
-                send(
-                    p_ref.at[self.rows(yy, h), column(2 * xx + (c ^ 1))],
-                    rc.at[f, xx, place(yy, h)],
-                    self.base + number,
-                    to_c,
-                )
-                for number, (xx, yy, h) in enumerate(order)
-            ]
-
-        def settle(self, *numbers):
-            for number in numbers:
-                self.core[number].wait_recv()
-                xx, yy, h = order[number]
-                s1[self.f, xx, place(yy, h), :] = (
-                    p_ref[self.rows(yy, h), column(2 * xx + c)].astype(f32)
-                    + rc[self.f, xx, place(yy, h), :].astype(f32)
-                ).astype(s1.dtype)
-
-        def first(self, i):
-            f = self.f
-            ya = send(s1.at[f, i, place(y ^ 1, 0), :], ry.at[f, i], self.base + 8 + i, to_y)
-            part = s1.at[f, x ^ 1, pl.ds(i * rows + half, half), :]
-            xa = send(part, rx.at[f, i], self.base + 10 + i, to_x)
-            return ya, xa
-
-        def second(self, copies):
-            f = self.f
-            for ya, _ in copies:
-                ya.wait_recv()
-            s2[f, 0] = (
-                s1[f, x ^ 1, place(y, 0), :].astype(f32) + ry[f, x ^ 1].astype(f32)
-            ).astype(s2.dtype)
-            xb = send(s2.at[f, 0], fx.at[f], self.base + 12, to_x)
-            for _, xa in copies:
-                xa.wait_recv()
-            s2[f, 1] = (
-                s1[f, x, place(y ^ 1, 1), :].astype(f32) + rx[f, y ^ 1].astype(f32)
-            ).astype(s2.dtype)
-            yb = send(s2.at[f, 1], fy.at[f], self.base + 13, to_y)
-            return xb, yb
-
-        def last(self, copies):
-            f = self.f
-            xb, yb = copies
-            keep = s1[f, x, place(y, 0), :].astype(f32) + ry[f, x].astype(f32)
-            xb.wait_recv()
-            low = keep + fx[f].astype(f32)
-            keep = s1[f, x, place(y, 1), :].astype(f32) + rx[f, y].astype(f32)
-            yb.wait_recv()
-            return low, keep + fy[f].astype(f32)
-
-    if pair:
-        far = Flow(0, p ^ 1)
-        near = Flow(1, p)
-        far.settle(0, 1, 2, 3)
-        far_first = [far.first(0), far.first(1)]
-        far.settle(4, 5, 6, 7)
-        near.settle(0, 1, 2, 3)
-        near_first = [near.first(0)]
-        near.settle(4, 5, 6, 7)
-        far_second = far.second(far_first)
-        near_first.append(near.first(1))
-        low, high = far.last(far_second)
-        sz[pl.ds(0, half), :] = low.astype(bf16)
-        z0 = send(sz.at[pl.ds(0, half)], fz.at[pl.ds(0, half)], 28, to_z)
-        sz[pl.ds(half, half), :] = high.astype(bf16)
-        z1 = send(sz.at[pl.ds(half, half)], fz.at[pl.ds(half, half)], 29, to_z)
-        low, high = near.last(near.second(near_first))
-        z0.wait_recv()
-        out_ref[pl.ds(0, half), :] = low + fz[pl.ds(0, half), :].astype(f32)
-        z1.wait_recv()
-        out_ref[pl.ds(half, half), :] = high + fz[pl.ds(half, half), :].astype(f32)
-    else:
-        near = Flow(0, 0)
-        near.settle(0, 1, 2, 3)
-        near_first = [near.first(0), near.first(1)]
-        near.settle(4, 5, 6, 7)
-        low, high = near.last(near.second(near_first))
-        out_ref[pl.ds(0, half), :] = low
-        out_ref[pl.ds(half, half), :] = high
-    if rider:
-        cargo.wait_recv()
+    mixed[:, :split] = low_ref[...]
+    low, high = scatter_flow(p_ref, buffers, send)
+    mixed[:half, split:] = low
+    mixed[half:, split:] = high
+    stat[0:1, :] = jnp.sum(mixed[...] * mixed[...], axis=1, keepdims=True).T
+    stat[1:2, :] = jnp.sum(incoming_ref[...] * gain_ref[...] * mixed[...], axis=1, keepdims=True).T
+    total = column_total(slots, exchange(stat, slots, send, 14)) / width
+    inverse = lax.rsqrt(total[0:1, :] + norm_eps)
+    first = inverse.T
+    second = (inverse * inverse * inverse * total[1:2, :]).T
+
+    def slope(cols):
+        return (
+            first * (incoming_ref[:, cols] * gain_ref[:, cols]) - mixed[:, cols] * second
+        ).astype(bf16)
+
+    x_ref[...] = slope(slice(0, split))
+
+    def meanwhile():
+        rest_ref[...] = slope(slice(split, 2 * split))
+        normed = mixed[...] * first
+        block_ref[...] = ((resid_ref[...] + normed * gain_ref[...]) * valid_ref[...].T).astype(bf16)
+        raw_ref[...] = jnp.sum(incoming_ref[...] * normed, axis=0, keepdims=True)
+
+    gather_flow(x_ref, wide_ref, local_sem, send, 17, meanwhile)
     for copy in started:
         copy.wait_send()
 
 
-def scatter_wide(partial, pair, number, name, cargo=None):
-    flows = 2 if pair else 1
-    rows, width = partial.shape[0] // (2 * flows), partial.shape[1] // 4
-    half = rows // 2
-    rider = cargo is not None
-    copies = 31 if pair else 14
-    out_shape, out_spec = [jax.ShapeDtypeStruct((rows, width), f32)], [pl.BlockSpec(memory_space=pltpu.VMEM)]
-    anywhere = [pl.BlockSpec(memory_space=pl.ANY)] * rider
-    if rider:
-        out_shape.append(jax.ShapeDtypeStruct((cargo.shape[0], cargo.shape[1] // 2), cargo.dtype))
-    last = (rows, width) if pair else (16, 128)
-    out = pl.pallas_call(
-        functools.partial(scatter_kernel, pair, rider),
-        name=name,
-        out_shape=out_shape,
-        in_specs=[pl.BlockSpec(memory_space=pltpu.VMEM)] + anywhere,
-        out_specs=out_spec + anywhere,
+def mixed_junction(partial, mixed_low, incoming, resid, valid, gain, width, number):
+    rows, part = incoming.shape
+    split = mixed_low.shape[1]
+    vmem = pl.BlockSpec(memory_space=pltpu.VMEM)
+    return pl.pallas_call(
+        functools.partial(mixed_kernel, width),
+        name="mixed_junction",
+        out_shape=(
+            jax.ShapeDtypeStruct((rows, part), bf16),
+            jax.ShapeDtypeStruct((1, part), f32),
+            jax.ShapeDtypeStruct((rows, part - split), bf16),
+            jax.ShapeDtypeStruct((2 * rows, 4 * split), bf16),
+        ),
+        in_specs=[vmem] * 6,
+        out_specs=(vmem, vmem, vmem, pl.BlockSpec(memory_space=pl.ANY)),
         scratch_shapes=[
-            pltpu.VMEM((flows, 2, 2 * rows, width), bf16),
-            pltpu.VMEM((flows, 2, 2 * rows, width), bf16),
-            pltpu.VMEM((flows, 2, half, width), bf16),
-            pltpu.VMEM((flows, 2, half, width), bf16),
-            pltpu.VMEM((flows, 2, half, width), bf16),
-            pltpu.VMEM((flows, half, width), bf16),
-            pltpu.VMEM((flows, half, width), bf16),
-            pltpu.VMEM(last, bf16),
-            pltpu.VMEM(last, bf16),
-            pltpu.SemaphoreType.DMA((copies,)),
-            pltpu.SemaphoreType.DMA((copies,)),
+            pltpu.VMEM((rows, part), f32),
+            pltpu.VMEM((rows, split), bf16),
+            pltpu.VMEM((2, rows), f32),
+            pltpu.VMEM((4, 2, rows), f32),
+        ]
+        + scatter_buffers(rows, split)
+        + [
+            pltpu.SemaphoreType.DMA,
+            pltpu.SemaphoreType.DMA((31,)),
+            pltpu.SemaphoreType.DMA((31,)),
         ],
         compiler_params=pltpu.CompilerParams(
             collective_id=number, has_side_effects=True, vmem_limit_bytes=48 * 2**20
         ),
         cost_estimate=COST,
-    )(partial, *([cargo] * rider))
-    return out if rider else out[0]
+    )(partial, mixed_low, incoming, resid, valid, gain)
+
+
+def d_resid_kernel(
+    width,
+    p_ref,
+    incoming_ref,
+    branch_ref,
+    inv_ref,
+    gain_ref,
+    resid_ref,
+    raw_ref,
+    wide_ref,
+    x_ref,
+    stat,
+    slots,
+    *refs,
+):
+    buffers, (local_sem, send_sem, recv_sem) = refs[:7], refs[7:]
+    half = x_ref.shape[0] // 2
+    greet(junction_peers())
+    started = []
+    send = sender(send_sem, recv_sem, started)
+    low, high = scatter_flow(p_ref, buffers, send)
+    resid_ref[:half, :] = low + incoming_ref[:half, :]
+    resid_ref[half:, :] = high + incoming_ref[half:, :]
+    stat[...] = jnp.sum(resid_ref[...] * gain_ref[...] * branch_ref[...], axis=1, keepdims=True).T
+    inner = column_total(slots, exchange(stat, slots, send, 14)) / width
+    inverse = inv_ref[...]
+    first = inverse.T
+    second = (inverse * inverse * inverse * inner).T
+    x_ref[...] = (first * (resid_ref[...] * gain_ref[...]) - branch_ref[...] * second).astype(bf16)
+
+    def meanwhile():
+        raw_ref[...] = jnp.sum(resid_ref[...] * branch_ref[...] * first, axis=0, keepdims=True)
+
+    gather_flow(x_ref, wide_ref, local_sem, send, 17, meanwhile)
+    for copy in started:
+        copy.wait_send()
+
+
+def d_resid_junction(partial, incoming, branch, inverse, gain, width, number):
+    rows, part = incoming.shape
+    vmem = pl.BlockSpec(memory_space=pltpu.VMEM)
+    return pl.pallas_call(
+        functools.partial(d_resid_kernel, width),
+        name="d_resid_junction",
+        out_shape=(
+            jax.ShapeDtypeStruct((rows, part), f32),
+            jax.ShapeDtypeStruct((1, part), f32),
+            jax.ShapeDtypeStruct((2 * rows, 4 * part), bf16),
+        ),
+        in_specs=[vmem] * 5,
+        out_specs=(vmem, vmem, pl.BlockSpec(memory_space=pl.ANY)),
+        scratch_shapes=[
+            pltpu.VMEM((rows, part), bf16),
+            pltpu.VMEM((1, rows), f32),
+            pltpu.VMEM((4, 1, rows), f32),
+        ]
+        + scatter_buffers(rows, part)
+        + [
+            pltpu.SemaphoreType.DMA,
+            pltpu.SemaphoreType.DMA((31,)),
+            pltpu.SemaphoreType.DMA((31,)),
+        ],
+        compiler_params=pltpu.CompilerParams(
+            collective_id=number, has_side_effects=True, vmem_limit_bytes=48 * 2**20
+        ),
+        cost_estimate=COST,
+    )(partial, incoming, branch, inverse, gain)
 
 
 def feature_peers(wide):
@@ -866,7 +959,6 @@
     down_half = y_half(w_down, 0)
     split = down_half.shape[1] // 2
     low_weight = lax.all_gather(down_half[:, :split], "row", axis=1, tiled=True)
-    high_weight = lax.all_gather(down_half[:, split:], "row", axis=1, tiled=True)
 
     positions = z * tok_rows + jnp.arange(tok_rows)
     length = seq_lengths[0]
@@ -882,44 +974,40 @@
     unit_length = lax.dynamic_slice_in_dim(pair_lengths, z // heads, 1)
     qk_gain = jnp.stack([y_half(q_gain, 0), y_half(k_gain, 0)])
 
-    tokens_wide = gather_wide(tokens, False, 0, "gather_tokens")
+    tokens_wide = gather_wide(tokens, 0, "gather_tokens")
+    high_weight = lax.all_gather(after(down_half[:, split:], tokens_wide), "row", axis=1, tiled=True)
     qkv = matmul(tokens_wide, qkv_weight)
     units, inverse = front(qkv, cosine, sine_signed, qk_gain, width, 2 * heads, 2)
     q_unit, k_unit, v_unit = (units[:, i].reshape(slots, HEAD_DIM) for i in range(3))
     attn_unit, attn_exact, log_total = attend(unit_length, q_unit, k_unit, v_unit)
     attn_low = turn(attn_unit, True, tok_rows, heads, 3, "turn_attn")
-    branch = scatter_wide(matmul(attn_low, out_weight).astype(bf16), False, 4, "scatter_branch")
+    branch = scatter_wide(matmul(attn_low, out_weight).astype(bf16), 4, "scatter_branch")
     branch_inv = lax.rsqrt(
         feature_total(jnp.sum(branch * branch, axis=1)[None, :], 5, "total_branch")[0] / width
         + norm_eps
     )[:, None]
     resid = tokens.astype(f32) + branch * branch_inv * attn_gain
-    resid_wide = gather_wide(resid.astype(bf16), False, 6, "gather_resid")
+    resid_wide = gather_wide(resid.astype(bf16), 6, "gather_resid")
     gate = matmul(resid_wide, gate_weight)
     upper = matmul(resid_wide, up_weight)
     sigma = jax.nn.sigmoid(gate)
     hidden = (gate * sigma * upper).astype(bf16)
-    mixed_low = scatter_wide(matmul(hidden, low_weight).astype(bf16), False, 7, "scatter_mixed_low")
+    mixed_low = scatter_wide(matmul(hidden, low_weight).astype(bf16), 7, "scatter_mixed_low")
     high_weight = after(high_weight, mixed_low)
-    mixed_high = scatter_wide(matmul(hidden, high_weight).astype(bf16), False, 17, "scatter_mixed_high")
-    mixed = jnp.concatenate([mixed_low, mixed_high], axis=1)
     incoming = cotangent.astype(f32) * valid
-    gained = incoming * mlp_gain
-    sums = feature_total(
-        jnp.stack([jnp.sum(mixed * mixed, axis=1), jnp.sum(gained * mixed, axis=1)]),
-        8,
-        "total_mixed",
-    )
-    mixed_inv = lax.rsqrt(sums[0] / width + norm_eps)[:, None]
-    inner = (sums[1] / width)[:, None]
-    block_output = ((resid + mixed * mixed_inv * mlp_gain) * valid).astype(bf16)
-    mlp_gain_raw = jnp.sum(incoming * mixed * mixed_inv, axis=0)
-    d_mixed = (mixed_inv * gained - mixed * mixed_inv**3 * inner).astype(bf16)
     factor = 1.0 / math.sqrt(slots * data_count)
-    d_low_wide = gather_wide(d_mixed[:, :split], False, 9, "gather_d_mixed_low")
+    block_output, mlp_gain_raw, d_high, d_low_wide = mixed_junction(
+        matmul(hidden, high_weight).astype(bf16),
+        mixed_low,
+        incoming,
+        resid,
+        valid.T,
+        mlp_gain[None, :],
+        width,
+        17,
+    )
     low_raw = (contract_first(hidden, d_low_wide) * factor).astype(bf16)
-    d_high = after(d_mixed[:, split:], low_raw)
-    d_high_wide = gather_wide(d_high, False, 18, "gather_d_mixed_high")
+    d_high_wide = gather_wide(after(d_high, low_raw), 18, "gather_d_mixed_high")
     high_raw = (contract_first(hidden, d_high_wide) * factor).astype(bf16)
 
     def cut(values, index, count, axis):
@@ -956,19 +1044,11 @@
     )
     down_piece = jnp.concatenate([low_piece, reduce_rows(high_raw, 1)], axis=1)
     gate_piece, up_piece = reduce_rows(gate_raw, 0), reduce_rows(up_raw, 0)
-    d_resid = scatter_wide(d_resid_wide, False, 10, "scatter_d_resid")
-    d_resid = incoming + d_resid
-    attn_gain_raw = jnp.sum(d_resid * branch * branch_inv, axis=0)
-    gained = d_resid * attn_gain
-    inner = (
-        feature_total(jnp.sum(gained * branch, axis=1)[None, :], 11, "total_d_resid")[0][:, None]
-        / width
-    )
-    d_branch = (branch_inv * gained - branch * branch_inv**3 * inner).astype(bf16)
+    d_resid, attn_gain_raw, d_branch_wide = d_resid_junction(
+        d_resid_wide, incoming, branch, branch_inv.T, attn_gain[None, :], width, 10
+    )
     down_piece = over_dp(down_piece)
-    d_branch_wide, down_piece = lax.optimization_barrier(
-        (gather_wide(d_branch, False, 12, "gather_d_branch"), down_piece)
-    )
+    d_branch_wide, down_piece = lax.optimization_barrier((d_branch_wide, down_piece))
     d_attn = contract_last(d_branch_wide, out_weight).astype(bf16)
     other_down = from_twin(down_piece)
     d_attn_unit, other_down = lax.optimization_barrier(
@@ -988,15 +1068,8 @@
     qkv_raw = (contract_first(tokens_wide, d_qkv) * factor).astype(bf16)
     projected = contract_last(after(d_qkv, qkv_raw), qkv_weight).astype(bf16)
     qkv_piece = over_dp(reduce_rows(qkv_raw, 0))
-    scattered, other_down, other_gate, other_up, out_piece, gain_sums = lax.optimization_barrier(
-        (
-            scatter_wide(projected, False, 16, "scatter_projected"),
-            other_down,
-            other_gate,
-            other_up,
-            over_dp(out_piece),
-            gain_sums,
-        )
+    scattered, out_piece, gain_sums = lax.optimization_barrier(
+        (scatter_wide(projected, 16, "scatter_projected"), over_dp(out_piece), gain_sums)
     )
     other_out = from_twin(out_piece)
     input_grad = d_resid + scattered
@@ -1006,13 +1079,15 @@
 
     gains = over_dp(
         gain_total(
-            jnp.stack([spread(gain_sums[0]), spread(gain_sums[1]), attn_gain_raw, mlp_gain_raw])
+            jnp.stack([spread(gain_sums[0]), spread(gain_sums[1]), attn_gain_raw[0], mlp_gain_raw[0]])
             * factor,
             15,
         )
     )
 
-    gains, qkv_piece = lax.optimization_barrier((gains, qkv_piece))
+    gains, qkv_piece, other_down, other_gate, other_up = lax.optimization_barrier(
+        (gains, qkv_piece, other_down, other_gate, other_up)
+    )
 
     def whole(piece, other, axis):
         return two_sides(piece, other, y, axis).astype(f32)

time: 930 us -> 911 us (0.980)
  other arithmetic: 38.3 us -> 25.8 us
    pallas_call x3 -> x1, Pallas kernels: 14.9 us -> 4.93 us  [feature_total(): pl.pallas_call(total_kernel, name=name, out_shape=jax.ShapeDtypeStruct(fl...]
    pallas_call x10 -> x8, Pallas kernels: 290 us -> 297 us  [the longest x3 100 us: scatter_wide(): pl.pallas_call(scatter_kernel, name=name, out_shape=jax.ShapeDtypeStruct(...]
    unnamed x87 -> x103, local copies, waits for them, and re-layouts: 16.2 us -> 22.2 us
  transfers between devices with their start and end apart: 17 -> 17, of which waited for: 3 -> 3; matrix products, arithmetic and copies ran while one was open for 20% -> 19% of each run, Pallas kernels for 64% -> 65%
where the time goes in v8:
time: 911 us; the launch traced here: 903 us
  Pallas kernels  626 us (69%)
  matrix products  157 us (17%)
  waiting for transfers between devices  38.2 us (4%)
  local copies, waits for them, and re-layouts  30.6 us (3%)
  other arithmetic  25.8 us (3%)
  between operations  15.8 us (2%)
  starting transfers between devices  9.95 us (1%)
    pallas_call x1, Pallas kernels, front(): pl.pallas_call(functools.partial(front_kernel, width), name='front', out_...  104 us
    pallas_call x3, Pallas kernels, scatter_wide(): pl.pallas_call(scatter_kernel, name=name, out_shape=jax.ShapeDtypeStruct(...  100 us
    pallas_call x2, Pallas kernels, turn(): pl.pallas_call(functools.partial(turn_kernel, back, tok, heads), name=nam...  89.1 us
    pallas_call x3, Pallas kernels, gather_wide(): pl.pallas_call(gather_kernel, name=name, out_shape=jax.ShapeDtypeStruct((...  82 us
    pallas_call x1, Pallas kernels, rear(): pl.pallas_call(functools.partial(rear_kernel, width), name='rear', out_sh...  73.9 us
    pallas_call x1, Pallas kernels, d_resid_junction(): pl.pallas_call(functools.partial(d_resid_kernel, width), name='d_resid_ju...  72 us
    dot_general x6, matrix products, contract_last(): lax.dot_general(left, right, (((1,), (1,)), ((), ())), preferred_element_...  59.9 us
    dot_general x6, matrix products, contract_first(): lax.dot_general(left, right, (((0,), (0,)), ((), ())), preferred_element_...  49.1 us
  transfers between devices with their start and end apart: 17, of which 3 were waited for; matrix products, arithmetic and copies ran while one was open for 19% of the time, Pallas kernels for 65%

profile of v8, /device:TPU:0, one launch (start us, length us, event | category | flops | bytes accessed | tf_op | source)
XLA Modules:
  0.0 903.3 jit_solution(14520582840389386520)
XLA Ops:
  16.1 3.1 collective-permute-start
  19.1 31.4 %gather_tokens.1 = bf16[1536,2048]{1,0:T(8,128)(2,1)} custom-call(bf16[768,512]{1,0:T(8,128)(2,1)} %x_ref.1), custom_call_target="tpu_custom_call" | custom-call | bytes 1000 | tf_op jit(solution)/shard_map/gather_tokens/pallas_call | solution.py:136
  51.7 1.6 negate_select_fusion
  53.3 1.6 convert_multiply_fusion.incoming_ref
  56.3 20.3 %all-gather.6.cloned.1.call-done = bf16[2048,768]{1,0:T(8,128)(2,1)} async-done(((bf16[512,768]{1,0:T(8,128)(2,1)}), bf16[2048,768]{1,0:T(8,128)(2,1)}) %all-gather.6.cloned.1.call-update) | async-done | bytes 3145744 | tf_op jit(solution)/shard_map/all_gather | solution.py:947
  76.6 8.1 convolution_bitcast_fusion.qkv_ref
  84.7 104.3 %front.1 = (bf16[4,3,768,128]{3,2,1,0:T(8,128)(2,1)S(1)}, f32[2,1536]{1,0:T(2,128)S(1)}) custom-call(f32[1536,768]{1,0:T(8,128)S(1)} %convolution_bitcast_fusion.qkv_ref, f32[768,128]{1,0:T(8,128)S(1)} %get-tuple-element.132.cos_ref, f32[768,128]{1,0:T(8,128)S(1)} %get-tuple-element.131.sin_ref, f32[2,256]{1,0:T(2,128)S(1)} %pad_maximum_fusion.4.gain_ref), custom_call_target="tpu_custom_call" | custom-call | bytes 1000 | tf_op jit(solution)/shard_map/front/pallas_call | solution.py:651
  190.5 20.7 %attend.1 = (bf16[3072,128]{1,0:T(8,128)(2,1)}, f32[3072,128]{1,0:T(8,128)}, f32[8,3072]{1,0:T(8,128)}) custom-call(s32[1]{0:T(128)} %dynamic_slice.48.len_ref, bf16[3072,128]{1,0:T(8,128)(2,1)} %bitcast.66, bf16[3072,128]{1,0:T(8,128)(2,1)} %bitcast.64, bf16[3072,128]{1,0:T(8,128)(2,1)} %bitcast.62), custom_call_target="tpu_custom_call" | custom-call | bytes 1000 | tf_op jit(solution)/shard_map/attend/pallas_call | solution.py:831
  211.1 45.3 %turn_attn.1 = bf16[1536,256]{1,0:T(8,128)(2,1)} custom-call(bf16[3072,128]{1,0:T(8,128)(2,1)} %get-tuple-element.55.x_ref), custom_call_target="tpu_custom_call" | custom-call | bytes 1000 | tf_op jit(solution)/shard_map/turn_attn/pallas_call | solution.py:552
  256.5 5.9 convolution_convert_fusion.1.p_ref
  262.4 37.6 %scatter_branch.1.branch_ref = f32[768,512]{1,0:T(8,128)S(1)} custom-call(bf16[1536,2048]{1,0:T(8,128)(2,1)} %convolution_convert_fusion.1.p_ref), custom_call_target="tpu_custom_call" | custom-call | bytes 1000 | tf_op jit(solution)/shard_map/scatter_branch/pallas_call | solution.py:236
  300.8 4.9 total_branch.1
  306.4 2.8 fusion.15
  309.2 31.9 %gather_resid.1 = bf16[1536,2048]{1,0:T(8,128)(2,1)} custom-call(bf16[768,512]{1,0:T(8,128)(2,1)} %get-tuple-element.108.x_ref), custom_call_target="tpu_custom_call" | custom-call | bytes 1000 | tf_op jit(solution)/shard_map/gather_resid/pallas_call | solution.py:136
  341.2 10.2 %fusion.5 = f32[1536,1024]{1,0:T(8,128)S(1)} fusion(bf16[1536,2048]{1,0:T(8,128)(2,1)} %gather_resid.1, bf16[2048,2048]{1,0:T(8,128)(2,1)} %all-gather.10.cloned.1.call-done), kind=kOutput, calls=%fused_computation.21 | convolution fusion | flops 6442450944 | bytes 16777216 | tf_op jit(solution)/shard_map/dot_general | solution.py:31
  351.4 2.6 copy-done.44
  354.1 10.1 %multiply_convert_fusion.5 = (bf16[1536,1024]{1,0:T(8,128)(2,1)}, f32[1536,1024]{1,0:T(8,128)}) fusion(f32[1536,1024]{1,0:T(8,128)S(1)} %fusion.5, bf16[1536,2048]{1,0:T(8,128)(2,1)S(1)} %copy-done.24, bf16[2048,2048]{1,0:T(8,128)(2,1)S(1)} %copy-done.41), kind=kOutput, calls=%fused_computation.8 | convolution fusion | flops 6451888128 | bytes 26214400 | tf_op jit(solution)/shard_map/dot_general | solution.py:31
  364.2 6.1 convolution_convert_fusion.3.p_ref
  370.3 20.6 %scatter_mixed_low.1.low_ref = f32[768,256]{1,0:T(8,128)S(1)} custom-call(bf16[1536,1024]{1,0:T(8,128)(2,1)S(1)} %convolution_convert_fusion.3.p_ref), custom_call_target="tpu_custom_call" | custom-call | bytes 1000 | tf_op jit(solution)/shard_map/scatter_mixed_low/pallas_call | solution.py:236
  391.8 10.2 %all-gather.12.cloned.1.call-done = bf16[1024,1024]{1,0:T(8,128)(2,1)} async-done(((bf16[1024,256]{1,0:T(8,128)(2,1)}), bf16[1024,1024]{1,0:T(8,128)(2,1)}) %all-gather.12.cloned.1.call-update) | async-done | bytes 2097168 | tf_op jit(solution)/shard_map/all_gather | solution.py:978
  401.9 7.8 convolution_convert_fusion.2.p_ref
  409.8 43.0 %mixed_junction.1 = (bf16[768,512]{1,0:T(8,128)(2,1)S(1)}, f32[1,512]{1,0:T(1,128)S(1)}, bf16[768,256]{1,0:T(8,128)(2,1)S(1)}, bf16[1536,1024]{1,0:T(8,128)(2,1)}) custom-call(bf16[1536,1024]{1,0:T(8,128)(2,1)} %convolution_convert_fusion.2.p_ref, f32[768,256]{1,0:T(8,128)S(1)} %copy-done.11, f32[768,512]{1,0:T(8,128)S(1)} %convert_multiply_fusion.incoming_ref, ...), custom_call_target="tpu_custom_call" | custom-call | bytes 1000 | tf_op jit(solution)/shard_map/mixed_junction/pallas_call | solution.py:326
  454.4 6.6 multiply_convert_fusion.7
  461.4 18.7 %gather_d_mixed_high.1 = bf16[1536,1024]{1,0:T(8,128)(2,1)} custom-call(bf16[768,256]{1,0:T(8,128)(2,1)} %copy-done.16), custom_call_target="tpu_custom_call" | custom-call | bytes 1000 | tf_op jit(solution)/shard_map/gather_d_mixed_high/pallas_call | solution.py:136
  480.2 7.7 multiply_convert_fusion.6
  488.0 8.8 fusion.18
  496.8 11.1 %multiply_convert_fusion.3 = (bf16[1536,1024]{1,0:T(8,128)(2,1)}, bf16[1536,1024]{1,0:T(8,128)(2,1)S(1)}) fusion(f32[1536,1024]{1,0:T(8,128)} %copy-done.44, f32[1536,1024]{1,0:T(8,128)} %get-tuple-element.140, f32[1536,1024]{1,0:T(8,128)} %fusion.18, bf16[1536,1024]{1,0:T(8,128)(2,1)S(1)} %copy-done.27, bf16[1024,1024]{1,0:T(8,128)(2,1)S(1)} %copy-done.42), kind=kOutput, calls=%fused_computation.6 | convolution fusion | flops 3243245568 | bytes 30408704 | tf_op jit(solution)/shard_map/dot_general | solution.py:39
  507.9 1.7 copy-done.45
  509.6 8.5 multiply_convert_fusion.1
  518.4 11.2 %multiply_convert_fusion = bf16[2048,1024]{1,0:T(8,128)(2,1)} fusion(bf16[1536,2048]{1,0:T(8,128)(2,1)} %gather_resid.1, bf16[1536,1024]{1,0:T(8,128)(2,1)} %get-tuple-element.110), kind=kOutput, calls=%fused_computation.1 | convolution fusion | flops 6446645248 | bytes 13631488 | tf_op jit(solution)/shard_map/dot_general | solution.py:35
  529.7 12.5 %fusion.3 = f32[1536,2048]{1,0:T(8,128)} fusion(bf16[1536,1024]{1,0:T(8,128)(2,1)} %copy-done.45, bf16[2048,2048]{1,0:T(8,128)(2,1)} %all-gather.10.cloned.1.call-done), kind=kOutput, calls=%fused_computation.19 | convolution fusion | flops 6442450944 | bytes 19922944 | tf_op jit(solution)/shard_map/dot_general | solution.py:39
  542.3 12.8 %add_convert_fusion.p_ref = bf16[1536,2048]{1,0:T(8,128)(2,1)} fusion(f32[1536,2048]{1,0:T(8,128)} %fusion.3, bf16[1536,1024]{1,0:T(8,128)(2,1)S(1)} %copy-done.46, bf16[2048,2048]{1,0:T(8,128)(2,1)} %all-gather.10.cloned.1.call-done), kind=kOutput, calls=%fused_computation | convolution fusion | flops 6448742400 | bytes 26214400 | tf_op jit(solution)/shard_map/dot_general | solution.py:39
  555.1 72.0 %d_resid_junction.1 = (f32[768,512]{1,0:T(8,128)S(1)}, f32[1,512]{1,0:T(1,128)S(1)}, bf16[1536,2048]{1,0:T(8,128)(2,1)}) custom-call(bf16[1536,2048]{1,0:T(8,128)(2,1)} %add_convert_fusion.p_ref, f32[768,512]{1,0:T(8,128)S(1)} %convert_multiply_fusion.incoming_ref, f32[768,512]{1,0:T(8,128)S(1)} %scatter_branch.1.branch_ref, f32[1,768]{1,0:T(1,128)S(1)} %bitcast.59, ...), custom_call_target="tpu_custom_call" | custom-call | bytes 1000 | tf_op jit(solution)/shard_map/d_resid_junction/pallas_call | solution.py:397
  630.1 5.8 convolution_convert_fusion.4.x_ref
  635.9 43.8 %turn_d_attn.1.do_ref = bf16[3072,128]{1,0:T(8,128)(2,1)} custom-call(bf16[1536,256]{1,0:T(8,128)(2,1)} %convolution_convert_fusion.4.x_ref), custom_call_target="tpu_custom_call" | custom-call | bytes 1000 | tf_op jit(solution)/shard_map/turn_d_attn/pallas_call | solution.py:552
  679.8 5.9 fusion.8
  685.7 27.5 %attend_back.1.d_ref = bf16[3,3072,128]{2,1,0:T(8,128)(2,1)} custom-call(s32[1]{0:T(128)} %dynamic_slice.48.len_ref, bf16[3072,128]{1,0:T(8,128)(2,1)} %bitcast.67, bf16[3072,128]{1,0:T(8,128)(2,1)} %bitcast.65, bf16[3072,128]{1,0:T(8,128)(2,1)} %bitcast.63, bf16[3072,128]{1,0:T(8,128)(2,1)} %turn_d_attn.1.do_ref, f32[3072,128]{1,0:T(8,128)} %get-tuple-element.72.o_ref, ...), custom_call_target="tpu_custom_call" | custom-call | bytes 1000 | tf_op jit(solution)/shard_map/attend_back/pallas_call | solution.py:905
  715.0 2.3 copy-done.3
  717.4 1.7 copy-done.4
  719.0 73.9 %rear.1 = (bf16[1536,768]{1,0:T(8,128)(2,1)S(1)}, f32[2,256]{1,0:T(2,128)S(1)}) custom-call(bf16[3,3072,128]{2,1,0:T(8,128)(2,1)S(1)} %copy-done.4, f32[1536,768]{1,0:T(8,128)S(1)} %copy-done.3, f32[768,128]{1,0:T(8,128)S(1)} %copy-done.9, f32[768,128]{1,0:T(8,128)S(1)} %copy-done.7, f32[2,256]{1,0:T(2,128)S(1)} %copy-done.18, ...), custom_call_target="tpu_custom_call" | custom-call | bytes 1000 | tf_op jit(solution)/shard_map/rear/pallas_call | solution.py:760
  795.3 9.1 %fusion.7 = bf16[2048,768]{0,1:T(8,128)(2,1)} fusion(bf16[1536,768]{1,0:T(8,128)(2,1)} %copy-done.21, bf16[1536,2048]{1,0:T(8,128)(2,1)} %gather_tokens.1), kind=kOutput, calls=%fused_computation.23 | convolution fusion | flops 4834983936 | bytes 11796480 | tf_op jit(solution)/shard_map/dot_general | solution.py:35
  806.1 8.8 convolution_convert_fusion.p_ref
  814.9 42.1 %scatter_projected.1 = f32[768,512]{1,0:T(8,128)S(1)} custom-call(bf16[1536,2048]{1,0:T(8,128)(2,1)} %convolution_convert_fusion.p_ref), custom_call_target="tpu_custom_call" | custom-call | bytes 1000 | tf_op jit(solution)/shard_map/scatter_projected/pallas_call | solution.py:236
  859.3 8.2 total_gains.1
  875.3 2.6 maximum_convert_fusion.1
  878.5 2.6 maximum_convert_fusion.2
  881.1 2.5 maximum_convert_fusion
  883.6 7.3 collective-permute-done.4
  (181 shorter events, 41.5 us)
Async XLA Ops:
  7.2 3.1 copy-start.38
  7.2 3.9 copy-start.35
  7.2 69.4 %all-gather.6.cloned.1.call-start = ((), (), s32[]{:S(2)}) async-start(), calls=%async_computation.6 | async-start | bytes 3932160 | tf_op jit(solution)/shard_map/all_gather | solution.py:947
  10.3 246.2 %all-gather.8.cloned.1.call-start = ((), (), s32[]{:S(2)}) async-start(), calls=%async_computation.7 | async-start | bytes 1310720 | tf_op jit(solution)/shard_map/all_gather | solution.py:953
  11.1 330.1 %all-gather.10.cloned.1.call-start = ((), (), s32[]{:S(2)}) async-start(), calls=%async_computation.8 | async-start | bytes 10485760 | tf_op jit(solution)/shard_map/all_gather | solution.py:954
  14.1 350.1 %all-gather.14.cloned.1.call-start = ((), (), s32[]{:S(2)}) async-start(), calls=%async_computation.10 | async-start | bytes 2621440 | tf_op jit(solution)/shard_map/all_gather | solution.py:961
  16.0 35.3 %copy-start.39 = (f32[512]{0:T(512)S(1)}, f32[512]{0:T(512)}, u32[]{:S(2)}) copy-start(f32[512]{0:T(512)} %param.23) | copy-start | bytes 6148
  16.0 35.4 %copy-start.40 = (f32[512]{0:T(512)S(1)}, f32[512]{0:T(512)}, u32[]{:S(2)}) copy-start(f32[512]{0:T(512)} %param.24) | copy-start | bytes 6148
  16.0 385.9 %all-gather.12.cloned.1.call-start = ((), (), s32[]{:S(2)}) async-start(), calls=%async_computation.9 | async-start | bytes 2621440 | tf_op jit(solution)/shard_map/all_gather | solution.py:978
  16.1 38.9 %collective-permute-start = (s32[1]{0:T(128)}, s32[1]{0:T(128)}, u32[]{:S(2)}, u32[]{:S(2)}) collective-permute-start(s32[1]{0:T(128)} %param.15), channel_id=1, source_target_pairs={{0,16},{16,0},{1,17},{17,1},{2,18},{18,2},{3,19},{19,3},{4,20},{20... | collective-permute-start | bytes 20 | tf_op jit(solution)/shard_map/ppermute | solution.py:968
  50.5 504.5 %reduce-scatter.7.cloned.1.call-start = ((), (), s32[]{:S(2)}) async-start(), calls=%async_computation.11 | async-start | bytes 2621440 | tf_op jit(solution)/shard_map/reduce_scatter | solution.py:1032
  51.5 33.2 %copy-start.17 = (f32[2,256]{1,0:T(2,128)}, f32[2,256]{1,0:T(2,128)S(1)}, u32[]{:S(2)}) copy-start(f32[2,256]{1,0:T(2,128)S(1)} %pad_maximum_fusion.4.gain_ref) | copy-start | bytes 6148
  53.3 31.4 %copy-start.6 = (f32[768,128]{1,0:T(8,128)}, f32[768,128]{1,0:T(8,128)S(1)}, u32[]{:S(2)}) copy-start(f32[768,128]{1,0:T(8,128)S(1)} %get-tuple-element.131.sin_ref) | copy-start | bytes 1179652
  53.3 31.4 %copy-start.8 = (f32[768,128]{1,0:T(8,128)}, f32[768,128]{1,0:T(8,128)S(1)}, u32[]{:S(2)}) copy-start(f32[768,128]{1,0:T(8,128)S(1)} %get-tuple-element.132.cos_ref) | copy-start | bytes 1179652
  84.7 105.8 %copy-start.2 = (f32[1536,768]{1,0:T(8,128)}, f32[1536,768]{1,0:T(8,128)S(1)}, u32[]{:S(2)}) copy-start(f32[1536,768]{1,0:T(8,128)S(1)} %convolution_bitcast_fusion.qkv_ref) | copy-start | bytes 14155780
  262.4 44.0 %copy-start.19 = (f32[512]{0:T(512)S(1)}, f32[512]{0:T(512)}, u32[]{:S(2)}) copy-start(f32[512]{0:T(512)} %param.25) | copy-start | bytes 6148
  341.2 12.9 %copy-start.24 = (bf16[1536,2048]{1,0:T(8,128)(2,1)S(1)}, bf16[1536,2048]{1,0:T(8,128)(2,1)}, u32[]{:S(2)}) copy-start(bf16[1536,2048]{1,0:T(8,128)(2,1)} %gather_resid.1) | copy-start | bytes 18874372
  341.2 12.9 %copy-start.41 = (bf16[2048,2048]{1,0:T(8,128)(2,1)S(1)}, bf16[2048,2048]{1,0:T(8,128)(2,1)}, u32[]{:S(2)}) copy-start(bf16[2048,2048]{1,0:T(8,128)(2,1)} %all-gather.10.cloned.1.call-done) | copy-start | bytes 25165828
  391.8 18.0 %copy-start.20 = (f32[512]{0:T(512)S(1)}, f32[512]{0:T(512)}, u32[]{:S(2)}) copy-start(f32[512]{0:T(512)} %param.26) | copy-start | bytes 6148
  401.9 7.8 copy-start.5
  401.9 7.8 copy-start.11
  409.7 44.6 %copy-start.43 = (bf16[1536,1024]{1,0:T(8,128)(2,1)S(1)}, bf16[1536,1024]{1,0:T(8,128)(2,1)}, u32[]{:S(2)}) copy-start(bf16[1536,1024]{1,0:T(8,128)(2,1)} %get-tuple-element.139) | copy-start | bytes 9437188
  461.0 167.3 %reduce-scatter.9.cloned.1.call-start = ((), (), s32[]{:S(2)}) async-start(), calls=%async_computation.12 | async-start | bytes 2621440 | tf_op jit(solution)/shard_map/reduce_scatter | solution.py:1032
  487.9 225.4 %reduce-scatter.11.cloned.1.call-start = ((), (), s32[]{:S(2)}) async-start(), calls=%async_computation.13 | async-start | bytes 5242880 | tf_op jit(solution)/shard_map/reduce_scatter | solution.py:1032
  487.9 8.8 copy-start.27
  487.9 8.8 copy-start.42
  488.0 21.7 %slice-start = ((s8[6291456]{0:T(1024)(128)(4,1)}), s8[4194304]{0:T(1024)(128)(4,1)S(1)}, s32[]{:S(2)}) async-start(s8[6291456]{0:T(1024)(128)(4,1)} %bitcast.68), calls=%async_computation.17 | async-start | bytes 8388608
  496.8 12.8 %slice-start.1 = ((s8[6291456]{0:T(1024)(128)(4,1)}), s8[2097152]{0:T(1024)(128)(4,1)S(1)}, s32[]{:S(2)}) async-start(s8[6291456]{0:T(1024)(128)(4,1)} %bitcast.68), calls=%async_computation.18 | async-start | bytes 4194304
  518.2 276.2 %reduce-scatter.13.cloned.1.call-start = ((), (), s32[]{:S(2)}) async-start(), calls=%async_computation.14 | async-start | bytes 5242880 | tf_op jit(solution)/shard_map/reduce_scatter | solution.py:1032
  529.7 327.4 %reduce-scatter.15.cloned.1.call-start = ((), (), s32[]{:S(2)}) async-start(), calls=%async_computation.15 | async-start | bytes 1310720 | tf_op jit(solution)/shard_map/reduce_scatter | solution.py:1032
  529.7 12.5 %copy-start.46 = (bf16[1536,1024]{1,0:T(8,128)(2,1)S(1)}, bf16[1536,1024]{1,0:T(8,128)(2,1)}, u32[]{:S(2)}) copy-start(bf16[1536,1024]{1,0:T(8,128)(2,1)} %get-tuple-element.110) | copy-start | bytes 9437188
  629.5 6.4 copy-start.25
  629.5 50.2 %copy-start.23 = (bf16[1536,256]{1,0:T(8,128)(2,1)S(1)}, bf16[1536,256]{1,0:T(8,128)(2,1)}, u32[]{:S(2)}) copy-start(bf16[1536,256]{1,0:T(8,128)(2,1)} %turn_attn.1) | copy-start | bytes 2359300
  629.5 50.2 %collective-permute-start.1 = (bf16[1024,512]{1,0:T(8,128)(2,1)S(1)}, bf16[1024,512]{1,0:T(8,128)(2,1)S(1)}, u32[]{:S(2)}, u32[]{:S(2)}) collective-permute-start(bf16[1024,512]{1,0:T(8,128)(2,1)S(1)} %pad_maximum_fusion.1), channel_id=1, source_target_pairs={{0,16},{16,0},{1,17},{17,1},{2,18},{18,2},{3,19},{19,3},{4,20},{20... | collective-permute-start | bytes 3145736 | tf_op jit(solution)/shard_map/ppermute | solution.py:1029
  679.7 6.0 copy-start.30
  685.7 29.3 %copy-start.7 = (f32[768,128]{1,0:T(8,128)S(1)}, f32[768,128]{1,0:T(8,128)}, u32[]{:S(2)}) copy-start(f32[768,128]{1,0:T(8,128)} %copy-done.6) | copy-start | bytes 1179652
  685.7 29.3 %copy-start.9 = (f32[768,128]{1,0:T(8,128)S(1)}, f32[768,128]{1,0:T(8,128)}, u32[]{:S(2)}) copy-start(f32[768,128]{1,0:T(8,128)} %copy-done.8) | copy-start | bytes 1179652
  685.7 29.3 %copy-start.18 = (f32[2,256]{1,0:T(2,128)S(1)}, f32[2,256]{1,0:T(2,128)}, u32[]{:S(2)}) copy-start(f32[2,256]{1,0:T(2,128)} %copy-done.17) | copy-start | bytes 6148
  713.2 81.1 %collective-permute-start.2 = (bf16[512,1024]{1,0:T(8,128)(2,1)}, bf16[512,1024]{1,0:T(8,128)(2,1)S(1)}, u32[]{:S(2)}, u32[]{:S(2)}) collective-permute-start(bf16[512,1024]{1,0:T(8,128)(2,1)} %reduce-scatter.11.cloned.1.call-done), channel_id=1, source_target_pairs={{0,16},{16,0},{1,17},{17,1},{2,18},{18,2},{3,19},{19,3},{4,20},{20... | collective-permute-start | bytes 3145736 | tf_op jit(solution)/shard_map/ppermute | solution.py:1029
  714.7 157.3 %reduce-scatter.17.cloned.1.call-start = ((), (), s32[]{:S(2)}) async-start(), calls=%async_computation.16 | async-start | bytes 3932160 | tf_op jit(solution)/shard_map/reduce_scatter | solution.py:1032
  804.5 67.5 %collective-permute-start.3 = (bf16[512,1024]{1,0:T(8,128)(2,1)}, bf16[512,1024]{1,0:T(8,128)(2,1)}, u32[]{:S(2)}, u32[]{:S(2)}) collective-permute-start(bf16[512,1024]{1,0:T(8,128)(2,1)} %reduce-scatter.13.cloned.1.call-done), channel_id=1, source_target_pairs={{0,16},{16,0},{1,17},{17,1},{2,18},{18,2},{3,19},{19,3},{4,20},{20... | collective-permute-start | bytes 3145736 | tf_op jit(solution)/shard_map/ppermute | solution.py:1029
  814.9 53.3 %copy-start.13 = (f32[768,512]{1,0:T(8,128)S(1)}, f32[768,512]{1,0:T(8,128)}, u32[]{:S(2)}) copy-start(f32[768,512]{1,0:T(8,128)} %copy-done.12) | copy-start | bytes 4718596
  857.1 12.6 %copy-start.37 = (bf16[256,512]{1,0:T(8,128)(2,1)S(1)}, bf16[256,512]{1,0:T(8,128)(2,1)}, u32[]{:S(2)}) copy-start(bf16[256,512]{1,0:T(8,128)(2,1)} %reduce-scatter.15.cloned.1.call-done) | copy-start | bytes 786436
  857.1 12.6 %collective-permute-start.5 = (bf16[256,512]{1,0:T(8,128)(2,1)}, bf16[256,512]{1,0:T(8,128)(2,1)}, u32[]{:S(2)}, u32[]{:S(2)}) collective-permute-start(bf16[256,512]{1,0:T(8,128)(2,1)} %reduce-scatter.15.cloned.1.call-done), channel_id=1, source_target_pairs={{0,16},{16,0},{1,17},{17,1},{2,18},{18,2},{3,19},{19,3},{4,20},{20... | collective-permute-start | bytes 786440 | tf_op jit(solution)/shard_map/ppermute | solution.py:1029
  870.9 2.8 copy-start.29
  873.2 17.8 %collective-permute-start.4 = (bf16[512,768]{0,1:T(8,128)(2,1)S(1)}, bf16[512,768]{0,1:T(8,128)(2,1)S(1)}, u32[]{:S(2)}, u32[]{:S(2)}) collective-permute-start(bf16[512,768]{0,1:T(8,128)(2,1)S(1)} %copy-done.34), channel_id=1, source_target_pairs={{0,16},{16,0},{1,17},{17,1},{2,18},{18,2},{3,19},{19,3},{4,20},{20... | collective-permute-start | bytes 2359304 | tf_op jit(solution)/shard_map/ppermute | solution.py:1029
  892.6 2.8 copy-start.15
  892.6 3.6 copy-start.1
  (18 other events, 29.3 us)
Sparse Core Ops, SparseCore 0:
  10.4 66.1 all-gather.5
  78.7 51.6 all-gather.7
  132.6 175.7 all-gather.9
  310.4 45.0 all-gather.13
  357.5 44.4 all-gather.11
  461.1 41.6 reduce-scatter.6
  505.1 42.8 reduce-scatter.8
  550.8 75.9 reduce-scatter.10
  629.7 89.9 reduce-scatter.12
  722.3 55.8 reduce-scatter.14
  804.6 59.4 reduce-scatter.16

commit v9 on v8

--- a/solution.py
+++ b/solution.py
@@ -477,41 +477,52 @@
     return peers
 
 
-def gain_kernel(v_ref, out_ref, slots, send_sem, recv_sem):
+def last_kernel(p_ref, gains_ref, out_ref, total_ref, slots, *refs):
+    buffers, (send_sem, recv_sem) = refs[:7], refs[7:]
+    half = out_ref.shape[0] // 2
     me = side("dp") * 4 + lax.axis_index("row")
+    to_x, _, to_c = neighbours()
     peers = gain_peers()
-    greet(peers)
+    greet([to_x, to_c] + peers)
     started = []
     send = sender(send_sem, recv_sem, started)
-    for d, peer in enumerate(peers):
-        send(v_ref, slots.at[me], d, peer)
-    slots[me] = v_ref[...]
-    for copy in started:
+    copies = [send(gains_ref, slots.at[me], 14 + d, peer) for d, peer in enumerate(peers)]
+    slots[me] = gains_ref[...]
+    low, high = scatter_flow(p_ref, buffers, send)
+    out_ref[:half, :] = low
+    out_ref[half:, :] = high
+    for copy in copies:
         copy.wait_recv()
     total = slots[0]
     for i in range(1, 8):
         total = total + slots[i]
-    out_ref[...] = total
+    total_ref[...] = total
     for copy in started:
         copy.wait_send()
 
 
-def gain_total(values, number):
-    flat = values.reshape(-1, 128)
-    total = pl.pallas_call(
-        gain_kernel,
-        name="total_gains",
-        out_shape=jax.ShapeDtypeStruct(flat.shape, f32),
-        in_specs=[pl.BlockSpec(memory_space=pltpu.VMEM)],
-        out_specs=pl.BlockSpec(memory_space=pltpu.VMEM),
-        scratch_shapes=[
-            pltpu.VMEM((8,) + flat.shape, f32),
-            pltpu.SemaphoreType.DMA((7,)),
-            pltpu.SemaphoreType.DMA((7,)),
-        ],
-        compiler_params=pltpu.CompilerParams(collective_id=number, has_side_effects=True),
-    )(flat)
-    return total.reshape(values.shape)
+def last_scatter(partial, gains, number):
+    rows, width = partial.shape[0] // 2, partial.shape[1] // 4
+    flat = gains.reshape(-1, 128)
+    vmem = pl.BlockSpec(memory_space=pltpu.VMEM)
+    out, total = pl.pallas_call(
+        last_kernel,
+        name="scatter_projected",
+        out_shape=(
+            jax.ShapeDtypeStruct((rows, width), f32),
+            jax.ShapeDtypeStruct(flat.shape, f32),
+        ),
+        in_specs=[vmem, vmem],
+        out_specs=(vmem, vmem),
+        scratch_shapes=[pltpu.VMEM((8,) + flat.shape, f32)]
+        + scatter_buffers(rows, width)
+        + [pltpu.SemaphoreType.DMA((21,)), pltpu.SemaphoreType.DMA((21,))],
+        compiler_params=pltpu.CompilerParams(
+            collective_id=number, has_side_effects=True, vmem_limit_bytes=48 * 2**20
+        ),
+        cost_estimate=COST,
+    )(partial, flat)
+    return out, total.reshape(gains.shape)
 
 
 def row_peers():
@@ -703,14 +714,13 @@
     greet(peers + [peer for _, peer in row_peers()])
     started, moved = [], []
     move = sender(send_sem, recv_sem, moved)
-    for i in (0, 1, 2):
+    for i in (0, 1):
         for d, peer in row_peers():
             there = pl.ds(pl.multiple_of((z ^ d) * tok, tok), tok)
             move(d_ref.at[i, there], landed.at[z, i], 3 * i + d - 1, peer)
     here = pl.ds(pl.multiple_of(z * tok, tok), tok)
-    for i in (0, 1, 2):
+    for i in (0, 1):
         landed[z, i] = d_ref[i, here, :]
-    spots = [(s, h, s * heads + h) for s in range(2) for h in range(heads)]
     for i in (0, 1):
         for copy in moved[3 * i : 3 * i + 3]:
             copy.wait_recv()
@@ -737,11 +747,6 @@
     for d, peer in enumerate(peers):
         send(stat, slots.at[me], d, peer)
     slots[me] = stat[...]
-    for copy in moved[6:]:
-        copy.wait_recv()
-    for s, h, unit in spots:
-        cols = slice(2 * part + h * HEAD_DIM, 2 * part + (h + 1) * HEAD_DIM)
-        out_ref[s * tok : (s + 1) * tok, cols] = landed[unit, 2]
     inner = totals(stat, slots, started) / width
     for i in (0, 1):
         inverse = inv_ref[i : i + 1, :]
@@ -761,20 +766,20 @@
         functools.partial(rear_kernel, width),
         name="rear",
         out_shape=(
-            jax.ShapeDtypeStruct((count, 3 * part), bf16),
+            jax.ShapeDtypeStruct((count, 2 * part), bf16),
             jax.ShapeDtypeStruct((2, part), f32),
         ),
         in_specs=[pl.BlockSpec(memory_space=pltpu.VMEM)] * 6,
         out_specs=[pl.BlockSpec(memory_space=pltpu.VMEM)] * 2,
         scratch_shapes=[
-            pltpu.VMEM((units, 3, tok, HEAD_DIM), bf16),
+            pltpu.VMEM((units, 2, tok, HEAD_DIM), bf16),
             pltpu.VMEM((count, 2 * part), f32),
             pltpu.VMEM((2, count), f32),
             pltpu.VMEM((8, 2, count), f32),
             pltpu.SemaphoreType.DMA((7,)),
             pltpu.SemaphoreType.DMA((7,)),
-            pltpu.SemaphoreType.DMA((9,)),
-            pltpu.SemaphoreType.DMA((9,)),
+            pltpu.SemaphoreType.DMA((6,)),
+            pltpu.SemaphoreType.DMA((6,)),
         ],
         compiler_params=pltpu.CompilerParams(
             collective_id=number, has_side_effects=True, vmem_limit_bytes=40 * 2**20
@@ -844,7 +849,7 @@
 
 
 def attend_back_kernel(
-    len_ref, q_ref, k_ref, v_ref, do_ref, o_ref, lse_ref, out_ref, dq_acc, delta_ref
+    len_ref, q_ref, k_ref, v_ref, do_ref, o_ref, lse_ref, out_ref, dv_ref, dq_acc, delta_ref
 ):
     j = pl.program_id(0)
     bk, bq = k_ref.shape[0], BLOCK
@@ -890,7 +895,7 @@
     dk, dv = lax.fori_loop(first, stop, lambda i, s: step(i, s, False), carry)
     there = pl.ds(pl.multiple_of(j0, bk), bk)
     out_ref[1, there, :] = (dk * scale).astype(bf16)
-    out_ref[2, there, :] = dv.astype(bf16)
+    dv_ref[...] = dv.astype(bf16)
 
     @pl.when(j == pl.num_programs(0) - 1)
     def _():
@@ -906,9 +911,12 @@
         attend_back_kernel,
         name="attend_back",
         grid=(slots // BLOCK,),
-        out_shape=jax.ShapeDtypeStruct((3, slots, HEAD_DIM), bf16),
+        out_shape=(
+            jax.ShapeDtypeStruct((2, slots, HEAD_DIM), bf16),
+            jax.ShapeDtypeStruct((slots, HEAD_DIM), bf16),
+        ),
         in_specs=[pl.BlockSpec(memory_space=pltpu.SMEM), whole, part, part, whole, whole, line],
-        out_specs=pl.BlockSpec((3, slots, HEAD_DIM), lambda j: (0, 0, 0)),
+        out_specs=(pl.BlockSpec((2, slots, HEAD_DIM), lambda j: (0, 0, 0)), part),
         scratch_shapes=[pltpu.VMEM((slots, HEAD_DIM), f32), pltpu.VMEM((8, slots), f32)],
         cost_estimate=COST,
     )(length, q, k, v, do, o, lse)
@@ -1057,46 +1065,49 @@
     out_raw = (contract_first(attn_low, after(d_branch_wide, d_attn_unit)) * factor).astype(bf16)
     d_attn_unit = after(d_attn_unit, out_raw)
     out_piece = reduce_rows(out_raw, 1)
-    d_units = attend_back(unit_length, q_unit, k_unit, v_unit, d_attn_unit, attn_exact, log_total)
-    d_units, gate_piece = lax.optimization_barrier((d_units, over_dp(gate_piece)))
+    d_units, d_value_unit = attend_back(
+        unit_length, q_unit, k_unit, v_unit, d_attn_unit, attn_exact, log_total
+    )
+    d_value = turn(d_value_unit, True, tok_rows, heads, 12, "turn_d_value")
+    v_raw = (contract_first(tokens_wide, d_value) * factor).astype(bf16)
+    v_piece = reduce_rows(v_raw, 0)
+    d_units, gate_piece = lax.optimization_barrier((after(d_units, v_raw), over_dp(gate_piece)))
     other_gate = from_twin(gate_piece)
-    d_qkv, gain_sums = rear(d_units, qkv, cosine, sine_signed, qk_gain, inverse, width, 14)
-    d_qkv, gain_sums, other_gate, up_piece = lax.optimization_barrier(
-        (d_qkv, gain_sums, other_gate, over_dp(up_piece))
+    d_qk, gain_sums = rear(d_units, qkv, cosine, sine_signed, qk_gain, inverse, width, 14)
+    d_qk, gain_sums, other_gate, up_piece = lax.optimization_barrier(
+        (d_qk, gain_sums, other_gate, over_dp(up_piece))
     )
     other_up = from_twin(up_piece)
-    qkv_raw = (contract_first(tokens_wide, d_qkv) * factor).astype(bf16)
-    projected = contract_last(after(d_qkv, qkv_raw), qkv_weight).astype(bf16)
-    qkv_piece = over_dp(reduce_rows(qkv_raw, 0))
-    scattered, out_piece, gain_sums = lax.optimization_barrier(
-        (scatter_wide(projected, 16, "scatter_projected"), over_dp(out_piece), gain_sums)
-    )
-    other_out = from_twin(out_piece)
-    input_grad = d_resid + scattered
+    qk_raw = (contract_first(tokens_wide, d_qk) * factor).astype(bf16)
+    d_qkv = jnp.concatenate([after(d_qk, qk_raw), d_value], axis=1)
+    projected = contract_last(d_qkv, qkv_weight).astype(bf16)
+    qk_piece = over_dp(reduce_rows(qk_raw, 0))
 
     def spread(half):
         return lax.dynamic_update_slice_in_dim(jnp.zeros((feat_part,), f32), half, y * half_feat, 0)
 
-    gains = over_dp(
-        gain_total(
-            jnp.stack([spread(gain_sums[0]), spread(gain_sums[1]), attn_gain_raw[0], mlp_gain_raw[0]])
-            * factor,
-            15,
-        )
-    )
-
-    gains, qkv_piece, other_down, other_gate, other_up = lax.optimization_barrier(
-        (gains, qkv_piece, other_down, other_gate, other_up)
+    gains_raw = jnp.stack(
+        [spread(gain_sums[0]), spread(gain_sums[1]), attn_gain_raw[0], mlp_gain_raw[0]]
+    )
+    scattered, gains = last_scatter(projected, gains_raw * factor, 16)
+    scattered, gains, out_piece, v_piece = lax.optimization_barrier(
+        (scattered, gains, over_dp(out_piece), over_dp(v_piece))
+    )
+    other_out, other_v = from_twin(out_piece), from_twin(v_piece)
+    input_grad = d_resid + scattered
+    gains = over_dp(gains)
+    input_grad, qk_piece, other_down, other_gate, other_up = lax.optimization_barrier(
+        (input_grad, qk_piece, other_down, other_gate, other_up)
     )
 
     def whole(piece, other, axis):
         return two_sides(piece, other, y, axis).astype(f32)
 
-    qkv_other = from_twin(qkv_piece)
-    q_grad, k_grad, v_grad = (
-        two_sides(cut(qkv_piece, i, 3, 1), cut(qkv_other, i, 3, 1), y, 1).astype(f32)
-        for i in range(3)
-    )
+    qk_other = from_twin(qk_piece)
+    q_grad, k_grad = (
+        whole(cut(qk_piece, i, 2, 1), cut(qk_other, i, 2, 1), 1) for i in range(2)
+    )
+    v_grad = whole(v_piece, other_v, 1)
     return (
         block_output,
         input_grad,

time: 911 us -> 916 us (level)
    pallas_call x3 -> x2, Pallas kernels: 100 us -> 58.2 us  [scatter_wide(): pl.pallas_call(scatter_kernel, name=name, out_shape=jax.ShapeDtypeStruct(...]
    pallas_call x1, Pallas kernels: 8.22 us -> 43.7 us  [last_scatter(): pl.pallas_call(last_kernel, name='scatter_projected', out_shape=(jax.Shap...]
    pallas_call x2 -> x3, Pallas kernels: 89.1 us -> 116 us  [turn(): pl.pallas_call(functools.partial(turn_kernel, back, tok, heads), name=nam...]
    pallas_call x1, Pallas kernels: 73.9 us -> 57 us  [rear(): pl.pallas_call(functools.partial(rear_kernel, width), name='rear', out_sh...]
    dot_general x6 -> x7, matrix products: 49.1 us -> 54.1 us  [contract_first(): lax.dot_general(left, right, (((0,), (0,)), ((), ())), preferred_element_...]
  transfers between devices with their start and end apart: 17 -> 19, of which waited for: 3 -> 5; matrix products, arithmetic and copies ran while one was open for 19% -> 20% of each run, Pallas kernels for 65% -> 65%
where the time goes in v9:
time: 916 us; the launch traced here: 908 us
  Pallas kernels  630 us (69%)
  matrix products  162 us (18%)
  waiting for transfers between devices  38.9 us (4%)
  other arithmetic  25.9 us (3%)
  local copies, waits for them, and re-layouts  25.6 us (3%)
  between operations  16.2 us (2%)
  starting transfers between devices  9.79 us (1%)
    pallas_call x3, Pallas kernels, turn(): pl.pallas_call(functools.partial(turn_kernel, back, tok, heads), name=nam...  116 us
    pallas_call x1, Pallas kernels, front(): pl.pallas_call(functools.partial(front_kernel, width), name='front', out_...  104 us
    pallas_call x3, Pallas kernels, gather_wide(): pl.pallas_call(gather_kernel, name=name, out_shape=jax.ShapeDtypeStruct((...  82 us
    pallas_call x1, Pallas kernels, d_resid_junction(): pl.pallas_call(functools.partial(d_resid_kernel, width), name='d_resid_ju...  72 us
    dot_general x6, matrix products, contract_last(): lax.dot_general(left, right, (((1,), (1,)), ((), ())), preferred_element_...  60.2 us
    pallas_call x2, Pallas kernels, scatter_wide(): pl.pallas_call(scatter_kernel, name=name, out_shape=jax.ShapeDtypeStruct(...  58.2 us
    pallas_call x1, Pallas kernels, rear(): pl.pallas_call(functools.partial(rear_kernel, width), name='rear', out_sh...  57 us
    dot_general x7, matrix products, contract_first(): lax.dot_general(left, right, (((0,), (0,)), ((), ())), preferred_element_...  54.1 us
  transfers between devices with their start and end apart: 19, of which 5 were waited for; matrix products, arithmetic and copies ran while one was open for 20% of the time, Pallas kernels for 65%

profile of v9, /device:TPU:0, one launch (start us, length us, event | category | flops | bytes accessed | tf_op | source)
XLA Modules:
  0.0 908.4 jit_solution(90239200216531156)
XLA Ops:
  16.1 3.1 collective-permute-start
  19.1 31.4 %gather_tokens.1 = bf16[1536,2048]{1,0:T(8,128)(2,1)} custom-call(bf16[768,512]{1,0:T(8,128)(2,1)} %x_ref.1), custom_call_target="tpu_custom_call" | custom-call | bytes 1000 | tf_op jit(solution)/shard_map/gather_tokens/pallas_call | solution.py:136
  51.7 1.6 negate_select_fusion
  56.2 20.4 %all-gather.6.cloned.1.call-done = bf16[2048,768]{1,0:T(8,128)(2,1)} async-done(((bf16[512,768]{1,0:T(8,128)(2,1)}), bf16[2048,768]{1,0:T(8,128)(2,1)}) %all-gather.6.cloned.1.call-update) | async-done | bytes 3145744 | tf_op jit(solution)/shard_map/all_gather | solution.py:955
  76.6 8.1 convolution_bitcast_fusion.qkv_ref
  84.7 104.3 %front.1 = (bf16[4,3,768,128]{3,2,1,0:T(8,128)(2,1)S(1)}, f32[2,1536]{1,0:T(2,128)S(1)}) custom-call(f32[1536,768]{1,0:T(8,128)S(1)} %convolution_bitcast_fusion.qkv_ref, f32[768,128]{1,0:T(8,128)S(1)} %get-tuple-element.144.cos_ref, f32[768,128]{1,0:T(8,128)S(1)} %get-tuple-element.143.sin_ref, f32[2,256]{1,0:T(2,128)S(1)} %pad_maximum_fusion.4.gain_ref), custom_call_target="tpu_custom_call" | custom-call | bytes 1000 | tf_op jit(solution)/shard_map/front/pallas_call | solution.py:662
  190.5 20.7 %attend.1 = (bf16[3072,128]{1,0:T(8,128)(2,1)}, f32[3072,128]{1,0:T(8,128)}, f32[8,3072]{1,0:T(8,128)}) custom-call(s32[1]{0:T(128)} %dynamic_slice.42.len_ref, bf16[3072,128]{1,0:T(8,128)(2,1)} %bitcast.69, bf16[3072,128]{1,0:T(8,128)(2,1)} %bitcast.67, bf16[3072,128]{1,0:T(8,128)(2,1)} %bitcast.65), custom_call_target="tpu_custom_call" | custom-call | bytes 1000 | tf_op jit(solution)/shard_map/attend/pallas_call | solution.py:836
  211.1 45.3 %turn_attn.1 = bf16[1536,256]{1,0:T(8,128)(2,1)} custom-call(bf16[3072,128]{1,0:T(8,128)(2,1)} %get-tuple-element.61.x_ref), custom_call_target="tpu_custom_call" | custom-call | bytes 1000 | tf_op jit(solution)/shard_map/turn_attn/pallas_call | solution.py:563
  256.5 5.9 convolution_convert_fusion.1.p_ref
  262.4 37.6 %scatter_branch.1.branch_ref = f32[768,512]{1,0:T(8,128)S(1)} custom-call(bf16[1536,2048]{1,0:T(8,128)(2,1)} %convolution_convert_fusion.1.p_ref), custom_call_target="tpu_custom_call" | custom-call | bytes 1000 | tf_op jit(solution)/shard_map/scatter_branch/pallas_call | solution.py:236
  300.8 4.9 total_branch.1
  306.4 2.8 fusion.21
  309.2 31.9 %gather_resid.1 = bf16[1536,2048]{1,0:T(8,128)(2,1)} custom-call(bf16[768,512]{1,0:T(8,128)(2,1)} %get-tuple-element.120.x_ref), custom_call_target="tpu_custom_call" | custom-call | bytes 1000 | tf_op jit(solution)/shard_map/gather_resid/pallas_call | solution.py:136
  341.2 10.2 %fusion.5 = f32[1536,1024]{1,0:T(8,128)S(1)} fusion(bf16[1536,2048]{1,0:T(8,128)(2,1)} %gather_resid.1, bf16[2048,2048]{1,0:T(8,128)(2,1)} %all-gather.10.cloned.1.call-done), kind=kOutput, calls=%fused_computation.21 | convolution fusion | flops 6442450944 | bytes 16777216 | tf_op jit(solution)/shard_map/dot_general | solution.py:31
  351.4 2.6 copy-done.44
  354.1 10.1 %multiply_convert_fusion.4 = (bf16[1536,1024]{1,0:T(8,128)(2,1)}, f32[1536,1024]{1,0:T(8,128)}) fusion(f32[1536,1024]{1,0:T(8,128)S(1)} %fusion.5, bf16[1536,2048]{1,0:T(8,128)(2,1)S(1)} %copy-done.25, bf16[2048,2048]{1,0:T(8,128)(2,1)S(1)} %copy-done.41), kind=kOutput, calls=%fused_computation.7 | convolution fusion | flops 6451888128 | bytes 26214400 | tf_op jit(solution)/shard_map/dot_general | solution.py:31
  364.2 6.1 convolution_convert_fusion.3.p_ref
  370.3 20.6 %scatter_mixed_low.1.low_ref = f32[768,256]{1,0:T(8,128)S(1)} custom-call(bf16[1536,1024]{1,0:T(8,128)(2,1)S(1)} %convolution_convert_fusion.3.p_ref), custom_call_target="tpu_custom_call" | custom-call | bytes 1000 | tf_op jit(solution)/shard_map/scatter_mixed_low/pallas_call | solution.py:236
  391.7 10.2 %all-gather.12.cloned.1.call-done = bf16[1024,1024]{1,0:T(8,128)(2,1)} async-done(((bf16[1024,256]{1,0:T(8,128)(2,1)}), bf16[1024,1024]{1,0:T(8,128)(2,1)}) %all-gather.12.cloned.1.call-update) | async-done | bytes 2097168 | tf_op jit(solution)/shard_map/all_gather | solution.py:986
  402.0 7.8 convolution_convert_fusion.2.p_ref
  409.8 42.9 %mixed_junction.1 = (bf16[768,512]{1,0:T(8,128)(2,1)S(1)}, f32[1,512]{1,0:T(1,128)S(1)}, bf16[768,256]{1,0:T(8,128)(2,1)S(1)}, bf16[1536,1024]{1,0:T(8,128)(2,1)}) custom-call(bf16[1536,1024]{1,0:T(8,128)(2,1)} %convolution_convert_fusion.2.p_ref, f32[768,256]{1,0:T(8,128)S(1)} %copy-done.10, f32[768,512]{1,0:T(8,128)S(1)} %convert_multiply_fusion.incoming_ref, ...), custom_call_target="tpu_custom_call" | custom-call | bytes 1000 | tf_op jit(solution)/shard_map/mixed_junction/pallas_call | solution.py:326
  454.3 6.5 multiply_convert_fusion.7
  461.4 18.7 %gather_d_mixed_high.1 = bf16[1536,1024]{1,0:T(8,128)(2,1)} custom-call(bf16[768,256]{1,0:T(8,128)(2,1)} %copy-done.16), custom_call_target="tpu_custom_call" | custom-call | bytes 1000 | tf_op jit(solution)/shard_map/gather_d_mixed_high/pallas_call | solution.py:136
  480.1 7.7 multiply_convert_fusion.6
  487.9 8.8 fusion.24
  496.7 11.1 %multiply_convert_fusion.2 = (bf16[1536,1024]{1,0:T(8,128)(2,1)}, bf16[1536,1024]{1,0:T(8,128)(2,1)S(1)}) fusion(f32[1536,1024]{1,0:T(8,128)} %copy-done.44, f32[1536,1024]{1,0:T(8,128)} %get-tuple-element.152, f32[1536,1024]{1,0:T(8,128)} %fusion.24, bf16[1536,1024]{1,0:T(8,128)(2,1)S(1)} %copy-done.28, bf16[1024,1024]{1,0:T(8,128)(2,1)S(1)} %copy-done.42), kind=kOutput, calls=%fused_computation.5 | convolution fusion | flops 3243245568 | bytes 30408704 | tf_op jit(solution)/shard_map/dot_general | solution.py:39
  507.8 1.7 copy-done.45
  509.5 8.5 multiply_convert_fusion.1
  518.3 11.2 %multiply_convert_fusion = bf16[2048,1024]{1,0:T(8,128)(2,1)} fusion(bf16[1536,2048]{1,0:T(8,128)(2,1)} %gather_resid.1, bf16[1536,1024]{1,0:T(8,128)(2,1)} %get-tuple-element.122), kind=kOutput, calls=%fused_computation.1 | convolution fusion | flops 6446645248 | bytes 13631488 | tf_op jit(solution)/shard_map/dot_general | solution.py:35
  529.6 12.5 %fusion.3 = f32[1536,2048]{1,0:T(8,128)} fusion(bf16[1536,1024]{1,0:T(8,128)(2,1)} %copy-done.45, bf16[2048,2048]{1,0:T(8,128)(2,1)} %all-gather.10.cloned.1.call-done), kind=kOutput, calls=%fused_computation.19 | convolution fusion | flops 6442450944 | bytes 19922944 | tf_op jit(solution)/shard_map/dot_general | solution.py:39
  542.1 12.8 %add_convert_fusion.p_ref = bf16[1536,2048]{1,0:T(8,128)(2,1)} fusion(f32[1536,2048]{1,0:T(8,128)} %fusion.3, bf16[1536,1024]{1,0:T(8,128)(2,1)S(1)} %copy-done.46, bf16[2048,2048]{1,0:T(8,128)(2,1)} %all-gather.10.cloned.1.call-done), kind=kOutput, calls=%fused_computation | convolution fusion | flops 6448742400 | bytes 26214400 | tf_op jit(solution)/shard_map/dot_general | solution.py:39
  555.0 72.0 %d_resid_junction.1 = (f32[768,512]{1,0:T(8,128)S(1)}, f32[1,512]{1,0:T(1,128)S(1)}, bf16[1536,2048]{1,0:T(8,128)(2,1)}) custom-call(bf16[1536,2048]{1,0:T(8,128)(2,1)} %add_convert_fusion.p_ref, f32[768,512]{1,0:T(8,128)S(1)} %convert_multiply_fusion.incoming_ref, f32[768,512]{1,0:T(8,128)S(1)} %scatter_branch.1.branch_ref, f32[1,768]{1,0:T(1,128)S(1)} %bitcast.62, ...), custom_call_target="tpu_custom_call" | custom-call | bytes 1000 | tf_op jit(solution)/shard_map/d_resid_junction/pallas_call | solution.py:397
  629.9 5.8 convolution_convert_fusion.4.x_ref
  635.8 43.9 %turn_d_attn.1.do_ref = bf16[3072,128]{1,0:T(8,128)(2,1)} custom-call(bf16[1536,256]{1,0:T(8,128)(2,1)} %convolution_convert_fusion.4.x_ref), custom_call_target="tpu_custom_call" | custom-call | bytes 1000 | tf_op jit(solution)/shard_map/turn_d_attn/pallas_call | solution.py:563
  679.7 5.9 fusion.8
  685.8 27.4 %attend_back.1 = (bf16[2,3072,128]{2,1,0:T(8,128)(2,1)}, bf16[3072,128]{1,0:T(8,128)(2,1)}) custom-call(s32[1]{0:T(128)} %dynamic_slice.42.len_ref, bf16[3072,128]{1,0:T(8,128)(2,1)} %bitcast.70, bf16[3072,128]{1,0:T(8,128)(2,1)} %bitcast.68, bf16[3072,128]{1,0:T(8,128)(2,1)} %bitcast.66, bf16[3072,128]{1,0:T(8,128)(2,1)} %turn_d_attn.1.do_ref, ...), custom_call_target="tpu_custom_call" | custom-call | bytes 1000 | tf_op jit(solution)/shard_map/attend_back/pallas_call | solution.py:910
  713.1 27.2 %turn_d_value.1 = bf16[1536,256]{1,0:T(8,128)(2,1)} custom-call(bf16[3072,128]{1,0:T(8,128)(2,1)} %get-tuple-element.81.x_ref), custom_call_target="tpu_custom_call" | custom-call | bytes 1000 | tf_op jit(solution)/shard_map/turn_d_value/pallas_call | solution.py:563
  740.4 6.0 fusion.10
  748.3 2.3 copy-done.3
  750.6 57.0 %rear.1 = (bf16[1536,512]{1,0:T(8,128)(2,1)S(1)}, f32[2,256]{1,0:T(2,128)S(1)}) custom-call(bf16[2,3072,128]{2,1,0:T(8,128)(2,1)S(1)} %copy-done.13, f32[1536,768]{1,0:T(8,128)S(1)} %copy-done.3, f32[768,128]{1,0:T(8,128)S(1)} %copy-done.8, f32[768,128]{1,0:T(8,128)S(1)} %copy-done.6, f32[2,256]{1,0:T(2,128)S(1)} %copy-done.18, ...), custom_call_target="tpu_custom_call" | custom-call | bytes 1000 | tf_op jit(solution)/shard_map/rear/pallas_call | solution.py:765
  808.8 8.2 fusion.7
  817.7 9.2 %convolution_convert_fusion.p_ref = bf16[1536,2048]{1,0:T(8,128)(2,1)} fusion(bf16[2048,768]{1,0:T(8,128)(2,1)} %all-gather.6.cloned.1.call-done, bf16[1536,256]{1,0:T(8,128)(2,1)S(1)} %copy-done.24, bf16[1536,512]{1,0:T(8,128)(2,1)S(1)} %copy-done.22), kind=kOutput, calls=%fused_computation.3 | convolution fusion | flops 4839702528 | bytes 11796480 | tf_op jit(solution)/shard_map/dot_general | solution.py:39
  826.9 43.7 %scatter_projected.1 = (f32[768,512]{1,0:T(8,128)S(1)}, f32[16,128]{1,0:T(8,128)S(1)}) custom-call(bf16[1536,2048]{1,0:T(8,128)(2,1)} %convolution_convert_fusion.p_ref, f32[16,128]{1,0:T(8,128)S(1)} %mul.154.gains_ref), custom_call_target="tpu_custom_call" | custom-call | bytes 1000 | tf_op jit(solution)/shard_map/scatter_projected/pallas_call | solution.py:508
  874.8 5.3 collective-permute-done.5
  881.6 2.2 collective-permute-done.6
  889.0 2.6 maximum_convert_fusion.1
  891.5 2.6 maximum_convert_fusion.2
  894.1 2.5 maximum_convert_fusion
  (188 shorter events, 40.3 us)
Async XLA Ops:
  7.2 69.4 %all-gather.6.cloned.1.call-start = ((), (), s32[]{:S(2)}) async-start(), calls=%async_computation.7 | async-start | bytes 3932160 | tf_op jit(solution)/shard_map/all_gather | solution.py:955
  10.3 246.2 %all-gather.8.cloned.1.call-start = ((), (), s32[]{:S(2)}) async-start(), calls=%async_computation.8 | async-start | bytes 1310720 | tf_op jit(solution)/shard_map/all_gather | solution.py:961
  11.1 330.1 %all-gather.10.cloned.1.call-start = ((), (), s32[]{:S(2)}) async-start(), calls=%async_computation.9 | async-start | bytes 10485760 | tf_op jit(solution)/shard_map/all_gather | solution.py:962
  14.1 350.0 %all-gather.14.cloned.1.call-start = ((), (), s32[]{:S(2)}) async-start(), calls=%async_computation.11 | async-start | bytes 2621440 | tf_op jit(solution)/shard_map/all_gather | solution.py:969
  16.0 35.3 %copy-start.39 = (f32[512]{0:T(512)S(1)}, f32[512]{0:T(512)}, u32[]{:S(2)}) copy-start(f32[512]{0:T(512)} %param.23) | copy-start | bytes 6148
  16.0 35.4 %copy-start.40 = (f32[512]{0:T(512)S(1)}, f32[512]{0:T(512)}, u32[]{:S(2)}) copy-start(f32[512]{0:T(512)} %param.24) | copy-start | bytes 6148
  16.0 385.9 %all-gather.12.cloned.1.call-start = ((), (), s32[]{:S(2)}) async-start(), calls=%async_computation.10 | async-start | bytes 2621440 | tf_op jit(solution)/shard_map/all_gather | solution.py:986
  16.1 38.9 %collective-permute-start = (s32[1]{0:T(128)}, s32[1]{0:T(128)}, u32[]{:S(2)}, u32[]{:S(2)}) collective-permute-start(s32[1]{0:T(128)} %param.15), channel_id=1, source_target_pairs={{0,16},{16,0},{1,17},{17,1},{2,18},{18,2},{3,19},{19,3},{4,20},{20... | collective-permute-start | bytes 20 | tf_op jit(solution)/shard_map/ppermute | solution.py:976
  50.5 504.4 %reduce-scatter.8.cloned.1.call-start = ((), (), s32[]{:S(2)}) async-start(), calls=%async_computation.12 | async-start | bytes 2621440 | tf_op jit(solution)/shard_map/reduce_scatter | solution.py:1040
  51.5 33.2 %copy-start.17 = (f32[2,256]{1,0:T(2,128)}, f32[2,256]{1,0:T(2,128)S(1)}, u32[]{:S(2)}) copy-start(f32[2,256]{1,0:T(2,128)S(1)} %pad_maximum_fusion.4.gain_ref) | copy-start | bytes 6148
  53.3 31.4 %copy-start.5 = (f32[768,128]{1,0:T(8,128)}, f32[768,128]{1,0:T(8,128)S(1)}, u32[]{:S(2)}) copy-start(f32[768,128]{1,0:T(8,128)S(1)} %get-tuple-element.143.sin_ref) | copy-start | bytes 1179652
  53.3 31.4 %copy-start.7 = (f32[768,128]{1,0:T(8,128)}, f32[768,128]{1,0:T(8,128)S(1)}, u32[]{:S(2)}) copy-start(f32[768,128]{1,0:T(8,128)S(1)} %get-tuple-element.144.cos_ref) | copy-start | bytes 1179652
  84.7 105.8 %copy-start.2 = (f32[1536,768]{1,0:T(8,128)}, f32[1536,768]{1,0:T(8,128)S(1)}, u32[]{:S(2)}) copy-start(f32[1536,768]{1,0:T(8,128)S(1)} %convolution_bitcast_fusion.qkv_ref) | copy-start | bytes 14155780
  262.4 44.0 %copy-start.19 = (f32[512]{0:T(512)S(1)}, f32[512]{0:T(512)}, u32[]{:S(2)}) copy-start(f32[512]{0:T(512)} %param.25) | copy-start | bytes 6148
  341.2 12.9 %copy-start.25 = (bf16[1536,2048]{1,0:T(8,128)(2,1)S(1)}, bf16[1536,2048]{1,0:T(8,128)(2,1)}, u32[]{:S(2)}) copy-start(bf16[1536,2048]{1,0:T(8,128)(2,1)} %gather_resid.1) | copy-start | bytes 18874372
  341.2 12.8 %copy-start.41 = (bf16[2048,2048]{1,0:T(8,128)(2,1)S(1)}, bf16[2048,2048]{1,0:T(8,128)(2,1)}, u32[]{:S(2)}) copy-start(bf16[2048,2048]{1,0:T(8,128)(2,1)} %all-gather.10.cloned.1.call-done) | copy-start | bytes 25165828
  391.7 18.0 %copy-start.20 = (f32[512]{0:T(512)S(1)}, f32[512]{0:T(512)}, u32[]{:S(2)}) copy-start(f32[512]{0:T(512)} %param.26) | copy-start | bytes 6148
  401.9 7.8 copy-start.4
  402.0 7.8 copy-start.10
  409.8 44.6 %copy-start.43 = (bf16[1536,1024]{1,0:T(8,128)(2,1)S(1)}, bf16[1536,1024]{1,0:T(8,128)(2,1)}, u32[]{:S(2)}) copy-start(bf16[1536,1024]{1,0:T(8,128)(2,1)} %get-tuple-element.151) | copy-start | bytes 9437188
  460.9 167.2 %reduce-scatter.10.cloned.1.call-start = ((), (), s32[]{:S(2)}) async-start(), calls=%async_computation.13 | async-start | bytes 2621440 | tf_op jit(solution)/shard_map/reduce_scatter | solution.py:1040
  487.8 258.9 %reduce-scatter.12.cloned.1.call-start = ((), (), s32[]{:S(2)}) async-start(), calls=%async_computation.14 | async-start | bytes 5242880 | tf_op jit(solution)/shard_map/reduce_scatter | solution.py:1040
  487.9 8.8 copy-start.28
  487.9 8.8 copy-start.42
  487.9 21.6 %slice-start = ((s8[6291456]{0:T(1024)(128)(4,1)}), s8[4194304]{0:T(1024)(128)(4,1)S(1)}, s32[]{:S(2)}) async-start(s8[6291456]{0:T(1024)(128)(4,1)} %bitcast.71), calls=%async_computation.19 | async-start | bytes 8388608
  496.7 12.8 %slice-start.1 = ((s8[6291456]{0:T(1024)(128)(4,1)}), s8[2097152]{0:T(1024)(128)(4,1)S(1)}, s32[]{:S(2)}) async-start(s8[6291456]{0:T(1024)(128)(4,1)} %bitcast.71), calls=%async_computation.20 | async-start | bytes 4194304
  518.1 290.7 %reduce-scatter.14.cloned.1.call-start = ((), (), s32[]{:S(2)}) async-start(), calls=%async_computation.15 | async-start | bytes 5242880 | tf_op jit(solution)/shard_map/reduce_scatter | solution.py:1040
  529.6 341.1 %reduce-scatter.16.cloned.1.call-start = ((), (), s32[]{:S(2)}) async-start(), calls=%async_computation.16 | async-start | bytes 1310720 | tf_op jit(solution)/shard_map/reduce_scatter | solution.py:1040
  529.6 12.5 %copy-start.46 = (bf16[1536,1024]{1,0:T(8,128)(2,1)S(1)}, bf16[1536,1024]{1,0:T(8,128)(2,1)}, u32[]{:S(2)}) copy-start(bf16[1536,1024]{1,0:T(8,128)(2,1)} %get-tuple-element.122) | copy-start | bytes 9437188
  629.4 6.4 copy-start.26
  629.4 50.3 %copy-start.23 = (bf16[1536,256]{1,0:T(8,128)(2,1)S(1)}, bf16[1536,256]{1,0:T(8,128)(2,1)}, u32[]{:S(2)}) copy-start(bf16[1536,256]{1,0:T(8,128)(2,1)} %turn_attn.1) | copy-start | bytes 2359300
  629.4 50.3 %collective-permute-start.1 = (bf16[1024,512]{1,0:T(8,128)(2,1)S(1)}, bf16[1024,512]{1,0:T(8,128)(2,1)S(1)}, u32[]{:S(2)}, u32[]{:S(2)}) collective-permute-start(bf16[1024,512]{1,0:T(8,128)(2,1)S(1)} %pad_maximum_fusion.1), channel_id=1, source_target_pairs={{0,16},{16,0},{1,17},{17,1},{2,18},{18,2},{3,19},{19,3},{4,20},{20... | collective-permute-start | bytes 3145736 | tf_op jit(solution)/shard_map/ppermute | solution.py:1037
  685.7 184.9 %reduce-scatter.18.cloned.1.call-start = ((), (), s32[]{:S(2)}) async-start(), calls=%async_computation.17 | async-start | bytes 1310720 | tf_op jit(solution)/shard_map/reduce_scatter | solution.py:1040
  740.4 7.9 copy-start.6
  740.4 7.9 copy-start.8
  740.4 7.9 copy-start.13
  740.4 7.9 copy-start.18
  746.4 138.6 %reduce-scatter.20.cloned.1.call-start = ((), (), s32[]{:S(2)}) async-start(), calls=%async_computation.18 | async-start | bytes 2621440 | tf_op jit(solution)/shard_map/reduce_scatter | solution.py:1040
  746.7 62.0 %collective-permute-start.2 = (bf16[512,1024]{1,0:T(8,128)(2,1)}, bf16[512,1024]{1,0:T(8,128)(2,1)}, u32[]{:S(2)}, u32[]{:S(2)}) collective-permute-start(bf16[512,1024]{1,0:T(8,128)(2,1)} %reduce-scatter.12.cloned.1.call-done), channel_id=1, source_target_pairs={{0,16},{16,0},{1,17},{17,1},{2,18},{18,2},{3,19},{19,3},{4,20},{20... | collective-permute-start | bytes 3145736 | tf_op jit(solution)/shard_map/ppermute | solution.py:1037
  808.7 8.9 copy-start.22
  808.7 8.9 copy-start.24
  817.0 67.9 %collective-permute-start.3 = (bf16[512,1024]{1,0:T(8,128)(2,1)}, bf16[512,1024]{1,0:T(8,128)(2,1)}, u32[]{:S(2)}, u32[]{:S(2)}) collective-permute-start(bf16[512,1024]{1,0:T(8,128)(2,1)} %reduce-scatter.14.cloned.1.call-done), channel_id=1, source_target_pairs={{0,16},{16,0},{1,17},{17,1},{2,18},{18,2},{3,19},{19,3},{4,20},{20... | collective-permute-start | bytes 3145736 | tf_op jit(solution)/shard_map/ppermute | solution.py:1037
  826.9 45.9 %copy-start.12 = (f32[768,512]{1,0:T(8,128)S(1)}, f32[768,512]{1,0:T(8,128)}, u32[]{:S(2)}) copy-start(f32[768,512]{1,0:T(8,128)} %copy-done.11) | copy-start | bytes 4718596
  870.7 9.5 %copy-start.37 = (bf16[512,256]{0,1:T(8,128)(2,1)S(1)}, bf16[512,256]{0,1:T(8,128)(2,1)}, u32[]{:S(2)}) copy-start(bf16[512,256]{0,1:T(8,128)(2,1)} %reduce-scatter.18.cloned.1.call-done) | copy-start | bytes 786436
  870.7 9.5 %collective-permute-start.5 = (bf16[512,256]{0,1:T(8,128)(2,1)}, bf16[512,256]{0,1:T(8,128)(2,1)S(1)}, u32[]{:S(2)}, u32[]{:S(2)}) collective-permute-start(bf16[512,256]{0,1:T(8,128)(2,1)} %reduce-scatter.18.cloned.1.call-done), channel_id=1, source_target_pairs={{0,16},{16,0},{1,17},{17,1},{2,18},{18,2},{3,19},{19,3},{4,20},{20... | collective-permute-start | bytes 786440 | tf_op jit(solution)/shard_map/ppermute | solution.py:1037
  871.6 12.2 %collective-permute-start.6 = (bf16[256,512]{1,0:T(8,128)(2,1)}, bf16[256,512]{1,0:T(8,128)(2,1)S(1)}, u32[]{:S(2)}, u32[]{:S(2)}) collective-permute-start(bf16[256,512]{1,0:T(8,128)(2,1)} %reduce-scatter.16.cloned.1.call-done), channel_id=1, source_target_pairs={{0,16},{16,0},{1,17},{17,1},{2,18},{18,2},{3,19},{19,3},{4,20},{20... | collective-permute-start | bytes 786440 | tf_op jit(solution)/shard_map/ppermute | solution.py:1037
  874.3 9.5 %copy-start.36 = (bf16[256,512]{1,0:T(8,128)(2,1)S(1)}, bf16[256,512]{1,0:T(8,128)(2,1)}, u32[]{:S(2)}) copy-start(bf16[256,512]{1,0:T(8,128)(2,1)} %reduce-scatter.16.cloned.1.call-done) | copy-start | bytes 786436
  885.0 12.2 %collective-permute-start.4 = (bf16[512,512]{0,1:T(8,128)(2,1)}, bf16[512,512]{0,1:T(8,128)(2,1)S(1)}, u32[]{:S(2)}, u32[]{:S(2)}) collective-permute-start(bf16[512,512]{0,1:T(8,128)(2,1)} %reduce-scatter.20.cloned.1.call-done), channel_id=1, source_target_pairs={{0,16},{16,0},{1,17},{17,1},{2,18},{18,2},{3,19},{19,3},{4,20},{20... | collective-permute-start | bytes 1572872 | tf_op jit(solution)/shard_map/ppermute | solution.py:1037
  (20 other events, 49.3 us)
Sparse Core Ops, SparseCore 0:
  10.4 66.1 all-gather.5
  78.7 51.6 all-gather.7
  132.6 175.7 all-gather.9
  310.4 45.0 all-gather.13
  357.5 44.4 all-gather.11
  461.0 41.6 reduce-scatter.7
  505.0 42.8 reduce-scatter.9
  550.7 75.9 reduce-scatter.11
  629.6 90.5 reduce-scatter.13
  722.9 54.9 reduce-scatter.15
  780.8 36.7 reduce-scatter.17
  820.4 43.1 reduce-scatter.19

commit v10 on v9

--- a/solution.py
+++ b/solution.py
@@ -714,13 +714,14 @@
     greet(peers + [peer for _, peer in row_peers()])
     started, moved = [], []
     move = sender(send_sem, recv_sem, moved)
-    for i in (0, 1):
+    for i in (0, 1, 2):
         for d, peer in row_peers():
             there = pl.ds(pl.multiple_of((z ^ d) * tok, tok), tok)
             move(d_ref.at[i, there], landed.at[z, i], 3 * i + d - 1, peer)
     here = pl.ds(pl.multiple_of(z * tok, tok), tok)
-    for i in (0, 1):
+    for i in (0, 1, 2):
         landed[z, i] = d_ref[i, here, :]
+    spots = [(s, h, s * heads + h) for s in range(2) for h in range(heads)]
     for i in (0, 1):
         for copy in moved[3 * i : 3 * i + 3]:
             copy.wait_recv()
@@ -747,6 +748,11 @@
     for d, peer in enumerate(peers):
         send(stat, slots.at[me], d, peer)
     slots[me] = stat[...]
+    for copy in moved[6:]:
+        copy.wait_recv()
+    for s, h, unit in spots:
+        cols = slice(2 * part + h * HEAD_DIM, 2 * part + (h + 1) * HEAD_DIM)
+        out_ref[s * tok : (s + 1) * tok, cols] = landed[unit, 2]
     inner = totals(stat, slots, started) / width
     for i in (0, 1):
         inverse = inv_ref[i : i + 1, :]
@@ -766,20 +772,20 @@
         functools.partial(rear_kernel, width),
         name="rear",
         out_shape=(
-            jax.ShapeDtypeStruct((count, 2 * part), bf16),
+            jax.ShapeDtypeStruct((count, 3 * part), bf16),
             jax.ShapeDtypeStruct((2, part), f32),
         ),
         in_specs=[pl.BlockSpec(memory_space=pltpu.VMEM)] * 6,
         out_specs=[pl.BlockSpec(memory_space=pltpu.VMEM)] * 2,
         scratch_shapes=[
-            pltpu.VMEM((units, 2, tok, HEAD_DIM), bf16),
+            pltpu.VMEM((units, 3, tok, HEAD_DIM), bf16),
             pltpu.VMEM((count, 2 * part), f32),
             pltpu.VMEM((2, count), f32),
             pltpu.VMEM((8, 2, count), f32),
             pltpu.SemaphoreType.DMA((7,)),
             pltpu.SemaphoreType.DMA((7,)),
-            pltpu.SemaphoreType.DMA((6,)),
-            pltpu.SemaphoreType.DMA((6,)),
+            pltpu.SemaphoreType.DMA((9,)),
+            pltpu.SemaphoreType.DMA((9,)),
         ],
         compiler_params=pltpu.CompilerParams(
             collective_id=number, has_side_effects=True, vmem_limit_bytes=40 * 2**20
@@ -849,7 +855,7 @@
 
 
 def attend_back_kernel(
-    len_ref, q_ref, k_ref, v_ref, do_ref, o_ref, lse_ref, out_ref, dv_ref, dq_acc, delta_ref
+    len_ref, q_ref, k_ref, v_ref, do_ref, o_ref, lse_ref, out_ref, dq_acc, delta_ref
 ):
     j = pl.program_id(0)
     bk, bq = k_ref.shape[0], BLOCK
@@ -895,7 +901,7 @@
     dk, dv = lax.fori_loop(first, stop, lambda i, s: step(i, s, False), carry)
     there = pl.ds(pl.multiple_of(j0, bk), bk)
     out_ref[1, there, :] = (dk * scale).astype(bf16)
-    dv_ref[...] = dv.astype(bf16)
+    out_ref[2, there, :] = dv.astype(bf16)
 
     @pl.when(j == pl.num_programs(0) - 1)
     def _():
@@ -911,12 +917,9 @@
         attend_back_kernel,
         name="attend_back",
         grid=(slots // BLOCK,),
-        out_shape=(
-            jax.ShapeDtypeStruct((2, slots, HEAD_DIM), bf16),
-            jax.ShapeDtypeStruct((slots, HEAD_DIM), bf16),
-        ),
+        out_shape=jax.ShapeDtypeStruct((3, slots, HEAD_DIM), bf16),
         in_specs=[pl.BlockSpec(memory_space=pltpu.SMEM), whole, part, part, whole, whole, line],
-        out_specs=(pl.BlockSpec((2, slots, HEAD_DIM), lambda j: (0, 0, 0)), part),
+        out_specs=pl.BlockSpec((3, slots, HEAD_DIM), lambda j: (0, 0, 0)),
         scratch_shapes=[pltpu.VMEM((slots, HEAD_DIM), f32), pltpu.VMEM((8, slots), f32)],
         cost_estimate=COST,
     )(length, q, k, v, do, o, lse)
@@ -1042,16 +1045,14 @@
     d_hidden = contract_last(d_low_wide, low_weight) + contract_last(d_high_wide, high_weight)
     d_gate = (d_hidden * upper * sigma * (1.0 + gate * (1.0 - sigma))).astype(bf16)
     d_upper = (d_hidden * gate * sigma).astype(bf16)
-    gate_raw = (contract_first(resid_wide, d_gate) * factor).astype(bf16)
-    up_raw = (contract_first(resid_wide, d_upper) * factor).astype(bf16)
-    d_resid_wide = (
-        contract_last(d_gate, gate_weight) + contract_last(d_upper, up_weight)
-    ).astype(bf16)
+    d_gate_up = jnp.concatenate([d_gate, d_upper], axis=1)
+    gate_up_raw = (contract_first(resid_wide, d_gate_up) * factor).astype(bf16)
+    d_resid_wide = contract_last(d_gate_up, gate_up_weight).astype(bf16)
     d_resid_wide, low_piece = lax.optimization_barrier(
-        (after(d_resid_wide, high_raw, gate_raw, up_raw), reduce_rows(low_raw, 1))
+        (after(d_resid_wide, high_raw, gate_up_raw), reduce_rows(low_raw, 1))
     )
     down_piece = jnp.concatenate([low_piece, reduce_rows(high_raw, 1)], axis=1)
-    gate_piece, up_piece = reduce_rows(gate_raw, 0), reduce_rows(up_raw, 0)
+    gate_up_piece = reduce_rows(gate_up_raw, 0)
     d_resid, attn_gain_raw, d_branch_wide = d_resid_junction(
         d_resid_wide, incoming, branch, branch_inv.T, attn_gain[None, :], width, 10
     )
@@ -1065,23 +1066,14 @@
     out_raw = (contract_first(attn_low, after(d_branch_wide, d_attn_unit)) * factor).astype(bf16)
     d_attn_unit = after(d_attn_unit, out_raw)
     out_piece = reduce_rows(out_raw, 1)
-    d_units, d_value_unit = attend_back(
-        unit_length, q_unit, k_unit, v_unit, d_attn_unit, attn_exact, log_total
-    )
-    d_value = turn(d_value_unit, True, tok_rows, heads, 12, "turn_d_value")
-    v_raw = (contract_first(tokens_wide, d_value) * factor).astype(bf16)
-    v_piece = reduce_rows(v_raw, 0)
-    d_units, gate_piece = lax.optimization_barrier((after(d_units, v_raw), over_dp(gate_piece)))
-    other_gate = from_twin(gate_piece)
-    d_qk, gain_sums = rear(d_units, qkv, cosine, sine_signed, qk_gain, inverse, width, 14)
-    d_qk, gain_sums, other_gate, up_piece = lax.optimization_barrier(
-        (d_qk, gain_sums, other_gate, over_dp(up_piece))
-    )
-    other_up = from_twin(up_piece)
-    qk_raw = (contract_first(tokens_wide, d_qk) * factor).astype(bf16)
-    d_qkv = jnp.concatenate([after(d_qk, qk_raw), d_value], axis=1)
-    projected = contract_last(d_qkv, qkv_weight).astype(bf16)
-    qk_piece = over_dp(reduce_rows(qk_raw, 0))
+    d_units = attend_back(unit_length, q_unit, k_unit, v_unit, d_attn_unit, attn_exact, log_total)
+    d_units, gate_up_piece = lax.optimization_barrier((d_units, over_dp(gate_up_piece)))
+    other_gate_up = from_twin(gate_up_piece)
+    d_qkv, gain_sums = rear(d_units, qkv, cosine, sine_signed, qk_gain, inverse, width, 14)
+    d_qkv, gain_sums, other_gate_up = lax.optimization_barrier((d_qkv, gain_sums, other_gate_up))
+    qkv_raw = (contract_first(tokens_wide, d_qkv) * factor).astype(bf16)
+    projected = contract_last(after(d_qkv, qkv_raw), qkv_weight).astype(bf16)
+    qkv_piece = over_dp(reduce_rows(qkv_raw, 0))
 
     def spread(half):
         return lax.dynamic_update_slice_in_dim(jnp.zeros((feat_part,), f32), half, y * half_feat, 0)
@@ -1090,24 +1082,25 @@
         [spread(gain_sums[0]), spread(gain_sums[1]), attn_gain_raw[0], mlp_gain_raw[0]]
     )
     scattered, gains = last_scatter(projected, gains_raw * factor, 16)
-    scattered, gains, out_piece, v_piece = lax.optimization_barrier(
-        (scattered, gains, over_dp(out_piece), over_dp(v_piece))
-    )
-    other_out, other_v = from_twin(out_piece), from_twin(v_piece)
+    scattered, gains, out_piece = lax.optimization_barrier((scattered, gains, over_dp(out_piece)))
+    other_out = from_twin(out_piece)
     input_grad = d_resid + scattered
     gains = over_dp(gains)
-    input_grad, qk_piece, other_down, other_gate, other_up = lax.optimization_barrier(
-        (input_grad, qk_piece, other_down, other_gate, other_up)
+    input_grad, qkv_piece, other_down, other_gate_up = lax.optimization_barrier(
+        (input_grad, qkv_piece, other_down, other_gate_up)
+    )
+    (gate_piece, up_piece), (other_gate, other_up) = (
+        [cut(values, i, 2, 1) for i in range(2)] for values in (gate_up_piece, other_gate_up)
     )
 
     def whole(piece, other, axis):
         return two_sides(piece, other, y, axis).astype(f32)
 
-    qk_other = from_twin(qk_piece)
-    q_grad, k_grad = (
-        whole(cut(qk_piece, i, 2, 1), cut(qk_other, i, 2, 1), 1) for i in range(2)
-    )
-    v_grad = whole(v_piece, other_v, 1)
+    qkv_other = from_twin(qkv_piece)
+    q_grad, k_grad, v_grad = (
+        two_sides(cut(qkv_piece, i, 3, 1), cut(qkv_other, i, 3, 1), y, 1).astype(f32)
+        for i in range(3)
+    )
     return (
         block_output,
         input_grad,

time: 916 us -> 900 us (0.983)
  Pallas kernels: 630 us -> 617 us
  waiting for transfers between devices: 38.9 us -> 49.4 us
    pallas_call x3 -> x2, Pallas kernels: 116 us -> 87.5 us  [turn(): pl.pallas_call(functools.partial(turn_kernel, back, tok, heads), name=nam...]
    pallas_call x1, Pallas kernels: 57 us -> 78.9 us  [rear(): pl.pallas_call(functools.partial(rear_kernel, width), name='rear', out_sh...]
    dot_general x7 -> x5, matrix products: 54.1 us -> 48.1 us  [contract_first(): lax.dot_general(left, right, (((0,), (0,)), ((), ())), preferred_element_...]
    dot_general x6 -> x5, matrix products: 60.2 us -> 54.3 us  [contract_last(): lax.dot_general(left, right, (((1,), (1,)), ((), ())), preferred_element_...]
    unnamed x103 -> x89, local copies, waits for them, and re-layouts: 18.5 us -> 17 us
  transfers between devices with their start and end apart: 19 -> 15, of which waited for: 5 -> 6; matrix products, arithmetic and copies ran while one was open for 20% -> 19% of each run, Pallas kernels for 65% -> 64%
where the time goes in v10:
time: 900 us; the launch traced here: 893 us
  Pallas kernels  617 us (69%)
  matrix products  153 us (17%)
  waiting for transfers between devices  49.4 us (5%)
  other arithmetic  24.6 us (3%)
  local copies, waits for them, and re-layouts  24.1 us (3%)
  between operations  16 us (2%)
    pallas_call x1, Pallas kernels, front(): pl.pallas_call(functools.partial(front_kernel, width), name='front', out_...  104 us
    pallas_call x2, Pallas kernels, turn(): pl.pallas_call(functools.partial(turn_kernel, back, tok, heads), name=nam...  87.5 us
    pallas_call x3, Pallas kernels, gather_wide(): pl.pallas_call(gather_kernel, name=name, out_shape=jax.ShapeDtypeStruct((...  82.1 us
    pallas_call x1, Pallas kernels, rear(): pl.pallas_call(functools.partial(rear_kernel, width), name='rear', out_sh...  78.9 us
    pallas_call x1, Pallas kernels, d_resid_junction(): pl.pallas_call(functools.partial(d_resid_kernel, width), name='d_resid_ju...  71.2 us
    pallas_call x2, Pallas kernels, scatter_wide(): pl.pallas_call(scatter_kernel, name=name, out_shape=jax.ShapeDtypeStruct(...  58.2 us
    dot_general x5, matrix products, contract_last(): lax.dot_general(left, right, (((1,), (1,)), ((), ())), preferred_element_...  54.3 us
    dot_general x6, matrix products, matmul(): return jnp.dot(left, right, preferred_element_type=f32)  50.9 us
  transfers between devices with their start and end apart: 15, of which 6 were waited for; matrix products, arithmetic and copies ran while one was open for 19% of the time, Pallas kernels for 64%

profile of v10, /device:TPU:0, one launch (start us, length us, event | category | flops | bytes accessed | tf_op | source)
XLA Modules:
  0.0 893.0 jit_solution(4406047896618069886)
XLA Ops:
  12.6 1.5 pad_maximum_fusion.3
  16.1 3.1 collective-permute-start
  19.1 31.4 %gather_tokens.1 = bf16[1536,2048]{1,0:T(8,128)(2,1)} custom-call(bf16[768,512]{1,0:T(8,128)(2,1)} %x_ref.1), custom_call_target="tpu_custom_call" | custom-call | bytes 1000 | tf_op jit(solution)/shard_map/gather_tokens/pallas_call | solution.py:136
  51.7 1.6 negate_select_fusion
  53.3 1.6 convert_multiply_fusion.incoming_ref
  56.2 20.4 %all-gather.6.cloned.1.call-done = bf16[2048,768]{1,0:T(8,128)(2,1)} async-done(((bf16[512,768]{1,0:T(8,128)(2,1)}), bf16[2048,768]{1,0:T(8,128)(2,1)}) %all-gather.6.cloned.1.call-update) | async-done | bytes 3145744 | tf_op jit(solution)/shard_map/all_gather | solution.py:958
  76.6 8.1 convolution_bitcast_fusion.qkv_ref
  84.7 104.3 %front.1 = (bf16[4,3,768,128]{3,2,1,0:T(8,128)(2,1)S(1)}, f32[2,1536]{1,0:T(2,128)S(1)}) custom-call(f32[1536,768]{1,0:T(8,128)S(1)} %convolution_bitcast_fusion.qkv_ref, f32[768,128]{1,0:T(8,128)S(1)} %get-tuple-element.132.cos_ref, f32[768,128]{1,0:T(8,128)S(1)} %get-tuple-element.131.sin_ref, f32[2,256]{1,0:T(2,128)S(1)} %pad_maximum_fusion.7.gain_ref), custom_call_target="tpu_custom_call" | custom-call | bytes 1000 | tf_op jit(solution)/shard_map/front/pallas_call | solution.py:662
  190.5 20.7 %attend.1 = (bf16[3072,128]{1,0:T(8,128)(2,1)}, f32[3072,128]{1,0:T(8,128)}, f32[8,3072]{1,0:T(8,128)}) custom-call(s32[1]{0:T(128)} %dynamic_slice.60.len_ref, bf16[3072,128]{1,0:T(8,128)(2,1)} %bitcast.62, bf16[3072,128]{1,0:T(8,128)(2,1)} %bitcast.60, bf16[3072,128]{1,0:T(8,128)(2,1)} %bitcast.58), custom_call_target="tpu_custom_call" | custom-call | bytes 1000 | tf_op jit(solution)/shard_map/attend/pallas_call | solution.py:842
  211.1 45.3 %turn_attn.1 = bf16[1536,256]{1,0:T(8,128)(2,1)} custom-call(bf16[3072,128]{1,0:T(8,128)(2,1)} %get-tuple-element.55.x_ref), custom_call_target="tpu_custom_call" | custom-call | bytes 1000 | tf_op jit(solution)/shard_map/turn_attn/pallas_call | solution.py:563
  256.5 6.0 convolution_convert_fusion.1.p_ref
  262.5 37.6 %scatter_branch.1.branch_ref = f32[768,512]{1,0:T(8,128)S(1)} custom-call(bf16[1536,2048]{1,0:T(8,128)(2,1)} %convolution_convert_fusion.1.p_ref), custom_call_target="tpu_custom_call" | custom-call | bytes 1000 | tf_op jit(solution)/shard_map/scatter_branch/pallas_call | solution.py:236
  300.9 4.9 total_branch.1
  306.5 2.8 fusion.14
  309.3 31.9 %gather_resid.1 = bf16[1536,2048]{1,0:T(8,128)(2,1)} custom-call(bf16[768,512]{1,0:T(8,128)(2,1)} %get-tuple-element.108.x_ref), custom_call_target="tpu_custom_call" | custom-call | bytes 1000 | tf_op jit(solution)/shard_map/gather_resid/pallas_call | solution.py:136
  341.3 10.8 %fusion.2 = f32[1536,1024]{0,1:T(8,128)S(1)} fusion(bf16[1536,2048]{1,0:T(8,128)(2,1)} %gather_resid.1, bf16[2048,2048]{1,0:T(8,128)(2,1)} %all-gather.10.cloned.1.call-done), kind=kOutput, calls=%fused_computation.13 | convolution fusion | flops 6442450944 | bytes 16777216 | tf_op jit(solution)/shard_map/dot_general | solution.py:31
  352.1 2.6 copy-done.39
  354.7 12.2 %multiply_convert_fusion.4 = (bf16[1536,1024]{0,1:T(8,128)(2,1)}, f32[1536,1024]{0,1:T(8,128)}) fusion(f32[1536,1024]{0,1:T(8,128)S(1)} %fusion.2, bf16[1536,2048]{1,0:T(8,128)(2,1)S(1)} %copy-done.22, bf16[2048,2048]{1,0:T(8,128)(2,1)} %all-gather.10.cloned.1.call-done), kind=kOutput, calls=%fused_computation.8 | convolution fusion | flops 6451888128 | bytes 26214400 | tf_op jit(solution)/shard_map/dot_general | solution.py:31
  367.0 6.0 convolution_convert_fusion.4.p_ref
  373.0 20.6 %scatter_mixed_low.1.low_ref = f32[768,256]{1,0:T(8,128)S(1)} custom-call(bf16[1536,1024]{1,0:T(8,128)(2,1)S(1)} %convolution_convert_fusion.4.p_ref), custom_call_target="tpu_custom_call" | custom-call | bytes 1000 | tf_op jit(solution)/shard_map/scatter_mixed_low/pallas_call | solution.py:236
  394.5 7.5 all-gather.12.cloned.1.call-done
  402.0 7.8 convolution_convert_fusion.3.p_ref
  409.8 42.9 %mixed_junction.1 = (bf16[768,512]{1,0:T(8,128)(2,1)S(1)}, f32[1,512]{1,0:T(1,128)S(1)}, bf16[768,256]{1,0:T(8,128)(2,1)S(1)}, bf16[1536,1024]{1,0:T(8,128)(2,1)}) custom-call(bf16[1536,1024]{1,0:T(8,128)(2,1)} %convolution_convert_fusion.3.p_ref, f32[768,256]{1,0:T(8,128)S(1)} %copy-done.11, f32[768,512]{1,0:T(8,128)S(1)} %convert_multiply_fusion.incoming_ref, ...), custom_call_target="tpu_custom_call" | custom-call | bytes 1000 | tf_op jit(solution)/shard_map/mixed_junction/pallas_call | solution.py:326
  454.4 6.5 multiply_convert_fusion.6
  461.4 18.7 %gather_d_mixed_high.1 = bf16[1536,1024]{1,0:T(8,128)(2,1)} custom-call(bf16[768,256]{1,0:T(8,128)(2,1)} %copy-done.16), custom_call_target="tpu_custom_call" | custom-call | bytes 1000 | tf_op jit(solution)/shard_map/gather_d_mixed_high/pallas_call | solution.py:136
  480.1 7.6 multiply_convert_fusion.5
  487.8 8.8 fusion.17
  496.6 11.0 %multiply_convert_fusion.3 = (bf16[1536,1024]{0,1:T(8,128)(2,1)}, bf16[1536,1024]{0,1:T(8,128)(2,1)}) fusion(f32[1536,1024]{0,1:T(8,128)} %copy-done.39, f32[1536,1024]{0,1:T(8,128)} %get-tuple-element.140, f32[1536,1024]{0,1:T(8,128)} %fusion.17, bf16[1536,1024]{1,0:T(8,128)(2,1)S(1)} %copy-done.25, bf16[1024,1024]{1,0:T(8,128)(2,1)S(1)} %copy-done.37), kind=kOutput, calls=%fused_computation.7 | convolution fusion | flops 3243245568 | bytes 30408704 | tf_op jit(solution)/shard_map/dot_general | solution.py:39
  507.6 18.3 %multiply_convert_fusion = bf16[2048,2048]{1,0:T(8,128)(2,1)} fusion(bf16[1536,2048]{1,0:T(8,128)(2,1)S(1)} %bitcast.65, bf16[1536,1024]{0,1:T(8,128)(2,1)} %get-tuple-element.111, bf16[1536,1024]{0,1:T(8,128)(2,1)} %get-tuple-element.110), kind=kOutput, calls=%fused_computation | convolution fusion | flops 12905873408 | bytes 20971520 | tf_op jit(solution)/shard_map/dot_general | solution.py:35
  526.2 19.3 %convolution_convert_fusion.2.p_ref = bf16[1536,2048]{1,0:T(8,128)(2,1)} fusion(bf16[2048,2048]{1,0:T(8,128)(2,1)} %all-gather.10.cloned.1.call-done, bf16[1536,1024]{0,1:T(8,128)(2,1)} %get-tuple-element.111, bf16[1536,1024]{0,1:T(8,128)(2,1)} %get-tuple-element.110), kind=kOutput, calls=%fused_computation.3 | convolution fusion | flops 12900630528 | bytes 20971520 | tf_op jit(solution)/shard_map/dot_general | solution.py:39
  545.4 71.2 %d_resid_junction.1 = (f32[768,512]{1,0:T(8,128)S(1)}, f32[1,512]{1,0:T(1,128)S(1)}, bf16[1536,2048]{1,0:T(8,128)(2,1)}) custom-call(bf16[1536,2048]{1,0:T(8,128)(2,1)} %convolution_convert_fusion.2.p_ref, f32[768,512]{1,0:T(8,128)S(1)} %convert_multiply_fusion.incoming_ref, f32[768,512]{1,0:T(8,128)S(1)} %scatter_branch.1.branch_ref, ...), custom_call_target="tpu_custom_call" | custom-call | bytes 1000 | tf_op jit(solution)/shard_map/d_resid_junction/pallas_call | solution.py:397
  619.8 6.0 convolution_convert_fusion.5.x_ref
  625.8 42.2 %turn_d_attn.1.do_ref = bf16[3072,128]{1,0:T(8,128)(2,1)} custom-call(bf16[1536,256]{1,0:T(8,128)(2,1)} %convolution_convert_fusion.5.x_ref), custom_call_target="tpu_custom_call" | custom-call | bytes 1000 | tf_op jit(solution)/shard_map/turn_d_attn/pallas_call | solution.py:563
  668.0 5.9 fusion.5
  674.0 27.7 %attend_back.1.d_ref = bf16[3,3072,128]{2,1,0:T(8,128)(2,1)} custom-call(s32[1]{0:T(128)} %dynamic_slice.60.len_ref, bf16[3072,128]{1,0:T(8,128)(2,1)} %bitcast.63, bf16[3072,128]{1,0:T(8,128)(2,1)} %bitcast.61, bf16[3072,128]{1,0:T(8,128)(2,1)} %bitcast.59, bf16[3072,128]{1,0:T(8,128)(2,1)} %turn_d_attn.1.do_ref, f32[3072,128]{1,0:T(8,128)} %get-tuple-element.72.o_ref, ...), custom_call_target="tpu_custom_call" | custom-call | bytes 1000 | tf_op jit(solution)/shard_map/attend_back/pallas_call | solution.py:916
  701.7 5.5 reduce-scatter.10.cloned.1.call-done
  708.8 2.3 copy-done.3
  711.1 1.7 copy-done.4
  712.8 78.9 %rear.1 = (bf16[1536,768]{1,0:T(8,128)(2,1)}, f32[2,256]{1,0:T(2,128)S(1)}) custom-call(bf16[3,3072,128]{2,1,0:T(8,128)(2,1)S(1)} %copy-done.4, f32[1536,768]{1,0:T(8,128)S(1)} %copy-done.3, f32[768,128]{1,0:T(8,128)S(1)} %copy-done.9, f32[768,128]{1,0:T(8,128)S(1)} %copy-done.7, f32[2,256]{1,0:T(2,128)S(1)} %copy-done.18, ...), custom_call_target="tpu_custom_call" | custom-call | bytes 1000 | tf_op jit(solution)/shard_map/rear/pallas_call | solution.py:771
  791.7 9.8 %fusion.4 = bf16[2048,768]{0,1:T(8,128)(2,1)} fusion(bf16[1536,768]{1,0:T(8,128)(2,1)} %get-tuple-element.80, bf16[1536,2048]{1,0:T(8,128)(2,1)} %gather_tokens.1), kind=kOutput, calls=%fused_computation.20 | convolution fusion | flops 4834983936 | bytes 11796480 | tf_op jit(solution)/shard_map/dot_general | solution.py:35
  801.6 9.2 %convolution_convert_fusion.p_ref = bf16[1536,2048]{1,0:T(8,128)(2,1)} fusion(bf16[1536,768]{1,0:T(8,128)(2,1)} %get-tuple-element.80, bf16[2048,768]{1,0:T(8,128)(2,1)} %all-gather.6.cloned.1.call-done), kind=kOutput, calls=%fused_computation.1 | convolution fusion | flops 4834983936 | bytes 11796480 | tf_op jit(solution)/shard_map/dot_general | solution.py:39
  810.8 38.8 %scatter_projected.1 = (f32[768,512]{1,0:T(8,128)S(1)}, f32[16,128]{1,0:T(8,128)S(1)}) custom-call(bf16[1536,2048]{1,0:T(8,128)(2,1)} %convolution_convert_fusion.p_ref, f32[16,128]{1,0:T(8,128)S(1)} %mul.148.gains_ref), custom_call_target="tpu_custom_call" | custom-call | bytes 1000 | tf_op jit(solution)/shard_map/scatter_projected/pallas_call | solution.py:508
  852.6 5.4 collective-permute-done.4
  859.2 2.0 reduce-scatter.14.cloned.1.call-done
  864.4 2.6 maximum_convert_fusion.2
  867.0 2.5 maximum_convert_fusion.1
  869.5 2.5 maximum_convert_fusion
  872.1 8.3 collective-permute-done.3
  (158 shorter events, 32.6 us)
Async XLA Ops:
  7.2 3.1 copy-start.34
  7.2 3.9 copy-start.31
  7.2 69.4 %all-gather.6.cloned.1.call-start = ((), (), s32[]{:S(2)}) async-start(), calls=%async_computation.5 | async-start | bytes 3932160 | tf_op jit(solution)/shard_map/all_gather | solution.py:958
  10.3 246.2 %all-gather.8.cloned.1.call-start = ((), (), s32[]{:S(2)}) async-start(), calls=%async_computation.6 | async-start | bytes 1310720 | tf_op jit(solution)/shard_map/all_gather | solution.py:964
  11.1 330.2 %all-gather.10.cloned.1.call-start = ((), (), s32[]{:S(2)}) async-start(), calls=%async_computation.7 | async-start | bytes 10485760 | tf_op jit(solution)/shard_map/all_gather | solution.py:965
  14.1 352.8 %all-gather.14.cloned.1.call-start = ((), (), s32[]{:S(2)}) async-start(), calls=%async_computation.9 | async-start | bytes 2621440 | tf_op jit(solution)/shard_map/all_gather | solution.py:972
  16.0 35.3 %copy-start.35 = (f32[512]{0:T(512)S(1)}, f32[512]{0:T(512)}, u32[]{:S(2)}) copy-start(f32[512]{0:T(512)} %param.23) | copy-start | bytes 6148
  16.0 35.4 %copy-start.36 = (f32[512]{0:T(512)S(1)}, f32[512]{0:T(512)}, u32[]{:S(2)}) copy-start(f32[512]{0:T(512)} %param.24) | copy-start | bytes 6148
  16.0 386.0 %all-gather.12.cloned.1.call-start = ((), (), s32[]{:S(2)}) async-start(), calls=%async_computation.8 | async-start | bytes 2621440 | tf_op jit(solution)/shard_map/all_gather | solution.py:989
  16.1 38.9 %collective-permute-start = (s32[1]{0:T(128)}, s32[1]{0:T(128)}, u32[]{:S(2)}, u32[]{:S(2)}) collective-permute-start(s32[1]{0:T(128)} %param.15), channel_id=1, source_target_pairs={{0,16},{16,0},{1,17},{17,1},{2,18},{18,2},{3,19},{19,3},{4,20},{20... | collective-permute-start | bytes 20 | tf_op jit(solution)/shard_map/ppermute | solution.py:979
  50.5 494.9 %reduce-scatter.6.cloned.1.call-start = ((), (), s32[]{:S(2)}) async-start(), calls=%async_computation.10 | async-start | bytes 2621440 | tf_op jit(solution)/shard_map/reduce_scatter | solution.py:1043
  51.5 33.2 %copy-start.17 = (f32[2,256]{1,0:T(2,128)}, f32[2,256]{1,0:T(2,128)S(1)}, u32[]{:S(2)}) copy-start(f32[2,256]{1,0:T(2,128)S(1)} %pad_maximum_fusion.7.gain_ref) | copy-start | bytes 6148
  53.3 31.4 %copy-start.6 = (f32[768,128]{1,0:T(8,128)}, f32[768,128]{1,0:T(8,128)S(1)}, u32[]{:S(2)}) copy-start(f32[768,128]{1,0:T(8,128)S(1)} %get-tuple-element.131.sin_ref) | copy-start | bytes 1179652
  53.3 31.4 %copy-start.8 = (f32[768,128]{1,0:T(8,128)}, f32[768,128]{1,0:T(8,128)S(1)}, u32[]{:S(2)}) copy-start(f32[768,128]{1,0:T(8,128)S(1)} %get-tuple-element.132.cos_ref) | copy-start | bytes 1179652
  84.7 105.8 %copy-start.2 = (f32[1536,768]{1,0:T(8,128)}, f32[1536,768]{1,0:T(8,128)S(1)}, u32[]{:S(2)}) copy-start(f32[1536,768]{1,0:T(8,128)S(1)} %convolution_bitcast_fusion.qkv_ref) | copy-start | bytes 14155780
  262.5 44.0 %copy-start.19 = (f32[512]{0:T(512)S(1)}, f32[512]{0:T(512)}, u32[]{:S(2)}) copy-start(f32[512]{0:T(512)} %param.25) | copy-start | bytes 6148
  341.3 13.4 %copy-start.22 = (bf16[1536,2048]{1,0:T(8,128)(2,1)S(1)}, bf16[1536,2048]{1,0:T(8,128)(2,1)}, u32[]{:S(2)}) copy-start(bf16[1536,2048]{1,0:T(8,128)(2,1)} %gather_resid.1) | copy-start | bytes 18874372
  394.5 15.4 %copy-start.20 = (f32[512]{0:T(512)S(1)}, f32[512]{0:T(512)}, u32[]{:S(2)}) copy-start(f32[512]{0:T(512)} %param.26) | copy-start | bytes 6148
  402.0 7.8 copy-start.5
  402.0 7.8 copy-start.11
  409.8 44.6 %copy-start.38 = (bf16[1536,1024]{0,1:T(8,128)(2,1)S(1)}, bf16[1536,1024]{0,1:T(8,128)(2,1)}, u32[]{:S(2)}) copy-start(bf16[1536,1024]{0,1:T(8,128)(2,1)} %get-tuple-element.139) | copy-start | bytes 9437188
  460.9 157.0 %reduce-scatter.8.cloned.1.call-start = ((), (), s32[]{:S(2)}) async-start(), calls=%async_computation.11 | async-start | bytes 2621440 | tf_op jit(solution)/shard_map/reduce_scatter | solution.py:1043
  487.7 219.5 %reduce-scatter.10.cloned.1.call-start = ((), (), s32[]{:S(2)}) async-start(), calls=%async_computation.12 | async-start | bytes 10485760 | tf_op jit(solution)/shard_map/reduce_scatter | solution.py:1043
  487.8 8.9 copy-start.25
  487.8 8.9 copy-start.37
  487.8 19.8 %slice-start = ((s8[6291456]{0:T(1024)(128)(4,1)}), s8[4194304]{0:T(1024)(128)(4,1)S(1)}, s32[]{:S(2)}) async-start(s8[6291456]{0:T(1024)(128)(4,1)} %bitcast.64), calls=%async_computation.15 | async-start | bytes 8388608
  496.6 11.0 %slice-start.1 = ((s8[6291456]{0:T(1024)(128)(4,1)}), s8[2097152]{0:T(1024)(128)(4,1)S(1)}, s32[]{:S(2)}) async-start(s8[6291456]{0:T(1024)(128)(4,1)} %bitcast.64), calls=%async_computation.16 | async-start | bytes 4194304
  525.9 323.8 %reduce-scatter.12.cloned.1.call-start = ((), (), s32[]{:S(2)}) async-start(), calls=%async_computation.13 | async-start | bytes 1310720 | tf_op jit(solution)/shard_map/reduce_scatter | solution.py:1043
  619.2 6.7 copy-start.23
  619.2 48.8 %copy-start.21 = (bf16[1536,256]{1,0:T(8,128)(2,1)S(1)}, bf16[1536,256]{1,0:T(8,128)(2,1)}, u32[]{:S(2)}) copy-start(bf16[1536,256]{1,0:T(8,128)(2,1)} %turn_attn.1) | copy-start | bytes 2359300
  619.2 48.8 %collective-permute-start.1 = (bf16[1024,512]{1,0:T(8,128)(2,1)S(1)}, bf16[1024,512]{1,0:T(8,128)(2,1)S(1)}, u32[]{:S(2)}, u32[]{:S(2)}) collective-permute-start(bf16[1024,512]{1,0:T(8,128)(2,1)S(1)} %pad_maximum_fusion.4), channel_id=1, source_target_pairs={{0,16},{16,0},{1,17},{17,1},{2,18},{18,2},{3,19},{19,3},{4,20},{20... | collective-permute-start | bytes 3145736 | tf_op jit(solution)/shard_map/ppermute | solution.py:1040
  668.0 6.0 copy-start.29
  674.0 34.8 %copy-start.7 = (f32[768,128]{1,0:T(8,128)S(1)}, f32[768,128]{1,0:T(8,128)}, u32[]{:S(2)}) copy-start(f32[768,128]{1,0:T(8,128)} %copy-done.6) | copy-start | bytes 1179652
  674.0 34.8 %copy-start.9 = (f32[768,128]{1,0:T(8,128)S(1)}, f32[768,128]{1,0:T(8,128)}, u32[]{:S(2)}) copy-start(f32[768,128]{1,0:T(8,128)} %copy-done.8) | copy-start | bytes 1179652
  674.0 34.8 %copy-start.18 = (f32[2,256]{1,0:T(2,128)S(1)}, f32[2,256]{1,0:T(2,128)}, u32[]{:S(2)}) copy-start(f32[2,256]{1,0:T(2,128)} %copy-done.17) | copy-start | bytes 6148
  707.2 84.5 %collective-permute-start.2 = (bf16[512,2048]{1,0:T(8,128)(2,1)}, bf16[512,2048]{1,0:T(8,128)(2,1)S(1)}, u32[]{:S(2)}, u32[]{:S(2)}) collective-permute-start(bf16[512,2048]{1,0:T(8,128)(2,1)} %reduce-scatter.10.cloned.1.call-done), channel_id=1, source_target_pairs={{0,16},{16,0},{1,17},{17,1},{2,18},{18,2},{3,19},{19,3},{4,20},{20... | collective-permute-start | bytes 6291464 | tf_op jit(solution)/shard_map/ppermute | solution.py:1040
  708.7 152.5 %reduce-scatter.14.cloned.1.call-start = ((), (), s32[]{:S(2)}) async-start(), calls=%async_computation.14 | async-start | bytes 3932160 | tf_op jit(solution)/shard_map/reduce_scatter | solution.py:1043
  791.7 9.8 %copy-start.27 = (bf16[512,2048]{1,0:T(8,128)(2,1)}, bf16[512,2048]{1,0:T(8,128)(2,1)S(1)}, u32[]{:S(2)}) copy-start(bf16[512,2048]{1,0:T(8,128)(2,1)S(1)} %collective-permute-done.2) | copy-start | bytes 6291460
  810.8 39.7 %copy-start.13 = (f32[768,512]{1,0:T(8,128)S(1)}, f32[768,512]{1,0:T(8,128)}, u32[]{:S(2)}) copy-start(f32[768,512]{1,0:T(8,128)} %copy-done.12) | copy-start | bytes 4718596
  849.7 8.4 copy-start.33
  849.7 8.3 collective-permute-start.4
  852.0 10.7 %copy-start.24 = (bf16[1024,512]{1,0:T(8,128)(2,1)S(1)}, bf16[1024,512]{1,0:T(8,128)(2,1)}, u32[]{:S(2)}) copy-start(bf16[1024,512]{1,0:T(8,128)(2,1)} %copy-done.23) | copy-start | bytes 3145732
  858.1 6.0 copy-start.26
  861.2 2.9 copy-start.28
  861.2 19.1 %collective-permute-start.3 = (bf16[512,768]{0,1:T(8,128)(2,1)}, bf16[512,768]{0,1:T(8,128)(2,1)S(1)}, u32[]{:S(2)}, u32[]{:S(2)}) collective-permute-start(bf16[512,768]{0,1:T(8,128)(2,1)} %reduce-scatter.14.cloned.1.call-done), channel_id=1, source_target_pairs={{0,16},{16,0},{1,17},{17,1},{2,18},{18,2},{3,19},{19,3},{4,20},{20... | collective-permute-start | bytes 2359304 | tf_op jit(solution)/shard_map/ppermute | solution.py:1040
  869.5 10.8 %copy-start.30 = (bf16[512,768]{0,1:T(8,128)(2,1)S(1)}, bf16[512,768]{0,1:T(8,128)(2,1)}, u32[]{:S(2)}) copy-start(bf16[512,768]{0,1:T(8,128)(2,1)} %reduce-scatter.14.cloned.1.call-done) | copy-start | bytes 2359300
  882.1 2.8 copy-start.15
  882.1 3.6 copy-start.1
  (9 other events, 13.8 us)
Sparse Core Ops, SparseCore 0:
  10.4 66.1 all-gather.5
  78.7 51.6 all-gather.7
  132.6 175.7 all-gather.9
  310.4 45.0 all-gather.13
  357.5 44.4 all-gather.11
  461.0 41.6 reduce-scatter.5
  505.6 42.8 reduce-scatter.7
  550.8 156.3 reduce-scatter.9
  710.1 49.0 reduce-scatter.11
  801.7 59.5 reduce-scatter.13

commit v11 on v10

--- a/solution.py
+++ b/solution.py
@@ -144,7 +144,9 @@
             pltpu.SemaphoreType.DMA((14,)),
             pltpu.SemaphoreType.DMA((14,)),
         ],
-        compiler_params=pltpu.CompilerParams(collective_id=number, has_side_effects=True),
+        compiler_params=pltpu.CompilerParams(
+            collective_id=number, has_side_effects=True, vmem_limit_bytes=8 * 2**20
+        ),
         cost_estimate=COST,
     )(values)
 
@@ -465,7 +467,9 @@
             pltpu.SemaphoreType.DMA((3,)),
             pltpu.SemaphoreType.DMA((3,)),
         ],
-        compiler_params=pltpu.CompilerParams(collective_id=number, has_side_effects=True),
+        compiler_params=pltpu.CompilerParams(
+            collective_id=number, has_side_effects=True, vmem_limit_bytes=8 * 2**20
+        ),
     )(flat)
     return total.reshape(k, t)
 
@@ -571,7 +575,9 @@
             pltpu.SemaphoreType.DMA((3,)),
             pltpu.SemaphoreType.DMA((3,)),
         ],
-        compiler_params=pltpu.CompilerParams(collective_id=number, has_side_effects=True),
+        compiler_params=pltpu.CompilerParams(
+            collective_id=number, has_side_effects=True, vmem_limit_bytes=8 * 2**20
+        ),
         cost_estimate=COST,
     )(values)
 
@@ -850,6 +856,7 @@
         ),
         in_specs=[pl.BlockSpec(memory_space=pltpu.SMEM), part, whole, whole],
         out_specs=(part, part, pl.BlockSpec((8, BLOCK), lambda i: (0, i))),
+        compiler_params=pltpu.CompilerParams(vmem_limit_bytes=24 * 2**20),
         cost_estimate=COST,
     )(length, q, k, v)
 
@@ -921,6 +928,7 @@
         in_specs=[pl.BlockSpec(memory_space=pltpu.SMEM), whole, part, part, whole, whole, line],
         out_specs=pl.BlockSpec((3, slots, HEAD_DIM), lambda j: (0, 0, 0)),
         scratch_shapes=[pltpu.VMEM((slots, HEAD_DIM), f32), pltpu.VMEM((8, slots), f32)],
+        compiler_params=pltpu.CompilerParams(vmem_limit_bytes=32 * 2**20),
         cost_estimate=COST,
     )(length, q, k, v, do, o, lse)
 

time: 900 us -> 902 us (level)
  local copies, waits for them, and re-layouts: 24.1 us -> 40.2 us
  Pallas kernels: 617 us -> 607 us
    unnamed x89 -> x135, local copies, waits for them, and re-layouts: 17 us -> 34.4 us
  transfers between devices with their start and end apart: 15 -> 15, of which waited for: 6 -> 6; matrix products, arithmetic and copies ran while one was open for 19% -> 18% of each run, Pallas kernels for 64% -> 63%
where the time goes in v11:
time: 902 us; the launch traced here: 892 us
  Pallas kernels  607 us (67%)
  matrix products  146 us (16%)
  waiting for transfers between devices  49.9 us (6%)
  local copies, waits for them, and re-layouts  40.2 us (4%)
  other arithmetic  24.2 us (3%)
  between operations  16.1 us (2%)
    pallas_call x1, Pallas kernels, front(): pl.pallas_call(functools.partial(front_kernel, width), name='front', out_...  104 us
    pallas_call x2, Pallas kernels, turn(): pl.pallas_call(functools.partial(turn_kernel, back, tok, heads), name=nam...  90.1 us
    pallas_call x1, Pallas kernels, rear(): pl.pallas_call(functools.partial(rear_kernel, width), name='rear', out_sh...  78.9 us
    pallas_call x3, Pallas kernels, gather_wide(): pl.pallas_call(gather_kernel, name=name, out_shape=jax.ShapeDtypeStruct((...  77.3 us
    pallas_call x1, Pallas kernels, d_resid_junction(): pl.pallas_call(functools.partial(d_resid_kernel, width), name='d_resid_ju...  71.2 us
    pallas_call x2, Pallas kernels, scatter_wide(): pl.pallas_call(scatter_kernel, name=name, out_shape=jax.ShapeDtypeStruct(...  57.4 us
    dot_general x5, matrix products, contract_last(): lax.dot_general(left, right, (((1,), (1,)), ((), ())), preferred_element_...  54 us
    dot_general x6, matrix products, matmul(): return jnp.dot(left, right, preferred_element_type=f32)  50.6 us
  transfers between devices with their start and end apart: 15, of which 6 were waited for; matrix products, arithmetic and copies ran while one was open for 18% of the time, Pallas kernels for 63%

profile of v11, /device:TPU:0, one launch (start us, length us, event | category | flops | bytes accessed | tf_op | source)
XLA Modules:
  0.0 891.7 jit_solution(14826345042604371369)
XLA Ops:
  16.1 3.1 collective-permute-start
  19.1 29.7 %gather_tokens.1 = bf16[1536,2048]{1,0:T(8,128)(2,1)S(1)} custom-call(bf16[768,512]{1,0:T(8,128)(2,1)S(1)} %copy-done.20), custom_call_target="tpu_custom_call" | custom-call | bytes 1000 | tf_op jit(solution)/shard_map/gather_tokens/pallas_call | solution.py:136
  48.9 2.6 copy-done.13
  52.7 1.6 negate_select_fusion
  54.3 1.6 convert_multiply_fusion.incoming_ref
  57.1 19.5 %all-gather.6.cloned.1.call-done = bf16[2048,768]{1,0:T(8,128)(2,1)} async-done(((bf16[512,768]{1,0:T(8,128)(2,1)}), bf16[2048,768]{1,0:T(8,128)(2,1)}) %all-gather.6.cloned.1.call-update) | async-done | bytes 3145744 | tf_op jit(solution)/shard_map/all_gather | solution.py:966
  76.6 8.1 convolution_bitcast_fusion.qkv_ref
  84.7 104.3 %front.1 = (bf16[4,3,768,128]{3,2,1,0:T(8,128)(2,1)S(1)}, f32[2,1536]{1,0:T(2,128)S(1)}) custom-call(f32[1536,768]{1,0:T(8,128)S(1)} %convolution_bitcast_fusion.qkv_ref, f32[768,128]{1,0:T(8,128)S(1)} %get-tuple-element.132.cos_ref, f32[768,128]{1,0:T(8,128)S(1)} %get-tuple-element.131.sin_ref, f32[2,256]{1,0:T(2,128)S(1)} %pad_maximum_fusion.7.gain_ref), custom_call_target="tpu_custom_call" | custom-call | bytes 1000 | tf_op jit(solution)/shard_map/front/pallas_call | solution.py:668
  189.2 18.3 %attend.1 = (bf16[3072,128]{1,0:T(8,128)(2,1)S(1)}, f32[3072,128]{1,0:T(8,128)S(1)}, f32[8,3072]{1,0:T(8,128)S(1)}) custom-call(s32[1]{0:T(128)} %dynamic_slice.60.len_ref, bf16[3072,128]{1,0:T(8,128)(2,1)S(1)} %bitcast.59, bf16[3072,128]{1,0:T(8,128)(2,1)S(1)} %bitcast.57, bf16[3072,128]{1,0:T(8,128)(2,1)S(1)} %bitcast.55), custom_call_target="tpu_custom_call" | custom-call | bytes 1000 | tf_op jit(solution)/shard_map/attend/pallas_call | solution.py:848
  209.3 46.4 %turn_attn.1 = bf16[1536,256]{1,0:T(8,128)(2,1)S(1)} custom-call(bf16[3072,128]{1,0:T(8,128)(2,1)S(1)} %get-tuple-element.55.x_ref), custom_call_target="tpu_custom_call" | custom-call | bytes 1000 | tf_op jit(solution)/shard_map/turn_attn/pallas_call | solution.py:567
  256.6 5.6 convolution_convert_fusion.1.p_ref
  262.3 37.7 %scatter_branch.1.branch_ref = f32[768,512]{1,0:T(8,128)S(1)} custom-call(bf16[1536,2048]{1,0:T(8,128)(2,1)} %convolution_convert_fusion.1.p_ref), custom_call_target="tpu_custom_call" | custom-call | bytes 1000 | tf_op jit(solution)/shard_map/scatter_branch/pallas_call | solution.py:238
  300.1 3.7 total_branch.1
  305.9 30.3 %gather_resid.1 = bf16[1536,2048]{1,0:T(8,128)(2,1)S(1)} custom-call(bf16[768,512]{1,0:T(8,128)(2,1)S(1)} %get-tuple-element.108.x_ref), custom_call_target="tpu_custom_call" | custom-call | bytes 1000 | tf_op jit(solution)/shard_map/gather_resid/pallas_call | solution.py:136
  336.2 2.6 copy-done.14
  338.8 10.8 %fusion.2 = f32[1536,1024]{0,1:T(8,128)S(1)} fusion(bf16[1536,2048]{1,0:T(8,128)(2,1)} %copy-done.14, bf16[2048,2048]{1,0:T(8,128)(2,1)} %all-gather.10.cloned.1.call-done), kind=kOutput, calls=%fused_computation.13 | convolution fusion | flops 6442450944 | bytes 16777216 | tf_op jit(solution)/shard_map/dot_general | solution.py:31
  349.6 2.7 copy-done.60
  352.3 12.2 %multiply_convert_fusion.4 = (bf16[1536,1024]{0,1:T(8,128)(2,1)}, f32[1536,1024]{0,1:T(8,128)}) fusion(f32[1536,1024]{0,1:T(8,128)S(1)} %fusion.2, bf16[1536,2048]{1,0:T(8,128)(2,1)S(1)} %copy-done.15, bf16[2048,2048]{1,0:T(8,128)(2,1)} %all-gather.10.cloned.1.call-done), kind=kOutput, calls=%fused_computation.8 | convolution fusion | flops 6451888128 | bytes 26214400 | tf_op jit(solution)/shard_map/dot_general | solution.py:31
  364.5 6.1 convolution_convert_fusion.4.p_ref
  370.6 19.7 %scatter_mixed_low.1.low_ref = f32[768,256]{1,0:T(8,128)S(1)} custom-call(bf16[1536,1024]{1,0:T(8,128)(2,1)S(1)} %convolution_convert_fusion.4.p_ref), custom_call_target="tpu_custom_call" | custom-call | bytes 1000 | tf_op jit(solution)/shard_map/scatter_mixed_low/pallas_call | solution.py:238
  391.2 10.8 %all-gather.12.cloned.1.call-done = bf16[1024,1024]{1,0:T(8,128)(2,1)} async-done(((bf16[1024,256]{1,0:T(8,128)(2,1)}), bf16[1024,1024]{1,0:T(8,128)(2,1)}) %all-gather.12.cloned.1.call-update) | async-done | bytes 2097168 | tf_op jit(solution)/shard_map/all_gather | solution.py:997
  402.0 7.8 convolution_convert_fusion.3.p_ref
  409.8 42.9 %mixed_junction.1 = (bf16[768,512]{1,0:T(8,128)(2,1)S(1)}, f32[1,512]{1,0:T(1,128)S(1)}, bf16[768,256]{1,0:T(8,128)(2,1)S(1)}, bf16[1536,1024]{1,0:T(8,128)(2,1)}) custom-call(bf16[1536,1024]{1,0:T(8,128)(2,1)} %convolution_convert_fusion.3.p_ref, f32[768,256]{1,0:T(8,128)S(1)} %copy-done.27, f32[768,512]{1,0:T(8,128)S(1)} %convert_multiply_fusion.incoming_ref, ...), custom_call_target="tpu_custom_call" | custom-call | bytes 1000 | tf_op jit(solution)/shard_map/mixed_junction/pallas_call | solution.py:328
  454.2 6.5 multiply_convert_fusion.6
  460.8 17.3 %gather_d_mixed_high.1 = bf16[1536,1024]{1,0:T(8,128)(2,1)S(1)} custom-call(bf16[768,256]{1,0:T(8,128)(2,1)S(1)} %get-tuple-element.61.x_ref), custom_call_target="tpu_custom_call" | custom-call | bytes 1000 | tf_op jit(solution)/shard_map/gather_d_mixed_high/pallas_call | solution.py:136
  478.1 1.7 copy-done.24
  479.8 4.6 multiply_convert_fusion.5
  484.5 8.8 fusion.17
  493.3 11.0 %multiply_convert_fusion.3 = (bf16[1536,1024]{0,1:T(8,128)(2,1)}, bf16[1536,1024]{0,1:T(8,128)(2,1)}) fusion(f32[1536,1024]{0,1:T(8,128)} %copy-done.60, f32[1536,1024]{0,1:T(8,128)} %get-tuple-element.140, f32[1536,1024]{0,1:T(8,128)} %fusion.17, bf16[1536,1024]{1,0:T(8,128)(2,1)S(1)} %copy-done.25, bf16[1024,1024]{1,0:T(8,128)(2,1)S(1)} %copy-done.57), kind=kOutput, calls=%fused_computation.7 | convolution fusion | flops 3243245568 | bytes 30408704 | tf_op jit(solution)/shard_map/dot_general | solution.py:39
  504.3 18.2 %multiply_convert_fusion = bf16[2048,2048]{1,0:T(8,128)(2,1)} fusion(bf16[1536,2048]{1,0:T(8,128)(2,1)S(1)} %bitcast.62, bf16[1536,1024]{0,1:T(8,128)(2,1)} %get-tuple-element.111, bf16[1536,1024]{0,1:T(8,128)(2,1)} %get-tuple-element.110), kind=kOutput, calls=%fused_computation | convolution fusion | flops 12905873408 | bytes 20971520 | tf_op jit(solution)/shard_map/dot_general | solution.py:35
  523.2 19.3 %convolution_convert_fusion.2.p_ref = bf16[1536,2048]{1,0:T(8,128)(2,1)} fusion(bf16[2048,2048]{1,0:T(8,128)(2,1)} %all-gather.10.cloned.1.call-done, bf16[1536,1024]{0,1:T(8,128)(2,1)} %get-tuple-element.111, bf16[1536,1024]{0,1:T(8,128)(2,1)} %get-tuple-element.110), kind=kOutput, calls=%fused_computation.3 | convolution fusion | flops 12900630528 | bytes 20971520 | tf_op jit(solution)/shard_map/dot_general | solution.py:39
  542.5 71.2 %d_resid_junction.1 = (f32[768,512]{1,0:T(8,128)S(1)}, f32[1,512]{1,0:T(1,128)S(1)}, bf16[1536,2048]{1,0:T(8,128)(2,1)}) custom-call(bf16[1536,2048]{1,0:T(8,128)(2,1)} %convolution_convert_fusion.2.p_ref, f32[768,512]{1,0:T(8,128)S(1)} %convert_multiply_fusion.incoming_ref, f32[768,512]{1,0:T(8,128)S(1)} %scatter_branch.1.branch_ref, ...), custom_call_target="tpu_custom_call" | custom-call | bytes 1000 | tf_op jit(solution)/shard_map/d_resid_junction/pallas_call | solution.py:399
  617.0 5.7 convolution_convert_fusion.5.x_ref
  622.7 43.7 %turn_d_attn.1.do_ref = bf16[3072,128]{1,0:T(8,128)(2,1)S(1)} custom-call(bf16[1536,256]{1,0:T(8,128)(2,1)S(1)} %convolution_convert_fusion.5.x_ref), custom_call_target="tpu_custom_call" | custom-call | bytes 1000 | tf_op jit(solution)/shard_map/turn_d_attn/pallas_call | solution.py:567
  668.2 2.8 fusion.5
  676.8 24.3 %attend_back.1.d_ref = bf16[3,3072,128]{2,1,0:T(8,128)(2,1)S(1)} custom-call(s32[1]{0:T(128)} %dynamic_slice.60.len_ref, bf16[3072,128]{1,0:T(8,128)(2,1)S(1)} %bitcast.60, bf16[3072,128]{1,0:T(8,128)(2,1)S(1)} %bitcast.58, bf16[3072,128]{1,0:T(8,128)(2,1)S(1)} %bitcast.56, bf16[3072,128]{1,0:T(8,128)(2,1)S(1)} %copy-done.23, f32[3072,128]{1,0:T(8,128)S(1)} %copy-done.29, ...), custom_call_target="tpu_custom_call" | custom-call | bytes 1000 | tf_op jit(solution)/shard_map/attend_back/pallas_call | solution.py:923
  701.1 5.9 reduce-scatter.10.cloned.1.call-done
  708.6 2.3 copy-done.3
  711.9 78.9 %rear.1 = (bf16[1536,768]{1,0:T(8,128)(2,1)}, f32[2,256]{1,0:T(2,128)S(1)}) custom-call(bf16[3,3072,128]{2,1,0:T(8,128)(2,1)S(1)} %attend_back.1.d_ref, f32[1536,768]{1,0:T(8,128)S(1)} %copy-done.3, f32[768,128]{1,0:T(8,128)S(1)} %copy-done.19, f32[768,128]{1,0:T(8,128)S(1)} %copy-done.17, f32[2,256]{1,0:T(2,128)S(1)} %copy-done.37, ...), custom_call_target="tpu_custom_call" | custom-call | bytes 1000 | tf_op jit(solution)/shard_map/rear/pallas_call | solution.py:777
  790.8 9.4 %fusion.4 = bf16[2048,768]{0,1:T(8,128)(2,1)} fusion(bf16[1536,768]{1,0:T(8,128)(2,1)} %get-tuple-element.80, bf16[1536,2048]{1,0:T(8,128)(2,1)} %copy-done.13), kind=kOutput, calls=%fused_computation.20 | convolution fusion | flops 4834983936 | bytes 11796480 | tf_op jit(solution)/shard_map/dot_general | solution.py:35
  800.9 9.2 %convolution_convert_fusion.p_ref = bf16[1536,2048]{1,0:T(8,128)(2,1)} fusion(bf16[1536,768]{1,0:T(8,128)(2,1)} %get-tuple-element.80, bf16[2048,768]{1,0:T(8,128)(2,1)} %all-gather.6.cloned.1.call-done), kind=kOutput, calls=%fused_computation.1 | convolution fusion | flops 4834983936 | bytes 11796480 | tf_op jit(solution)/shard_map/dot_general | solution.py:39
  810.1 38.9 %scatter_projected.1 = (f32[768,512]{1,0:T(8,128)S(1)}, f32[16,128]{1,0:T(8,128)S(1)}) custom-call(bf16[1536,2048]{1,0:T(8,128)(2,1)} %convolution_convert_fusion.p_ref, f32[16,128]{1,0:T(8,128)S(1)} %mul.148.gains_ref), custom_call_target="tpu_custom_call" | custom-call | bytes 1000 | tf_op jit(solution)/shard_map/scatter_projected/pallas_call | solution.py:512
  852.0 5.4 collective-permute-done.4
  862.8 1.8 broadcast_select_fusion.3
  864.6 2.6 maximum_convert_fusion.2
  867.2 2.5 maximum_convert_fusion.1
  869.8 2.5 maximum_convert_fusion
  872.3 6.7 collective-permute-done.3
  (205 shorter events, 46.2 us)
Async XLA Ops:
  7.2 69.4 %all-gather.6.cloned.1.call-start = ((), (), s32[]{:S(2)}) async-start(), calls=%async_computation.5 | async-start | bytes 3932160 | tf_op jit(solution)/shard_map/all_gather | solution.py:966
  10.3 245.5 %all-gather.8.cloned.1.call-start = ((), (), s32[]{:S(2)}) async-start(), calls=%async_computation.6 | async-start | bytes 1310720 | tf_op jit(solution)/shard_map/all_gather | solution.py:972
  11.1 327.7 %all-gather.10.cloned.1.call-start = ((), (), s32[]{:S(2)}) async-start(), calls=%async_computation.7 | async-start | bytes 10485760 | tf_op jit(solution)/shard_map/all_gather | solution.py:973
  14.1 350.4 %all-gather.14.cloned.1.call-start = ((), (), s32[]{:S(2)}) async-start(), calls=%async_computation.9 | async-start | bytes 2621440 | tf_op jit(solution)/shard_map/all_gather | solution.py:980
  16.0 36.3 %copy-start.55 = (f32[512]{0:T(512)S(1)}, f32[512]{0:T(512)}, u32[]{:S(2)}) copy-start(f32[512]{0:T(512)} %param.23) | copy-start | bytes 6148
  16.0 36.3 %copy-start.56 = (f32[512]{0:T(512)S(1)}, f32[512]{0:T(512)}, u32[]{:S(2)}) copy-start(f32[512]{0:T(512)} %param.24) | copy-start | bytes 6148
  16.0 386.0 %all-gather.12.cloned.1.call-start = ((), (), s32[]{:S(2)}) async-start(), calls=%async_computation.8 | async-start | bytes 2621440 | tf_op jit(solution)/shard_map/all_gather | solution.py:997
  16.1 39.8 %collective-permute-start = (s32[1]{0:T(128)}, s32[1]{0:T(128)}, u32[]{:S(2)}, u32[]{:S(2)}) collective-permute-start(s32[1]{0:T(128)} %param.15), channel_id=1, source_target_pairs={{0,16},{16,0},{1,17},{17,1},{2,18},{18,2},{3,19},{19,3},{4,20},{20... | collective-permute-start | bytes 20 | tf_op jit(solution)/shard_map/ppermute | solution.py:987
  51.5 491.0 %reduce-scatter.6.cloned.1.call-start = ((), (), s32[]{:S(2)}) async-start(), calls=%async_computation.10 | async-start | bytes 2621440 | tf_op jit(solution)/shard_map/reduce_scatter | solution.py:1051
  52.5 32.2 %copy-start.36 = (f32[2,256]{1,0:T(2,128)}, f32[2,256]{1,0:T(2,128)S(1)}, u32[]{:S(2)}) copy-start(f32[2,256]{1,0:T(2,128)S(1)} %pad_maximum_fusion.7.gain_ref) | copy-start | bytes 6148
  54.3 30.4 %copy-start.16 = (f32[768,128]{1,0:T(8,128)}, f32[768,128]{1,0:T(8,128)S(1)}, u32[]{:S(2)}) copy-start(f32[768,128]{1,0:T(8,128)S(1)} %get-tuple-element.131.sin_ref) | copy-start | bytes 1179652
  54.3 30.4 %copy-start.18 = (f32[768,128]{1,0:T(8,128)}, f32[768,128]{1,0:T(8,128)S(1)}, u32[]{:S(2)}) copy-start(f32[768,128]{1,0:T(8,128)S(1)} %get-tuple-element.132.cos_ref) | copy-start | bytes 1179652
  84.7 104.5 %copy-start.2 = (f32[1536,768]{1,0:T(8,128)}, f32[1536,768]{1,0:T(8,128)S(1)}, u32[]{:S(2)}) copy-start(f32[1536,768]{1,0:T(8,128)S(1)} %convolution_bitcast_fusion.qkv_ref) | copy-start | bytes 14155780
  189.2 18.3 %copy-start.6 = (bf16[4,1,768,128]{3,2,1,0:T(8,128)(2,1)}, bf16[4,1,768,128]{3,2,1,0:T(8,128)(2,1)S(1)}, u32[]{:S(2)}) copy-start(bf16[4,1,768,128]{3,2,1,0:T(8,128)(2,1)S(1)} %get-tuple-element.116) | copy-start | bytes 2359300
  189.2 20.1 %copy-start.8 = (bf16[4,1,768,128]{3,2,1,0:T(8,128)(2,1)}, bf16[4,1,768,128]{3,2,1,0:T(8,128)(2,1)S(1)}, u32[]{:S(2)}) copy-start(bf16[4,1,768,128]{3,2,1,0:T(8,128)(2,1)S(1)} %get-tuple-element.117) | copy-start | bytes 2359300
  189.2 20.1 %copy-start.10 = (bf16[4,1,768,128]{3,2,1,0:T(8,128)(2,1)}, bf16[4,1,768,128]{3,2,1,0:T(8,128)(2,1)S(1)}, u32[]{:S(2)}) copy-start(bf16[4,1,768,128]{3,2,1,0:T(8,128)(2,1)S(1)} %get-tuple-element.118) | copy-start | bytes 2359300
  262.3 42.2 %copy-start.21 = (bf16[768,512]{1,0:T(8,128)(2,1)S(1)}, bf16[768,512]{1,0:T(8,128)(2,1)}, u32[]{:S(2)}) copy-start(bf16[768,512]{1,0:T(8,128)(2,1)} %x_ref.1) | copy-start | bytes 2359300
  262.3 42.2 %copy-start.38 = (f32[512]{0:T(512)S(1)}, f32[512]{0:T(512)}, u32[]{:S(2)}) copy-start(f32[512]{0:T(512)} %param.25) | copy-start | bytes 6148
  338.8 13.5 %copy-start.15 = (bf16[1536,2048]{1,0:T(8,128)(2,1)S(1)}, bf16[1536,2048]{1,0:T(8,128)(2,1)}, u32[]{:S(2)}) copy-start(bf16[1536,2048]{1,0:T(8,128)(2,1)} %copy-done.14) | copy-start | bytes 18874372
  402.0 7.8 copy-start.12
  402.0 7.8 copy-start.27
  402.0 7.8 copy-start.40
  409.8 44.4 %copy-start.58 = (bf16[1536,1024]{0,1:T(8,128)(2,1)S(1)}, bf16[1536,1024]{0,1:T(8,128)(2,1)}, u32[]{:S(2)}) copy-start(bf16[1536,1024]{0,1:T(8,128)(2,1)} %get-tuple-element.139) | copy-start | bytes 9437188
  460.7 154.2 %reduce-scatter.8.cloned.1.call-start = ((), (), s32[]{:S(2)}) async-start(), calls=%async_computation.11 | async-start | bytes 2621440 | tf_op jit(solution)/shard_map/reduce_scatter | solution.py:1051
  460.8 19.0 %copy-start.59 = (bf16[1536,1024]{0,1:T(8,128)(2,1)S(1)}, bf16[1536,1024]{0,1:T(8,128)(2,1)}, u32[]{:S(2)}) copy-start(bf16[1536,1024]{0,1:T(8,128)(2,1)} %get-tuple-element.139) | copy-start | bytes 9437188
  484.4 222.6 %reduce-scatter.10.cloned.1.call-start = ((), (), s32[]{:S(2)}) async-start(), calls=%async_computation.12 | async-start | bytes 10485760 | tf_op jit(solution)/shard_map/reduce_scatter | solution.py:1051
  484.4 8.8 copy-start.25
  484.4 8.8 copy-start.57
  484.5 19.8 %slice-start = ((s8[6291456]{0:T(1024)(128)(4,1)}), s8[4194304]{0:T(1024)(128)(4,1)S(1)}, s32[]{:S(2)}) async-start(s8[6291456]{0:T(1024)(128)(4,1)} %bitcast.61), calls=%async_computation.15 | async-start | bytes 8388608
  493.3 11.0 %slice-start.1 = ((s8[6291456]{0:T(1024)(128)(4,1)}), s8[2097152]{0:T(1024)(128)(4,1)S(1)}, s32[]{:S(2)}) async-start(s8[6291456]{0:T(1024)(128)(4,1)} %bitcast.61), calls=%async_computation.16 | async-start | bytes 4194304
  522.5 326.5 %reduce-scatter.12.cloned.1.call-start = ((), (), s32[]{:S(2)}) async-start(), calls=%async_computation.13 | async-start | bytes 1310720 | tf_op jit(solution)/shard_map/reduce_scatter | solution.py:1051
  523.2 19.3 %copy-start.39 = (f32[512]{0:T(512)S(1)}, f32[512]{0:T(512)}, u32[]{:S(2)}) copy-start(f32[512]{0:T(512)} %param.25) | copy-start | bytes 6148
  614.9 7.7 copy-start.43
  614.9 53.3 %slice-start.2 = ((s8[6291456]{0:T(1024)(128)(4,1)}), s8[4194304]{0:T(1024)(128)(4,1)S(1)}, s32[]{:S(2)}) async-start(s8[6291456]{0:T(1024)(128)(4,1)} %bitcast.67), calls=%async_computation.17 | async-start | bytes 8388608
  616.5 6.2 copy-start.45
  616.5 51.7 %copy-start.5 = (bf16[1536,256]{1,0:T(8,128)(2,1)S(1)}, bf16[1536,256]{1,0:T(8,128)(2,1)}, u32[]{:S(2)}) copy-start(bf16[1536,256]{1,0:T(8,128)(2,1)} %copy-done.4) | copy-start | bytes 2359300
  616.5 51.7 %slice-start.3 = ((s8[6291456]{0:T(1024)(128)(4,1)}), s8[2097152]{0:T(1024)(128)(4,1)S(1)}, s32[]{:S(2)}) async-start(s8[6291456]{0:T(1024)(128)(4,1)} %bitcast.67), calls=%async_computation.18 | async-start | bytes 4194304
  616.5 50.7 %collective-permute-start.1 = (bf16[1024,512]{1,0:T(8,128)(2,1)S(1)}, bf16[1024,512]{1,0:T(8,128)(2,1)S(1)}, u32[]{:S(2)}, u32[]{:S(2)}) collective-permute-start(bf16[1024,512]{1,0:T(8,128)(2,1)S(1)} %pad_maximum_fusion.4), channel_id=1, source_target_pairs={{0,16},{16,0},{1,17},{17,1},{2,18},{18,2},{3,19},{19,3},{4,20},{20... | collective-permute-start | bytes 3145736 | tf_op jit(solution)/shard_map/ppermute | solution.py:1048
  676.8 31.8 %copy-start.17 = (f32[768,128]{1,0:T(8,128)S(1)}, f32[768,128]{1,0:T(8,128)}, u32[]{:S(2)}) copy-start(f32[768,128]{1,0:T(8,128)} %copy-done.16) | copy-start | bytes 1179652
  676.8 31.8 %copy-start.37 = (f32[2,256]{1,0:T(2,128)S(1)}, f32[2,256]{1,0:T(2,128)}, u32[]{:S(2)}) copy-start(f32[2,256]{1,0:T(2,128)} %copy-done.36) | copy-start | bytes 6148
  707.0 83.8 %collective-permute-start.2 = (bf16[512,2048]{1,0:T(8,128)(2,1)}, bf16[512,2048]{1,0:T(8,128)(2,1)}, u32[]{:S(2)}, u32[]{:S(2)}) collective-permute-start(bf16[512,2048]{1,0:T(8,128)(2,1)} %reduce-scatter.10.cloned.1.call-done), channel_id=1, source_target_pairs={{0,16},{16,0},{1,17},{17,1},{2,18},{18,2},{3,19},{19,3},{4,20},{20... | collective-permute-start | bytes 6291464 | tf_op jit(solution)/shard_map/ppermute | solution.py:1048
  708.5 151.4 %reduce-scatter.14.cloned.1.call-start = ((), (), s32[]{:S(2)}) async-start(), calls=%async_computation.14 | async-start | bytes 3932160 | tf_op jit(solution)/shard_map/reduce_scatter | solution.py:1051
  810.1 39.8 %copy-start.31 = (f32[768,512]{1,0:T(8,128)S(1)}, f32[768,512]{1,0:T(8,128)}, u32[]{:S(2)}) copy-start(f32[768,512]{1,0:T(8,128)} %copy-done.30) | copy-start | bytes 4718596
  849.0 8.3 copy-start.52
  849.0 8.3 collective-permute-start.4
  851.4 10.0 %copy-start.46 = (bf16[1024,512]{1,0:T(8,128)(2,1)S(1)}, bf16[1024,512]{1,0:T(8,128)(2,1)}, u32[]{:S(2)}) copy-start(bf16[1024,512]{1,0:T(8,128)(2,1)} %copy-done.45) | copy-start | bytes 3145732
  859.9 19.1 %collective-permute-start.3 = (bf16[512,768]{0,1:T(8,128)(2,1)}, bf16[512,768]{0,1:T(8,128)(2,1)S(1)}, u32[]{:S(2)}, u32[]{:S(2)}) collective-permute-start(bf16[512,768]{0,1:T(8,128)(2,1)} %reduce-scatter.14.cloned.1.call-done), channel_id=1, source_target_pairs={{0,16},{16,0},{1,17},{17,1},{2,18},{18,2},{3,19},{19,3},{4,20},{20... | collective-permute-start | bytes 2359304 | tf_op jit(solution)/shard_map/ppermute | solution.py:1048
  869.7 9.3 %copy-start.49 = (bf16[512,768]{0,1:T(8,128)(2,1)S(1)}, bf16[512,768]{0,1:T(8,128)(2,1)}, u32[]{:S(2)}) copy-start(bf16[512,768]{0,1:T(8,128)(2,1)} %reduce-scatter.14.cloned.1.call-done) | copy-start | bytes 2359300
  (32 other events, 59.7 us)
Sparse Core Ops, SparseCore 0:
  10.4 66.1 all-gather.5
  78.7 51.6 all-gather.7
  132.6 175.7 all-gather.9
  310.5 45.0 all-gather.13
  357.5 44.4 all-gather.11
  460.9 41.6 reduce-scatter.5
  505.4 42.8 reduce-scatter.7
  550.7 156.3 reduce-scatter.9
  709.9 48.6 reduce-scatter.11
  800.3 59.5 reduce-scatter.13

commit v12 on v10

--- a/solution.py
+++ b/solution.py
@@ -1067,10 +1067,9 @@
     d_attn_unit = after(d_attn_unit, out_raw)
     out_piece = reduce_rows(out_raw, 1)
     d_units = attend_back(unit_length, q_unit, k_unit, v_unit, d_attn_unit, attn_exact, log_total)
-    d_units, gate_up_piece = lax.optimization_barrier((d_units, over_dp(gate_up_piece)))
+    d_qkv, gain_sums = rear(d_units, qkv, cosine, sine_signed, qk_gain, inverse, width, 14)
+    d_qkv, gate_up_piece = lax.optimization_barrier((d_qkv, over_dp(gate_up_piece)))
     other_gate_up = from_twin(gate_up_piece)
-    d_qkv, gain_sums = rear(d_units, qkv, cosine, sine_signed, qk_gain, inverse, width, 14)
-    d_qkv, gain_sums, other_gate_up = lax.optimization_barrier((d_qkv, gain_sums, other_gate_up))
     qkv_raw = (contract_first(tokens_wide, d_qkv) * factor).astype(bf16)
     projected = contract_last(after(d_qkv, qkv_raw), qkv_weight).astype(bf16)
     qkv_piece = over_dp(reduce_rows(qkv_raw, 0))

time: 900 us -> 912 us (1.013)
  Pallas kernels: 617 us -> 638 us
  waiting for transfers between devices: 49.4 us -> 36.4 us
    pallas_call x1, Pallas kernels: 38.8 us -> 64.6 us  [last_scatter(): pl.pallas_call(last_kernel, name='scatter_projected', out_shape=(jax.Shap...]
    unnamed x89 -> x87, local copies, waits for them, and re-layouts: 17 us -> 18.4 us
  transfers between devices with their start and end apart: 15 -> 15, of which waited for: 6 -> 4; matrix products, arithmetic and copies ran while one was open for 19% -> 19% of each run, Pallas kernels for 64% -> 66%
where the time goes in v12:
time: 912 us; the launch traced here: 904 us
  Pallas kernels  638 us (70%)
  matrix products  153 us (17%)
  waiting for transfers between devices  36.4 us (4%)
  local copies, waits for them, and re-layouts  25.5 us (3%)
  other arithmetic  25.5 us (3%)
  between operations  16 us (2%)
  starting transfers between devices  9.99 us (1%)
    pallas_call x1, Pallas kernels, front(): pl.pallas_call(functools.partial(front_kernel, width), name='front', out_...  104 us
    pallas_call x2, Pallas kernels, turn(): pl.pallas_call(functools.partial(turn_kernel, back, tok, heads), name=nam...  87.5 us
    pallas_call x3, Pallas kernels, gather_wide(): pl.pallas_call(gather_kernel, name=name, out_shape=jax.ShapeDtypeStruct((...  82.1 us
    pallas_call x1, Pallas kernels, rear(): pl.pallas_call(functools.partial(rear_kernel, width), name='rear', out_sh...  74.3 us
    pallas_call x1, Pallas kernels, d_resid_junction(): pl.pallas_call(functools.partial(d_resid_kernel, width), name='d_resid_ju...  71.2 us
    pallas_call x1, Pallas kernels, last_scatter(): pl.pallas_call(last_kernel, name='scatter_projected', out_shape=(jax.Shap...  64.6 us
    pallas_call x2, Pallas kernels, scatter_wide(): pl.pallas_call(scatter_kernel, name=name, out_shape=jax.ShapeDtypeStruct(...  58.2 us
    dot_general x5, matrix products, contract_last(): lax.dot_general(left, right, (((1,), (1,)), ((), ())), preferred_element_...  54.5 us
  transfers between devices with their start and end apart: 15, of which 4 were waited for; matrix products, arithmetic and copies ran while one was open for 19% of the time, Pallas kernels for 66%

profile of v12, /device:TPU:0, one launch (start us, length us, event | category | flops | bytes accessed | tf_op | source)
XLA Modules:
  0.0 904.3 jit_solution(8994804921462691613)
XLA Ops:
  16.1 3.1 collective-permute-start
  19.1 31.4 %gather_tokens.1 = bf16[1536,2048]{1,0:T(8,128)(2,1)} custom-call(bf16[768,512]{1,0:T(8,128)(2,1)} %x_ref.1), custom_call_target="tpu_custom_call" | custom-call | bytes 1000 | tf_op jit(solution)/shard_map/gather_tokens/pallas_call | solution.py:136
  51.7 1.6 negate_select_fusion
  53.3 1.6 convert_multiply_fusion.incoming_ref
  56.2 20.4 %all-gather.6.cloned.1.call-done = bf16[2048,768]{1,0:T(8,128)(2,1)} async-done(((bf16[512,768]{1,0:T(8,128)(2,1)}), bf16[2048,768]{1,0:T(8,128)(2,1)}) %all-gather.6.cloned.1.call-update) | async-done | bytes 3145744 | tf_op jit(solution)/shard_map/all_gather | solution.py:958
  76.6 8.1 convolution_bitcast_fusion.qkv_ref
  84.7 104.3 %front.1 = (bf16[4,3,768,128]{3,2,1,0:T(8,128)(2,1)S(1)}, f32[2,1536]{1,0:T(2,128)S(1)}) custom-call(f32[1536,768]{1,0:T(8,128)S(1)} %convolution_bitcast_fusion.qkv_ref, f32[768,128]{1,0:T(8,128)S(1)} %get-tuple-element.126.cos_ref, f32[768,128]{1,0:T(8,128)S(1)} %get-tuple-element.125.sin_ref, f32[2,256]{1,0:T(2,128)S(1)} %pad_maximum_fusion.7.gain_ref), custom_call_target="tpu_custom_call" | custom-call | bytes 1000 | tf_op jit(solution)/shard_map/front/pallas_call | solution.py:662
  190.5 20.7 %attend.1 = (bf16[3072,128]{1,0:T(8,128)(2,1)}, f32[3072,128]{1,0:T(8,128)}, f32[8,3072]{1,0:T(8,128)}) custom-call(s32[1]{0:T(128)} %dynamic_slice.60.len_ref, bf16[3072,128]{1,0:T(8,128)(2,1)} %bitcast.62, bf16[3072,128]{1,0:T(8,128)(2,1)} %bitcast.60, bf16[3072,128]{1,0:T(8,128)(2,1)} %bitcast.58), custom_call_target="tpu_custom_call" | custom-call | bytes 1000 | tf_op jit(solution)/shard_map/attend/pallas_call | solution.py:842
  211.1 45.3 %turn_attn.1 = bf16[1536,256]{1,0:T(8,128)(2,1)} custom-call(bf16[3072,128]{1,0:T(8,128)(2,1)} %get-tuple-element.52.x_ref), custom_call_target="tpu_custom_call" | custom-call | bytes 1000 | tf_op jit(solution)/shard_map/turn_attn/pallas_call | solution.py:563
  256.5 6.0 convolution_convert_fusion.1.p_ref
  262.4 37.6 %scatter_branch.1.branch_ref = f32[768,512]{1,0:T(8,128)S(1)} custom-call(bf16[1536,2048]{1,0:T(8,128)(2,1)} %convolution_convert_fusion.1.p_ref), custom_call_target="tpu_custom_call" | custom-call | bytes 1000 | tf_op jit(solution)/shard_map/scatter_branch/pallas_call | solution.py:236
  300.8 4.9 total_branch.1
  306.5 2.8 fusion.14
  309.3 31.9 %gather_resid.1 = bf16[1536,2048]{1,0:T(8,128)(2,1)} custom-call(bf16[768,512]{1,0:T(8,128)(2,1)} %get-tuple-element.102.x_ref), custom_call_target="tpu_custom_call" | custom-call | bytes 1000 | tf_op jit(solution)/shard_map/gather_resid/pallas_call | solution.py:136
  341.3 10.8 %fusion.2 = f32[1536,1024]{0,1:T(8,128)S(1)} fusion(bf16[1536,2048]{1,0:T(8,128)(2,1)} %gather_resid.1, bf16[2048,2048]{1,0:T(8,128)(2,1)} %all-gather.10.cloned.1.call-done), kind=kOutput, calls=%fused_computation.13 | convolution fusion | flops 6442450944 | bytes 16777216 | tf_op jit(solution)/shard_map/dot_general | solution.py:31
  352.1 2.6 copy-done.38
  354.7 12.2 %multiply_convert_fusion.4 = (bf16[1536,1024]{0,1:T(8,128)(2,1)}, f32[1536,1024]{0,1:T(8,128)}) fusion(f32[1536,1024]{0,1:T(8,128)S(1)} %fusion.2, bf16[1536,2048]{1,0:T(8,128)(2,1)S(1)} %copy-done.23, bf16[2048,2048]{1,0:T(8,128)(2,1)} %all-gather.10.cloned.1.call-done), kind=kOutput, calls=%fused_computation.8 | convolution fusion | flops 6451888128 | bytes 26214400 | tf_op jit(solution)/shard_map/dot_general | solution.py:31
  367.0 6.0 convolution_convert_fusion.4.p_ref
  373.0 20.6 %scatter_mixed_low.1.low_ref = f32[768,256]{1,0:T(8,128)S(1)} custom-call(bf16[1536,1024]{1,0:T(8,128)(2,1)S(1)} %convolution_convert_fusion.4.p_ref), custom_call_target="tpu_custom_call" | custom-call | bytes 1000 | tf_op jit(solution)/shard_map/scatter_mixed_low/pallas_call | solution.py:236
  394.5 7.5 all-gather.12.cloned.1.call-done
  402.0 7.8 convolution_convert_fusion.3.p_ref
  409.8 42.9 %mixed_junction.1 = (bf16[768,512]{1,0:T(8,128)(2,1)S(1)}, f32[1,512]{1,0:T(1,128)S(1)}, bf16[768,256]{1,0:T(8,128)(2,1)S(1)}, bf16[1536,1024]{1,0:T(8,128)(2,1)}) custom-call(bf16[1536,1024]{1,0:T(8,128)(2,1)} %convolution_convert_fusion.3.p_ref, f32[768,256]{1,0:T(8,128)S(1)} %copy-done.11, f32[768,512]{1,0:T(8,128)S(1)} %convert_multiply_fusion.incoming_ref, ...), custom_call_target="tpu_custom_call" | custom-call | bytes 1000 | tf_op jit(solution)/shard_map/mixed_junction/pallas_call | solution.py:326
  454.4 6.5 multiply_convert_fusion.6
  461.3 18.7 %gather_d_mixed_high.1 = bf16[1536,1024]{1,0:T(8,128)(2,1)} custom-call(bf16[768,256]{1,0:T(8,128)(2,1)} %copy-done.16), custom_call_target="tpu_custom_call" | custom-call | bytes 1000 | tf_op jit(solution)/shard_map/gather_d_mixed_high/pallas_call | solution.py:136
  480.1 7.6 multiply_convert_fusion.5
  487.8 8.8 fusion.17
  496.6 11.0 %multiply_convert_fusion.3 = (bf16[1536,1024]{0,1:T(8,128)(2,1)}, bf16[1536,1024]{0,1:T(8,128)(2,1)}) fusion(f32[1536,1024]{0,1:T(8,128)} %copy-done.38, f32[1536,1024]{0,1:T(8,128)} %get-tuple-element.134, f32[1536,1024]{0,1:T(8,128)} %fusion.17, bf16[1536,1024]{1,0:T(8,128)(2,1)S(1)} %copy-done.26, bf16[1024,1024]{1,0:T(8,128)(2,1)S(1)} %copy-done.36), kind=kOutput, calls=%fused_computation.7 | convolution fusion | flops 3243245568 | bytes 30408704 | tf_op jit(solution)/shard_map/dot_general | solution.py:39
  507.6 18.2 %multiply_convert_fusion = bf16[2048,2048]{1,0:T(8,128)(2,1)} fusion(bf16[1536,2048]{1,0:T(8,128)(2,1)S(1)} %bitcast.65, bf16[1536,1024]{0,1:T(8,128)(2,1)} %get-tuple-element.105, bf16[1536,1024]{0,1:T(8,128)(2,1)} %get-tuple-element.104), kind=kOutput, calls=%fused_computation | convolution fusion | flops 12905873408 | bytes 20971520 | tf_op jit(solution)/shard_map/dot_general | solution.py:35
  526.1 19.3 %convolution_convert_fusion.2.p_ref = bf16[1536,2048]{1,0:T(8,128)(2,1)} fusion(bf16[2048,2048]{1,0:T(8,128)(2,1)} %all-gather.10.cloned.1.call-done, bf16[1536,1024]{0,1:T(8,128)(2,1)} %get-tuple-element.105, bf16[1536,1024]{0,1:T(8,128)(2,1)} %get-tuple-element.104), kind=kOutput, calls=%fused_computation.3 | convolution fusion | flops 12900630528 | bytes 20971520 | tf_op jit(solution)/shard_map/dot_general | solution.py:39
  545.4 71.2 %d_resid_junction.1 = (f32[768,512]{1,0:T(8,128)S(1)}, f32[1,512]{1,0:T(1,128)S(1)}, bf16[1536,2048]{1,0:T(8,128)(2,1)}) custom-call(bf16[1536,2048]{1,0:T(8,128)(2,1)} %convolution_convert_fusion.2.p_ref, f32[768,512]{1,0:T(8,128)S(1)} %convert_multiply_fusion.incoming_ref, f32[768,512]{1,0:T(8,128)S(1)} %scatter_branch.1.branch_ref, ...), custom_call_target="tpu_custom_call" | custom-call | bytes 1000 | tf_op jit(solution)/shard_map/d_resid_junction/pallas_call | solution.py:397
  619.8 6.0 convolution_convert_fusion.5.x_ref
  625.8 42.1 %turn_d_attn.1.do_ref = bf16[3072,128]{1,0:T(8,128)(2,1)} custom-call(bf16[1536,256]{1,0:T(8,128)(2,1)} %convolution_convert_fusion.5.x_ref), custom_call_target="tpu_custom_call" | custom-call | bytes 1000 | tf_op jit(solution)/shard_map/turn_d_attn/pallas_call | solution.py:563
  668.0 5.9 fusion.5
  674.3 27.5 %attend_back.1.d_ref = bf16[3,3072,128]{2,1,0:T(8,128)(2,1)} custom-call(s32[1]{0:T(128)} %dynamic_slice.60.len_ref, bf16[3072,128]{1,0:T(8,128)(2,1)} %bitcast.63, bf16[3072,128]{1,0:T(8,128)(2,1)} %bitcast.61, bf16[3072,128]{1,0:T(8,128)(2,1)} %bitcast.59, bf16[3072,128]{1,0:T(8,128)(2,1)} %turn_d_attn.1.do_ref, f32[3072,128]{1,0:T(8,128)} %get-tuple-element.69.o_ref, ...), custom_call_target="tpu_custom_call" | custom-call | bytes 1000 | tf_op jit(solution)/shard_map/attend_back/pallas_call | solution.py:916
  701.8 2.3 copy-done.3
  704.1 1.7 copy-done.4
  705.8 74.3 %rear.1 = (bf16[1536,768]{1,0:T(8,128)(2,1)S(1)}, f32[2,256]{1,0:T(2,128)S(1)}) custom-call(bf16[3,3072,128]{2,1,0:T(8,128)(2,1)S(1)} %copy-done.4, f32[1536,768]{1,0:T(8,128)S(1)} %copy-done.3, f32[768,128]{1,0:T(8,128)S(1)} %copy-done.9, f32[768,128]{1,0:T(8,128)S(1)} %copy-done.7, f32[2,256]{1,0:T(2,128)S(1)} %copy-done.18, ...), custom_call_target="tpu_custom_call" | custom-call | bytes 1000 | tf_op jit(solution)/shard_map/rear/pallas_call | solution.py:771
  781.6 9.1 %fusion.4 = bf16[2048,768]{0,1:T(8,128)(2,1)} fusion(bf16[1536,768]{1,0:T(8,128)(2,1)} %copy-done.21, bf16[1536,2048]{1,0:T(8,128)(2,1)} %gather_tokens.1), kind=kOutput, calls=%fused_computation.20 | convolution fusion | flops 4834983936 | bytes 11796480 | tf_op jit(solution)/shard_map/dot_general | solution.py:35
  792.3 9.4 %convolution_convert_fusion.p_ref = bf16[1536,2048]{1,0:T(8,128)(2,1)} fusion(bf16[1536,768]{1,0:T(8,128)(2,1)} %copy-done.21, bf16[2048,768]{1,0:T(8,128)(2,1)} %all-gather.6.cloned.1.call-done), kind=kOutput, calls=%fused_computation.1 | convolution fusion | flops 4834983936 | bytes 11796480 | tf_op jit(solution)/shard_map/dot_general | solution.py:39
  801.7 64.6 %scatter_projected.1 = (f32[768,512]{1,0:T(8,128)S(1)}, f32[16,128]{1,0:T(8,128)S(1)}) custom-call(bf16[1536,2048]{1,0:T(8,128)(2,1)} %convolution_convert_fusion.p_ref, f32[16,128]{1,0:T(8,128)S(1)} %mul.148.gains_ref), custom_call_target="tpu_custom_call" | custom-call | bytes 1000 | tf_op jit(solution)/shard_map/scatter_projected/pallas_call | solution.py:508
  866.4 1.8 collective-permute-start.4
  870.3 3.0 collective-permute-done.4
  874.4 1.7 collective-permute-start.3
  876.3 2.5 broadcast_select_fusion.3
  878.8 2.6 maximum_convert_fusion.2
  881.4 2.5 maximum_convert_fusion.1
  883.9 2.5 maximum_convert_fusion
  886.5 5.2 collective-permute-done.3
  (156 shorter events, 32.0 us)
Async XLA Ops:
  7.2 3.1 copy-start.33
  7.2 3.9 copy-start.30
  7.2 69.4 %all-gather.6.cloned.1.call-start = ((), (), s32[]{:S(2)}) async-start(), calls=%async_computation.5 | async-start | bytes 3932160 | tf_op jit(solution)/shard_map/all_gather | solution.py:958
  10.3 246.2 %all-gather.8.cloned.1.call-start = ((), (), s32[]{:S(2)}) async-start(), calls=%async_computation.6 | async-start | bytes 1310720 | tf_op jit(solution)/shard_map/all_gather | solution.py:964
  11.1 330.2 %all-gather.10.cloned.1.call-start = ((), (), s32[]{:S(2)}) async-start(), calls=%async_computation.7 | async-start | bytes 10485760 | tf_op jit(solution)/shard_map/all_gather | solution.py:965
  12.6 2.4 copy-start.31
  14.1 352.8 %all-gather.14.cloned.1.call-start = ((), (), s32[]{:S(2)}) async-start(), calls=%async_computation.9 | async-start | bytes 2621440 | tf_op jit(solution)/shard_map/all_gather | solution.py:972
  16.0 35.3 %copy-start.34 = (f32[512]{0:T(512)S(1)}, f32[512]{0:T(512)}, u32[]{:S(2)}) copy-start(f32[512]{0:T(512)} %param.23) | copy-start | bytes 6148
  16.0 35.4 %copy-start.35 = (f32[512]{0:T(512)S(1)}, f32[512]{0:T(512)}, u32[]{:S(2)}) copy-start(f32[512]{0:T(512)} %param.24) | copy-start | bytes 6148
  16.0 385.9 %all-gather.12.cloned.1.call-start = ((), (), s32[]{:S(2)}) async-start(), calls=%async_computation.8 | async-start | bytes 2621440 | tf_op jit(solution)/shard_map/all_gather | solution.py:989
  16.1 38.9 %collective-permute-start = (s32[1]{0:T(128)}, s32[1]{0:T(128)}, u32[]{:S(2)}, u32[]{:S(2)}) collective-permute-start(s32[1]{0:T(128)} %param.15), channel_id=1, source_target_pairs={{0,16},{16,0},{1,17},{17,1},{2,18},{18,2},{3,19},{19,3},{4,20},{20... | collective-permute-start | bytes 20 | tf_op jit(solution)/shard_map/ppermute | solution.py:979
  50.5 494.8 %reduce-scatter.6.cloned.1.call-start = ((), (), s32[]{:S(2)}) async-start(), calls=%async_computation.10 | async-start | bytes 2621440 | tf_op jit(solution)/shard_map/reduce_scatter | solution.py:1043
  51.5 33.2 %copy-start.17 = (f32[2,256]{1,0:T(2,128)}, f32[2,256]{1,0:T(2,128)S(1)}, u32[]{:S(2)}) copy-start(f32[2,256]{1,0:T(2,128)S(1)} %pad_maximum_fusion.7.gain_ref) | copy-start | bytes 6148
  53.3 31.4 %copy-start.6 = (f32[768,128]{1,0:T(8,128)}, f32[768,128]{1,0:T(8,128)S(1)}, u32[]{:S(2)}) copy-start(f32[768,128]{1,0:T(8,128)S(1)} %get-tuple-element.125.sin_ref) | copy-start | bytes 1179652
  53.3 31.4 %copy-start.8 = (f32[768,128]{1,0:T(8,128)}, f32[768,128]{1,0:T(8,128)S(1)}, u32[]{:S(2)}) copy-start(f32[768,128]{1,0:T(8,128)S(1)} %get-tuple-element.126.cos_ref) | copy-start | bytes 1179652
  84.7 105.8 %copy-start.2 = (f32[1536,768]{1,0:T(8,128)}, f32[1536,768]{1,0:T(8,128)S(1)}, u32[]{:S(2)}) copy-start(f32[1536,768]{1,0:T(8,128)S(1)} %convolution_bitcast_fusion.qkv_ref) | copy-start | bytes 14155780
  262.4 44.0 %copy-start.19 = (f32[512]{0:T(512)S(1)}, f32[512]{0:T(512)}, u32[]{:S(2)}) copy-start(f32[512]{0:T(512)} %param.25) | copy-start | bytes 6148
  341.3 13.4 %copy-start.23 = (bf16[1536,2048]{1,0:T(8,128)(2,1)S(1)}, bf16[1536,2048]{1,0:T(8,128)(2,1)}, u32[]{:S(2)}) copy-start(bf16[1536,2048]{1,0:T(8,128)(2,1)} %gather_resid.1) | copy-start | bytes 18874372
  352.1 2.6 copy-start.38
  394.5 15.3 %copy-start.20 = (f32[512]{0:T(512)S(1)}, f32[512]{0:T(512)}, u32[]{:S(2)}) copy-start(f32[512]{0:T(512)} %param.26) | copy-start | bytes 6148
  401.9 7.8 copy-start.5
  401.9 7.8 copy-start.11
  409.8 44.6 %copy-start.37 = (bf16[1536,1024]{0,1:T(8,128)(2,1)S(1)}, bf16[1536,1024]{0,1:T(8,128)(2,1)}, u32[]{:S(2)}) copy-start(bf16[1536,1024]{0,1:T(8,128)(2,1)} %get-tuple-element.133) | copy-start | bytes 9437188
  460.9 157.0 %reduce-scatter.8.cloned.1.call-start = ((), (), s32[]{:S(2)}) async-start(), calls=%async_computation.11 | async-start | bytes 2621440 | tf_op jit(solution)/shard_map/reduce_scatter | solution.py:1043
  487.7 293.9 %reduce-scatter.10.cloned.1.call-start = ((), (), s32[]{:S(2)}) async-start(), calls=%async_computation.12 | async-start | bytes 10485760 | tf_op jit(solution)/shard_map/reduce_scatter | solution.py:1043
  487.7 8.9 copy-start.26
  487.7 8.9 copy-start.36
  487.8 19.8 %slice-start = ((s8[6291456]{0:T(1024)(128)(4,1)}), s8[4194304]{0:T(1024)(128)(4,1)S(1)}, s32[]{:S(2)}) async-start(s8[6291456]{0:T(1024)(128)(4,1)} %bitcast.64), calls=%async_computation.15 | async-start | bytes 8388608
  496.6 11.0 %slice-start.1 = ((s8[6291456]{0:T(1024)(128)(4,1)}), s8[2097152]{0:T(1024)(128)(4,1)S(1)}, s32[]{:S(2)}) async-start(s8[6291456]{0:T(1024)(128)(4,1)} %bitcast.64), calls=%async_computation.16 | async-start | bytes 4194304
  525.9 340.5 %reduce-scatter.12.cloned.1.call-start = ((), (), s32[]{:S(2)}) async-start(), calls=%async_computation.13 | async-start | bytes 1310720 | tf_op jit(solution)/shard_map/reduce_scatter | solution.py:1043
  619.1 6.7 copy-start.24
  619.1 48.9 %copy-start.22 = (bf16[1536,256]{1,0:T(8,128)(2,1)S(1)}, bf16[1536,256]{1,0:T(8,128)(2,1)}, u32[]{:S(2)}) copy-start(bf16[1536,256]{1,0:T(8,128)(2,1)} %turn_attn.1) | copy-start | bytes 2359300
  619.1 48.8 %collective-permute-start.1 = (bf16[1024,512]{1,0:T(8,128)(2,1)S(1)}, bf16[1024,512]{1,0:T(8,128)(2,1)S(1)}, u32[]{:S(2)}, u32[]{:S(2)}) collective-permute-start(bf16[1024,512]{1,0:T(8,128)(2,1)S(1)} %pad_maximum_fusion.4), channel_id=1, source_target_pairs={{0,16},{16,0},{1,17},{17,1},{2,18},{18,2},{3,19},{19,3},{4,20},{20... | collective-permute-start | bytes 3145736 | tf_op jit(solution)/shard_map/ppermute | solution.py:1040
  668.0 6.0 copy-start.27
  674.0 200.5 %reduce-scatter.14.cloned.1.call-start = ((), (), s32[]{:S(2)}) async-start(), calls=%async_computation.14 | async-start | bytes 3932160 | tf_op jit(solution)/shard_map/reduce_scatter | solution.py:1043
  674.2 27.6 %copy-start.7 = (f32[768,128]{1,0:T(8,128)S(1)}, f32[768,128]{1,0:T(8,128)}, u32[]{:S(2)}) copy-start(f32[768,128]{1,0:T(8,128)} %copy-done.6) | copy-start | bytes 1179652
  674.2 27.6 %copy-start.9 = (f32[768,128]{1,0:T(8,128)S(1)}, f32[768,128]{1,0:T(8,128)}, u32[]{:S(2)}) copy-start(f32[768,128]{1,0:T(8,128)} %copy-done.8) | copy-start | bytes 1179652
  674.2 27.5 %copy-start.18 = (f32[2,256]{1,0:T(2,128)S(1)}, f32[2,256]{1,0:T(2,128)}, u32[]{:S(2)}) copy-start(f32[2,256]{1,0:T(2,128)} %copy-done.17) | copy-start | bytes 6148
  790.7 83.8 %collective-permute-start.2 = (bf16[512,2048]{1,0:T(8,128)(2,1)}, bf16[512,2048]{1,0:T(8,128)(2,1)}, u32[]{:S(2)}, u32[]{:S(2)}) collective-permute-start(bf16[512,2048]{1,0:T(8,128)(2,1)} %reduce-scatter.10.cloned.1.call-done), channel_id=1, source_target_pairs={{0,16},{16,0},{1,17},{17,1},{2,18},{18,2},{3,19},{19,3},{4,20},{20... | collective-permute-start | bytes 6291464 | tf_op jit(solution)/shard_map/ppermute | solution.py:1040
  801.7 66.5 %copy-start.13 = (f32[768,512]{1,0:T(8,128)S(1)}, f32[768,512]{1,0:T(8,128)}, u32[]{:S(2)}) copy-start(f32[768,512]{1,0:T(8,128)} %copy-done.12) | copy-start | bytes 4718596
  866.3 6.9 copy-start.32
  866.4 6.9 collective-permute-start.4
  869.7 6.5 copy-start.25
  869.7 6.5 copy-start.28
  874.4 17.2 %collective-permute-start.3 = (bf16[512,768]{0,1:T(8,128)(2,1)}, bf16[512,768]{0,1:T(8,128)(2,1)S(1)}, u32[]{:S(2)}, u32[]{:S(2)}) collective-permute-start(bf16[512,768]{0,1:T(8,128)(2,1)} %reduce-scatter.14.cloned.1.call-done), channel_id=1, source_target_pairs={{0,16},{16,0},{1,17},{17,1},{2,18},{18,2},{3,19},{19,3},{4,20},{20... | collective-permute-start | bytes 2359304 | tf_op jit(solution)/shard_map/ppermute | solution.py:1040
  883.9 7.8 copy-start.29
  893.4 2.8 copy-start.15
  893.4 3.6 copy-start.1
  (8 other events, 10.2 us)
Sparse Core Ops, SparseCore 0:
  10.4 66.1 all-gather.5
  78.7 51.6 all-gather.7
  132.6 175.7 all-gather.9
  310.4 45.0 all-gather.13
  357.5 44.4 all-gather.11
  461.0 41.6 reduce-scatter.5
  505.5 42.8 reduce-scatter.7
  550.8 156.3 reduce-scatter.9
  710.0 55.8 reduce-scatter.11
  790.8 60.4 reduce-scatter.13
